TPU v7x, 32 devices: a whole 2x2x4 slice. The times are simulated.
32 devices in a mesh: lon: 2 (over x), lat: 4 (over z), mem: 4 (over y, core).
Axes of the slice: x: 2, y: 2, z: 4, core: 2. Of those that a mesh axis runs over, the one named last changes fastest.
Arguments:
- control: float32 [640, 32, 256], P('mem', 'lat', 'lon'), may hold values from -6 to 6
- residual: float32 [640, 32, 256], P('mem', 'lat', 'lon'), may hold values from -6 to 6
- direction: float32 [640, 32, 256], P('mem', 'lat', 'lon'), may hold values from -6 to 6
- members: bfloat16 [80, 32, 32, 256], P('mem', None, 'lat', 'lon'), may hold values from -0.625 to 0.625
- vert_modes: float32 [8, 32], replicated, may hold values from -2 to 2
- eig_count: int32 [80], P('mem'), may hold values from 1 to 8, as said below
- lon_decay: float32 [32], P('lat'), may hold values from 0.001953125 to 0.125
- lat_decay: float32 [256], P('lon'), may hold values from 0.015625 to 1
- obs_weight: float32 [32, 32, 256], P(None, 'lat', 'lon'), may hold values from 0.25 to 4
Outputs:
- new_control: float32 [640, 32, 256], P('mem', 'lat', 'lon')
- new_residual: float32 [640, 32, 256], P('mem', 'lat', 'lon')
- new_direction: float32 [640, 32, 256], P('mem', 'lat', 'lon')
Inputs may be any that keep to these rules, and one draw needn't show every extreme that they name: Member m uses its first eig_count[m] vertical modes; some member uses all 8.
All inputs are finite; a program needn't handle non-finite values.
Results may differ from a plain program's by a relative error of at most 0.0009.
Values sent between devices are 32-bit elements; how exact they have to be, the bound alone decides.
No kernel may reach another device: no remote copies, remote signals or barrier semaphores. Data moves between devices by JAX's collectives and lax.ppermute only.
A program may use at most 64 MiB of HBM per device.

v0:
```python
import jax
import jax.numpy as jnp
from jax import lax
from jax.sharding import PartitionSpec as P

highest = lax.Precision.HIGHEST


def carried_in(x, axis, combine, identity, reverse):
    count, mine = (lax.axis_size(axis), lax.axis_index(axis))
    everything = jax.tree.map(lambda part: lax.all_gather(part, axis), x)
    start = jax.tree.map(
        lambda part, zero: jnp.broadcast_to(jnp.asarray(zero, part.dtype), part.shape), x, identity
    )

    def step(k, before):
        at = count - 1 - k if reverse else k
        reached = at > mine if reverse else at < mine
        new = combine(before, jax.tree.map(lambda part: part[at], everything))
        return jax.tree.map(lambda a, b: jnp.where(reached, a, b), new, before)

    return lax.fori_loop(0, count, step, start)


def binomial(offset, degree):
    result = jnp.ones_like(offset)
    for factor in range(degree):
        result = result * (offset + factor + 1.0) / (factor + 1.0)
    return result


def transition(decays, length):
    leakage = 1.0 - jnp.exp(-decays)
    closing = jnp.exp(-length * decays)
    zeroes = jnp.zeros_like(decays)
    matrix_rows = []
    for target in range(4):
        entries = []
        for source in range(4):
            if source <= target:
                spread = target - source
                entries.append(
                    binomial(jnp.full_like(decays, length - 1.0), spread)
                    * leakage**spread
                    * closing
                )
            else:
                entries.append(zeroes)
        matrix_rows.append(jnp.stack(entries))
    return jnp.stack(matrix_rows)


def periodic_start(matrix, totals):
    solved = []
    for target in range(4):
        running = totals[target]
        for source in range(target):
            running = running + matrix[target, source] * solved[source]
        solved.append(running / (1.0 - matrix[target, target]))
    return jnp.stack(solved)


def travel_places(length, backward):
    places = jnp.arange(length).astype(jnp.float32)
    if backward:
        places = length - 1.0 - places
    return places


def kernel_table(decays, length, backward):
    leakage = 1.0 - jnp.exp(-decays)
    scaling = 2.5 / jnp.sqrt(leakage)
    places = travel_places(length, backward)
    offsets = places[:, None] - places[None, :]
    lagged = jnp.maximum(offsets, 0.0)
    shaped = binomial(lagged, 3)[None] * jnp.exp(-lagged[None] * decays[:, None, None])
    return jnp.where(offsets[None] >= 0.0, (leakage**4 * scaling)[:, None, None] * shaped, 0.0)


def edge_tables(decays, length, backward):
    leakage = 1.0 - jnp.exp(-decays)
    scaling = 2.5 / jnp.sqrt(leakage)
    places = travel_places(length, backward)
    remain = length - 1.0 - places
    finals = jnp.stack(
        [
            (leakage ** (section_index + 1) * scaling)[:, None]
            * binomial(remain, section_index)[None, :]
            * jnp.exp(-remain[None, :] * decays[:, None])
            for section_index in range(4)
        ]
    )
    entering = jnp.stack(
        [
            (leakage ** (3 - section_index))[:, None]
            * binomial(places, 3 - section_index)[None, :]
            * jnp.exp(-(places[None, :] + 1.0) * decays[:, None])
            for section_index in range(4)
        ],
        axis=2,
    )
    return (finals, entering, transition(decays, length))


def compose(earlier, later):
    matrix = jnp.einsum("kir,ijr->kjr", later[0], earlier[0], precision=highest)
    carried = jnp.einsum("kjr,jfr->kfr", later[0], earlier[1], precision=highest) + later[1]
    return (matrix, carried)


def neutral_of(matrix, carried):
    return (
        jnp.broadcast_to(jnp.eye(4, dtype=jnp.float32)[:, :, None], matrix.shape),
        jnp.zeros_like(carried),
    )


def lon_filter(fields, decays, backward):
    length = fields.shape[2]
    kernel = kernel_table(decays, length, backward)
    finals, entering, matrix = edge_tables(decays, length, backward)
    inside = jnp.einsum("aij,kaj->kai", kernel, fields, precision=highest)
    carried = jnp.einsum("saj,kaj->ska", finals, fields, precision=highest)
    own_block = (matrix, carried)
    neutral = neutral_of(matrix, carried)
    devices_lon = lax.axis_size("lon")
    cycle_matrix = transition(decays, length * devices_lon)
    gathered = (
        lax.all_gather(own_block[0], "lon", axis=0, tiled=True),
        lax.all_gather(own_block[1], "lon", axis=0, tiled=True),
    )
    stacked_matrix = gathered[0].reshape((devices_lon, 4) + matrix.shape[1:])
    stacked_carried = gathered[1].reshape((devices_lon, 4) + carried.shape[1:])
    if backward:
        stacked_matrix = stacked_matrix[::-1]
        stacked_carried = stacked_carried[::-1]

    def fold_step(running, element):
        return (compose(running, element), running)

    totals, prefixes = lax.scan(fold_step, neutral, (stacked_matrix, stacked_carried))
    position = lax.axis_index("lon")
    if backward:
        position = devices_lon - 1 - position
    before = (
        lax.dynamic_index_in_dim(prefixes[0], position, 0, keepdims=False),
        lax.dynamic_index_in_dim(prefixes[1], position, 0, keepdims=False),
    )
    cycle_states = totals[1]
    anchor = periodic_start(cycle_matrix, cycle_states)
    incoming = jnp.einsum("kjr,jfr->kfr", before[0], anchor, precision=highest) + before[1]
    return inside + jnp.einsum("ais,ska->kai", entering, incoming, precision=highest)


def lat_filter(fields, decays, backward):
    length = fields.shape[1]
    kernel = kernel_table(decays, length, backward)
    finals, entering, matrix = edge_tables(decays, length, backward)
    inside = jnp.einsum("cij,kjc->kic", kernel, fields, precision=highest)
    carried = jnp.einsum("scj,kjc->skc", finals, fields, precision=highest)
    own_block = (matrix, carried)
    before = carried_in(own_block, "lat", compose, neutral_of(matrix, carried), backward)
    return inside + jnp.einsum("cis,skc->kic", entering, before[1], precision=highest)


def body(
    control, residual, direction, members, vert_modes, eig_count, lon_decay, lat_decay, obs_weight
):
    mode_count = vert_modes.shape[0]
    member_count = eig_count.shape[0]
    lat_cells = direction.shape[1]
    lon_cells = direction.shape[2]
    active = (jnp.arange(mode_count)[None, :] < eig_count[:, None]).astype(jnp.float32).reshape(-1)
    norm_old = lax.psum(jnp.sum(residual * residual), ("lon", "lat", "mem"))
    smooth = (
        lat_filter(lon_filter(direction, lon_decay, False), lat_decay, False)
        * active[:, None, None]
    )
    weights = smooth.reshape(member_count, mode_count, lat_cells, lon_cells)
    profile = jnp.einsum("el,meyx->mlyx", vert_modes, weights, precision=highest)
    partial_value = jnp.sum(members.astype(jnp.float32) * profile, axis=0)
    increment = lax.psum(partial_value, "mem")
    weighted = obs_weight * increment
    projected = jnp.einsum(
        "el,mlyx->meyx", vert_modes, members.astype(jnp.float32) * weighted[None], precision=highest
    )
    gradient = (
        projected.reshape(member_count * mode_count, lat_cells, lon_cells) * active[:, None, None]
    )
    hessian = direction + lon_filter(lat_filter(gradient, lat_decay, True), lon_decay, True)
    curvature = lax.psum(jnp.sum(direction * hessian), ("lon", "lat", "mem"))
    step_size = norm_old / curvature
    new_control = control + step_size * direction
    new_residual = residual - step_size * hessian
    norm_new = lax.psum(jnp.sum(new_residual * new_residual), ("lon", "lat", "mem"))
    new_direction = new_residual + norm_new / norm_old * direction
    return (new_control, new_residual, new_direction)


def solution(mesh):
    placed = (
        P("mem", "lat", "lon"),
        P("mem", "lat", "lon"),
        P("mem", "lat", "lon"),
        P("mem", None, "lat", "lon"),
        P(),
        P("mem"),
        P("lat"),
        P("lon"),
        P(None, "lat", "lon"),
    )
    return jax.shard_map(
        body,
        mesh=mesh,
        in_specs=placed,
        out_specs=(P("mem", "lat", "lon"), P("mem", "lat", "lon"), P("mem", "lat", "lon")),
        check_vma=False,
    )
```

profile of v0, /device:TPU:0, one launch (start us, length us, event | category | flops | bytes accessed | tf_op | source)
XLA Modules:
  0.0 278.6 jit_solution(5466088829924664988)
XLA Ops:
  9.7 2.2 convolution_bitcast_fusion.13
  12.0 5.5 %all_gather.31 = f32[8,160,8]{1,2,0:T(8,128)S(1)} all-gather(f32[4,160,8]{1,2,0:T(8,128)S(1)} %copy.172), channel_id=1, replica_groups=mesh['lon'=2,'lat'=4,'mem'=4] {'lon'}, dimensions={0}, use_global_device_ids=true | all-gather | bytes 61440 | tf_op jit(solution)/shard_map/all_gather | solution.py:130
  17.7 4.3 %all_gather.30 = f32[8,4,8]{2,1,0:T(4,128)S(1)} all-gather(f32[4,4,8]{2,1,0:T(4,128)S(1)} %pad_maximum_fusion.10), channel_id=1, replica_groups=mesh['lon'=2,'lat'=4,'mem'=4] {'lon'}, dimensions={0}, use_global_device_ids=true | all-gather | bytes 1536 | tf_op jit(solution)/shard_map/all_gather | solution.py:129
  22.1 1.4 while.64
  26.2 1.4 fusion.37
  31.3 14.2 %all-gather = f32[16,4,128]{2,1,0:T(4,128)S(1)} all-gather(f32[4,4,128]{2,1,0:T(4,128)S(1)} %pad_maximum_fusion.11), channel_id=2, replica_groups=mesh['lon'=2,'lat'=4,'mem'=4] {'lat'}, dimensions={0}, use_global_device_ids=true | all-gather | bytes 40960 | tf_op jit(solution)/shard_map/all_gather | solution.py:11
  45.4 1.3 copy.185
  48.5 2.2 fusion.54
  50.7 15.1 %all-gather.6.cloned.1.call-done = f32[16,160,128]{2,1,0:T(8,128)} async-done(((f32[4,160,128]{2,1,0:T(8,128)}), f32[16,160,128]{2,1,0:T(8,128)}) %all-gather.6.cloned.1.call-update) | async-done | bytes 1310736 | tf_op jit(solution)/shard_map/all_gather | solution.py:11
  65.8 14.1 %while.65 = (s32[]{:T(128)}, f32[4,160,128]{1,0,2:T(4,128)S(1)}, s32[]{:T(128)}, f32[4,4,4,128]{2,1,3,0:T(4,128)}, f32[4,4,160,128]{3,2,1,0:T(8,128)}, /*index=5*/s32[]{:T(128)}, s32[]{:T(128)}) while((s32[]{:T(128)}, f32[4,160,128]{1,0,2:T(4,128)S(1)}, s32[]{:T(128)}, f32[4,4,4,128]{2,1,3,0:T(4,128)}, ...), condition=%wide.region_5.6_spmd.clone, body=%wide.region_4.5_spmd.clone.sunk | while | flops 4259844 | bytes 4130915 | solution.py:22
  67.2 2.2 fusion.228
  70.7 2.2 fusion.228
  74.2 2.2 fusion.228
  77.7 2.2 fusion.228
  79.9 1.9 fusion.32
  81.9 1.4 copy.188
  83.3 4.1 %fusion.28 = f32[32,8,128]{2,0,1:T(8,128)} fusion(bf16[20,32,8,128]{3,2,1,0:T(8,128)(2,1)S(1)} %copy-done.6, f32[20,8,8,128]{3,2,1,0:T(8,128)} %bitcast.251, f32[8,32]{1,0:T(8,128)S(1)} %copy-done), kind=kOutput, calls=%fused_computation.46 | convolution fusion | flops 64847872 | bytes 2098176 | tf_op jit(solution)/shard_map/el,meyx->mlyx/dot_general | solution.py:180
  87.9 30.4 %all-reduce.3.cloned.1.call-done = f32[32,8,128]{2,0,1:T(8,128)} async-done(((f32[32,8,128]{2,0,1:T(8,128)}), f32[32,8,128]{2,0,1:T(8,128)}) %all-reduce.3.cloned.1.call-update) | async-done | bytes 131088 | tf_op jit(solution)/shard_map/psum | solution.py:182
  119.2 1.6 fusion.34
  125.8 2.2 fusion.48
  128.0 28.5 %all-gather.8.cloned.1.call-done = f32[16,160,128]{2,1,0:T(8,128)} async-done(((f32[4,160,128]{2,1,0:T(8,128)}), f32[16,160,128]{2,1,0:T(8,128)}) %all-gather.8.cloned.1.call-update) | async-done | bytes 1310736 | tf_op jit(solution)/shard_map/all_gather | solution.py:11
  156.5 14.1 %while.66 = (s32[]{:T(128)}, f32[4,160,128]{1,0,2:T(4,128)S(1)}, s32[]{:T(128)}, f32[4,4,4,128]{2,1,3,0:T(4,128)}, f32[4,4,160,128]{3,2,1,0:T(8,128)}, /*index=5*/s32[]{:T(128)}, s32[]{:T(128)}, s32[]{:T(128)}, s32[]{:T(128)}) while((s32[]{:T(128)}, f32[4,160,128]{1,0,2:T(4,128)S(1)}, s32[]{:T(128)}, f32[4,4,4,128]{2,1,3,0:T(4,128)}, ...), condition=%wide.region_9.10_spmd.clone, body=%wide.region_8.9_spmd.clone.sunk | while | flops 4259848 | bytes 4130977 | solution.py:22
  157.9 2.2 fusion.231
  161.4 2.2 fusion.231
  164.9 2.2 fusion.231
  168.4 2.2 fusion.231
  170.6 2.2 fusion.30
  174.7 4.8 %all_gather.38 = f32[8,160,8]{1,2,0:T(8,128)S(1)} all-gather(f32[4,160,8]{1,2,0:T(8,128)S(1)} %copy.202), channel_id=1, replica_groups=mesh['lon'=2,'lat'=4,'mem'=4] {'lon'}, dimensions={0}, use_global_device_ids=true | all-gather | bytes 61440 | tf_op jit(solution)/shard_map/all_gather | solution.py:130
  179.7 1.4 while.67
  183.0 2.0 multiply_reduce_fusion.1
  185.0 39.8 %all-reduce = (f32[]{:T(128)}, f32[]{:T(128)}) all-reduce(f32[]{:T(128)} %multiply_reduce_fusion.2, f32[]{:T(128)} %get-tuple-element.655), channel_id=1, replica_groups=mesh['lon'=2,'lat'=4,'mem'=4] {'lon','lat','mem'}, use_global_device_ids=true, to_apply=%region_1.0 | all-reduce | flops 2 | bytes 16 | tf_op jit(solution)/shard_map/psum | solution.py:174
  227.0 39.9 %psum.31 = f32[]{:T(128)} all-reduce(f32[]{:T(128)} %get-tuple-element.549), channel_id=1, replica_groups=mesh['lon'=2,'lat'=4,'mem'=4] {'lon','lat','mem'}, use_global_device_ids=true, to_apply=%region_15.16 | all-reduce | flops 1 | bytes 8 | tf_op jit(solution)/shard_map/psum | solution.py:195
  (267 shorter events, 37.9 us)
Async XLA Ops:
  7.2 76.1 %copy-start = (f32[8,32]{1,0:T(8,128)S(1)}, f32[8,32]{1,0:T(8,128)}, u32[]{:S(2)}) copy-start(f32[8,32]{1,0:T(8,128)} %param.21) | copy-start | bytes 3076
  7.2 58.7 %all-gather.6.cloned.1.call-start = ((), (), s32[]{:S(2)}) async-start(), calls=%async_computation.1 | async-start | bytes 1638400 | tf_op jit(solution)/shard_map/all_gather | solution.py:11
  8.4 17.7 %copy-start.20 = (f32[8]{0:T(128)}, f32[8]{0:T(128)S(1)}, u32[]{:S(2)}) copy-start(f32[8]{0:T(128)S(1)} %get-tuple-element.642) | copy-start | bytes 100
  22.1 2.0 copy-start.16
  22.1 4.1 %copy-start.1 = (f32[160,8,128]{2,1,0:T(8,128)S(1)}, f32[160,8,128]{2,1,0:T(8,128)}, u32[]{:S(2)}) copy-start(f32[160,8,128]{2,1,0:T(8,128)} %param.19) | copy-start | bytes 1966084
  23.5 2.6 copy-start.8
  23.7 2.4 copy-start.22
  23.7 2.4 copy-start.24
  23.7 2.4 copy-start.26
  23.7 2.4 copy-start.28
  23.7 2.4 copy-start.30
  23.7 2.4 copy-start.32
  23.7 2.4 copy-start.34
  23.7 2.4 copy-start.36
  23.8 2.4 copy-start.38
  23.8 2.4 copy-start.40
  28.2 20.3 %copy-start.18 = (f32[128]{0:T(128)}, f32[128]{0:T(128)S(1)}, u32[]{:S(2)}) copy-start(f32[128]{0:T(128)S(1)} %get-tuple-element.635) | copy-start | bytes 1540
  30.1 17.5 %copy-start.42 = (s32[20]{0:T(128)S(1)}, s32[20]{0:T(128)}, u32[]{:S(2)}) copy-start(s32[20]{0:T(128)} %param.22) | copy-start | bytes 244
  31.1 87.2 %all-reduce.3.cloned.1.call-start = ((), (), s32[]{:S(2)}) async-start(), calls=%async_computation | async-start | bytes 262144 | tf_op jit(solution)/shard_map/psum | solution.py:182
  65.8 14.1 %copy-start.2 = (f32[128,160,8]{1,2,0:T(8,128)S(1)}, f32[128,160,8]{1,2,0:T(8,128)}, u32[]{:S(2)}) copy-start(f32[128,160,8]{1,2,0:T(8,128)} %fusion.54) | copy-start | bytes 1966084
  83.3 4.5 %copy-start.13 = (f32[4,128,8]{1,2,0:T(8,128)S(1)}, f32[4,128,8]{1,2,0:T(8,128)}, u32[]{:S(2)}) copy-start(f32[4,128,8]{1,2,0:T(8,128)} %get-tuple-element.666) | copy-start | bytes 49156
  83.3 35.0 %copy-start.10 = (f32[32,8,128]{2,1,0:T(8,128)S(1)}, f32[32,8,128]{2,1,0:T(8,128)}, u32[]{:S(2)}) copy-start(f32[32,8,128]{2,1,0:T(8,128)} %param.25) | copy-start | bytes 393220
  87.4 69.1 %all-gather.8.cloned.1.call-start = ((), (), s32[]{:S(2)}) async-start(), calls=%async_computation.2 | async-start | bytes 1638400 | tf_op jit(solution)/shard_map/all_gather | solution.py:11
  121.8 2.1 copy-start.9
  121.8 2.1 copy-start.14
  121.8 2.9 %copy-start.4 = (f32[160,8,128]{2,1,0:T(8,128)S(1)}, f32[160,8,128]{2,1,0:T(8,128)}, u32[]{:S(2)}) copy-start(f32[160,8,128]{2,1,0:T(8,128)} %param.18) | copy-start | bytes 1966084
  122.8 3.0 %copy-start.19 = (f32[128]{0:T(128)S(1)}, f32[128]{0:T(128)}, u32[]{:S(2)}) copy-start(f32[128]{0:T(128)} %copy-done.18) | copy-start | bytes 1540
  156.5 14.1 %copy-start.3 = (f32[128,160,8]{1,2,0:T(8,128)S(1)}, f32[128,160,8]{1,2,0:T(8,128)}, u32[]{:S(2)}) copy-start(f32[128,160,8]{1,2,0:T(8,128)} %fusion.48) | copy-start | bytes 1966084
  179.7 2.0 copy-start.21
  181.1 1.9 copy-start.11
  183.0 43.1 %copy-start.5 = (f32[160,8,128]{2,1,0:T(8,128)S(1)}, f32[160,8,128]{2,1,0:T(8,128)}, u32[]{:S(2)}) copy-start(f32[160,8,128]{2,1,0:T(8,128)} %param.18) | copy-start | bytes 1966084
  226.2 43.3 %copy-start.7 = (f32[160,8,128]{2,1,0:T(8,128)S(1)}, f32[160,8,128]{2,1,0:T(8,128)}, u32[]{:S(2)}) copy-start(f32[160,8,128]{2,1,0:T(8,128)} %param.17) | copy-start | bytes 1966084
  (14 other events, 20.9 us)
Sparse Core Ops, SparseCore 0:
  31.2 34.5 all-gather.5
  87.6 30.6 all-reduce.2
  124.0 32.5 all-gather.7
where the time goes:
time: 280 us; the launch traced here: 279 us
  blocking collectives  109 us (39%)
  waiting for transfers between devices  74.1 us (26%)
  matrix products  45 us (16%)
  local copies, waits for them, and re-layouts  24 us (9%)
  between operations  17.5 us (6%)
  other arithmetic  8.48 us (3%)
    all_gather x2, waiting for transfers between devices, carried_in(): everything = jax.tree.map(lambda part: lax.all_gather(part, axis), x)  43.6 us
    psum x1, blocking collectives, body(): lax.psum(jnp.sum(new_residual * new_residual), ('lon', 'lat', 'mem'))  39.9 us
    psum x1, blocking collectives, body(): norm_old = lax.psum(jnp.sum(residual * residual), ('lon', 'lat', 'mem'))  39.8 us
    psum x1, waiting for transfers between devices, body(): increment = lax.psum(partial_value, 'mem')  30.4 us
    dot_general x12, matrix products, compose(): jnp.einsum('kjr,jfr->kfr', later[0], earlier[1], precision=highest)  18.3 us
    all_gather x1, blocking collectives, carried_in(): everything = jax.tree.map(lambda part: lax.all_gather(part, axis), x)  14.2 us
    all_gather x2, blocking collectives, lon_filter(): lax.all_gather(own_block[1], 'lon', axis=0, tiled=True)  10.4 us
    dynamic_slice x16, local copies, waits for them, and re-layouts, step(): new = combine(before, jax.tree.map(lambda part: part[at], everything))  10 us
  transfers between devices with their start and end apart: 3, of which 3 were waited for; matrix products, arithmetic and copies ran while one was open for 3% of the time, Pallas kernels for 0%

commit v1 on v0

v1 whole, which is shorter than its diff:
```python
import functools
import jax
import jax.numpy as jnp
from jax import lax
from jax.experimental import pallas as pl
from jax.experimental.pallas import tpu as pltpu
from jax.sharding import PartitionSpec as P

f32 = jnp.float32
VM = pl.BlockSpec(memory_space=pltpu.VMEM)
SM = pl.BlockSpec(memory_space=pltpu.SMEM)
HI = lax.Precision.HIGHEST


def choose(length, i):
    r = 1.0
    for k in range(i):
        r = r * (length + k) / (k + 1)
    return r


def rising(v, degree):
    r = jnp.ones_like(v)
    for k in range(degree):
        r = r * (v + (k + 1.0)) * (1.0 / (k + 1.0))
    return r


def mm(a, b, dims):
    return lax.dot_general(a, b, (dims, ((), ())), precision=HI, preferred_element_type=f32)


def iota(shape, dim):
    return lax.broadcasted_iota(jnp.int32, shape, dim).astype(f32)


def lon_consts(dec_ref, cells):
    c = jnp.broadcast_to(dec_ref[...], (dec_ref.shape[0], cells))
    q = jnp.exp(-c)
    leak = 1.0 - q
    return c, leak, 2.5 / jnp.sqrt(leak)


def lon_kernel_matrix(c_row, gain_row, cells, backward):
    a = iota((cells, cells), 0)
    b = iota((cells, cells), 1)
    lag = a - b if backward else b - a
    pos = jnp.maximum(lag, 0.0)
    shaped = rising(pos, 3) * jnp.exp(-pos * c_row) * gain_row
    return jnp.where(lag >= 0.0, shaped, 0.0)


def masked_rows(parts, y):
    rows = iota(parts[0].shape, 0)
    return jnp.concatenate([jnp.where(rows == float(y), p, 0.0) for p in parts], axis=0)


def lon_finals(c, leak, scale, cells, backward):
    x = iota(c.shape, 1)
    remain = x if backward else (cells - 1.0) - x
    decay = jnp.exp(-remain * c)
    return [leak ** (s + 1) * scale * rising(remain, s) * decay for s in range(4)]


def lon_entering(c, leak, cells, backward):
    x = iota(c.shape, 1)
    place = (cells - 1.0) - x if backward else x
    decay = jnp.exp(-(place + 1.0) * c)
    return [leak ** (3 - s) * rising(place, 3 - s) * decay for s in range(4)]


def lon_local_rows(load_row, dec_ref, rows, cells, backward, inside_ref, carried_ref):
    c, leak, scale = lon_consts(dec_ref, cells)
    gain = leak**4 * scale
    finals = lon_finals(c, leak, scale, cells, backward)
    carried = None
    for y in range(rows):
        f = load_row(y)
        table = lon_kernel_matrix(c[y : y + 1], gain[y : y + 1], cells, backward)
        inside_ref[y] = mm(f, table, ((1,), (0,)))
        part = mm(masked_rows(finals, y), f, ((1,), (1,)))
        carried = part if carried is None else carried + part
    carried_ref[...] = carried


def lon_incoming(dec_ref, own, others, rows):
    count = len(others) + 1
    k = own.shape[1]
    return count, k


def lon_incoming_states(dec_ref, blocks, rows, cells):
    k = blocks[0].shape[1]
    n = len(blocks)
    c = jnp.broadcast_to(dec_ref[...], (rows, k))
    leak = 1.0 - jnp.exp(-c)

    def trans(r):
        closing = jnp.exp(-float(r * cells) * c)
        return [choose(r * cells, i) * leak**i * closing for i in range(4)]

    total = [jnp.zeros((rows, k), f32) for _ in range(4)]
    for r in range(n):
        part = [blocks[r][s * rows : (s + 1) * rows] for s in range(4)]
        if r:
            t = trans(r)
            part = [sum(t[i - j] * part[j] for j in range(i + 1)) for i in range(4)]
        total = [a + b for a, b in zip(total, part)]
    t = trans(n)
    solved = []
    for i in range(4):
        v = total[i]
        for j in range(i):
            v = v + t[i - j] * solved[j]
        solved.append(v / (1.0 - t[0]))
    return jnp.concatenate(solved, axis=0)


def lon_correction(states_t, entering, y):
    return mm(states_t, masked_rows(entering, y), ((1,), (0,)))


def lat_consts(dec_ref):
    q = jnp.exp(-dec_ref[...])
    leak = 1.0 - q
    return q, leak, leak * (2.5 / jnp.sqrt(leak))


def lat_sweep(load, store, start, dec_ref, rows, k, backward, block):
    q1, l1, g1 = lat_consts(dec_ref)
    x = dec_ref.shape[1]
    q = jnp.broadcast_to(q1, (block, x))
    leak = jnp.broadcast_to(l1, (block, x))
    gain = jnp.broadcast_to(g1, (block, x))
    order = range(rows - 1, -1, -1) if backward else range(rows)

    def step(i, carry):
        at = pl.ds(pl.multiple_of(i * block, 8), block)
        u = start(at)
        for y in order:
            feed = gain * load(y, at, i * block)
            u0 = q * u[0] + feed
            u1 = q * u[1] + leak * u0
            u2 = q * u[2] + leak * u1
            u3 = q * u[3] + leak * u2
            u = [u0, u1, u2, u3]
            store(y, at, i * block, u3, u if y == order[-1] else None)
        return carry

    lax.fori_loop(0, k // block, step, 0)


def k_lon_fwd(rows, k, cells, d_ref, dec_ref, inside_ref, carried_ref):
    lon_local_rows(
        lambda y: d_ref[pl.ds(y, k, stride=rows), :], dec_ref, rows, cells, False, inside_ref, carried_ref
    )


def k_lat_first(rows, k, cells, n, *refs):
    inside_ref, lon_ref, lat_ref, *rest = refs
    blocks = [r[...] for r in rest[:n]]
    f_ref, lat_carried_ref = rest[n:]
    states = lon_incoming_states(lon_ref, blocks, rows, cells).T
    c, leak, _ = lon_consts(lon_ref, cells)
    entering = lon_entering(c, leak, cells, False)
    for y in range(rows):
        f_ref[y] = inside_ref[y] + lon_correction(states, entering, y)
    zero = jnp.zeros((8, cells), f32)

    def store(y, at, base, value, last):
        if last is not None:
            for s in range(4):
                lat_carried_ref[s, at, :] = last[s]

    lat_sweep(
        lambda y, at, base: f_ref[y, at, :], store, lambda at: [zero] * 4, lat_ref, rows, k, False, 8
    )


def k_pass_on(rows, carried_ref, got_ref, dec_ref, out_ref):
    c = dec_ref[...]
    leak = 1.0 - jnp.exp(-c)
    closing = jnp.exp(-float(rows) * c)
    t = [choose(rows, i) * leak**i * closing for i in range(4)]
    got = [got_ref[s] for s in range(4)]
    for i in range(4):
        v = carried_ref[i]
        for j in range(i + 1):
            v = v + t[i - j] * got[j]
        out_ref[i] = v


def sum_states(parts):
    def at_state(s, at):
        v = parts[0][s, at, :]
        for p in parts[1:]:
            v = v + p[s, at, :]
        return v

    return at_state


def member_blocks(members):
    for size in (4, 5, 2, 1):
        if members % size == 0:
            return size


def k_increment(rows, k, chunks, hops, members, modes, levels, *refs):
    f_ref, lat_ref, m_ref, v_ref, eig_ref, *rest = refs
    got = rest[: chunks * hops]
    inc_ref, s_ref = rest[chunks * hops :]
    cells = lat_ref.shape[1]
    size = k // chunks
    for ch in range(chunks):
        at_state = sum_states(got[ch * hops : (ch + 1) * hops])

        def load(y, at, base, ch=ch):
            return f_ref[y, pl.ds(pl.multiple_of(ch * size + base, 8), 8), :]

        def store(y, at, base, value, last, ch=ch):
            s_ref[pl.ds((ch * size + base) * rows + y, 8, stride=rows), :] = value

        lat_sweep(load, store, lambda at: [at_state(s, at) for s in range(4)], lat_ref, rows, size, False, 8)

    per = member_blocks(members)
    for b in range(members // per):
        fields = []
        for m in range(per):
            count = eig_ref[b * per + m]
            for e in range(modes):
                scale = jnp.where(e < count, 1.0, 0.0).astype(f32)
                at = ((b * per + m) * modes + e) * rows
                fields.append(s_ref[at : at + rows, :] * scale)

        def level(l, carry, b=b, fields=fields):
            total = None
            for m in range(per):
                p = None
                for e in range(modes):
                    t = v_ref[e, l] * fields[m * modes + e]
                    p = t if p is None else p + t
                p = m_ref[b * per + m, l].astype(f32) * p
                total = p if total is None else total + p
            if b == 0:
                inc_ref[l] = total
            else:
                inc_ref[l] += total
            return carry

        lax.fori_loop(0, levels, level, 0, unroll=4)


def k_gradient(rows, k, cells, members, modes, levels, inc_ref, got_ref, obs_ref, m_ref, v_ref, eig_ref, lat_ref, g_ref, carried_ref, w_ref):
    w_ref[...] = (inc_ref[...] + got_ref[...]) * obs_ref[...]
    per = member_blocks(members)
    for b in range(members // per):

        def level(l, acc, b=b):
            w = w_ref[l]
            vs = [v_ref[e, l] for e in range(modes)]
            out = []
            for m in range(per):
                t = m_ref[b * per + m, l].astype(f32) * w
                for e in range(modes):
                    out.append(acc[m * modes + e] + vs[e] * t)
            return tuple(out)

        zero = jnp.zeros((rows, cells), f32)
        acc = lax.fori_loop(0, levels, level, (zero,) * (per * modes), unroll=4)
        for m in range(per):
            count = eig_ref[b * per + m]
            for e in range(modes):
                scale = jnp.where(e < count, 1.0, 0.0).astype(f32)
                at = ((b * per + m) * modes + e) * rows
                g_ref[at : at + rows, :] = acc[m * modes + e] * scale
    zero8 = jnp.zeros((8, cells), f32)

    def store(y, at, base, value, last):
        if last is not None:
            for s in range(4):
                carried_ref[s, at, :] = last[s]

    lat_sweep(
        lambda y, at, base: g_ref[pl.ds(base * rows + y, 8, stride=rows), :],
        store,
        lambda at: [zero8] * 4,
        lat_ref,
        rows,
        k,
        True,
        8,
    )


def k_lon_bwd(rows, k, cells, chunks, hops, *refs):
    g_ref, lat_ref, lon_ref, *rest = refs
    got = rest[: chunks * hops]
    inside_ref, carried_ref, p_ref = rest[chunks * hops :]
    size = k // chunks
    for ch in range(chunks):
        at_state = sum_states(got[ch * hops : (ch + 1) * hops])

        def load(y, at, base, ch=ch):
            return g_ref[pl.ds((ch * size + base) * rows + y, 8, stride=rows), :]

        def store(y, at, base, value, last, ch=ch):
            p_ref[y, pl.ds(pl.multiple_of(ch * size + base, 8), 8), :] = value

        lat_sweep(load, store, lambda at: [at_state(s, at) for s in range(4)], lat_ref, rows, size, True, 8)
    lon_local_rows(lambda y: p_ref[y], lon_ref, rows, cells, True, inside_ref, carried_ref)


def k_sums(rows, k, cells, n, *refs):
    inside_ref, lon_ref, d_ref, r_ref, *rest = refs
    blocks = [r[...] for r in rest[:n]]
    h_ref, sums_ref = rest[n:]
    states = lon_incoming_states(lon_ref, blocks, rows, cells).T
    c, leak, _ = lon_consts(lon_ref, cells)
    entering = lon_entering(c, leak, cells, True)
    for y in range(rows):
        at = pl.ds(y, k, stride=rows)
        h_ref[at, :] = inside_ref[y] + lon_correction(states, entering, y)
    block = 64
    zero = jnp.zeros((8, cells), f32)

    def step(i, acc):
        at = pl.ds(pl.multiple_of(i * block, 8), block)
        d = d_ref[at, :]
        r = r_ref[at, :]
        h = h_ref[at, :] + d
        h_ref[at, :] = h
        fold = lambda v: v.reshape(block // 8, 8, cells).sum(axis=0)
        return (acc[0] + fold(r * r), acc[1] + fold(d * h), acc[2] + fold(r * h), acc[3] + fold(h * h))

    acc = lax.fori_loop(0, (k * rows) // block, step, (zero,) * 4)
    out = [a.sum(axis=0, keepdims=True) for a in acc]
    sums_ref[...] = jnp.concatenate(out + [jnp.zeros((4, cells), f32)], axis=0)


def k_update(sums_ref, control_ref, r_ref, d_ref, h_ref, nc_ref, nr_ref, nd_ref):
    sums = jnp.sum(sums_ref[...], axis=1, keepdims=True)
    rr, dh, rh, hh = (sums[i : i + 1, :] for i in range(4))
    step = rr / dh
    norm_new = rr - 2.0 * step * rh + step * step * hh
    beta = norm_new / rr
    d = d_ref[...]
    nr = r_ref[...] - step * h_ref[...]
    nc_ref[...] = control_ref[...] + step * d
    nr_ref[...] = nr
    nd_ref[...] = nr + beta * d


def call(body, outs, ins, specs=None, scratch=(), name=None, cost=None):
    return pl.pallas_call(
        body,
        out_shape=outs,
        in_specs=specs or [VM] * len(ins),
        out_specs=jax.tree.map(lambda _: VM, outs),
        scratch_shapes=scratch,
        name=name,
        cost_estimate=cost,
        compiler_params=pltpu.CompilerParams(vmem_limit_bytes=56 * 1024 * 1024),
    )(*ins)


def sds(*shape):
    return jax.ShapeDtypeStruct(shape, f32)


def lon_exchange(carried, backward):
    n = lax.axis_size("lon")
    sign = -1 if backward else 1
    got = [
        lax.ppermute(carried, "lon", [(j, (j + sign * r) % n) for j in range(n)]) for r in range(1, n)
    ]
    return got + [carried]


def lat_chain(carried, lat_dec, rows, chunks, backward):
    n = lax.axis_size("lat")
    size = carried.shape[1] // chunks
    cells = carried.shape[2]
    parts = [carried[:, c * size : (c + 1) * size] for c in range(chunks)]
    sends = list(parts)
    got = [[] for _ in range(chunks)]
    for h in range(n - 1):
        pair = (n - 1 - h, n - 2 - h) if backward else (h, h + 1)
        for c in range(chunks):
            if h:
                sends[c] = call(
                    functools.partial(k_pass_on, rows),
                    sds(4, size, cells),
                    [parts[c], got[c][-1], lat_dec],
                    name="pass_on",
                )
            got[c].append(lax.ppermute(sends[c], "lat", [pair]))
    return [g for c in range(chunks) for g in got[c]]


def butterfly(v, axis):
    n = lax.axis_size(axis)
    d = 1
    while d < n:
        v = v + lax.ppermute(v, axis, [(i, i ^ d) for i in range(n)])
        d *= 2
    return v


def body(control, residual, direction, members, vert_modes, eig_count, lon_decay, lat_decay, obs_weight):
    k, rows, cells = direction.shape
    mcount, levels = members.shape[:2]
    modes = vert_modes.shape[0]
    n_lon, n_lat, n_mem = (lax.axis_size(a) for a in ("lon", "lat", "mem"))
    chunks = 2
    hops = n_lat - 1
    flat = lambda v: v.reshape(k * rows, cells)
    d, r, ctl = flat(direction), flat(residual), flat(control)
    lon_dec = lon_decay.reshape(rows, 1)
    lat_dec = lat_decay.reshape(1, cells)

    inside, carried = call(
        functools.partial(k_lon_fwd, rows, k, cells),
        (sds(rows, k, cells), sds(4 * rows, k)),
        [d, lon_dec],
        name="lon_fwd",
    )
    blocks = lon_exchange(carried, False)
    f, lat_carried = call(
        functools.partial(k_lat_first, rows, k, cells, n_lon),
        (sds(rows, k, cells), sds(4, k, cells)),
        [inside, lon_dec, lat_dec, *blocks],
        name="lat_first",
    )
    got = lat_chain(lat_carried, lat_dec, rows, chunks, False)
    inc = call(
        functools.partial(k_increment, rows, k, chunks, hops, mcount, modes, levels),
        sds(levels, rows, cells),
        [f, lat_dec, members, vert_modes, eig_count, *got],
        specs=[VM, VM, VM, SM, SM] + [VM] * len(got),
        scratch=[pltpu.VMEM((k * rows, cells), f32)],
        name="increment",
    )
    step = 1
    while step * 2 < n_mem:
        inc = inc + lax.ppermute(inc, "mem", [(i, i ^ step) for i in range(n_mem)])
        step *= 2
    other = lax.ppermute(inc, "mem", [(i, i ^ step) for i in range(n_mem)])
    g, lat_carried = call(
        functools.partial(k_gradient, rows, k, cells, mcount, modes, levels),
        (sds(k * rows, cells), sds(4, k, cells)),
        [inc, other, obs_weight, members, vert_modes, eig_count, lat_dec],
        specs=[VM, VM, VM, VM, SM, SM, VM],
        scratch=[pltpu.VMEM((levels, rows, cells), f32)],
        name="gradient",
    )
    got = lat_chain(lat_carried, lat_dec, rows, chunks, True)
    inside, carried = call(
        functools.partial(k_lon_bwd, rows, k, cells, chunks, hops),
        (sds(rows, k, cells), sds(4 * rows, k)),
        [g, lat_dec, lon_dec, *got],
        scratch=[pltpu.VMEM((rows, k, cells), f32)],
        name="lon_bwd",
    )
    blocks = lon_exchange(carried, True)
    h, sums = call(
        functools.partial(k_sums, rows, k, cells, n_lon),
        (sds(k * rows, cells), sds(8, cells)),
        [inside, lon_dec, d, r, *blocks],
        name="sums",
    )
    for axis in ("mem", "lon", "lat"):
        sums = butterfly(sums, axis)
    outs = call(
        k_update,
        (sds(k * rows, cells),) * 3,
        [sums, ctl, r, d, h],
        name="update",
    )
    return tuple(o.reshape(k, rows, cells) for o in outs)


def solution(mesh):
    field = P("mem", "lat", "lon")
    placed = (
        field,
        field,
        field,
        P("mem", None, "lat", "lon"),
        P(),
        P("mem"),
        P("lat"),
        P("lon"),
        P(None, "lat", "lon"),
    )
    return jax.shard_map(body, mesh=mesh, in_specs=placed, out_specs=(field,) * 3, check_vma=False)
```

time: 280 us -> 132 us (0.47)
  blocking collectives: 109 us -> 0 us
  matrix products: 45 us -> 0 us
  Pallas kernels: 0 us -> 43.1 us
  waiting for transfers between devices: 74.1 us -> 51.3 us
  starting transfers between devices: 0.34 us -> 22.3 us
  between operations: 17.5 us -> 0.97 us
  local copies, waits for them, and re-layouts: 24 us -> 11.9 us
  other arithmetic: 8.48 us -> 2.22 us
    psum x2 -> x0, blocking collectives: 79.7 us -> none  [the longest x1 39.9 us: body(): lax.psum(jnp.sum(new_residual * new_residual), ('lon', 'lat', 'mem'))]
    ppermute x0 -> x21, waiting for transfers between devices: none -> 51.3 us  [the longest x12 27.3 us: lat_chain(): got[c].append(lax.ppermute(sends[c], 'lat', [pair]))]
    dot_general x32 -> x0, matrix products: 45 us -> none  [the longest x12 18.3 us: compose(): jnp.einsum('kjr,jfr->kfr', later[0], earlier[1], precision=highest)]
    all_gather x2 -> x0, waiting for transfers between devices: 43.6 us -> none  [carried_in(): everything = jax.tree.map(lambda part: lax.all_gather(part, axis), x)]
    pallas_call x0 -> x15, Pallas kernels: none -> 43.1 us  [call(): pl.pallas_call(body, out_shape=outs, in_specs=specs or [VM] * len(ins), o...]
    psum x1 -> x0, waiting for transfers between devices: 30.4 us -> none  [body(): increment = lax.psum(partial_value, 'mem')]
    all_gather x4 -> x0, blocking collectives: 28.9 us -> none  [the longest x1 14.2 us: carried_in(): everything = jax.tree.map(lambda part: lax.all_gather(part, axis), x)]
    ppermute x0 -> x21, starting transfers between devices: none -> 22.3 us  [the longest x12 13.2 us: lat_chain(): got[c].append(lax.ppermute(sends[c], 'lat', [pair]))]
  transfers between devices with their start and end apart: 3 -> 21, of which waited for: 3 -> 12; matrix products, arithmetic and copies ran while one was open for 3% -> 0% of each run, Pallas kernels for 0% -> 10%
where the time goes in v1:
time: 132 us
  waiting for transfers between devices  51.3 us (39%)
  Pallas kernels  43.1 us (33%)
  starting transfers between devices  22.3 us (17%)
  local copies, waits for them, and re-layouts  11.9 us (9%)
  other arithmetic  2.22 us (2%)
    pallas_call x15, Pallas kernels, call(): pl.pallas_call(body, out_shape=outs, in_specs=specs or [VM] * len(ins), o...  43.1 us
    ppermute x12, waiting for transfers between devices, lat_chain(): got[c].append(lax.ppermute(sends[c], 'lat', [pair]))  27.3 us
    ppermute x5, waiting for transfers between devices, butterfly(): v = v + lax.ppermute(v, axis, [(i, i ^ d) for i in range(n)])  13.7 us
    ppermute x12, starting transfers between devices, lat_chain(): got[c].append(lax.ppermute(sends[c], 'lat', [pair]))  13.2 us
    unnamed x40, local copies, waits for them, and re-layouts  8.55 us
    ppermute x2, waiting for transfers between devices, lon_exchange(): lax.ppermute(carried, 'lon', [(j, (j + sign * r) % n) for j in range(n)])  4.73 us
    ppermute x2, starting transfers between devices, lon_exchange(): lax.ppermute(carried, 'lon', [(j, (j + sign * r) % n) for j in range(n)])  4.46 us
    ppermute x1, waiting for transfers between devices, body(): other = lax.ppermute(inc, 'mem', [(i, i ^ step) for i in range(n_mem)])  4.03 us
  transfers between devices with their start and end apart: 21, of which 12 were waited for; matrix products, arithmetic and copies ran while one was open for 0% of the time, Pallas kernels for 10%

profile of v1, /device:TPU:0, one launch (start us, length us, event | category | flops | bytes accessed | tf_op | source)
XLA Modules:
  0.0 131.7 jit_solution(2129629298586102469)
XLA Ops:
  1.9 3.8 %lon_fwd.1 = (f32[8,160,128]{2,1,0:T(8,128)}, f32[32,160]{1,0:T(8,128)}) custom-call(f32[1280,128]{1,0:T(8,128)} %bitcast.8, f32[8,1]{1,0:T(8,128)} %copy.12.dec_ref.refs_1_.refs_2_), custom_call_target="tpu_custom_call" | custom-call | tf_op jit(solution)/shard_map/lon_fwd/pallas_call | solution.py:355
  5.8 3.0 %collective-permute-start = (f32[32,160]{1,0:T(8,128)}, f32[32,160]{1,0:T(8,128)S(1)}, u32[]{:S(2)}, u32[]{:S(2)}) collective-permute-start(f32[32,160]{1,0:T(8,128)} %get-tuple-element.17.refs_4_), channel_id=1, source_target_pairs={{0,16},{16,0},{1,17},{17,1},{2,18},{18,2},{3,19},{19,3},{4,20},{20... | collective-permute-start | bytes 61448 | tf_op jit(solution)/shard_map/ppermute | solution.py:375
  8.7 2.1 %collective-permute-done.refs_3_ = f32[32,160]{1,0:T(8,128)S(1)} collective-permute-done((f32[32,160]{1,0:T(8,128)}, f32[32,160]{1,0:T(8,128)S(1)}, u32[]{:S(2)}, u32[]{:S(2)}) %collective-permute-start) | collective-permute-done | bytes 20512 | tf_op jit(solution)/shard_map/ppermute | solution.py:375
  11.4 3.4 %lat_first.1 = (f32[8,160,128]{2,1,0:T(8,128)}, f32[4,160,128]{2,1,0:T(8,128)}) custom-call(f32[8,160,128]{2,1,0:T(8,128)} %get-tuple-element.16.refs_0_, f32[8,1]{1,0:T(8,128)} %copy.12.dec_ref.refs_1_.refs_2_, f32[1,128]{1,0:T(1,128)} %bitcast.14, f32[32,160]{1,0:T(8,128)} %copy-done.19, f32[32,160]{1,0:T(8,128)} %get-tuple-element.17.refs_4_), custom_call_target="tpu_custom_call" | custom-call | tf_op jit(solution)/shard_map/lat_first/pallas_call | solution.py:355
  15.9 4.0 %collective-permute-start.4 = (f32[4,80,128]{2,1,0:T(8,128)S(1)}, f32[4,80,128]{2,1,0:T(8,128)S(1)}, u32[]{:S(2)}, u32[]{:S(2)}) collective-permute-start(f32[4,80,128]{2,1,0:T(8,128)S(1)} %get-tuple-element.31.carried_ref), channel_id=1, source_target_pairs={{0,4},{1,5},{2,6},{3,7},{16,20},{17,21},{18,22},{19,23}} | collective-permute-start | bytes 491528 | tf_op jit(solution)/shard_map/ppermute | solution.py:397
  21.2 2.7 %collective-permute-done.4.got_ref.refs_8_ = f32[4,80,128]{2,1,0:T(8,128)S(1)} collective-permute-done((f32[4,80,128]{2,1,0:T(8,128)S(1)}, f32[4,80,128]{2,1,0:T(8,128)S(1)}, u32[]{:S(2)}, u32[]{:S(2)}) %collective-permute-start.4) | collective-permute-done | bytes 163872 | tf_op jit(solution)/shard_map/ppermute | solution.py:397
  24.6 1.7 %pass_on.10 = f32[4,80,128]{2,1,0:T(8,128)} custom-call(f32[4,80,128]{2,1,0:T(8,128)} %copy-done.2, f32[4,80,128]{2,1,0:T(8,128)} %copy-done.4, f32[1,128]{1,0:T(1,128)} %bitcast.15), custom_call_target="tpu_custom_call" | custom-call | tf_op jit(solution)/shard_map/pass_on/pallas_call | solution.py:355
  27.7 1.7 %pass_on.8 = f32[4,80,128]{2,1,0:T(8,128)} custom-call(f32[4,80,128]{2,1,0:T(8,128)} %copy-done, f32[4,80,128]{2,1,0:T(8,128)} %copy-done.5, f32[1,128]{1,0:T(1,128)} %bitcast.16), custom_call_target="tpu_custom_call" | custom-call | tf_op jit(solution)/shard_map/pass_on/pallas_call | solution.py:355
  30.7 1.7 %pass_on.11 = f32[4,80,128]{2,1,0:T(8,128)} custom-call(f32[4,80,128]{2,1,0:T(8,128)} %copy-done.2, f32[4,80,128]{2,1,0:T(8,128)} %copy-done.6, f32[1,128]{1,0:T(1,128)} %bitcast.17), custom_call_target="tpu_custom_call" | custom-call | tf_op jit(solution)/shard_map/pass_on/pallas_call | solution.py:355
  33.7 1.7 %pass_on.9 = f32[4,80,128]{2,1,0:T(8,128)} custom-call(f32[4,80,128]{2,1,0:T(8,128)} %copy-done, f32[4,80,128]{2,1,0:T(8,128)} %copy-done.7, f32[1,128]{1,0:T(1,128)} %bitcast.18), custom_call_target="tpu_custom_call" | custom-call | tf_op jit(solution)/shard_map/pass_on/pallas_call | solution.py:355
  36.9 5.4 %increment.1 = f32[32,8,128]{2,1,0:T(8,128)} custom-call(f32[8,160,128]{2,1,0:T(8,128)} %get-tuple-element.18.refs_0_, f32[1,128]{1,0:T(1,128)} %bitcast.19, bf16[20,32,8,128]{3,2,1,0:T(8,128)(2,1)} %m_ref.1, f32[8,32]{1,0:T(8,128)} %v_ref.1, s32[20]{0:T(128)} %eig_ref.1, f32[4,80,128]{2,1,0:T(8,128)} %copy-done.5, f32[4,80,128]{2,1,0:T(8,128)} %copy-done.7, ...), custom_call_target="tpu_custom_call" | custom-call | tf_op jit(solution)/shard_map/increment/pallas_call | solution.py:355
  42.2 1.6 %collective-permute-done.7 = f32[32,8,128]{2,1,0:T(8,128)S(1)} collective-permute-done((f32[32,8,128]{2,1,0:T(8,128)}, f32[32,8,128]{2,1,0:T(8,128)S(1)}, u32[]{:S(2)}, u32[]{:S(2)}) %collective-permute-start.7) | collective-permute-done | bytes 131104 | tf_op jit(solution)/shard_map/ppermute | solution.py:446
  44.7 1.6 %collective-permute-start.8 = (f32[32,8,128]{2,1,0:T(8,128)S(1)}, f32[32,8,128]{2,1,0:T(8,128)S(1)}, u32[]{:S(2)}, u32[]{:S(2)}) collective-permute-start(f32[32,8,128]{2,1,0:T(8,128)S(1)} %add.18.inc_ref), channel_id=1, source_target_pairs={{0,2},{1,3},{2,0},{3,1},{4,6},{5,7},{6,4},{7,5},{8,10},{9,11},{10,... | collective-permute-start | bytes 393224 | tf_op jit(solution)/shard_map/ppermute | solution.py:448
  46.3 4.0 %collective-permute-done.8.got_ref = f32[32,8,128]{2,1,0:T(8,128)S(1)} collective-permute-done((f32[32,8,128]{2,1,0:T(8,128)S(1)}, f32[32,8,128]{2,1,0:T(8,128)S(1)}, u32[]{:S(2)}, u32[]{:S(2)}) %collective-permute-start.8) | collective-permute-done | bytes 131104 | tf_op jit(solution)/shard_map/ppermute | solution.py:448
  51.0 5.3 %gradient.1 = (f32[1280,128]{1,0:T(8,128)}, f32[4,160,128]{2,1,0:T(8,128)}) custom-call(f32[32,8,128]{2,1,0:T(8,128)} %copy-done.12, f32[32,8,128]{2,1,0:T(8,128)} %copy-done.17, f32[32,8,128]{2,1,0:T(8,128)} %obs_ref.1, bf16[20,32,8,128]{3,2,1,0:T(8,128)(2,1)} %m_ref.1, f32[8,32]{1,0:T(8,128)} %v_ref.1, s32[20]{0:T(128)} %eig_ref.1, f32[1,128]{1,0:T(1,128)} %bitcast.20), custom_call_target="tpu_custom_call" | custom-call | tf_op jit(solution)/shard_map/gradient/pallas_call | solution.py:355
  59.5 1.7 %pass_on.14 = f32[4,80,128]{2,1,0:T(8,128)} custom-call(f32[4,80,128]{2,1,0:T(8,128)} %copy-done.3, f32[4,80,128]{2,1,0:T(8,128)} %copy-done.8, f32[1,128]{1,0:T(1,128)} %bitcast.21), custom_call_target="tpu_custom_call" | custom-call | tf_op jit(solution)/shard_map/pass_on/pallas_call | solution.py:355
  62.5 1.7 %pass_on.12 = f32[4,80,128]{2,1,0:T(8,128)} custom-call(f32[4,80,128]{2,1,0:T(8,128)} %copy-done.1, f32[4,80,128]{2,1,0:T(8,128)} %copy-done.9, f32[1,128]{1,0:T(1,128)} %bitcast.22), custom_call_target="tpu_custom_call" | custom-call | tf_op jit(solution)/shard_map/pass_on/pallas_call | solution.py:355
  65.6 1.7 %pass_on.15 = f32[4,80,128]{2,1,0:T(8,128)} custom-call(f32[4,80,128]{2,1,0:T(8,128)} %copy-done.3, f32[4,80,128]{2,1,0:T(8,128)} %copy-done.10, f32[1,128]{1,0:T(1,128)} %bitcast.23), custom_call_target="tpu_custom_call" | custom-call | tf_op jit(solution)/shard_map/pass_on/pallas_call | solution.py:355
  69.2 1.7 %pass_on.13 = f32[4,80,128]{2,1,0:T(8,128)} custom-call(f32[4,80,128]{2,1,0:T(8,128)} %copy-done.1, f32[4,80,128]{2,1,0:T(8,128)} %copy-done.11, f32[1,128]{1,0:T(1,128)} %bitcast.24), custom_call_target="tpu_custom_call" | custom-call | tf_op jit(solution)/shard_map/pass_on/pallas_call | solution.py:355
  72.2 21.9 %collective-permute-done.14.refs_8_ = f32[4,80,128]{2,1,0:T(8,128)S(1)} collective-permute-done((f32[4,80,128]{2,1,0:T(8,128)}, f32[4,80,128]{2,1,0:T(8,128)S(1)}, u32[]{:S(2)}, u32[]{:S(2)}) %collective-permute-start.14) | collective-permute-done | bytes 163872 | tf_op jit(solution)/shard_map/ppermute | solution.py:397
  94.1 2.7 %collective-permute-done.11.refs_5_ = f32[4,80,128]{2,1,0:T(8,128)S(1)} collective-permute-done((f32[4,80,128]{2,1,0:T(8,128)}, f32[4,80,128]{2,1,0:T(8,128)S(1)}, u32[]{:S(2)}, u32[]{:S(2)}) %collective-permute-start.11) | collective-permute-done | bytes 163872 | tf_op jit(solution)/shard_map/ppermute | solution.py:397
  97.5 4.8 %lon_bwd.1 = (f32[8,160,128]{2,1,0:T(8,128)}, f32[32,160]{1,0:T(8,128)}) custom-call(f32[1280,128]{1,0:T(8,128)} %get-tuple-element.20.refs_0_, f32[1,128]{1,0:T(1,128)} %bitcast.25, f32[8,1]{1,0:T(8,128)} %copy.12.dec_ref.refs_1_.refs_2_, f32[4,80,128]{2,1,0:T(8,128)} %copy-done.9, f32[4,80,128]{2,1,0:T(8,128)} %copy-done.11, f32[4,80,128]{2,1,0:T(8,128)} %copy-done.16, ...), custom_call_target="tpu_custom_call" | custom-call | tf_op jit(solution)/shard_map/lon_bwd/pallas_call | solution.py:355
  102.3 1.5 %collective-permute-start.15 = (f32[32,160]{1,0:T(8,128)}, f32[32,160]{1,0:T(8,128)S(1)}, u32[]{:S(2)}, u32[]{:S(2)}) collective-permute-start(f32[32,160]{1,0:T(8,128)} %get-tuple-element.23.refs_5_), channel_id=1, source_target_pairs={{0,16},{16,0},{1,17},{17,1},{2,18},{18,2},{3,19},{19,3},{4,20},{20... | collective-permute-start | bytes 61448 | tf_op jit(solution)/shard_map/ppermute | solution.py:375
  103.8 2.6 %collective-permute-done.15.refs_4_ = f32[32,160]{1,0:T(8,128)S(1)} collective-permute-done((f32[32,160]{1,0:T(8,128)}, f32[32,160]{1,0:T(8,128)S(1)}, u32[]{:S(2)}, u32[]{:S(2)}) %collective-permute-start.15) | collective-permute-done | bytes 20512 | tf_op jit(solution)/shard_map/ppermute | solution.py:375
  107.0 3.5 %sums.1 = (f32[1280,128]{1,0:T(8,128)}, f32[8,128]{1,0:T(8,128)}) custom-call(f32[8,160,128]{2,1,0:T(8,128)} %get-tuple-element.22.refs_0_, f32[8,1]{1,0:T(8,128)} %copy.12.dec_ref.refs_1_.refs_2_, f32[1280,128]{1,0:T(8,128)} %bitcast.9, f32[1280,128]{1,0:T(8,128)} %bitcast.11, f32[32,160]{1,0:T(8,128)} %copy-done.18, f32[32,160]{1,0:T(8,128)} %get-tuple-element.23.refs_5_), custom_call_target="tpu_custom_call" | custom-call | tf_op jit(solution)/shard_map/sums/pallas_call | solution.py:355
  112.6 1.5 %collective-permute-start.17 = (f32[8,128]{1,0:T(8,128)S(1)}, f32[8,128]{1,0:T(8,128)S(1)}, u32[]{:S(2)}, u32[]{:S(2)}) collective-permute-start(f32[8,128]{1,0:T(8,128)S(1)} %add.19), channel_id=1, source_target_pairs={{0,2},{1,3},{2,0},{3,1},{4,6},{5,7},{6,4},{7,5},{8,10},{9,11},{10,... | collective-permute-start | bytes 12296 | tf_op jit(solution)/shard_map/ppermute | solution.py:405
  114.1 2.1 %collective-permute-done.17 = f32[8,128]{1,0:T(8,128)S(1)} collective-permute-done((f32[8,128]{1,0:T(8,128)S(1)}, f32[8,128]{1,0:T(8,128)S(1)}, u32[]{:S(2)}, u32[]{:S(2)}) %collective-permute-start.17) | collective-permute-done | bytes 4128 | tf_op jit(solution)/shard_map/ppermute | solution.py:405
  116.2 1.5 %collective-permute-start.18 = (f32[8,128]{1,0:T(8,128)S(1)}, f32[8,128]{1,0:T(8,128)S(1)}, u32[]{:S(2)}, u32[]{:S(2)}) collective-permute-start(f32[8,128]{1,0:T(8,128)S(1)} %add.20), channel_id=1, source_target_pairs={{0,16},{16,0},{1,17},{17,1},{2,18},{18,2},{3,19},{19,3},{4,20},{20... | collective-permute-start | bytes 12296 | tf_op jit(solution)/shard_map/ppermute | solution.py:405
  117.7 2.1 %collective-permute-done.18 = f32[8,128]{1,0:T(8,128)S(1)} collective-permute-done((f32[8,128]{1,0:T(8,128)S(1)}, f32[8,128]{1,0:T(8,128)S(1)}, u32[]{:S(2)}, u32[]{:S(2)}) %collective-permute-start.18) | collective-permute-done | bytes 4128 | tf_op jit(solution)/shard_map/ppermute | solution.py:405
  119.8 3.6 %collective-permute-done.19 = f32[8,128]{1,0:T(8,128)S(1)} collective-permute-done((f32[8,128]{1,0:T(8,128)S(1)}, f32[8,128]{1,0:T(8,128)S(1)}, u32[]{:S(2)}, u32[]{:S(2)}) %collective-permute-start.19) | collective-permute-done | bytes 4128 | tf_op jit(solution)/shard_map/ppermute | solution.py:405
  123.4 4.5 %collective-permute-done.20 = f32[8,128]{1,0:T(8,128)S(1)} collective-permute-done((f32[8,128]{1,0:T(8,128)S(1)}, f32[8,128]{1,0:T(8,128)S(1)}, u32[]{:S(2)}, u32[]{:S(2)}) %collective-permute-start.20) | collective-permute-done | bytes 4128 | tf_op jit(solution)/shard_map/ppermute | solution.py:405
  128.5 3.2 %update.1 = (f32[1280,128]{1,0:T(8,128)}, f32[1280,128]{1,0:T(8,128)}, f32[1280,128]{1,0:T(8,128)}) custom-call(f32[8,128]{1,0:T(8,128)} %add.23.sums_ref, f32[1280,128]{1,0:T(8,128)} %bitcast.13, f32[1280,128]{1,0:T(8,128)} %bitcast.12, f32[1280,128]{1,0:T(8,128)} %bitcast.10, f32[1280,128]{1,0:T(8,128)} %get-tuple-element.25.h_ref), custom_call_target="tpu_custom_call" | custom-call | tf_op jit(solution)/shard_map/update/pallas_call | solution.py:355
  (74 shorter events, 24.7 us)
Async XLA Ops:
  5.8 5.1 %collective-permute-start = (f32[32,160]{1,0:T(8,128)}, f32[32,160]{1,0:T(8,128)S(1)}, u32[]{:S(2)}, u32[]{:S(2)}) collective-permute-start(f32[32,160]{1,0:T(8,128)} %get-tuple-element.17.refs_4_), channel_id=1, source_target_pairs={{0,16},{16,0},{1,17},{17,1},{2,18},{18,2},{3,19},{19,3},{4,20},{20... | collective-permute-start | bytes 61448 | tf_op jit(solution)/shard_map/ppermute | solution.py:375
  15.8 8.1 %copy-start.2 = (f32[4,80,128]{2,1,0:T(8,128)}, f32[4,80,128]{2,1,0:T(8,128)S(1)}, u32[]{:S(2)}) copy-start(f32[4,80,128]{2,1,0:T(8,128)S(1)} %get-tuple-element.31.carried_ref) | copy-start | bytes 491524
  15.8 11.1 %copy-start = (f32[4,80,128]{2,1,0:T(8,128)}, f32[4,80,128]{2,1,0:T(8,128)S(1)}, u32[]{:S(2)}) copy-start(f32[4,80,128]{2,1,0:T(8,128)S(1)} %get-tuple-element.32.carried_ref) | copy-start | bytes 491524
  15.9 8.1 %collective-permute-start.4 = (f32[4,80,128]{2,1,0:T(8,128)S(1)}, f32[4,80,128]{2,1,0:T(8,128)S(1)}, u32[]{:S(2)}, u32[]{:S(2)}) collective-permute-start(f32[4,80,128]{2,1,0:T(8,128)S(1)} %get-tuple-element.31.carried_ref), channel_id=1, source_target_pairs={{0,4},{1,5},{2,6},{3,7},{16,20},{17,21},{18,22},{19,23}} | collective-permute-start | bytes 491528 | tf_op jit(solution)/shard_map/ppermute | solution.py:397
  19.9 7.1 %collective-permute-start.1 = (f32[4,80,128]{2,1,0:T(8,128)S(1)}, f32[4,80,128]{2,1,0:T(8,128)S(1)}, u32[]{:S(2)}, u32[]{:S(2)}) collective-permute-start(f32[4,80,128]{2,1,0:T(8,128)S(1)} %get-tuple-element.32.carried_ref), channel_id=1, source_target_pairs={{0,4},{1,5},{2,6},{3,7},{16,20},{17,21},{18,22},{19,23}} | collective-permute-start | bytes 491528 | tf_op jit(solution)/shard_map/ppermute | solution.py:397
  26.3 3.7 %collective-permute-start.5 = (f32[4,80,128]{2,1,0:T(8,128)}, f32[4,80,128]{2,1,0:T(8,128)S(1)}, u32[]{:S(2)}, u32[]{:S(2)}) collective-permute-start(f32[4,80,128]{2,1,0:T(8,128)} %pass_on.10), channel_id=1, source_target_pairs={{4,8},{5,9},{6,10},{7,11},{20,24},{21,25},{22,26},{23,27}} | collective-permute-start | bytes 491528 | tf_op jit(solution)/shard_map/ppermute | solution.py:397
  27.0 0.7 copy-start.5
  29.4 3.7 %collective-permute-start.2 = (f32[4,80,128]{2,1,0:T(8,128)}, f32[4,80,128]{2,1,0:T(8,128)S(1)}, u32[]{:S(2)}, u32[]{:S(2)}) collective-permute-start(f32[4,80,128]{2,1,0:T(8,128)} %pass_on.8), channel_id=1, source_target_pairs={{4,8},{5,9},{6,10},{7,11},{20,24},{21,25},{22,26},{23,27}} | collective-permute-start | bytes 491528 | tf_op jit(solution)/shard_map/ppermute | solution.py:397
  30.0 0.7 copy-start.6
  32.4 3.7 %collective-permute-start.6 = (f32[4,80,128]{2,1,0:T(8,128)}, f32[4,80,128]{2,1,0:T(8,128)S(1)}, u32[]{:S(2)}, u32[]{:S(2)}) collective-permute-start(f32[4,80,128]{2,1,0:T(8,128)} %pass_on.11), channel_id=1, source_target_pairs={{8,12},{9,13},{10,14},{11,15},{24,28},{25,29},{26,30},{27,31}} | collective-permute-start | bytes 491528 | tf_op jit(solution)/shard_map/ppermute | solution.py:397
  35.5 0.7 collective-permute-start.3
  36.2 0.7 copy-start.14
  42.2 1.6 %collective-permute-start.7 = (f32[32,8,128]{2,1,0:T(8,128)}, f32[32,8,128]{2,1,0:T(8,128)S(1)}, u32[]{:S(2)}, u32[]{:S(2)}) collective-permute-start(f32[32,8,128]{2,1,0:T(8,128)} %increment.1), channel_id=1, source_target_pairs={{0,1},{1,0},{2,3},{3,2},{4,5},{5,4},{6,7},{7,6},{8,9},{9,8},{10,11... | collective-permute-start | bytes 393224 | tf_op jit(solution)/shard_map/ppermute | solution.py:446
  44.7 5.6 %copy-start.12 = (f32[32,8,128]{2,1,0:T(8,128)}, f32[32,8,128]{2,1,0:T(8,128)S(1)}, u32[]{:S(2)}) copy-start(f32[32,8,128]{2,1,0:T(8,128)S(1)} %add.18.inc_ref) | copy-start | bytes 393220
  44.7 5.6 %collective-permute-start.8 = (f32[32,8,128]{2,1,0:T(8,128)S(1)}, f32[32,8,128]{2,1,0:T(8,128)S(1)}, u32[]{:S(2)}, u32[]{:S(2)}) collective-permute-start(f32[32,8,128]{2,1,0:T(8,128)S(1)} %add.18.inc_ref), channel_id=1, source_target_pairs={{0,2},{1,3},{2,0},{3,1},{4,6},{5,7},{6,4},{7,5},{8,10},{9,11},{10,... | collective-permute-start | bytes 393224 | tf_op jit(solution)/shard_map/ppermute | solution.py:448
  57.4 1.4 %copy-start.3 = (f32[4,80,128]{2,1,0:T(8,128)}, f32[4,80,128]{2,1,0:T(8,128)S(1)}, u32[]{:S(2)}) copy-start(f32[4,80,128]{2,1,0:T(8,128)S(1)} %get-tuple-element.29.carried_ref) | copy-start | bytes 491524
  57.4 4.4 %copy-start.1 = (f32[4,80,128]{2,1,0:T(8,128)}, f32[4,80,128]{2,1,0:T(8,128)S(1)}, u32[]{:S(2)}) copy-start(f32[4,80,128]{2,1,0:T(8,128)S(1)} %get-tuple-element.30.carried_ref) | copy-start | bytes 491524
  57.4 1.4 %collective-permute-start.12 = (f32[4,80,128]{2,1,0:T(8,128)S(1)}, f32[4,80,128]{2,1,0:T(8,128)S(1)}, u32[]{:S(2)}, u32[]{:S(2)}) collective-permute-start(f32[4,80,128]{2,1,0:T(8,128)S(1)} %get-tuple-element.29.carried_ref), channel_id=1, source_target_pairs={{12,8},{13,9},{14,10},{15,11},{28,24},{29,25},{30,26},{31,27}} | collective-permute-start | bytes 491528 | tf_op jit(solution)/shard_map/ppermute | solution.py:397
  58.1 3.7 %collective-permute-start.9 = (f32[4,80,128]{2,1,0:T(8,128)S(1)}, f32[4,80,128]{2,1,0:T(8,128)S(1)}, u32[]{:S(2)}, u32[]{:S(2)}) collective-permute-start(f32[4,80,128]{2,1,0:T(8,128)S(1)} %get-tuple-element.30.carried_ref), channel_id=1, source_target_pairs={{12,8},{13,9},{14,10},{15,11},{28,24},{29,25},{30,26},{31,27}} | collective-permute-start | bytes 491528 | tf_op jit(solution)/shard_map/ppermute | solution.py:397
  61.2 3.7 %collective-permute-start.13 = (f32[4,80,128]{2,1,0:T(8,128)}, f32[4,80,128]{2,1,0:T(8,128)S(1)}, u32[]{:S(2)}, u32[]{:S(2)}) collective-permute-start(f32[4,80,128]{2,1,0:T(8,128)} %pass_on.14), channel_id=1, source_target_pairs={{8,4},{9,5},{10,6},{11,7},{24,20},{25,21},{26,22},{27,23}} | collective-permute-start | bytes 491528 | tf_op jit(solution)/shard_map/ppermute | solution.py:397
  61.8 0.7 copy-start.9
  64.2 4.3 %collective-permute-start.10 = (f32[4,80,128]{2,1,0:T(8,128)}, f32[4,80,128]{2,1,0:T(8,128)S(1)}, u32[]{:S(2)}, u32[]{:S(2)}) collective-permute-start(f32[4,80,128]{2,1,0:T(8,128)} %pass_on.12), channel_id=1, source_target_pairs={{8,4},{9,5},{10,6},{11,7},{24,20},{25,21},{26,22},{27,23}} | collective-permute-start | bytes 491528 | tf_op jit(solution)/shard_map/ppermute | solution.py:397
  64.9 0.7 copy-start.10
  67.3 26.8 %collective-permute-start.14 = (f32[4,80,128]{2,1,0:T(8,128)}, f32[4,80,128]{2,1,0:T(8,128)S(1)}, u32[]{:S(2)}, u32[]{:S(2)}) collective-permute-start(f32[4,80,128]{2,1,0:T(8,128)} %pass_on.15), channel_id=1, source_target_pairs={{4,0},{5,1},{6,2},{7,3},{20,16},{21,17},{22,18},{23,19}} | collective-permute-start | bytes 491528 | tf_op jit(solution)/shard_map/ppermute | solution.py:397
  70.9 25.9 %collective-permute-start.11 = (f32[4,80,128]{2,1,0:T(8,128)}, f32[4,80,128]{2,1,0:T(8,128)S(1)}, u32[]{:S(2)}, u32[]{:S(2)}) collective-permute-start(f32[4,80,128]{2,1,0:T(8,128)} %pass_on.13), channel_id=1, source_target_pairs={{4,0},{5,1},{6,2},{7,3},{20,16},{21,17},{22,18},{23,19}} | collective-permute-start | bytes 491528 | tf_op jit(solution)/shard_map/ppermute | solution.py:397
  94.1 2.7 %copy-start.15 = (f32[4,80,128]{2,1,0:T(8,128)}, f32[4,80,128]{2,1,0:T(8,128)S(1)}, u32[]{:S(2)}) copy-start(f32[4,80,128]{2,1,0:T(8,128)S(1)} %collective-permute-done.14.refs_8_) | copy-start | bytes 491524
  102.3 4.1 %collective-permute-start.15 = (f32[32,160]{1,0:T(8,128)}, f32[32,160]{1,0:T(8,128)S(1)}, u32[]{:S(2)}, u32[]{:S(2)}) collective-permute-start(f32[32,160]{1,0:T(8,128)} %get-tuple-element.23.refs_5_), channel_id=1, source_target_pairs={{0,16},{16,0},{1,17},{17,1},{2,18},{18,2},{3,19},{19,3},{4,20},{20... | collective-permute-start | bytes 61448 | tf_op jit(solution)/shard_map/ppermute | solution.py:375
  110.5 1.4 %collective-permute-start.16 = (f32[8,128]{1,0:T(8,128)}, f32[8,128]{1,0:T(8,128)S(1)}, u32[]{:S(2)}, u32[]{:S(2)}) collective-permute-start(f32[8,128]{1,0:T(8,128)} %get-tuple-element.24), channel_id=1, source_target_pairs={{0,1},{1,0},{2,3},{3,2},{4,5},{5,4},{6,7},{7,6},{8,9},{9,8},{10,11... | collective-permute-start | bytes 12296 | tf_op jit(solution)/shard_map/ppermute | solution.py:405
  112.6 3.6 %collective-permute-start.17 = (f32[8,128]{1,0:T(8,128)S(1)}, f32[8,128]{1,0:T(8,128)S(1)}, u32[]{:S(2)}, u32[]{:S(2)}) collective-permute-start(f32[8,128]{1,0:T(8,128)S(1)} %add.19), channel_id=1, source_target_pairs={{0,2},{1,3},{2,0},{3,1},{4,6},{5,7},{6,4},{7,5},{8,10},{9,11},{10,... | collective-permute-start | bytes 12296 | tf_op jit(solution)/shard_map/ppermute | solution.py:405
  116.2 3.6 %collective-permute-start.18 = (f32[8,128]{1,0:T(8,128)S(1)}, f32[8,128]{1,0:T(8,128)S(1)}, u32[]{:S(2)}, u32[]{:S(2)}) collective-permute-start(f32[8,128]{1,0:T(8,128)S(1)} %add.20), channel_id=1, source_target_pairs={{0,16},{16,0},{1,17},{17,1},{2,18},{18,2},{3,19},{19,3},{4,20},{20... | collective-permute-start | bytes 12296 | tf_op jit(solution)/shard_map/ppermute | solution.py:405
  119.8 3.6 %collective-permute-start.19 = (f32[8,128]{1,0:T(8,128)S(1)}, f32[8,128]{1,0:T(8,128)S(1)}, u32[]{:S(2)}, u32[]{:S(2)}) collective-permute-start(f32[8,128]{1,0:T(8,128)S(1)} %add.21), channel_id=1, source_target_pairs={{0,4},{4,0},{8,12},{12,8},{1,5},{5,1},{9,13},{13,9},{2,6},{6,2},{1... | collective-permute-start | bytes 12296 | tf_op jit(solution)/shard_map/ppermute | solution.py:405
  123.4 4.5 %collective-permute-start.20 = (f32[8,128]{1,0:T(8,128)S(1)}, f32[8,128]{1,0:T(8,128)S(1)}, u32[]{:S(2)}, u32[]{:S(2)}) collective-permute-start(f32[8,128]{1,0:T(8,128)S(1)} %add.22), channel_id=1, source_target_pairs={{0,8},{4,12},{8,0},{12,4},{1,9},{5,13},{9,1},{13,5},{2,10},{6,14},... | collective-permute-start | bytes 12296 | tf_op jit(solution)/shard_map/ppermute | solution.py:405
  (9 other events, 5.9 us)

commit v2 on v1

--- a/solution.py
+++ b/solution.py
@@ -81,12 +81,6 @@
         part = mm(masked_rows(finals, y), f, ((1,), (1,)))
         carried = part if carried is None else carried + part
     carried_ref[...] = carried
-
-
-def lon_incoming(dec_ref, own, others, rows):
-    count = len(others) + 1
-    k = own.shape[1]
-    return count, k
 
 
 def lon_incoming_states(dec_ref, blocks, rows, cells):
@@ -151,6 +145,7 @@
 
 
 def k_lon_fwd(rows, k, cells, d_ref, dec_ref, inside_ref, carried_ref):
+    d_ref = d_ref.reshape(k * rows, cells)
     lon_local_rows(
         lambda y: d_ref[pl.ds(y, k, stride=rows), :], dec_ref, rows, cells, False, inside_ref, carried_ref
     )
@@ -159,7 +154,7 @@
 def k_lat_first(rows, k, cells, n, *refs):
     inside_ref, lon_ref, lat_ref, *rest = refs
     blocks = [r[...] for r in rest[:n]]
-    f_ref, lat_carried_ref = rest[n:]
+    f_ref, *chunk_refs = rest[n:]
     states = lon_incoming_states(lon_ref, blocks, rows, cells).T
     c, leak, _ = lon_consts(lon_ref, cells)
     entering = lon_entering(c, leak, cells, False)
@@ -167,14 +162,18 @@
         f_ref[y] = inside_ref[y] + lon_correction(states, entering, y)
     zero = jnp.zeros((8, cells), f32)
 
-    def store(y, at, base, value, last):
-        if last is not None:
-            for s in range(4):
-                lat_carried_ref[s, at, :] = last[s]
-
-    lat_sweep(
-        lambda y, at, base: f_ref[y, at, :], store, lambda at: [zero] * 4, lat_ref, rows, k, False, 8
-    )
+    size = k // len(chunk_refs)
+    for ch, out_ref in enumerate(chunk_refs):
+
+        def store(y, at, base, value, last, out_ref=out_ref):
+            if last is not None:
+                for s in range(4):
+                    out_ref[s, at, :] = last[s]
+
+        def load(y, at, base, ch=ch):
+            return f_ref[y, pl.ds(pl.multiple_of(ch * size + base, 8), 8), :]
+
+        lat_sweep(load, store, lambda at: [zero] * 4, lat_ref, rows, size, False, 8)
 
 
 def k_pass_on(rows, carried_ref, got_ref, dec_ref, out_ref):
@@ -251,7 +250,8 @@
         lax.fori_loop(0, levels, level, 0, unroll=4)
 
 
-def k_gradient(rows, k, cells, members, modes, levels, inc_ref, got_ref, obs_ref, m_ref, v_ref, eig_ref, lat_ref, g_ref, carried_ref, w_ref):
+def k_gradient(rows, k, cells, members, modes, levels, inc_ref, got_ref, obs_ref, m_ref, v_ref, eig_ref, lat_ref, g_ref, *rest):
+    *chunk_refs, w_ref = rest
     w_ref[...] = (inc_ref[...] + got_ref[...]) * obs_ref[...]
     per = member_blocks(members)
     for b in range(members // per):
@@ -276,21 +276,18 @@
                 g_ref[at : at + rows, :] = acc[m * modes + e] * scale
     zero8 = jnp.zeros((8, cells), f32)
 
-    def store(y, at, base, value, last):
-        if last is not None:
-            for s in range(4):
-                carried_ref[s, at, :] = last[s]
-
-    lat_sweep(
-        lambda y, at, base: g_ref[pl.ds(base * rows + y, 8, stride=rows), :],
-        store,
-        lambda at: [zero8] * 4,
-        lat_ref,
-        rows,
-        k,
-        True,
-        8,
-    )
+    size = k // len(chunk_refs)
+    for ch, out_ref in enumerate(chunk_refs):
+
+        def store(y, at, base, value, last, out_ref=out_ref):
+            if last is not None:
+                for s in range(4):
+                    out_ref[s, at, :] = last[s]
+
+        def load(y, at, base, ch=ch):
+            return g_ref[pl.ds((ch * size + base) * rows + y, 8, stride=rows), :]
+
+        lat_sweep(load, store, lambda at: [zero8] * 4, lat_ref, rows, size, True, 8)
 
 
 def k_lon_bwd(rows, k, cells, chunks, hops, *refs):
@@ -313,6 +310,8 @@
 
 def k_sums(rows, k, cells, n, *refs):
     inside_ref, lon_ref, d_ref, r_ref, *rest = refs
+    d_ref = d_ref.reshape(k * rows, cells)
+    r_ref = r_ref.reshape(k * rows, cells)
     blocks = [r[...] for r in rest[:n]]
     h_ref, sums_ref = rest[n:]
     states = lon_incoming_states(lon_ref, blocks, rows, cells).T
@@ -340,7 +339,7 @@
 
 def k_update(sums_ref, control_ref, r_ref, d_ref, h_ref, nc_ref, nr_ref, nd_ref):
     sums = jnp.sum(sums_ref[...], axis=1, keepdims=True)
-    rr, dh, rh, hh = (sums[i : i + 1, :] for i in range(4))
+    rr, dh, rh, hh = (sums[i : i + 1].reshape(1, 1, 1) for i in range(4))
     step = rr / dh
     norm_new = rr - 2.0 * step * rh + step * step * hh
     beta = norm_new / rr
@@ -360,7 +359,7 @@
         scratch_shapes=scratch,
         name=name,
         cost_estimate=cost,
-        compiler_params=pltpu.CompilerParams(vmem_limit_bytes=56 * 1024 * 1024),
+        compiler_params=pltpu.CompilerParams(vmem_limit_bytes=16 * 1024 * 1024),
     )(*ins)
 
 
@@ -377,11 +376,10 @@
     return got + [carried]
 
 
-def lat_chain(carried, lat_dec, rows, chunks, backward):
+def lat_chain(parts, lat_dec, rows, backward):
     n = lax.axis_size("lat")
-    size = carried.shape[1] // chunks
-    cells = carried.shape[2]
-    parts = [carried[:, c * size : (c + 1) * size] for c in range(chunks)]
+    chunks = len(parts)
+    _, size, cells = parts[0].shape
     sends = list(parts)
     got = [[] for _ in range(chunks)]
     for h in range(n - 1):
@@ -414,8 +412,7 @@
     n_lon, n_lat, n_mem = (lax.axis_size(a) for a in ("lon", "lat", "mem"))
     chunks = 2
     hops = n_lat - 1
-    flat = lambda v: v.reshape(k * rows, cells)
-    d, r, ctl = flat(direction), flat(residual), flat(control)
+    d, r, ctl = direction, residual, control
     lon_dec = lon_decay.reshape(rows, 1)
     lat_dec = lat_decay.reshape(1, cells)
 
@@ -426,13 +423,13 @@
         name="lon_fwd",
     )
     blocks = lon_exchange(carried, False)
-    f, lat_carried = call(
+    f, *parts = call(
         functools.partial(k_lat_first, rows, k, cells, n_lon),
-        (sds(rows, k, cells), sds(4, k, cells)),
+        (sds(rows, k, cells),) + (sds(4, k // chunks, cells),) * chunks,
         [inside, lon_dec, lat_dec, *blocks],
         name="lat_first",
     )
-    got = lat_chain(lat_carried, lat_dec, rows, chunks, False)
+    got = lat_chain(parts, lat_dec, rows, False)
     inc = call(
         functools.partial(k_increment, rows, k, chunks, hops, mcount, modes, levels),
         sds(levels, rows, cells),
@@ -446,15 +443,15 @@
         inc = inc + lax.ppermute(inc, "mem", [(i, i ^ step) for i in range(n_mem)])
         step *= 2
     other = lax.ppermute(inc, "mem", [(i, i ^ step) for i in range(n_mem)])
-    g, lat_carried = call(
+    g, *parts = call(
         functools.partial(k_gradient, rows, k, cells, mcount, modes, levels),
-        (sds(k * rows, cells), sds(4, k, cells)),
+        (sds(k * rows, cells),) + (sds(4, k // chunks, cells),) * chunks,
         [inc, other, obs_weight, members, vert_modes, eig_count, lat_dec],
         specs=[VM, VM, VM, VM, SM, SM, VM],
         scratch=[pltpu.VMEM((levels, rows, cells), f32)],
         name="gradient",
     )
-    got = lat_chain(lat_carried, lat_dec, rows, chunks, True)
+    got = lat_chain(parts, lat_dec, rows, True)
     inside, carried = call(
         functools.partial(k_lon_bwd, rows, k, cells, chunks, hops),
         (sds(rows, k, cells), sds(4 * rows, k)),
@@ -473,11 +470,11 @@
         sums = butterfly(sums, axis)
     outs = call(
         k_update,
-        (sds(k * rows, cells),) * 3,
-        [sums, ctl, r, d, h],
+        (sds(k, rows, cells),) * 3,
+        [sums, ctl, r, d, h.reshape(k, rows, cells)],
         name="update",
     )
-    return tuple(o.reshape(k, rows, cells) for o in outs)
+    return tuple(outs)
 
 
 def solution(mesh):

time: 132 us -> 98.3 us (0.74)
  Pallas kernels: 43.1 us -> 15.8 us
  local copies, waits for them, and re-layouts: 11.9 us -> 2.52 us
  waiting for transfers between devices: 51.3 us -> 55.9 us
  other arithmetic: 2.22 us -> 0.03 us
    pallas_call x15, Pallas kernels: 43.1 us -> 15.8 us  [call(): pl.pallas_call(body, out_shape=outs, in_specs=specs or [VM] * len(ins), o...]
    unnamed x40 -> x20, local copies, waits for them, and re-layouts: 8.55 us -> 1.78 us
    ppermute x12, waiting for transfers between devices: 27.3 us -> 32.7 us  [lat_chain(): got[c].append(lax.ppermute(sends[c], 'lat', [pair]))]
    slice x2 -> x0, local copies, waits for them, and re-layouts: 2.03 us -> none  [lat_chain(): parts = [carried[:, c * size:(c + 1) * size] for c in range(chunks)]]
  transfers between devices with their start and end apart: 21 -> 21, of which waited for: 12 -> 13; matrix products, arithmetic and copies ran while one was open for 0% -> 0% of each run, Pallas kernels for 10% -> 0%
where the time goes in v2:
time: 98.3 us; the launch traced here: 97.9 us
  waiting for transfers between devices  55.9 us (57%)
  starting transfers between devices  22.7 us (23%)
  Pallas kernels  15.8 us (16%)
  local copies, waits for them, and re-layouts  2.52 us (3%)
    ppermute x12, waiting for transfers between devices, lat_chain(): got[c].append(lax.ppermute(sends[c], 'lat', [pair]))  32.7 us
    pallas_call x15, Pallas kernels, call(): pl.pallas_call(body, out_shape=outs, in_specs=specs or [VM] * len(ins), o...  15.8 us
    ppermute x5, waiting for transfers between devices, butterfly(): v = v + lax.ppermute(v, axis, [(i, i ^ d) for i in range(n)])  13.5 us
    ppermute x12, starting transfers between devices, lat_chain(): got[c].append(lax.ppermute(sends[c], 'lat', [pair]))  13.4 us
    ppermute x2, starting transfers between devices, lon_exchange(): lax.ppermute(carried, 'lon', [(j, (j + sign * r) % n) for j in range(n)])  4.56 us
    ppermute x2, waiting for transfers between devices, lon_exchange(): lax.ppermute(carried, 'lon', [(j, (j + sign * r) % n) for j in range(n)])  4.34 us
    ppermute x1, waiting for transfers between devices, body(): other = lax.ppermute(inc, 'mem', [(i, i ^ step) for i in range(n_mem)])  4.03 us
    ppermute x5, starting transfers between devices, butterfly(): v = v + lax.ppermute(v, axis, [(i, i ^ d) for i in range(n)])  3.05 us
  transfers between devices with their start and end apart: 21, of which 13 were waited for; matrix products, arithmetic and copies ran while one was open for 0% of the time, Pallas kernels for 0%

profile of v2, /device:TPU:0, one launch (start us, length us, event | category | flops | bytes accessed | tf_op | source)
XLA Modules:
  0.0 97.9 jit_solution(14567595609585803543)
XLA Ops:
  0.6 0.7 copy.12.dec_ref.refs_1_.refs_2_
  1.4 1.1 %copy-done = f32[160,8,128]{2,1,0:T(8,128)S(1)} copy-done((f32[160,8,128]{2,1,0:T(8,128)S(1)}, f32[160,8,128]{2,1,0:T(8,128)}, u32[]{:S(2)}) %copy-start) | copy-done | bytes 655384
  2.5 1.9 %lon_fwd.1 = (f32[8,160,128]{2,1,0:T(8,128)S(1)}, f32[32,160]{1,0:T(8,128)S(1)}) custom-call(f32[160,8,128]{2,1,0:T(8,128)S(1)} %copy-done, f32[8,1]{1,0:T(8,128)S(1)} %copy.12.dec_ref.refs_1_.refs_2_), custom_call_target="tpu_custom_call" | custom-call | tf_op jit(solution)/shard_map/lon_fwd/pallas_call | solution.py:354
  4.4 3.0 %collective-permute-start = (f32[32,160]{1,0:T(8,128)S(1)}, f32[32,160]{1,0:T(8,128)S(1)}, u32[]{:S(2)}, u32[]{:S(2)}) collective-permute-start(f32[32,160]{1,0:T(8,128)S(1)} %get-tuple-element.16.refs_4_), channel_id=1, source_target_pairs={{0,16},{16,0},{1,17},{17,1},{2,18},{18,2},{3,19},{19,3},{4,20},{20... | collective-permute-start | bytes 61448 | tf_op jit(solution)/shard_map/ppermute | solution.py:374
  7.4 1.9 %collective-permute-done.refs_3_ = f32[32,160]{1,0:T(8,128)S(1)} collective-permute-done((f32[32,160]{1,0:T(8,128)S(1)}, f32[32,160]{1,0:T(8,128)S(1)}, u32[]{:S(2)}, u32[]{:S(2)}) %collective-permute-start) | collective-permute-done | bytes 20512 | tf_op jit(solution)/shard_map/ppermute | solution.py:374
  10.0 1.3 %lat_first.1 = (f32[8,160,128]{2,1,0:T(8,128)S(1)}, f32[4,80,128]{2,1,0:T(8,128)S(1)}, f32[4,80,128]{2,1,0:T(8,128)S(1)}) custom-call(f32[8,160,128]{2,1,0:T(8,128)S(1)} %get-tuple-element.15.refs_0_, f32[8,1]{1,0:T(8,128)S(1)} %copy.12.dec_ref.refs_1_.refs_2_, f32[1,128]{1,0:T(1,128)S(1)} %bitcast.4, f32[32,160]{1,0:T(8,128)S(1)} %collective-permute-done.refs_3_, ...), custom_call_target="tpu_custom_call" | custom-call | tf_op jit(solution)/shard_map/lat_first/pallas_call | solution.py:354
  11.3 4.0 %collective-permute-start.1 = (f32[4,80,128]{2,1,0:T(8,128)S(1)}, f32[4,80,128]{2,1,0:T(8,128)S(1)}, u32[]{:S(2)}, u32[]{:S(2)}) collective-permute-start(f32[4,80,128]{2,1,0:T(8,128)S(1)} %get-tuple-element.18.carried_ref), channel_id=1, source_target_pairs={{0,4},{1,5},{2,6},{3,7},{16,20},{17,21},{18,22},{19,23}} | collective-permute-start | bytes 491528 | tf_op jit(solution)/shard_map/ppermute | solution.py:395
  15.3 1.3 %collective-permute-start.4 = (f32[4,80,128]{2,1,0:T(8,128)S(1)}, f32[4,80,128]{2,1,0:T(8,128)S(1)}, u32[]{:S(2)}, u32[]{:S(2)}) collective-permute-start(f32[4,80,128]{2,1,0:T(8,128)S(1)} %get-tuple-element.19.carried_ref), channel_id=1, source_target_pairs={{0,4},{1,5},{2,6},{3,7},{16,20},{17,21},{18,22},{19,23}} | collective-permute-start | bytes 491528 | tf_op jit(solution)/shard_map/ppermute | solution.py:395
  16.6 2.7 %collective-permute-done.1.got_ref.refs_5_ = f32[4,80,128]{2,1,0:T(8,128)S(1)} collective-permute-done((f32[4,80,128]{2,1,0:T(8,128)S(1)}, f32[4,80,128]{2,1,0:T(8,128)S(1)}, u32[]{:S(2)}, u32[]{:S(2)}) %collective-permute-start.1) | collective-permute-done | bytes 163872 | tf_op jit(solution)/shard_map/ppermute | solution.py:395
  20.1 1.0 %collective-permute-done.4.got_ref.refs_8_ = f32[4,80,128]{2,1,0:T(8,128)S(1)} collective-permute-done((f32[4,80,128]{2,1,0:T(8,128)S(1)}, f32[4,80,128]{2,1,0:T(8,128)S(1)}, u32[]{:S(2)}, u32[]{:S(2)}) %collective-permute-start.4) | collective-permute-done | bytes 163872 | tf_op jit(solution)/shard_map/ppermute | solution.py:395
  23.4 3.5 %increment.1 = f32[32,8,128]{2,1,0:T(8,128)S(1)} custom-call(f32[8,160,128]{2,1,0:T(8,128)S(1)} %get-tuple-element.17.refs_0_, f32[1,128]{1,0:T(1,128)S(1)} %bitcast.9, bf16[20,32,8,128]{3,2,1,0:T(8,128)(2,1)S(1)} %copy-done.2, f32[8,32]{1,0:T(8,128)S(1)} %copy-done.8, s32[20]{0:T(128)S(1)} %copy-done.9, ...), custom_call_target="tpu_custom_call" | custom-call | tf_op jit(solution)/shard_map/increment/pallas_call | solution.py:354
  26.9 1.3 %collective-permute-done.7 = f32[32,8,128]{2,1,0:T(8,128)S(1)} collective-permute-done((f32[32,8,128]{2,1,0:T(8,128)S(1)}, f32[32,8,128]{2,1,0:T(8,128)S(1)}, u32[]{:S(2)}, u32[]{:S(2)}) %collective-permute-start.7) | collective-permute-done | bytes 131104 | tf_op jit(solution)/shard_map/ppermute | solution.py:443
  28.3 1.6 %collective-permute-start.8 = (f32[32,8,128]{2,1,0:T(8,128)S(1)}, f32[32,8,128]{2,1,0:T(8,128)S(1)}, u32[]{:S(2)}, u32[]{:S(2)}) collective-permute-start(f32[32,8,128]{2,1,0:T(8,128)S(1)} %add.18.inc_ref), channel_id=1, source_target_pairs={{0,2},{1,3},{2,0},{3,1},{4,6},{5,7},{6,4},{7,5},{8,10},{9,11},{10,... | collective-permute-start | bytes 393224 | tf_op jit(solution)/shard_map/ppermute | solution.py:445
  29.9 4.0 %collective-permute-done.8.got_ref = f32[32,8,128]{2,1,0:T(8,128)S(1)} collective-permute-done((f32[32,8,128]{2,1,0:T(8,128)S(1)}, f32[32,8,128]{2,1,0:T(8,128)S(1)}, u32[]{:S(2)}, u32[]{:S(2)}) %collective-permute-start.8) | collective-permute-done | bytes 131104 | tf_op jit(solution)/shard_map/ppermute | solution.py:445
  33.9 3.6 %gradient.1 = (f32[1280,128]{1,0:T(8,128)S(1)}, f32[4,80,128]{2,1,0:T(8,128)S(1)}, f32[4,80,128]{2,1,0:T(8,128)S(1)}) custom-call(f32[32,8,128]{2,1,0:T(8,128)S(1)} %add.18.inc_ref, f32[32,8,128]{2,1,0:T(8,128)S(1)} %collective-permute-done.8.got_ref, f32[32,8,128]{2,1,0:T(8,128)S(1)} %copy-done.5, bf16[20,32,8,128]{3,2,1,0:T(8,128)(2,1)S(1)} %copy-done.2, ...), custom_call_target="tpu_custom_call" | custom-call | tf_op jit(solution)/shard_map/gradient/pallas_call | solution.py:354
  39.7 0.8 collective-permute-start.13
  40.6 1.3 %collective-permute-start.11 = (f32[4,80,128]{2,1,0:T(8,128)S(1)}, f32[4,80,128]{2,1,0:T(8,128)S(1)}, u32[]{:S(2)}, u32[]{:S(2)}) collective-permute-start(f32[4,80,128]{2,1,0:T(8,128)S(1)} %pass_on.13), channel_id=1, source_target_pairs={{4,0},{5,1},{6,2},{7,3},{20,16},{21,17},{22,18},{23,19}} | collective-permute-start | bytes 491528 | tf_op jit(solution)/shard_map/ppermute | solution.py:395
  42.0 1.3 %collective-permute-start.14 = (f32[4,80,128]{2,1,0:T(8,128)S(1)}, f32[4,80,128]{2,1,0:T(8,128)S(1)}, u32[]{:S(2)}, u32[]{:S(2)}) collective-permute-start(f32[4,80,128]{2,1,0:T(8,128)S(1)} %pass_on.15), channel_id=1, source_target_pairs={{4,0},{5,1},{6,2},{7,3},{20,16},{21,17},{22,18},{23,19}} | collective-permute-start | bytes 491528 | tf_op jit(solution)/shard_map/ppermute | solution.py:395
  43.3 27.2 %collective-permute-done.11.refs_5_ = f32[4,80,128]{2,1,0:T(8,128)S(1)} collective-permute-done((f32[4,80,128]{2,1,0:T(8,128)S(1)}, f32[4,80,128]{2,1,0:T(8,128)S(1)}, u32[]{:S(2)}, u32[]{:S(2)}) %collective-permute-start.11) | collective-permute-done | bytes 163872 | tf_op jit(solution)/shard_map/ppermute | solution.py:395
  70.4 1.8 %collective-permute-done.14.refs_8_ = f32[4,80,128]{2,1,0:T(8,128)S(1)} collective-permute-done((f32[4,80,128]{2,1,0:T(8,128)S(1)}, f32[4,80,128]{2,1,0:T(8,128)S(1)}, u32[]{:S(2)}, u32[]{:S(2)}) %collective-permute-start.14) | collective-permute-done | bytes 163872 | tf_op jit(solution)/shard_map/ppermute | solution.py:395
  72.2 2.5 %lon_bwd.1 = (f32[8,160,128]{2,1,0:T(8,128)S(1)}, f32[32,160]{1,0:T(8,128)S(1)}) custom-call(f32[1280,128]{1,0:T(8,128)S(1)} %get-tuple-element.20.refs_0_, f32[1,128]{1,0:T(1,128)S(1)} %bitcast.15, f32[8,1]{1,0:T(8,128)S(1)} %copy.12.dec_ref.refs_1_.refs_2_, f32[4,80,128]{2,1,0:T(8,128)S(1)} %collective-permute-done.9.got_ref.refs_3_, ...), custom_call_target="tpu_custom_call" | custom-call | tf_op jit(solution)/shard_map/lon_bwd/pallas_call | solution.py:354
  74.7 1.5 %collective-permute-start.15 = (f32[32,160]{1,0:T(8,128)S(1)}, f32[32,160]{1,0:T(8,128)S(1)}, u32[]{:S(2)}, u32[]{:S(2)}) collective-permute-start(f32[32,160]{1,0:T(8,128)S(1)} %get-tuple-element.24.refs_5_), channel_id=1, source_target_pairs={{0,16},{16,0},{1,17},{17,1},{2,18},{18,2},{3,19},{19,3},{4,20},{20... | collective-permute-start | bytes 61448 | tf_op jit(solution)/shard_map/ppermute | solution.py:374
  76.2 2.4 %collective-permute-done.15.refs_4_ = f32[32,160]{1,0:T(8,128)S(1)} collective-permute-done((f32[32,160]{1,0:T(8,128)S(1)}, f32[32,160]{1,0:T(8,128)S(1)}, u32[]{:S(2)}, u32[]{:S(2)}) %collective-permute-start.15) | collective-permute-done | bytes 20512 | tf_op jit(solution)/shard_map/ppermute | solution.py:374
  78.7 1.1 %sums.1 = (f32[1280,128]{1,0:T(8,128)S(1)}, f32[8,128]{1,0:T(8,128)S(1)}) custom-call(f32[8,160,128]{2,1,0:T(8,128)S(1)} %get-tuple-element.23.refs_0_, f32[8,1]{1,0:T(8,128)S(1)} %copy.12.dec_ref.refs_1_.refs_2_, f32[160,8,128]{2,1,0:T(8,128)S(1)} %copy-done.1, f32[160,8,128]{2,1,0:T(8,128)S(1)} %copy-done.3, ...), custom_call_target="tpu_custom_call" | custom-call | tf_op jit(solution)/shard_map/sums/pallas_call | solution.py:354
  79.9 1.2 %collective-permute-done.16 = f32[8,128]{1,0:T(8,128)S(1)} collective-permute-done((f32[8,128]{1,0:T(8,128)S(1)}, f32[8,128]{1,0:T(8,128)S(1)}, u32[]{:S(2)}, u32[]{:S(2)}) %collective-permute-start.16) | collective-permute-done | bytes 4128 | tf_op jit(solution)/shard_map/ppermute | solution.py:403
  81.1 1.5 %collective-permute-start.17 = (f32[8,128]{1,0:T(8,128)S(1)}, f32[8,128]{1,0:T(8,128)S(1)}, u32[]{:S(2)}, u32[]{:S(2)}) collective-permute-start(f32[8,128]{1,0:T(8,128)S(1)} %add.19), channel_id=1, source_target_pairs={{0,2},{1,3},{2,0},{3,1},{4,6},{5,7},{6,4},{7,5},{8,10},{9,11},{10,... | collective-permute-start | bytes 12296 | tf_op jit(solution)/shard_map/ppermute | solution.py:403
  82.6 2.1 %collective-permute-done.17 = f32[8,128]{1,0:T(8,128)S(1)} collective-permute-done((f32[8,128]{1,0:T(8,128)S(1)}, f32[8,128]{1,0:T(8,128)S(1)}, u32[]{:S(2)}, u32[]{:S(2)}) %collective-permute-start.17) | collective-permute-done | bytes 4128 | tf_op jit(solution)/shard_map/ppermute | solution.py:403
  84.7 1.5 %collective-permute-start.18 = (f32[8,128]{1,0:T(8,128)S(1)}, f32[8,128]{1,0:T(8,128)S(1)}, u32[]{:S(2)}, u32[]{:S(2)}) collective-permute-start(f32[8,128]{1,0:T(8,128)S(1)} %add.20), channel_id=1, source_target_pairs={{0,16},{16,0},{1,17},{17,1},{2,18},{18,2},{3,19},{19,3},{4,20},{20... | collective-permute-start | bytes 12296 | tf_op jit(solution)/shard_map/ppermute | solution.py:403
  86.1 2.1 %collective-permute-done.18 = f32[8,128]{1,0:T(8,128)S(1)} collective-permute-done((f32[8,128]{1,0:T(8,128)S(1)}, f32[8,128]{1,0:T(8,128)S(1)}, u32[]{:S(2)}, u32[]{:S(2)}) %collective-permute-start.18) | collective-permute-done | bytes 4128 | tf_op jit(solution)/shard_map/ppermute | solution.py:403
  88.3 3.6 %collective-permute-done.19 = f32[8,128]{1,0:T(8,128)S(1)} collective-permute-done((f32[8,128]{1,0:T(8,128)S(1)}, f32[8,128]{1,0:T(8,128)S(1)}, u32[]{:S(2)}, u32[]{:S(2)}) %collective-permute-start.19) | collective-permute-done | bytes 4128 | tf_op jit(solution)/shard_map/ppermute | solution.py:403
  91.9 4.5 %collective-permute-done.20 = f32[8,128]{1,0:T(8,128)S(1)} collective-permute-done((f32[8,128]{1,0:T(8,128)S(1)}, f32[8,128]{1,0:T(8,128)S(1)}, u32[]{:S(2)}, u32[]{:S(2)}) %collective-permute-start.20) | collective-permute-done | bytes 4128 | tf_op jit(solution)/shard_map/ppermute | solution.py:403
  96.4 1.5 %update.1 = (f32[160,8,128]{2,1,0:T(8,128)}, f32[160,8,128]{2,1,0:T(8,128)}, f32[160,8,128]{2,1,0:T(8,128)}) custom-call(f32[8,128]{1,0:T(8,128)S(1)} %add.23.sums_ref, f32[160,8,128]{2,1,0:T(8,128)S(1)} %copy-done.4, f32[160,8,128]{2,1,0:T(8,128)S(1)} %copy-done.3, f32[160,8,128]{2,1,0:T(8,128)S(1)} %copy-done.1, f32[160,8,128]{2,1,0:T(8,128)S(1)} %bitcast.3), custom_call_target="tpu_custom_call" | custom-call | tf_op jit(solution)/shard_map/update/pallas_call | solution.py:354
  (52 shorter events, 6.0 us)
Async XLA Ops:
  0.6 18.7 %copy-start.7 = (f32[128]{0:T(128)S(1)}, f32[128]{0:T(128)}, u32[]{:S(2)}) copy-start(f32[128]{0:T(128)} %param.16) | copy-start | bytes 1540
  1.4 1.1 %copy-start = (f32[160,8,128]{2,1,0:T(8,128)S(1)}, f32[160,8,128]{2,1,0:T(8,128)}, u32[]{:S(2)}) copy-start(f32[160,8,128]{2,1,0:T(8,128)} %d_ref.3) | copy-start | bytes 1966084
  4.4 4.9 %collective-permute-start = (f32[32,160]{1,0:T(8,128)S(1)}, f32[32,160]{1,0:T(8,128)S(1)}, u32[]{:S(2)}, u32[]{:S(2)}) collective-permute-start(f32[32,160]{1,0:T(8,128)S(1)} %get-tuple-element.16.refs_4_), channel_id=1, source_target_pairs={{0,16},{16,0},{1,17},{17,1},{2,18},{18,2},{3,19},{19,3},{4,20},{20... | collective-permute-start | bytes 61448 | tf_op jit(solution)/shard_map/ppermute | solution.py:374
  9.3 0.7 copy-start.6
  9.9 13.4 %copy-start.2 = (bf16[20,32,8,128]{3,2,1,0:T(8,128)(2,1)S(1)}, bf16[20,32,8,128]{3,2,1,0:T(8,128)(2,1)}, u32[]{:S(2)}) copy-start(bf16[20,32,8,128]{3,2,1,0:T(8,128)(2,1)} %m_ref.1) | copy-start | bytes 3932164
  9.9 13.4 %copy-start.8 = (f32[8,32]{1,0:T(8,128)S(1)}, f32[8,32]{1,0:T(8,128)}, u32[]{:S(2)}) copy-start(f32[8,32]{1,0:T(8,128)} %v_ref.1) | copy-start | bytes 3076
  10.0 13.4 %copy-start.9 = (s32[20]{0:T(128)S(1)}, s32[20]{0:T(128)}, u32[]{:S(2)}) copy-start(s32[20]{0:T(128)} %eig_ref.1) | copy-start | bytes 244
  11.3 8.1 %collective-permute-start.1 = (f32[4,80,128]{2,1,0:T(8,128)S(1)}, f32[4,80,128]{2,1,0:T(8,128)S(1)}, u32[]{:S(2)}, u32[]{:S(2)}) collective-permute-start(f32[4,80,128]{2,1,0:T(8,128)S(1)} %get-tuple-element.18.carried_ref), channel_id=1, source_target_pairs={{0,4},{1,5},{2,6},{3,7},{16,20},{17,21},{18,22},{19,23}} | collective-permute-start | bytes 491528 | tf_op jit(solution)/shard_map/ppermute | solution.py:395
  15.3 5.8 %collective-permute-start.4 = (f32[4,80,128]{2,1,0:T(8,128)S(1)}, f32[4,80,128]{2,1,0:T(8,128)S(1)}, u32[]{:S(2)}, u32[]{:S(2)}) collective-permute-start(f32[4,80,128]{2,1,0:T(8,128)S(1)} %get-tuple-element.19.carried_ref), channel_id=1, source_target_pairs={{0,4},{1,5},{2,6},{3,7},{16,20},{17,21},{18,22},{19,23}} | collective-permute-start | bytes 491528 | tf_op jit(solution)/shard_map/ppermute | solution.py:395
  19.4 2.4 %collective-permute-start.2 = (f32[4,80,128]{2,1,0:T(8,128)S(1)}, f32[4,80,128]{2,1,0:T(8,128)S(1)}, u32[]{:S(2)}, u32[]{:S(2)}) collective-permute-start(f32[4,80,128]{2,1,0:T(8,128)S(1)} %pass_on.8), channel_id=1, source_target_pairs={{4,8},{5,9},{6,10},{7,11},{20,24},{21,25},{22,26},{23,27}} | collective-permute-start | bytes 491528 | tf_op jit(solution)/shard_map/ppermute | solution.py:395
  21.2 1.4 %collective-permute-start.5 = (f32[4,80,128]{2,1,0:T(8,128)S(1)}, f32[4,80,128]{2,1,0:T(8,128)S(1)}, u32[]{:S(2)}, u32[]{:S(2)}) collective-permute-start(f32[4,80,128]{2,1,0:T(8,128)S(1)} %pass_on.10), channel_id=1, source_target_pairs={{4,8},{5,9},{6,10},{7,11},{20,24},{21,25},{22,26},{23,27}} | collective-permute-start | bytes 491528 | tf_op jit(solution)/shard_map/ppermute | solution.py:395
  21.9 1.4 %collective-permute-start.3 = (f32[4,80,128]{2,1,0:T(8,128)S(1)}, f32[4,80,128]{2,1,0:T(8,128)S(1)}, u32[]{:S(2)}, u32[]{:S(2)}) collective-permute-start(f32[4,80,128]{2,1,0:T(8,128)S(1)} %pass_on.9), channel_id=1, source_target_pairs={{8,12},{9,13},{10,14},{11,15},{24,28},{25,29},{26,30},{27,31}} | collective-permute-start | bytes 491528 | tf_op jit(solution)/shard_map/ppermute | solution.py:395
  22.6 0.7 collective-permute-start.6
  23.4 10.5 %copy-start.5 = (f32[32,8,128]{2,1,0:T(8,128)S(1)}, f32[32,8,128]{2,1,0:T(8,128)}, u32[]{:S(2)}) copy-start(f32[32,8,128]{2,1,0:T(8,128)} %obs_ref.1) | copy-start | bytes 393220
  26.8 1.4 %collective-permute-start.7 = (f32[32,8,128]{2,1,0:T(8,128)S(1)}, f32[32,8,128]{2,1,0:T(8,128)S(1)}, u32[]{:S(2)}, u32[]{:S(2)}) collective-permute-start(f32[32,8,128]{2,1,0:T(8,128)S(1)} %increment.1), channel_id=1, source_target_pairs={{0,1},{1,0},{2,3},{3,2},{4,5},{5,4},{6,7},{7,6},{8,9},{9,8},{10,11... | collective-permute-start | bytes 393224 | tf_op jit(solution)/shard_map/ppermute | solution.py:443
  28.3 5.6 %collective-permute-start.8 = (f32[32,8,128]{2,1,0:T(8,128)S(1)}, f32[32,8,128]{2,1,0:T(8,128)S(1)}, u32[]{:S(2)}, u32[]{:S(2)}) collective-permute-start(f32[32,8,128]{2,1,0:T(8,128)S(1)} %add.18.inc_ref), channel_id=1, source_target_pairs={{0,2},{1,3},{2,0},{3,1},{4,6},{5,7},{6,4},{7,5},{8,10},{9,11},{10,... | collective-permute-start | bytes 393224 | tf_op jit(solution)/shard_map/ppermute | solution.py:445
  37.5 1.4 %collective-permute-start.9 = (f32[4,80,128]{2,1,0:T(8,128)S(1)}, f32[4,80,128]{2,1,0:T(8,128)S(1)}, u32[]{:S(2)}, u32[]{:S(2)}) collective-permute-start(f32[4,80,128]{2,1,0:T(8,128)S(1)} %get-tuple-element.21.carried_ref), channel_id=1, source_target_pairs={{12,8},{13,9},{14,10},{15,11},{28,24},{29,25},{30,26},{31,27}} | collective-permute-start | bytes 491528 | tf_op jit(solution)/shard_map/ppermute | solution.py:395
  38.2 1.4 %collective-permute-start.12 = (f32[4,80,128]{2,1,0:T(8,128)S(1)}, f32[4,80,128]{2,1,0:T(8,128)S(1)}, u32[]{:S(2)}, u32[]{:S(2)}) collective-permute-start(f32[4,80,128]{2,1,0:T(8,128)S(1)} %get-tuple-element.22.carried_ref), channel_id=1, source_target_pairs={{12,8},{13,9},{14,10},{15,11},{28,24},{29,25},{30,26},{31,27}} | collective-permute-start | bytes 491528 | tf_op jit(solution)/shard_map/ppermute | solution.py:395
  39.0 1.6 %collective-permute-start.10 = (f32[4,80,128]{2,1,0:T(8,128)S(1)}, f32[4,80,128]{2,1,0:T(8,128)S(1)}, u32[]{:S(2)}, u32[]{:S(2)}) collective-permute-start(f32[4,80,128]{2,1,0:T(8,128)S(1)} %pass_on.12), channel_id=1, source_target_pairs={{8,4},{9,5},{10,6},{11,7},{24,20},{25,21},{26,22},{27,23}} | collective-permute-start | bytes 491528 | tf_op jit(solution)/shard_map/ppermute | solution.py:395
  39.7 39.0 %copy-start.1 = (f32[160,8,128]{2,1,0:T(8,128)S(1)}, f32[160,8,128]{2,1,0:T(8,128)}, u32[]{:S(2)}) copy-start(f32[160,8,128]{2,1,0:T(8,128)} %d_ref.3) | copy-start | bytes 1966084
  39.7 39.0 %copy-start.3 = (f32[160,8,128]{2,1,0:T(8,128)S(1)}, f32[160,8,128]{2,1,0:T(8,128)}, u32[]{:S(2)}) copy-start(f32[160,8,128]{2,1,0:T(8,128)} %r_ref.1) | copy-start | bytes 1966084
  39.7 2.2 %collective-permute-start.13 = (f32[4,80,128]{2,1,0:T(8,128)S(1)}, f32[4,80,128]{2,1,0:T(8,128)S(1)}, u32[]{:S(2)}, u32[]{:S(2)}) collective-permute-start(f32[4,80,128]{2,1,0:T(8,128)S(1)} %pass_on.14), channel_id=1, source_target_pairs={{8,4},{9,5},{10,6},{11,7},{24,20},{25,21},{26,22},{27,23}} | collective-permute-start | bytes 491528 | tf_op jit(solution)/shard_map/ppermute | solution.py:395
  40.6 29.8 %collective-permute-start.11 = (f32[4,80,128]{2,1,0:T(8,128)S(1)}, f32[4,80,128]{2,1,0:T(8,128)S(1)}, u32[]{:S(2)}, u32[]{:S(2)}) collective-permute-start(f32[4,80,128]{2,1,0:T(8,128)S(1)} %pass_on.13), channel_id=1, source_target_pairs={{4,0},{5,1},{6,2},{7,3},{20,16},{21,17},{22,18},{23,19}} | collective-permute-start | bytes 491528 | tf_op jit(solution)/shard_map/ppermute | solution.py:395
  42.0 30.2 %collective-permute-start.14 = (f32[4,80,128]{2,1,0:T(8,128)S(1)}, f32[4,80,128]{2,1,0:T(8,128)S(1)}, u32[]{:S(2)}, u32[]{:S(2)}) collective-permute-start(f32[4,80,128]{2,1,0:T(8,128)S(1)} %pass_on.15), channel_id=1, source_target_pairs={{4,0},{5,1},{6,2},{7,3},{20,16},{21,17},{22,18},{23,19}} | collective-permute-start | bytes 491528 | tf_op jit(solution)/shard_map/ppermute | solution.py:395
  74.7 21.7 %copy-start.4 = (f32[160,8,128]{2,1,0:T(8,128)S(1)}, f32[160,8,128]{2,1,0:T(8,128)}, u32[]{:S(2)}) copy-start(f32[160,8,128]{2,1,0:T(8,128)} %control_ref.1) | copy-start | bytes 1966084
  74.7 4.0 %collective-permute-start.15 = (f32[32,160]{1,0:T(8,128)S(1)}, f32[32,160]{1,0:T(8,128)S(1)}, u32[]{:S(2)}, u32[]{:S(2)}) collective-permute-start(f32[32,160]{1,0:T(8,128)S(1)} %get-tuple-element.24.refs_5_), channel_id=1, source_target_pairs={{0,16},{16,0},{1,17},{17,1},{2,18},{18,2},{3,19},{19,3},{4,20},{20... | collective-permute-start | bytes 61448 | tf_op jit(solution)/shard_map/ppermute | solution.py:374
  79.8 1.2 %collective-permute-start.16 = (f32[8,128]{1,0:T(8,128)S(1)}, f32[8,128]{1,0:T(8,128)S(1)}, u32[]{:S(2)}, u32[]{:S(2)}) collective-permute-start(f32[8,128]{1,0:T(8,128)S(1)} %get-tuple-element.25), channel_id=1, source_target_pairs={{0,1},{1,0},{2,3},{3,2},{4,5},{5,4},{6,7},{7,6},{8,9},{9,8},{10,11... | collective-permute-start | bytes 12296 | tf_op jit(solution)/shard_map/ppermute | solution.py:403
  81.1 3.6 %collective-permute-start.17 = (f32[8,128]{1,0:T(8,128)S(1)}, f32[8,128]{1,0:T(8,128)S(1)}, u32[]{:S(2)}, u32[]{:S(2)}) collective-permute-start(f32[8,128]{1,0:T(8,128)S(1)} %add.19), channel_id=1, source_target_pairs={{0,2},{1,3},{2,0},{3,1},{4,6},{5,7},{6,4},{7,5},{8,10},{9,11},{10,... | collective-permute-start | bytes 12296 | tf_op jit(solution)/shard_map/ppermute | solution.py:403
  84.7 3.6 %collective-permute-start.18 = (f32[8,128]{1,0:T(8,128)S(1)}, f32[8,128]{1,0:T(8,128)S(1)}, u32[]{:S(2)}, u32[]{:S(2)}) collective-permute-start(f32[8,128]{1,0:T(8,128)S(1)} %add.20), channel_id=1, source_target_pairs={{0,16},{16,0},{1,17},{17,1},{2,18},{18,2},{3,19},{19,3},{4,20},{20... | collective-permute-start | bytes 12296 | tf_op jit(solution)/shard_map/ppermute | solution.py:403
  88.3 3.6 %collective-permute-start.19 = (f32[8,128]{1,0:T(8,128)S(1)}, f32[8,128]{1,0:T(8,128)S(1)}, u32[]{:S(2)}, u32[]{:S(2)}) collective-permute-start(f32[8,128]{1,0:T(8,128)S(1)} %add.21), channel_id=1, source_target_pairs={{0,4},{4,0},{8,12},{12,8},{1,5},{5,1},{9,13},{13,9},{2,6},{6,2},{1... | collective-permute-start | bytes 12296 | tf_op jit(solution)/shard_map/ppermute | solution.py:403
  91.9 4.5 %collective-permute-start.20 = (f32[8,128]{1,0:T(8,128)S(1)}, f32[8,128]{1,0:T(8,128)S(1)}, u32[]{:S(2)}, u32[]{:S(2)}) collective-permute-start(f32[8,128]{1,0:T(8,128)S(1)} %add.22), channel_id=1, source_target_pairs={{0,8},{4,12},{8,0},{12,4},{1,9},{5,13},{9,1},{13,5},{2,10},{6,14},... | collective-permute-start | bytes 12296 | tf_op jit(solution)/shard_map/ppermute | solution.py:403

commit v3 on v1

v3 whole, which is shorter than its diff:
```python
import functools
import jax
import jax.numpy as jnp
from jax import lax
from jax.experimental import pallas as pl
from jax.experimental.pallas import tpu as pltpu
from jax.sharding import PartitionSpec as P

f32 = jnp.float32
VM = pl.BlockSpec(memory_space=pltpu.VMEM)
SM = pl.BlockSpec(memory_space=pltpu.SMEM)
HI = lax.Precision.HIGHEST


def choose(length, i):
    r = 1.0
    for k in range(i):
        r = r * (length + k) / (k + 1)
    return r


def rising(v, degree):
    r = jnp.ones_like(v)
    for k in range(degree):
        r = r * (v + (k + 1.0)) * (1.0 / (k + 1.0))
    return r


def mm(a, b, dims):
    return lax.dot_general(a, b, (dims, ((), ())), precision=HI, preferred_element_type=f32)


def iota(shape, dim):
    return lax.broadcasted_iota(jnp.int32, shape, dim).astype(f32)


def lon_consts(lonc):
    c = lonc
    q = jnp.exp(-c)
    leak = 1.0 - q
    return c, leak, 2.5 / jnp.sqrt(leak)


def lon_kernel_matrix(c_row, gain_row, cells, backward):
    a = iota((cells, cells), 0)
    b = iota((cells, cells), 1)
    lag = a - b if backward else b - a
    pos = jnp.maximum(lag, 0.0)
    shaped = rising(pos, 3) * jnp.exp(-pos * c_row) * gain_row
    return jnp.where(lag >= 0.0, shaped, 0.0)


def masked_rows(parts, y):
    rows = iota(parts[0].shape, 0)
    return jnp.concatenate([jnp.where(rows == float(y), p, 0.0) for p in parts], axis=0)


def lon_finals(c, leak, scale, cells, backward):
    x = iota(c.shape, 1)
    remain = x if backward else (cells - 1.0) - x
    decay = jnp.exp(-remain * c)
    return [leak ** (s + 1) * scale * rising(remain, s) * decay for s in range(4)]


def lon_entering(c, leak, cells, backward):
    x = iota(c.shape, 1)
    place = (cells - 1.0) - x if backward else x
    decay = jnp.exp(-(place + 1.0) * c)
    return [leak ** (3 - s) * rising(place, 3 - s) * decay for s in range(4)]


def lon_local_rows(load_row, lonc, rows, cells, backward, inside_ref, carried_ref):
    c, leak, scale = lon_consts(lonc)
    gain = leak**4 * scale
    finals = lon_finals(c, leak, scale, cells, backward)
    carried = None
    for y in range(rows):
        f = load_row(y)
        table = lon_kernel_matrix(c[y : y + 1], gain[y : y + 1], cells, backward)
        inside_ref[y] = mm(f, table, ((1,), (0,)))
        part = mm(masked_rows(finals, y), f, ((1,), (1,)))
        carried = part if carried is None else carried + part
    carried_ref[...] = carried


def lon_incoming_states(lonc, blocks, rows, cells):
    k = blocks[0].shape[1]
    n = len(blocks)
    c = jnp.broadcast_to(lonc[:, :1], (rows, k))
    leak = 1.0 - jnp.exp(-c)

    def trans(r):
        closing = jnp.exp(-float(r * cells) * c)
        return [choose(r * cells, i) * leak**i * closing for i in range(4)]

    total = [jnp.zeros((rows, k), f32) for _ in range(4)]
    for r in range(n):
        part = [blocks[r][s * rows : (s + 1) * rows] for s in range(4)]
        if r:
            t = trans(r)
            part = [sum(t[i - j] * part[j] for j in range(i + 1)) for i in range(4)]
        total = [a + b for a, b in zip(total, part)]
    t = trans(n)
    solved = []
    for i in range(4):
        v = total[i]
        for j in range(i):
            v = v + t[i - j] * solved[j]
        solved.append(v / (1.0 - t[0]))
    return jnp.concatenate(solved, axis=0)


def lon_correction(states_t, entering, y):
    return mm(states_t, masked_rows(entering, y), ((1,), (0,)))


def lat_consts(dec):
    q = jnp.exp(-dec)
    leak = 1.0 - q
    return q, leak, leak * (2.5 / jnp.sqrt(leak))


def lat_sweep(load, store, start, dec, rows, k, backward, block):
    q1, l1, g1 = lat_consts(dec)
    x = dec.shape[1]
    q = jnp.broadcast_to(q1, (block, x))
    leak = jnp.broadcast_to(l1, (block, x))
    gain = jnp.broadcast_to(g1, (block, x))
    order = range(rows - 1, -1, -1) if backward else range(rows)

    def step(i, carry):
        at = pl.ds(pl.multiple_of(i * block, 8), block)
        u = start(at)
        for y in order:
            feed = gain * load(y, at, i * block)
            u0 = q * u[0] + feed
            u1 = q * u[1] + leak * u0
            u2 = q * u[2] + leak * u1
            u3 = q * u[3] + leak * u2
            u = [u0, u1, u2, u3]
            store(y, at, i * block, u3, u if y == order[-1] else None)
        return carry

    lax.fori_loop(0, k // block, step, 0)


def swap_halves(a, b):
    half = a.shape[-1] // 2
    low = iota((1,) * (a.ndim - 1) + (a.shape[-1],), a.ndim - 1) < float(half)
    turn = lambda v: pltpu.roll(v, half, v.ndim - 1)
    return jnp.where(low, a, turn(b)), jnp.where(low, turn(a), b)


def both_halves(v):
    return swap_halves(v, v)


def sum_states(parts):
    def at_state(s, at):
        v = parts[0][s, at, :]
        for p in parts[1:]:
            v = v + p[s, at, :]
        return v

    return at_state


def member_blocks(members):
    for size in (5, 4, 2, 1):
        if members % size == 0:
            return size


def k_lon_fwd(rows, k, cells, d_ref, lon_ref, lat_ref, inside_ref, carried_ref, lonc_ref, latc_ref):
    d_ref = d_ref.reshape(k * rows, cells)
    row = jnp.broadcast_to(lon_ref[...], (rows, rows))
    own = iota((rows, rows), 0) == iota((rows, rows), 1)
    column = jnp.sum(jnp.where(own, row, 0.0), axis=1, keepdims=True)
    lonc = jnp.broadcast_to(column, (rows, cells))
    lonc_ref[...] = lonc
    first, second = both_halves(jnp.broadcast_to(lat_ref[...], (8, cells)))
    latc_ref[0] = first
    latc_ref[1] = second
    lon_local_rows(
        lambda y: d_ref[pl.ds(y, k, stride=rows), :], lonc, rows, cells, False, inside_ref, carried_ref
    )


def k_pack_members(m_ref, a_ref, b_ref):
    half = a_ref.shape[0]

    def step(i, carry):
        a, b = swap_halves(m_ref[i].astype(f32), m_ref[i + half].astype(f32))
        a_ref[i] = a
        b_ref[i] = b
        return carry

    lax.fori_loop(0, half, step, 0)


def k_lat_first(rows, k, cells, n, *refs):
    inside_ref, lon_ref, lat_ref, *rest = refs
    blocks = [r[...] for r in rest[:n]]
    *f_refs, a_ref, b_ref = rest[n:]
    lonc = lon_ref[...]
    states = lon_incoming_states(lonc, blocks, rows, cells).T
    c, leak, _ = lon_consts(lonc)
    entering = lon_entering(c, leak, cells, False)
    half = k // 2
    for y in range(rows):
        row = inside_ref[y] + lon_correction(states, entering, y)
        f_refs[0][y], f_refs[1][y] = swap_halves(row[:half], row[half:])
    zero = jnp.zeros((8, cells), f32)
    for part, (f_ref, out_ref) in enumerate(zip(f_refs, (a_ref, b_ref))):

        def store(y, at, base, value, last, out_ref=out_ref):
            if last is not None:
                for s in range(4):
                    out_ref[s, at, :] = last[s]

        lat_sweep(
            lambda y, at, base: f_ref[y, at, :],
            store,
            lambda at: [zero] * 4,
            lat_ref[part, :1],
            rows,
            half,
            False,
            8,
        )


def k_pass_on(rows, part, carried_ref, got_ref, lat_ref, out_ref):
    c = lat_ref[part, :1]
    leak = 1.0 - jnp.exp(-c)
    closing = jnp.exp(-float(rows) * c)
    t = [choose(rows, i) * leak**i * closing for i in range(4)]
    got = [got_ref[s] for s in range(4)]
    for i in range(4):
        v = carried_ref[i]
        for j in range(i + 1):
            v = v + t[i - j] * got[j]
        out_ref[i] = v


def active_pair(eig_ref, m, pairs, e, cells):
    low = iota((1, cells), 1) < float(cells // 2)
    first = jnp.where(e < eig_ref[m], 1.0, 0.0).astype(f32)
    second = jnp.where(e < eig_ref[m + pairs], 1.0, 0.0).astype(f32)
    return jnp.where(low, first, second)


def k_increment(rows, k, part, hops, pairs, modes, levels, *refs):
    f_ref, lat_ref, m_ref, v_ref, eig_ref, *rest = refs
    got = rest[:hops]
    out_ref, s_ref, inc_ref = rest[hops:]
    cells = lat_ref.shape[-1]
    at_state = sum_states(got)

    def store(y, at, base, value, last):
        s_ref[pl.ds(base * rows + y, 8, stride=rows), :] = value

    lat_sweep(
        lambda y, at, base: f_ref[y, at, :],
        store,
        lambda at: [at_state(s, at) for s in range(4)],
        lat_ref[part, :1],
        rows,
        k,
        False,
        8,
    )
    per = member_blocks(pairs)
    for b in range(pairs // per):
        fields = []
        for m in range(per):
            for e in range(modes):
                scale = active_pair(eig_ref, b * per + m, pairs, e, cells)
                at = ((b * per + m) * modes + e) * rows
                fields.append(s_ref[at : at + rows, :] * scale)

        def level(l, carry, b=b, fields=fields):
            total = None
            for m in range(per):
                p = None
                for e in range(modes):
                    t = v_ref[e, l] * fields[m * modes + e]
                    p = t if p is None else p + t
                p = m_ref[b * per + m, l] * p
                total = p if total is None else total + p
            if b == 0:
                inc_ref[l] = total
            else:
                inc_ref[l] += total
            return carry

        lax.fori_loop(0, levels, level, 0, unroll=4)
    half = levels // 2
    low = iota((1, 1, cells), 2) < float(cells // 2)
    full = inc_ref[...]
    full = full + pltpu.roll(full, cells // 2, 2)
    out_ref[...] = jnp.where(low, full[:half], full[half:])


def k_gradient(rows, k, part, pairs, modes, levels, *refs):
    inc_ref, got_ref, obs_ref, m_ref, v_ref, eig_ref, lat_ref, g_ref, carried_ref, w_ref = refs
    cells = lat_ref.shape[-1]
    half = levels // 2
    first, second = both_halves(inc_ref[...] + got_ref[...])
    obs = both_halves(obs_ref[...])[part]
    w_ref[:half] = first * obs[:half]
    w_ref[half:] = second * obs[half:]
    per = member_blocks(pairs)
    for b in range(pairs // per):

        def level(l, acc, b=b):
            w = w_ref[l]
            vs = [v_ref[e, l] for e in range(modes)]
            out = []
            for m in range(per):
                t = m_ref[b * per + m, l] * w
                for e in range(modes):
                    out.append(acc[m * modes + e] + vs[e] * t)
            return tuple(out)

        zero = jnp.zeros((rows, cells), f32)
        acc = lax.fori_loop(0, levels, level, (zero,) * (per * modes), unroll=4)
        for m in range(per):
            for e in range(modes):
                scale = active_pair(eig_ref, b * per + m, pairs, e, cells)
                at = ((b * per + m) * modes + e) * rows
                g_ref[at : at + rows, :] = acc[m * modes + e] * scale
    zero8 = jnp.zeros((8, cells), f32)

    def store(y, at, base, value, last):
        if last is not None:
            for s in range(4):
                carried_ref[s, at, :] = last[s]

    lat_sweep(
        lambda y, at, base: g_ref[pl.ds(base * rows + y, 8, stride=rows), :],
        store,
        lambda at: [zero8] * 4,
        lat_ref[part, :1],
        rows,
        k,
        True,
        8,
    )


def k_lon_bwd(rows, k, cells, hops, *refs):
    g_refs, lat_ref, lon_ref, rest = refs[:2], refs[2], refs[3], refs[4:]
    got = rest[: 2 * hops]
    inside_ref, carried_ref, p_ref = rest[2 * hops :]
    half = k // 2
    for part in range(2):
        at_state = sum_states(got[part * hops : (part + 1) * hops])
        g_ref = g_refs[part]

        def store(y, at, base, value, last, part=part):
            p_ref[part, y, at, :] = value

        lat_sweep(
            lambda y, at, base: g_ref[pl.ds(base * rows + y, 8, stride=rows), :],
            store,
            lambda at: [at_state(s, at) for s in range(4)],
            lat_ref[part, :1],
            rows,
            half,
            True,
            8,
        )

    def load_row(y):
        return jnp.concatenate(swap_halves(p_ref[0, y], p_ref[1, y]), axis=0)

    lon_local_rows(load_row, lon_ref[...], rows, cells, True, inside_ref, carried_ref)


def k_sums(rows, k, cells, n, *refs):
    inside_ref, lon_ref, d_ref, r_ref, *rest = refs
    d_ref = d_ref.reshape(k * rows, cells)
    r_ref = r_ref.reshape(k * rows, cells)
    blocks = [r[...] for r in rest[:n]]
    h_ref, sums_ref = rest[n:]
    lonc = lon_ref[...]
    states = lon_incoming_states(lonc, blocks, rows, cells).T
    c, leak, _ = lon_consts(lonc)
    entering = lon_entering(c, leak, cells, True)
    for y in range(rows):
        at = pl.ds(y, k, stride=rows)
        h_ref[at, :] = inside_ref[y] + lon_correction(states, entering, y)
    block = 64
    zero = jnp.zeros((8, cells), f32)

    def step(i, acc):
        at = pl.ds(pl.multiple_of(i * block, 8), block)
        d = d_ref[at, :]
        r = r_ref[at, :]
        h = h_ref[at, :] + d
        h_ref[at, :] = h
        fold = lambda v: v.reshape(block // 8, 8, cells).sum(axis=0)
        return (acc[0] + fold(r * r), acc[1] + fold(d * h), acc[2] + fold(r * h), acc[3] + fold(h * h))

    acc = lax.fori_loop(0, (k * rows) // block, step, (zero,) * 4)
    out = [a.sum(axis=0, keepdims=True) for a in acc]
    sums_ref[...] = jnp.concatenate(out + [jnp.zeros((4, cells), f32)], axis=0)


def k_update(sums_ref, control_ref, r_ref, d_ref, h_ref, nc_ref, nr_ref, nd_ref):
    sums = jnp.sum(sums_ref[...], axis=1, keepdims=True)
    rr, dh, rh, hh = (sums[i : i + 1].reshape(1, 1, 1) for i in range(4))
    step = rr / dh
    norm_new = rr - 2.0 * step * rh + step * step * hh
    beta = norm_new / rr
    d = d_ref[...]
    nr = r_ref[...] - step * h_ref[...]
    nc_ref[...] = control_ref[...] + step * d
    nr_ref[...] = nr
    nd_ref[...] = nr + beta * d


def call(body, outs, ins, specs=None, scratch=(), name=None, cost=None):
    return pl.pallas_call(
        body,
        out_shape=outs,
        in_specs=specs or [VM] * len(ins),
        out_specs=jax.tree.map(lambda _: VM, outs),
        scratch_shapes=scratch,
        name=name,
        cost_estimate=None if cost is None else pl.CostEstimate(flops=cost, bytes_accessed=1000, transcendentals=0),
        compiler_params=pltpu.CompilerParams(vmem_limit_bytes=16 * 1024 * 1024),
    )(*ins)


def sds(*shape):
    return jax.ShapeDtypeStruct(shape, f32)


def lon_exchange(carried, backward):
    n = lax.axis_size("lon")
    sign = -1 if backward else 1
    got = [
        lax.ppermute(carried, "lon", [(j, (j + sign * r) % n) for j in range(n)]) for r in range(1, n)
    ]
    return got + [carried]


def lat_chain(parts, latc, rows, backward):
    n = lax.axis_size("lat")
    sends = list(parts)
    got = [[] for _ in parts]
    for h in range(n - 1):
        pair = (n - 1 - h, n - 2 - h) if backward else (h, h + 1)
        for c, part in enumerate(parts):
            if h:
                sends[c] = call(
                    functools.partial(k_pass_on, rows, c),
                    sds(*part.shape),
                    [part, got[c][-1], latc],
                    name="pass_on",
                )
            got[c].append(lax.ppermute(sends[c], "lat", [pair]))
    return got


def all_sum(v, axes, steps):
    total = 1
    for a in axes:
        total *= lax.axis_size(a)
    masks = [0]
    for s in steps:
        masks = masks + [m ^ s for m in masks]
    got = [lax.ppermute(v, axes, [(i, i ^ m) for i in range(total)]) for m in masks[1:]]
    for g in got:
        v = v + g
    return v


def powers(n):
    out, d = [], 1
    while d < n:
        out.append(d)
        d *= 2
    return out


def reduce_everywhere(v):
    n_lon, n_lat, n_mem = (lax.axis_size(a) for a in ("lon", "lat", "mem"))
    mem = powers(n_mem)
    if n_lon == 2 and len(mem) == 2:
        v = all_sum(v, ("mem",), mem[:1])
        v = all_sum(v, ("lon", "mem"), [mem[1], n_mem])
    else:
        for s in mem:
            v = all_sum(v, ("mem",), [s])
        for s in powers(n_lon):
            v = all_sum(v, ("lon",), [s])
    lat = powers(n_lat)
    for i in range(0, len(lat), 2):
        v = all_sum(v, ("lat",), lat[i : i + 2])
    return v


def body(control, residual, direction, members, vert_modes, eig_count, lon_decay, lat_decay, obs_weight):
    k, rows, cells = direction.shape
    mcount, levels = members.shape[:2]
    modes = vert_modes.shape[0]
    n_lon, n_lat, n_mem = (lax.axis_size(a) for a in ("lon", "lat", "mem"))
    hops = n_lat - 1
    half = k // 2
    pairs = mcount // 2
    state = sds(4, half, cells)

    inside, carried, lonc, latc = call(
        functools.partial(k_lon_fwd, rows, k, cells),
        (sds(rows, k, cells), sds(4 * rows, k), sds(rows, cells), sds(2, 8, cells)),
        [direction, lon_decay.reshape(1, rows), lat_decay.reshape(1, cells)],
        name="lon_fwd",
    )
    packed = call(
        k_pack_members, (sds(pairs, levels, rows, cells),) * 2, [members], name="pack_members", cost=10**9
    )
    blocks = lon_exchange(carried, False)
    fa, fb, pa, pb = call(
        functools.partial(k_lat_first, rows, k, cells, n_lon),
        (sds(rows, half, cells),) * 2 + (state,) * 2,
        [inside, lonc, latc, *blocks],
        name="lat_first",
    )
    got = lat_chain([pa, pb], latc, rows, False)
    fields = (fa, fb)
    inc = [None, None]
    for part in range(2):
        inc[part] = call(
            functools.partial(k_increment, rows, half, part, hops, pairs, modes, levels),
            sds(levels // 2, rows, cells),
            [fields[part], latc, packed[part], vert_modes, eig_count, *got[part]],
            specs=[VM, VM, VM, SM, SM] + [VM] * hops,
            scratch=[pltpu.VMEM((half * rows, cells), f32), pltpu.VMEM((levels, rows, cells), f32)],
            name="increment",
        )
    grads, sends = [None, None], [None, None]
    for part in range(2):
        v = inc[part]
        step = 1
        while step * 2 < n_mem:
            v = v + lax.ppermute(v, "mem", [(i, i ^ step) for i in range(n_mem)])
            step *= 2
        other = lax.ppermute(v, "mem", [(i, i ^ step) for i in range(n_mem)])
        grads[part], sends[part] = call(
            functools.partial(k_gradient, rows, half, part, pairs, modes, levels),
            (sds(half * rows, cells), state),
            [v, other, obs_weight, packed[part], vert_modes, eig_count, latc],
            specs=[VM, VM, VM, VM, SM, SM, VM],
            scratch=[pltpu.VMEM((levels, rows, cells), f32)],
            name="gradient",
        )
    got = lat_chain(sends, latc, rows, True)
    inside, carried = call(
        functools.partial(k_lon_bwd, rows, k, cells, hops),
        (sds(rows, k, cells), sds(4 * rows, k)),
        [*grads, latc, lonc, *got[0], *got[1]],
        scratch=[pltpu.VMEM((2, rows, half, cells), f32)],
        name="lon_bwd",
    )
    blocks = lon_exchange(carried, True)
    h, sums = call(
        functools.partial(k_sums, rows, k, cells, n_lon),
        (sds(k * rows, cells), sds(8, cells)),
        [inside, lonc, direction, residual, *blocks],
        name="sums",
    )
    sums = reduce_everywhere(sums)
    outs = call(
        k_update,
        (sds(k, rows, cells),) * 3,
        [sums, control, residual, direction, h.reshape(k, rows, cells)],
        name="update",
    )
    return tuple(outs)


def solution(mesh):
    field = P("mem", "lat", "lon")
    placed = (
        field,
        field,
        field,
        P("mem", None, "lat", "lon"),
        P(),
        P("mem"),
        P("lat"),
        P("lon"),
        P(None, "lat", "lon"),
    )
    return jax.shard_map(body, mesh=mesh, in_specs=placed, out_specs=(field,) * 3, check_vma=False)
```

time: 132 us -> 91.2 us (0.69)
  Pallas kernels: 43.1 us -> 18.4 us
  waiting for transfers between devices: 51.3 us -> 39.9 us
  local copies, waits for them, and re-layouts: 11.9 us -> 2.43 us
  starting transfers between devices: 22.3 us -> 29 us
  other arithmetic: 2.22 us -> 0.03 us
    pallas_call x15 -> x18, Pallas kernels: 43.1 us -> 18.4 us  [call(): pl.pallas_call(body, out_shape=outs, in_specs=specs or [VM] * len(ins), o...]
    ppermute x7 -> x11, waiting for transfers between devices: 19.3 us -> 9.28 us  [the longest x7 7.1 us: all_sum(): lax.ppermute(v, axes, [(i, i ^ m) for i in range(total)])]
    ppermute x7 -> x11, starting transfers between devices: 4.61 us -> 11 us  [the longest x7 7.94 us: all_sum(): lax.ppermute(v, axes, [(i, i ^ m) for i in range(total)])]
    unnamed x40 -> x20, local copies, waits for them, and re-layouts: 8.55 us -> 2.43 us
    add x6 -> x5, other arithmetic: 2.22 us -> 0.03 us  [the longest x2 0.02 us: body(): v = v + lax.ppermute(v, 'mem', [(i, i ^ step) for i in range(n_mem)])]
    slice x2 -> x0, local copies, waits for them, and re-layouts: 2.03 us -> none  [lat_chain(): parts = [carried[:, c * size:(c + 1) * size] for c in range(chunks)]]
  transfers between devices with their start and end apart: 21 -> 25, of which waited for: 12 -> 13; matrix products, arithmetic and copies ran while one was open for 0% -> 0% of each run, Pallas kernels for 10% -> 11%
where the time goes in v3:
time: 91.2 us; the launch traced here: 90.8 us
  waiting for transfers between devices  39.9 us (44%)
  starting transfers between devices  29 us (32%)
  Pallas kernels  18.4 us (20%)
  local copies, waits for them, and re-layouts  2.43 us (3%)
  between operations  1.02 us (1%)
    ppermute x12, waiting for transfers between devices, lat_chain(): got[c].append(lax.ppermute(sends[c], 'lat', [pair]))  26.3 us
    pallas_call x18, Pallas kernels, call(): pl.pallas_call(body, out_shape=outs, in_specs=specs or [VM] * len(ins), o...  18.4 us
    ppermute x12, starting transfers between devices, lat_chain(): got[c].append(lax.ppermute(sends[c], 'lat', [pair]))  13.4 us
    ppermute x7, starting transfers between devices, all_sum(): lax.ppermute(v, axes, [(i, i ^ m) for i in range(total)])  7.94 us
    ppermute x7, waiting for transfers between devices, all_sum(): lax.ppermute(v, axes, [(i, i ^ m) for i in range(total)])  7.1 us
    ppermute x2, starting transfers between devices, lon_exchange(): lax.ppermute(carried, 'lon', [(j, (j + sign * r) % n) for j in range(n)])  4.6 us
    ppermute x2, waiting for transfers between devices, lon_exchange(): lax.ppermute(carried, 'lon', [(j, (j + sign * r) % n) for j in range(n)])  4.31 us
    ppermute x2, starting transfers between devices, body(): other = lax.ppermute(v, 'mem', [(i, i ^ step) for i in range(n_mem)])  2.47 us
  transfers between devices with their start and end apart: 25, of which 13 were waited for; matrix products, arithmetic and copies ran while one was open for 0% of the time, Pallas kernels for 11%

profile of v3, /device:TPU:0, one launch (start us, length us, event | category | flops | bytes accessed | tf_op | source)
XLA Modules:
  0.0 90.8 jit_solution(1484049203458342166)
XLA Ops:
  0.6 1.1 %copy-done = f32[160,8,128]{2,1,0:T(8,128)S(1)} copy-done((f32[160,8,128]{2,1,0:T(8,128)S(1)}, f32[160,8,128]{2,1,0:T(8,128)}, u32[]{:S(2)}) %copy-start) | copy-done | bytes 655384
  3.0 1.9 %lon_fwd.1 = (f32[8,160,128]{2,1,0:T(8,128)S(1)}, f32[32,160]{1,0:T(8,128)S(1)}, f32[8,128]{1,0:T(8,128)S(1)}, f32[2,8,128]{2,1,0:T(8,128)S(1)}) custom-call(f32[160,8,128]{2,1,0:T(8,128)S(1)} %copy-done, f32[1,8]{1,0:T(1,128)S(1)} %bitcast.4, f32[1,128]{1,0:T(1,128)S(1)} %bitcast.5), custom_call_target="tpu_custom_call" | custom-call | tf_op jit(solution)/shard_map/lon_fwd/pallas_call | solution.py:425
  4.9 3.0 %collective-permute-start = (f32[32,160]{1,0:T(8,128)S(1)}, f32[32,160]{1,0:T(8,128)S(1)}, u32[]{:S(2)}, u32[]{:S(2)}) collective-permute-start(f32[32,160]{1,0:T(8,128)S(1)} %get-tuple-element.24.refs_4_), channel_id=1, source_target_pairs={{0,16},{16,0},{1,17},{17,1},{2,18},{18,2},{3,19},{19,3},{4,20},{20... | collective-permute-start | bytes 61448 | tf_op jit(solution)/shard_map/ppermute | solution.py:445
  8.0 1.9 %collective-permute-done.refs_3_ = f32[32,160]{1,0:T(8,128)S(1)} collective-permute-done((f32[32,160]{1,0:T(8,128)S(1)}, f32[32,160]{1,0:T(8,128)S(1)}, u32[]{:S(2)}, u32[]{:S(2)}) %collective-permute-start) | collective-permute-done | bytes 20512 | tf_op jit(solution)/shard_map/ppermute | solution.py:445
  9.9 1.4 %lat_first.1 = (f32[8,80,128]{2,1,0:T(8,128)S(1)}, f32[8,80,128]{2,1,0:T(8,128)S(1)}, f32[4,80,128]{2,1,0:T(8,128)S(1)}, f32[4,80,128]{2,1,0:T(8,128)S(1)}) custom-call(f32[8,160,128]{2,1,0:T(8,128)S(1)} %get-tuple-element.21.refs_0_, f32[8,128]{1,0:T(8,128)S(1)} %get-tuple-element.22.refs_1_.refs_3_, ...), custom_call_target="tpu_custom_call" | custom-call | tf_op jit(solution)/shard_map/lat_first/pallas_call | solution.py:425
  11.3 4.0 %collective-permute-start.6 = (f32[4,80,128]{2,1,0:T(8,128)S(1)}, f32[4,80,128]{2,1,0:T(8,128)S(1)}, u32[]{:S(2)}, u32[]{:S(2)}) collective-permute-start(f32[4,80,128]{2,1,0:T(8,128)S(1)} %get-tuple-element.31.carried_ref), channel_id=1, source_target_pairs={{0,4},{1,5},{2,6},{3,7},{16,20},{17,21},{18,22},{19,23}} | collective-permute-start | bytes 491528 | tf_op jit(solution)/shard_map/ppermute | solution.py:464
  15.3 1.3 %collective-permute-start.1 = (f32[4,80,128]{2,1,0:T(8,128)S(1)}, f32[4,80,128]{2,1,0:T(8,128)S(1)}, u32[]{:S(2)}, u32[]{:S(2)}) collective-permute-start(f32[4,80,128]{2,1,0:T(8,128)S(1)} %get-tuple-element.27.carried_ref), channel_id=1, source_target_pairs={{0,4},{1,5},{2,6},{3,7},{16,20},{17,21},{18,22},{19,23}} | collective-permute-start | bytes 491528 | tf_op jit(solution)/shard_map/ppermute | solution.py:464
  16.6 2.7 %collective-permute-done.6.got_ref.refs_5_ = f32[4,80,128]{2,1,0:T(8,128)S(1)} collective-permute-done((f32[4,80,128]{2,1,0:T(8,128)S(1)}, f32[4,80,128]{2,1,0:T(8,128)S(1)}, u32[]{:S(2)}, u32[]{:S(2)}) %collective-permute-start.6) | collective-permute-done | bytes 163872 | tf_op jit(solution)/shard_map/ppermute | solution.py:464
  20.1 1.0 %collective-permute-done.1.got_ref.refs_5_ = f32[4,80,128]{2,1,0:T(8,128)S(1)} collective-permute-done((f32[4,80,128]{2,1,0:T(8,128)S(1)}, f32[4,80,128]{2,1,0:T(8,128)S(1)}, u32[]{:S(2)}, u32[]{:S(2)}) %collective-permute-start.1) | collective-permute-done | bytes 163872 | tf_op jit(solution)/shard_map/ppermute | solution.py:464
  23.4 1.0 %pack_members.1 = (f32[10,32,8,128]{3,2,1,0:T(8,128)S(1)}, f32[10,32,8,128]{3,2,1,0:T(8,128)S(1)}) custom-call(bf16[20,32,8,128]{3,2,1,0:T(8,128)(2,1)S(1)} %copy-done.9), custom_call_target="tpu_custom_call" | custom-call | flops 1000000000 | bytes 1000 | tf_op jit(solution)/shard_map/pack_members/pallas_call | solution.py:425
  24.4 2.1 %increment.3 = f32[16,8,128]{2,1,0:T(8,128)S(1)} custom-call(f32[8,80,128]{2,1,0:T(8,128)S(1)} %get-tuple-element.29.refs_0_, f32[2,8,128]{2,1,0:T(8,128)S(1)} %get-tuple-element.23.refs_2_.lat_ref.refs_1_.refs_6_, f32[10,32,8,128]{3,2,1,0:T(8,128)S(1)} %get-tuple-element.30.refs_2_.refs_3_, f32[8,32]{1,0:T(8,128)S(1)} %copy-done.5, s32[20]{0:T(128)S(1)} %copy-done.6, ...), custom_call_target="tpu_custom_call" | custom-call | tf_op jit(solution)/shard_map/increment/pallas_call | solution.py:425
  26.7 2.1 %increment.2 = f32[16,8,128]{2,1,0:T(8,128)S(1)} custom-call(f32[8,80,128]{2,1,0:T(8,128)S(1)} %get-tuple-element.25.refs_0_, f32[2,8,128]{2,1,0:T(8,128)S(1)} %get-tuple-element.23.refs_2_.lat_ref.refs_1_.refs_6_, f32[10,32,8,128]{3,2,1,0:T(8,128)S(1)} %get-tuple-element.26.refs_2_.refs_3_, f32[8,32]{1,0:T(8,128)S(1)} %copy-done.5, s32[20]{0:T(128)S(1)} %copy-done.6, ...), custom_call_target="tpu_custom_call" | custom-call | tf_op jit(solution)/shard_map/increment/pallas_call | solution.py:425
  29.3 1.6 %collective-permute-start.10 = (f32[16,8,128]{2,1,0:T(8,128)S(1)}, f32[16,8,128]{2,1,0:T(8,128)S(1)}, u32[]{:S(2)}, u32[]{:S(2)}) collective-permute-start(f32[16,8,128]{2,1,0:T(8,128)S(1)} %add.28.refs_0_), channel_id=1, source_target_pairs={{0,2},{1,3},{2,0},{3,1},{4,6},{5,7},{6,4},{7,5},{8,10},{9,11},{10,... | collective-permute-start | bytes 196616 | tf_op jit(solution)/shard_map/ppermute | solution.py:551
  31.8 2.2 %collective-permute-done.10.refs_1_ = f32[16,8,128]{2,1,0:T(8,128)S(1)} collective-permute-done((f32[16,8,128]{2,1,0:T(8,128)S(1)}, f32[16,8,128]{2,1,0:T(8,128)S(1)}, u32[]{:S(2)}, u32[]{:S(2)}) %collective-permute-start.10) | collective-permute-done | bytes 65568 | tf_op jit(solution)/shard_map/ppermute | solution.py:551
  34.0 2.2 %gradient.3 = (f32[640,128]{1,0:T(8,128)S(1)}, f32[4,80,128]{2,1,0:T(8,128)S(1)}) custom-call(f32[16,8,128]{2,1,0:T(8,128)S(1)} %add.28.refs_0_, f32[16,8,128]{2,1,0:T(8,128)S(1)} %collective-permute-done.10.refs_1_, f32[32,8,128]{2,1,0:T(8,128)S(1)} %copy-done.4, f32[10,32,8,128]{3,2,1,0:T(8,128)S(1)} %get-tuple-element.30.refs_2_.refs_3_, ...), custom_call_target="tpu_custom_call" | custom-call | tf_op jit(solution)/shard_map/gradient/pallas_call | solution.py:425
  36.8 2.2 %gradient.2 = (f32[640,128]{1,0:T(8,128)S(1)}, f32[4,80,128]{2,1,0:T(8,128)S(1)}) custom-call(f32[16,8,128]{2,1,0:T(8,128)S(1)} %add.27.refs_0_, f32[16,8,128]{2,1,0:T(8,128)S(1)} %collective-permute-done.5.refs_1_, f32[32,8,128]{2,1,0:T(8,128)S(1)} %copy-done.4, f32[10,32,8,128]{3,2,1,0:T(8,128)S(1)} %get-tuple-element.26.refs_2_.refs_3_, ...), custom_call_target="tpu_custom_call" | custom-call | tf_op jit(solution)/shard_map/gradient/pallas_call | solution.py:425
  41.4 1.3 %collective-permute-start.16 = (f32[4,80,128]{2,1,0:T(8,128)S(1)}, f32[4,80,128]{2,1,0:T(8,128)S(1)}, u32[]{:S(2)}, u32[]{:S(2)}) collective-permute-start(f32[4,80,128]{2,1,0:T(8,128)S(1)} %pass_on.15), channel_id=1, source_target_pairs={{4,0},{5,1},{6,2},{7,3},{20,16},{21,17},{22,18},{23,19}} | collective-permute-start | bytes 491528 | tf_op jit(solution)/shard_map/ppermute | solution.py:464
  42.7 1.3 %collective-permute-start.13 = (f32[4,80,128]{2,1,0:T(8,128)S(1)}, f32[4,80,128]{2,1,0:T(8,128)S(1)}, u32[]{:S(2)}, u32[]{:S(2)}) collective-permute-start(f32[4,80,128]{2,1,0:T(8,128)S(1)} %pass_on.13), channel_id=1, source_target_pairs={{4,0},{5,1},{6,2},{7,3},{20,16},{21,17},{22,18},{23,19}} | collective-permute-start | bytes 491528 | tf_op jit(solution)/shard_map/ppermute | solution.py:464
  44.0 20.2 %collective-permute-done.16.refs_9_ = f32[4,80,128]{2,1,0:T(8,128)S(1)} collective-permute-done((f32[4,80,128]{2,1,0:T(8,128)S(1)}, f32[4,80,128]{2,1,0:T(8,128)S(1)}, u32[]{:S(2)}, u32[]{:S(2)}) %collective-permute-start.16) | collective-permute-done | bytes 163872 | tf_op jit(solution)/shard_map/ppermute | solution.py:464
  64.2 2.4 %collective-permute-done.13.refs_6_ = f32[4,80,128]{2,1,0:T(8,128)S(1)} collective-permute-done((f32[4,80,128]{2,1,0:T(8,128)S(1)}, f32[4,80,128]{2,1,0:T(8,128)S(1)}, u32[]{:S(2)}, u32[]{:S(2)}) %collective-permute-start.13) | collective-permute-done | bytes 163872 | tf_op jit(solution)/shard_map/ppermute | solution.py:464
  66.6 2.5 %lon_bwd.1 = (f32[8,160,128]{2,1,0:T(8,128)S(1)}, f32[32,160]{1,0:T(8,128)S(1)}) custom-call(f32[640,128]{1,0:T(8,128)S(1)} %get-tuple-element.28.refs_0_, f32[640,128]{1,0:T(8,128)S(1)} %get-tuple-element.32.refs_1_, f32[2,8,128]{2,1,0:T(8,128)S(1)} %get-tuple-element.23.refs_2_.lat_ref.refs_1_.refs_6_, f32[8,128]{1,0:T(8,128)S(1)} %get-tuple-element.22.refs_1_.refs_3_, ...), custom_call_target="tpu_custom_call" | custom-call | tf_op jit(solution)/shard_map/lon_bwd/pallas_call | solution.py:425
  69.1 1.6 %collective-permute-start.17 = (f32[32,160]{1,0:T(8,128)S(1)}, f32[32,160]{1,0:T(8,128)S(1)}, u32[]{:S(2)}, u32[]{:S(2)}) collective-permute-start(f32[32,160]{1,0:T(8,128)S(1)} %get-tuple-element.36.refs_5_), channel_id=1, source_target_pairs={{0,16},{16,0},{1,17},{17,1},{2,18},{18,2},{3,19},{19,3},{4,20},{20... | collective-permute-start | bytes 61448 | tf_op jit(solution)/shard_map/ppermute | solution.py:445
  70.7 2.4 %collective-permute-done.17.refs_4_ = f32[32,160]{1,0:T(8,128)S(1)} collective-permute-done((f32[32,160]{1,0:T(8,128)S(1)}, f32[32,160]{1,0:T(8,128)S(1)}, u32[]{:S(2)}, u32[]{:S(2)}) %collective-permute-start.17) | collective-permute-done | bytes 20512 | tf_op jit(solution)/shard_map/ppermute | solution.py:445
  73.1 1.1 %sums.1 = (f32[1280,128]{1,0:T(8,128)S(1)}, f32[8,128]{1,0:T(8,128)S(1)}) custom-call(f32[8,160,128]{2,1,0:T(8,128)S(1)} %get-tuple-element.35.refs_0_, f32[8,128]{1,0:T(8,128)S(1)} %get-tuple-element.22.refs_1_.refs_3_, f32[160,8,128]{2,1,0:T(8,128)S(1)} %copy-done.1, f32[160,8,128]{2,1,0:T(8,128)S(1)} %copy-done.2, ...), custom_call_target="tpu_custom_call" | custom-call | tf_op jit(solution)/shard_map/sums/pallas_call | solution.py:425
  74.3 1.2 %collective-permute-done.18 = f32[8,128]{1,0:T(8,128)S(1)} collective-permute-done((f32[8,128]{1,0:T(8,128)S(1)}, f32[8,128]{1,0:T(8,128)S(1)}, u32[]{:S(2)}, u32[]{:S(2)}) %collective-permute-start.18) | collective-permute-done | bytes 4128 | tf_op jit(solution)/shard_map/ppermute | solution.py:475
  75.5 1.8 %collective-permute-start.19 = (f32[8,128]{1,0:T(8,128)S(1)}, f32[8,128]{1,0:T(8,128)S(1)}, u32[]{:S(2)}, u32[]{:S(2)}) collective-permute-start(f32[8,128]{1,0:T(8,128)S(1)} %add.29), channel_id=1, source_target_pairs={{0,2},{1,3},{2,0},{3,1},{16,18},{17,19},{18,16},{19,17},{4,6},{5,7... | collective-permute-start | bytes 12296 | tf_op jit(solution)/shard_map/ppermute | solution.py:475
  77.3 1.5 %collective-permute-start.20 = (f32[8,128]{1,0:T(8,128)S(1)}, f32[8,128]{1,0:T(8,128)S(1)}, u32[]{:S(2)}, u32[]{:S(2)}) collective-permute-start(f32[8,128]{1,0:T(8,128)S(1)} %add.29), channel_id=1, source_target_pairs={{0,16},{1,17},{2,18},{3,19},{16,0},{17,1},{18,2},{19,3},{4,20},{5,... | collective-permute-start | bytes 12296 | tf_op jit(solution)/shard_map/ppermute | solution.py:475
  79.1 1.8 %collective-permute-done.20 = f32[8,128]{1,0:T(8,128)S(1)} collective-permute-done((f32[8,128]{1,0:T(8,128)S(1)}, f32[8,128]{1,0:T(8,128)S(1)}, u32[]{:S(2)}, u32[]{:S(2)}) %collective-permute-start.20) | collective-permute-done | bytes 4128 | tf_op jit(solution)/shard_map/ppermute | solution.py:475
  80.9 2.4 %collective-permute-done.21 = f32[8,128]{1,0:T(8,128)S(1)} collective-permute-done((f32[8,128]{1,0:T(8,128)S(1)}, f32[8,128]{1,0:T(8,128)S(1)}, u32[]{:S(2)}, u32[]{:S(2)}) %collective-permute-start.21) | collective-permute-done | bytes 4128 | tf_op jit(solution)/shard_map/ppermute | solution.py:475
  83.4 4.3 %collective-permute-start.24 = (f32[8,128]{1,0:T(8,128)S(1)}, f32[8,128]{1,0:T(8,128)S(1)}, u32[]{:S(2)}, u32[]{:S(2)}) collective-permute-start(f32[8,128]{1,0:T(8,128)S(1)} %add_add_fusion.1), channel_id=1, source_target_pairs={{0,12},{4,8},{8,4},{12,0},{1,13},{5,9},{9,5},{13,1},{2,14},{6,10},... | collective-permute-start | bytes 12296 | tf_op jit(solution)/shard_map/ppermute | solution.py:475
  87.9 1.4 %collective-permute-done.24 = f32[8,128]{1,0:T(8,128)S(1)} collective-permute-done((f32[8,128]{1,0:T(8,128)S(1)}, f32[8,128]{1,0:T(8,128)S(1)}, u32[]{:S(2)}, u32[]{:S(2)}) %collective-permute-start.24) | collective-permute-done | bytes 4128 | tf_op jit(solution)/shard_map/ppermute | solution.py:475
  89.3 1.5 %update.1 = (f32[160,8,128]{2,1,0:T(8,128)}, f32[160,8,128]{2,1,0:T(8,128)}, f32[160,8,128]{2,1,0:T(8,128)}) custom-call(f32[8,128]{1,0:T(8,128)S(1)} %add_add_fusion.sums_ref, f32[160,8,128]{2,1,0:T(8,128)S(1)} %copy-done.3, f32[160,8,128]{2,1,0:T(8,128)S(1)} %copy-done.2, f32[160,8,128]{2,1,0:T(8,128)S(1)} %copy-done.1, f32[160,8,128]{2,1,0:T(8,128)S(1)} %bitcast.3), custom_call_target="tpu_custom_call" | custom-call | tf_op jit(solution)/shard_map/update/pallas_call | solution.py:425
  (61 shorter events, 9.4 us)
Async XLA Ops:
  4.9 4.9 %collective-permute-start = (f32[32,160]{1,0:T(8,128)S(1)}, f32[32,160]{1,0:T(8,128)S(1)}, u32[]{:S(2)}, u32[]{:S(2)}) collective-permute-start(f32[32,160]{1,0:T(8,128)S(1)} %get-tuple-element.24.refs_4_), channel_id=1, source_target_pairs={{0,16},{16,0},{1,17},{17,1},{2,18},{18,2},{3,19},{19,3},{4,20},{20... | collective-permute-start | bytes 61448 | tf_op jit(solution)/shard_map/ppermute | solution.py:445
  9.9 13.5 %copy-start.9 = (bf16[20,32,8,128]{3,2,1,0:T(8,128)(2,1)S(1)}, bf16[20,32,8,128]{3,2,1,0:T(8,128)(2,1)}, u32[]{:S(2)}) copy-start(bf16[20,32,8,128]{3,2,1,0:T(8,128)(2,1)} %m_ref.1) | copy-start | bytes 3932164
  11.3 8.1 %collective-permute-start.6 = (f32[4,80,128]{2,1,0:T(8,128)S(1)}, f32[4,80,128]{2,1,0:T(8,128)S(1)}, u32[]{:S(2)}, u32[]{:S(2)}) collective-permute-start(f32[4,80,128]{2,1,0:T(8,128)S(1)} %get-tuple-element.31.carried_ref), channel_id=1, source_target_pairs={{0,4},{1,5},{2,6},{3,7},{16,20},{17,21},{18,22},{19,23}} | collective-permute-start | bytes 491528 | tf_op jit(solution)/shard_map/ppermute | solution.py:464
  15.3 5.8 %collective-permute-start.1 = (f32[4,80,128]{2,1,0:T(8,128)S(1)}, f32[4,80,128]{2,1,0:T(8,128)S(1)}, u32[]{:S(2)}, u32[]{:S(2)}) collective-permute-start(f32[4,80,128]{2,1,0:T(8,128)S(1)} %get-tuple-element.27.carried_ref), channel_id=1, source_target_pairs={{0,4},{1,5},{2,6},{3,7},{16,20},{17,21},{18,22},{19,23}} | collective-permute-start | bytes 491528 | tf_op jit(solution)/shard_map/ppermute | solution.py:464
  19.4 2.4 %collective-permute-start.7 = (f32[4,80,128]{2,1,0:T(8,128)S(1)}, f32[4,80,128]{2,1,0:T(8,128)S(1)}, u32[]{:S(2)}, u32[]{:S(2)}) collective-permute-start(f32[4,80,128]{2,1,0:T(8,128)S(1)} %pass_on.10), channel_id=1, source_target_pairs={{4,8},{5,9},{6,10},{7,11},{20,24},{21,25},{22,26},{23,27}} | collective-permute-start | bytes 491528 | tf_op jit(solution)/shard_map/ppermute | solution.py:464
  21.2 1.4 %collective-permute-start.2 = (f32[4,80,128]{2,1,0:T(8,128)S(1)}, f32[4,80,128]{2,1,0:T(8,128)S(1)}, u32[]{:S(2)}, u32[]{:S(2)}) collective-permute-start(f32[4,80,128]{2,1,0:T(8,128)S(1)} %pass_on.8), channel_id=1, source_target_pairs={{4,8},{5,9},{6,10},{7,11},{20,24},{21,25},{22,26},{23,27}} | collective-permute-start | bytes 491528 | tf_op jit(solution)/shard_map/ppermute | solution.py:464
  21.9 2.5 %collective-permute-start.8 = (f32[4,80,128]{2,1,0:T(8,128)S(1)}, f32[4,80,128]{2,1,0:T(8,128)S(1)}, u32[]{:S(2)}, u32[]{:S(2)}) collective-permute-start(f32[4,80,128]{2,1,0:T(8,128)S(1)} %pass_on.11), channel_id=1, source_target_pairs={{8,12},{9,13},{10,14},{11,15},{24,28},{25,29},{26,30},{27,31}} | collective-permute-start | bytes 491528 | tf_op jit(solution)/shard_map/ppermute | solution.py:464
  22.6 1.8 %copy-start.5 = (f32[8,32]{1,0:T(8,128)S(1)}, f32[8,32]{1,0:T(8,128)}, u32[]{:S(2)}) copy-start(f32[8,32]{1,0:T(8,128)} %refs_4_.7) | copy-start | bytes 3076
  22.7 1.8 %copy-start.6 = (s32[20]{0:T(128)S(1)}, s32[20]{0:T(128)}, u32[]{:S(2)}) copy-start(s32[20]{0:T(128)} %refs_5_.3) | copy-start | bytes 244
  22.7 4.0 %collective-permute-start.3 = (f32[4,80,128]{2,1,0:T(8,128)S(1)}, f32[4,80,128]{2,1,0:T(8,128)S(1)}, u32[]{:S(2)}, u32[]{:S(2)}) collective-permute-start(f32[4,80,128]{2,1,0:T(8,128)S(1)} %pass_on.9), channel_id=1, source_target_pairs={{8,12},{9,13},{10,14},{11,15},{24,28},{25,29},{26,30},{27,31}} | collective-permute-start | bytes 491528 | tf_op jit(solution)/shard_map/ppermute | solution.py:464
  26.5 7.4 %copy-start.4 = (f32[32,8,128]{2,1,0:T(8,128)S(1)}, f32[32,8,128]{2,1,0:T(8,128)}, u32[]{:S(2)}) copy-start(f32[32,8,128]{2,1,0:T(8,128)} %refs_2_.4) | copy-start | bytes 393220
  26.6 2.7 %collective-permute-start.9 = (f32[16,8,128]{2,1,0:T(8,128)S(1)}, f32[16,8,128]{2,1,0:T(8,128)S(1)}, u32[]{:S(2)}, u32[]{:S(2)}) collective-permute-start(f32[16,8,128]{2,1,0:T(8,128)S(1)} %increment.3), channel_id=1, source_target_pairs={{0,1},{1,0},{2,3},{3,2},{4,5},{5,4},{6,7},{7,6},{8,9},{9,8},{10,11... | collective-permute-start | bytes 196616 | tf_op jit(solution)/shard_map/ppermute | solution.py:549
  28.8 2.2 %collective-permute-start.4 = (f32[16,8,128]{2,1,0:T(8,128)S(1)}, f32[16,8,128]{2,1,0:T(8,128)S(1)}, u32[]{:S(2)}, u32[]{:S(2)}) collective-permute-start(f32[16,8,128]{2,1,0:T(8,128)S(1)} %increment.2), channel_id=1, source_target_pairs={{0,1},{1,0},{2,3},{3,2},{4,5},{5,4},{6,7},{7,6},{8,9},{9,8},{10,11... | collective-permute-start | bytes 196616 | tf_op jit(solution)/shard_map/ppermute | solution.py:549
  29.3 4.7 %collective-permute-start.10 = (f32[16,8,128]{2,1,0:T(8,128)S(1)}, f32[16,8,128]{2,1,0:T(8,128)S(1)}, u32[]{:S(2)}, u32[]{:S(2)}) collective-permute-start(f32[16,8,128]{2,1,0:T(8,128)S(1)} %add.28.refs_0_), channel_id=1, source_target_pairs={{0,2},{1,3},{2,0},{3,1},{4,6},{5,7},{6,4},{7,5},{8,10},{9,11},{10,... | collective-permute-start | bytes 196616 | tf_op jit(solution)/shard_map/ppermute | solution.py:551
  30.9 5.9 %collective-permute-start.5 = (f32[16,8,128]{2,1,0:T(8,128)S(1)}, f32[16,8,128]{2,1,0:T(8,128)S(1)}, u32[]{:S(2)}, u32[]{:S(2)}) collective-permute-start(f32[16,8,128]{2,1,0:T(8,128)S(1)} %add.27.refs_0_), channel_id=1, source_target_pairs={{0,2},{1,3},{2,0},{3,1},{4,6},{5,7},{6,4},{7,5},{8,10},{9,11},{10,... | collective-permute-start | bytes 196616 | tf_op jit(solution)/shard_map/ppermute | solution.py:551
  36.1 3.5 %collective-permute-start.14 = (f32[4,80,128]{2,1,0:T(8,128)S(1)}, f32[4,80,128]{2,1,0:T(8,128)S(1)}, u32[]{:S(2)}, u32[]{:S(2)}) collective-permute-start(f32[4,80,128]{2,1,0:T(8,128)S(1)} %get-tuple-element.34.carried_ref), channel_id=1, source_target_pairs={{12,8},{13,9},{14,10},{15,11},{28,24},{29,25},{30,26},{31,27}} | collective-permute-start | bytes 491528 | tf_op jit(solution)/shard_map/ppermute | solution.py:464
  39.0 1.4 %collective-permute-start.11 = (f32[4,80,128]{2,1,0:T(8,128)S(1)}, f32[4,80,128]{2,1,0:T(8,128)S(1)}, u32[]{:S(2)}, u32[]{:S(2)}) collective-permute-start(f32[4,80,128]{2,1,0:T(8,128)S(1)} %get-tuple-element.33.carried_ref), channel_id=1, source_target_pairs={{12,8},{13,9},{14,10},{15,11},{28,24},{29,25},{30,26},{31,27}} | collective-permute-start | bytes 491528 | tf_op jit(solution)/shard_map/ppermute | solution.py:464
  39.7 1.6 %collective-permute-start.15 = (f32[4,80,128]{2,1,0:T(8,128)S(1)}, f32[4,80,128]{2,1,0:T(8,128)S(1)}, u32[]{:S(2)}, u32[]{:S(2)}) collective-permute-start(f32[4,80,128]{2,1,0:T(8,128)S(1)} %pass_on.14), channel_id=1, source_target_pairs={{8,4},{9,5},{10,6},{11,7},{24,20},{25,21},{26,22},{27,23}} | collective-permute-start | bytes 491528 | tf_op jit(solution)/shard_map/ppermute | solution.py:464
  40.5 32.6 %copy-start.1 = (f32[160,8,128]{2,1,0:T(8,128)S(1)}, f32[160,8,128]{2,1,0:T(8,128)}, u32[]{:S(2)}) copy-start(f32[160,8,128]{2,1,0:T(8,128)} %d_ref.3) | copy-start | bytes 1966084
  40.5 32.6 %copy-start.2 = (f32[160,8,128]{2,1,0:T(8,128)S(1)}, f32[160,8,128]{2,1,0:T(8,128)}, u32[]{:S(2)}) copy-start(f32[160,8,128]{2,1,0:T(8,128)} %r_ref.1) | copy-start | bytes 1966084
  40.5 2.2 %collective-permute-start.12 = (f32[4,80,128]{2,1,0:T(8,128)S(1)}, f32[4,80,128]{2,1,0:T(8,128)S(1)}, u32[]{:S(2)}, u32[]{:S(2)}) collective-permute-start(f32[4,80,128]{2,1,0:T(8,128)S(1)} %pass_on.12), channel_id=1, source_target_pairs={{8,4},{9,5},{10,6},{11,7},{24,20},{25,21},{26,22},{27,23}} | collective-permute-start | bytes 491528 | tf_op jit(solution)/shard_map/ppermute | solution.py:464
  41.4 22.8 %collective-permute-start.16 = (f32[4,80,128]{2,1,0:T(8,128)S(1)}, f32[4,80,128]{2,1,0:T(8,128)S(1)}, u32[]{:S(2)}, u32[]{:S(2)}) collective-permute-start(f32[4,80,128]{2,1,0:T(8,128)S(1)} %pass_on.15), channel_id=1, source_target_pairs={{4,0},{5,1},{6,2},{7,3},{20,16},{21,17},{22,18},{23,19}} | collective-permute-start | bytes 491528 | tf_op jit(solution)/shard_map/ppermute | solution.py:464
  42.7 23.9 %collective-permute-start.13 = (f32[4,80,128]{2,1,0:T(8,128)S(1)}, f32[4,80,128]{2,1,0:T(8,128)S(1)}, u32[]{:S(2)}, u32[]{:S(2)}) collective-permute-start(f32[4,80,128]{2,1,0:T(8,128)S(1)} %pass_on.13), channel_id=1, source_target_pairs={{4,0},{5,1},{6,2},{7,3},{20,16},{21,17},{22,18},{23,19}} | collective-permute-start | bytes 491528 | tf_op jit(solution)/shard_map/ppermute | solution.py:464
  69.1 20.2 %copy-start.3 = (f32[160,8,128]{2,1,0:T(8,128)S(1)}, f32[160,8,128]{2,1,0:T(8,128)}, u32[]{:S(2)}) copy-start(f32[160,8,128]{2,1,0:T(8,128)} %control_ref.1) | copy-start | bytes 1966084
  69.1 4.0 %collective-permute-start.17 = (f32[32,160]{1,0:T(8,128)S(1)}, f32[32,160]{1,0:T(8,128)S(1)}, u32[]{:S(2)}, u32[]{:S(2)}) collective-permute-start(f32[32,160]{1,0:T(8,128)S(1)} %get-tuple-element.36.refs_5_), channel_id=1, source_target_pairs={{0,16},{16,0},{1,17},{17,1},{2,18},{18,2},{3,19},{19,3},{4,20},{20... | collective-permute-start | bytes 61448 | tf_op jit(solution)/shard_map/ppermute | solution.py:445
  74.2 1.2 %collective-permute-start.18 = (f32[8,128]{1,0:T(8,128)S(1)}, f32[8,128]{1,0:T(8,128)S(1)}, u32[]{:S(2)}, u32[]{:S(2)}) collective-permute-start(f32[8,128]{1,0:T(8,128)S(1)} %get-tuple-element.37), channel_id=1, source_target_pairs={{0,1},{1,0},{2,3},{3,2},{4,5},{5,4},{6,7},{7,6},{8,9},{9,8},{10,11... | collective-permute-start | bytes 12296 | tf_op jit(solution)/shard_map/ppermute | solution.py:475
  75.5 3.6 %collective-permute-start.19 = (f32[8,128]{1,0:T(8,128)S(1)}, f32[8,128]{1,0:T(8,128)S(1)}, u32[]{:S(2)}, u32[]{:S(2)}) collective-permute-start(f32[8,128]{1,0:T(8,128)S(1)} %add.29), channel_id=1, source_target_pairs={{0,2},{1,3},{2,0},{3,1},{16,18},{17,19},{18,16},{19,17},{4,6},{5,7... | collective-permute-start | bytes 12296 | tf_op jit(solution)/shard_map/ppermute | solution.py:475
  77.3 3.6 %collective-permute-start.20 = (f32[8,128]{1,0:T(8,128)S(1)}, f32[8,128]{1,0:T(8,128)S(1)}, u32[]{:S(2)}, u32[]{:S(2)}) collective-permute-start(f32[8,128]{1,0:T(8,128)S(1)} %add.29), channel_id=1, source_target_pairs={{0,16},{1,17},{2,18},{3,19},{16,0},{17,1},{18,2},{19,3},{4,20},{5,... | collective-permute-start | bytes 12296 | tf_op jit(solution)/shard_map/ppermute | solution.py:475
  78.8 4.5 %collective-permute-start.21 = (f32[8,128]{1,0:T(8,128)S(1)}, f32[8,128]{1,0:T(8,128)S(1)}, u32[]{:S(2)}, u32[]{:S(2)}) collective-permute-start(f32[8,128]{1,0:T(8,128)S(1)} %add.29), channel_id=1, source_target_pairs={{0,18},{1,19},{2,16},{3,17},{16,2},{17,3},{18,0},{19,1},{4,22},{5,... | collective-permute-start | bytes 12296 | tf_op jit(solution)/shard_map/ppermute | solution.py:475
  83.3 4.4 %collective-permute-start.22 = (f32[8,128]{1,0:T(8,128)S(1)}, f32[8,128]{1,0:T(8,128)S(1)}, u32[]{:S(2)}, u32[]{:S(2)}) collective-permute-start(f32[8,128]{1,0:T(8,128)S(1)} %add_add_fusion.1), channel_id=1, source_target_pairs={{0,4},{4,0},{8,12},{12,8},{1,5},{5,1},{9,13},{13,9},{2,6},{6,2},{1... | collective-permute-start | bytes 12296 | tf_op jit(solution)/shard_map/ppermute | solution.py:475
  83.3 4.6 %collective-permute-start.23 = (f32[8,128]{1,0:T(8,128)S(1)}, f32[8,128]{1,0:T(8,128)S(1)}, u32[]{:S(2)}, u32[]{:S(2)}) collective-permute-start(f32[8,128]{1,0:T(8,128)S(1)} %add_add_fusion.1), channel_id=1, source_target_pairs={{0,8},{4,12},{8,0},{12,4},{1,9},{5,13},{9,1},{13,5},{2,10},{6,14},... | collective-permute-start | bytes 12296 | tf_op jit(solution)/shard_map/ppermute | solution.py:475
  83.4 5.9 %collective-permute-start.24 = (f32[8,128]{1,0:T(8,128)S(1)}, f32[8,128]{1,0:T(8,128)S(1)}, u32[]{:S(2)}, u32[]{:S(2)}) collective-permute-start(f32[8,128]{1,0:T(8,128)S(1)} %add_add_fusion.1), channel_id=1, source_target_pairs={{0,12},{4,8},{8,4},{12,0},{1,13},{5,9},{9,5},{13,1},{2,14},{6,10},... | collective-permute-start | bytes 12296 | tf_op jit(solution)/shard_map/ppermute | solution.py:475
  (3 other events, 2.4 us)

commit v4 on v3

--- a/solution.py
+++ b/solution.py
@@ -6,6 +6,7 @@
 from jax.experimental.pallas import tpu as pltpu
 from jax.sharding import PartitionSpec as P
 
+
 f32 = jnp.float32
 VM = pl.BlockSpec(memory_space=pltpu.VMEM)
 SM = pl.BlockSpec(memory_space=pltpu.SMEM)
@@ -69,15 +70,20 @@
     return [leak ** (3 - s) * rising(place, 3 - s) * decay for s in range(4)]
 
 
-def lon_local_rows(load_row, lonc, rows, cells, backward, inside_ref, carried_ref):
+def lon_tables(lonc, rows, cells, backward, table_ref):
     c, leak, scale = lon_consts(lonc)
     gain = leak**4 * scale
+    for y in range(rows):
+        table_ref[y] = lon_kernel_matrix(c[y : y + 1], gain[y : y + 1], cells, backward)
+
+
+def lon_local_rows(load_row, lonc, table_ref, rows, cells, backward, inside_ref, carried_ref):
+    c, leak, scale = lon_consts(lonc)
     finals = lon_finals(c, leak, scale, cells, backward)
     carried = None
     for y in range(rows):
         f = load_row(y)
-        table = lon_kernel_matrix(c[y : y + 1], gain[y : y + 1], cells, backward)
-        inside_ref[y] = mm(f, table, ((1,), (0,)))
+        inside_ref[y] = mm(f, table_ref[y], ((1,), (0,)))
         part = mm(masked_rows(finals, y), f, ((1,), (1,)))
         carried = part if carried is None else carried + part
     carried_ref[...] = carried
@@ -155,14 +161,29 @@
     return swap_halves(v, v)
 
 
-def sum_states(parts):
-    def at_state(s, at):
-        v = parts[0][s, at, :]
-        for p in parts[1:]:
-            v = v + p[s, at, :]
-        return v
-
-    return at_state
+def lat_trans(dec, rows):
+    leak = 1.0 - jnp.exp(-dec)
+    closing = jnp.exp(-float(rows) * dec)
+    return [choose(rows, i) * leak**i * closing for i in range(4)]
+
+
+def incoming_states(plain, carried_on, dec, rows):
+    t = lat_trans(dec, rows)
+
+    def at(where):
+        out = []
+        far = [[p[s, where, :] for s in range(4)] for p in carried_on]
+        for s in range(4):
+            v = None
+            for p in plain:
+                v = p[s, where, :] if v is None else v + p[s, where, :]
+            for f in far:
+                for j in range(s + 1):
+                    v = v + t[s - j] * f[j]
+            out.append(v)
+        return out
+
+    return at
 
 
 def member_blocks(members):
@@ -171,23 +192,35 @@
             return size
 
 
-def k_lon_fwd(rows, k, cells, d_ref, lon_ref, lat_ref, inside_ref, carried_ref, lonc_ref, latc_ref):
-    d_ref = d_ref.reshape(k * rows, cells)
-    row = jnp.broadcast_to(lon_ref[...], (rows, rows))
+def k_tables(rows, cells, dec_ref, lonc_ref, latc_ref, table_ref):
+    row = jnp.broadcast_to(dec_ref[:1, :rows], (rows, rows))
     own = iota((rows, rows), 0) == iota((rows, rows), 1)
     column = jnp.sum(jnp.where(own, row, 0.0), axis=1, keepdims=True)
     lonc = jnp.broadcast_to(column, (rows, cells))
     lonc_ref[...] = lonc
-    first, second = both_halves(jnp.broadcast_to(lat_ref[...], (8, cells)))
+    first, second = both_halves(jnp.broadcast_to(dec_ref[1:], (8, cells)))
     latc_ref[0] = first
     latc_ref[1] = second
+    lon_tables(lonc, rows, cells, False, table_ref)
+
+
+def k_lon_fwd(rows, k, cells, d_ref, lon_ref, table_ref, inside_ref, carried_ref):
+    d_ref = d_ref.reshape(k * rows, cells)
     lon_local_rows(
-        lambda y: d_ref[pl.ds(y, k, stride=rows), :], lonc, rows, cells, False, inside_ref, carried_ref
-    )
-
-
-def k_pack_members(m_ref, a_ref, b_ref):
+        lambda y: d_ref[pl.ds(y, k, stride=rows), :],
+        lon_ref[...],
+        table_ref,
+        rows,
+        cells,
+        False,
+        inside_ref,
+        carried_ref,
+    )
+
+
+def k_prepare(m_ref, lon_ref, a_ref, b_ref, table_ref):
     half = a_ref.shape[0]
+    lon_tables(lon_ref[...], *lon_ref.shape, True, table_ref)
 
     def step(i, carry):
         a, b = swap_halves(m_ref[i].astype(f32), m_ref[i + half].astype(f32))
@@ -231,10 +264,7 @@
 
 
 def k_pass_on(rows, part, carried_ref, got_ref, lat_ref, out_ref):
-    c = lat_ref[part, :1]
-    leak = 1.0 - jnp.exp(-c)
-    closing = jnp.exp(-float(rows) * c)
-    t = [choose(rows, i) * leak**i * closing for i in range(4)]
+    t = lat_trans(lat_ref[part, :1], rows)
     got = [got_ref[s] for s in range(4)]
     for i in range(4):
         v = carried_ref[i]
@@ -250,12 +280,11 @@
     return jnp.where(low, first, second)
 
 
-def k_increment(rows, k, part, hops, pairs, modes, levels, *refs):
+def k_increment(rows, k, part, plain, far, pairs, modes, levels, *refs):
     f_ref, lat_ref, m_ref, v_ref, eig_ref, *rest = refs
-    got = rest[:hops]
-    out_ref, s_ref, inc_ref = rest[hops:]
+    out_ref, s_ref, inc_ref = rest[plain + far :]
     cells = lat_ref.shape[-1]
-    at_state = sum_states(got)
+    start = incoming_states(rest[:plain], rest[plain : plain + far], lat_ref[part, :1], rows)
 
     def store(y, at, base, value, last):
         s_ref[pl.ds(base * rows + y, 8, stride=rows), :] = value
@@ -263,7 +292,7 @@
     lat_sweep(
         lambda y, at, base: f_ref[y, at, :],
         store,
-        lambda at: [at_state(s, at) for s in range(4)],
+        start,
         lat_ref[part, :1],
         rows,
         k,
@@ -349,13 +378,14 @@
     )
 
 
-def k_lon_bwd(rows, k, cells, hops, *refs):
-    g_refs, lat_ref, lon_ref, rest = refs[:2], refs[2], refs[3], refs[4:]
-    got = rest[: 2 * hops]
-    inside_ref, carried_ref, p_ref = rest[2 * hops :]
+def k_lon_bwd(rows, k, cells, plain, far, *refs):
+    g_refs, lat_ref, lon_ref, table_ref, rest = refs[:2], refs[2], refs[3], refs[4], refs[5:]
+    each = plain + far
+    inside_ref, carried_ref, p_ref = rest[2 * each :]
     half = k // 2
     for part in range(2):
-        at_state = sum_states(got[part * hops : (part + 1) * hops])
+        got = rest[part * each : (part + 1) * each]
+        start = incoming_states(got[:plain], got[plain:], lat_ref[part, :1], rows)
         g_ref = g_refs[part]
 
         def store(y, at, base, value, last, part=part):
@@ -364,7 +394,7 @@
         lat_sweep(
             lambda y, at, base: g_ref[pl.ds(base * rows + y, 8, stride=rows), :],
             store,
-            lambda at: [at_state(s, at) for s in range(4)],
+            start,
             lat_ref[part, :1],
             rows,
             half,
@@ -375,7 +405,7 @@
     def load_row(y):
         return jnp.concatenate(swap_halves(p_ref[0, y], p_ref[1, y]), axis=0)
 
-    lon_local_rows(load_row, lon_ref[...], rows, cells, True, inside_ref, carried_ref)
+    lon_local_rows(load_row, lon_ref[...], table_ref, rows, cells, True, inside_ref, carried_ref)
 
 
 def k_sums(rows, k, cells, n, *refs):
@@ -421,14 +451,13 @@
     nd_ref[...] = nr + beta * d
 
 
-def call(body, outs, ins, specs=None, scratch=(), name=None, cost=None):
+def call(body, outs, ins, specs=None, scratch=(), cost=None):
     return pl.pallas_call(
         body,
         out_shape=outs,
         in_specs=specs or [VM] * len(ins),
         out_specs=jax.tree.map(lambda _: VM, outs),
         scratch_shapes=scratch,
-        name=name,
         cost_estimate=None if cost is None else pl.CostEstimate(flops=cost, bytes_accessed=1000, transcendentals=0),
         compiler_params=pltpu.CompilerParams(vmem_limit_bytes=16 * 1024 * 1024),
     )(*ins)
@@ -447,22 +476,33 @@
     return got + [carried]
 
 
-def lat_chain(parts, latc, rows, backward):
+def pass_on(part, got, latc, rows, c):
+    return call(functools.partial(k_pass_on, rows, c), sds(*part.shape), [part, got, latc])
+
+
+def lat_carry(parts, latc, rows, backward):
     n = lax.axis_size("lat")
+    at = (lambda i: n - 1 - i) if backward else (lambda i: i)
+
+    def send(v, *pairs):
+        return lax.ppermute(v, "lat", [(at(a), at(b)) for a, b in pairs])
+
+    if n == 4:
+        near = [send(v, (0, 1), (2, 3)) for v in parts]
+        both = [pass_on(v, g, latc, rows, c) for c, (v, g) in enumerate(zip(parts, near))]
+        mid, far = [], []
+        for v in both:
+            far.append(send(v, (1, 3)))
+            mid.append(send(v, (1, 2)))
+        return [([a, b], [c]) for a, b, c in zip(near, mid, far)]
     sends = list(parts)
     got = [[] for _ in parts]
     for h in range(n - 1):
-        pair = (n - 1 - h, n - 2 - h) if backward else (h, h + 1)
         for c, part in enumerate(parts):
             if h:
-                sends[c] = call(
-                    functools.partial(k_pass_on, rows, c),
-                    sds(*part.shape),
-                    [part, got[c][-1], latc],
-                    name="pass_on",
-                )
-            got[c].append(lax.ppermute(sends[c], "lat", [pair]))
-    return got
+                sends[c] = pass_on(part, got[c][-1], latc, rows, c)
+            got[c].append(send(sends[c], (h, h + 1)))
+    return [(g, []) for g in got]
 
 
 def all_sum(v, axes, steps):
@@ -488,58 +528,60 @@
 
 def reduce_everywhere(v):
     n_lon, n_lat, n_mem = (lax.axis_size(a) for a in ("lon", "lat", "mem"))
-    mem = powers(n_mem)
-    if n_lon == 2 and len(mem) == 2:
-        v = all_sum(v, ("mem",), mem[:1])
-        v = all_sum(v, ("lon", "mem"), [mem[1], n_mem])
-    else:
-        for s in mem:
-            v = all_sum(v, ("mem",), [s])
-        for s in powers(n_lon):
-            v = all_sum(v, ("lon",), [s])
+    for s in powers(n_mem):
+        v = all_sum(v, ("mem",), [s])
+    for s in powers(n_lon):
+        v = all_sum(v, ("lon",), [s])
     lat = powers(n_lat)
     for i in range(0, len(lat), 2):
         v = all_sum(v, ("lat",), lat[i : i + 2])
     return v
 
 
-def body(control, residual, direction, members, vert_modes, eig_count, lon_decay, lat_decay, obs_weight):
+def iteration(control, residual, direction, members, vert_modes, eig_count, lon_decay, lat_decay, obs_weight):
     k, rows, cells = direction.shape
     mcount, levels = members.shape[:2]
     modes = vert_modes.shape[0]
-    n_lon, n_lat, n_mem = (lax.axis_size(a) for a in ("lon", "lat", "mem"))
-    hops = n_lat - 1
+    n_lon, n_mem = lax.axis_size("lon"), lax.axis_size("mem")
     half = k // 2
     pairs = mcount // 2
     state = sds(4, half, cells)
 
-    inside, carried, lonc, latc = call(
+    decays = jnp.stack([jnp.pad(lon_decay, (0, cells - rows)), lat_decay])
+    lonc, latc, tables = call(
+        functools.partial(k_tables, rows, cells),
+        (sds(rows, cells), sds(2, 8, cells), sds(rows, cells, cells)),
+        [decays],
+        cost=10**9,
+    )
+    inside, carried = call(
         functools.partial(k_lon_fwd, rows, k, cells),
-        (sds(rows, k, cells), sds(4 * rows, k), sds(rows, cells), sds(2, 8, cells)),
-        [direction, lon_decay.reshape(1, rows), lat_decay.reshape(1, cells)],
-        name="lon_fwd",
-    )
-    packed = call(
-        k_pack_members, (sds(pairs, levels, rows, cells),) * 2, [members], name="pack_members", cost=10**9
+        (sds(rows, k, cells), sds(4 * rows, k)),
+        [direction, lonc, tables],
+    )
+    *packed, tables = call(
+        k_prepare,
+        (sds(pairs, levels, rows, cells),) * 2 + (sds(rows, cells, cells),),
+        [members, lonc],
+        cost=10**9,
     )
     blocks = lon_exchange(carried, False)
     fa, fb, pa, pb = call(
         functools.partial(k_lat_first, rows, k, cells, n_lon),
         (sds(rows, half, cells),) * 2 + (state,) * 2,
         [inside, lonc, latc, *blocks],
-        name="lat_first",
-    )
-    got = lat_chain([pa, pb], latc, rows, False)
+    )
+    got = lat_carry([pa, pb], latc, rows, False)
+    plain, far = (len(g) for g in got[0])
     fields = (fa, fb)
     inc = [None, None]
     for part in range(2):
         inc[part] = call(
-            functools.partial(k_increment, rows, half, part, hops, pairs, modes, levels),
+            functools.partial(k_increment, rows, half, part, plain, far, pairs, modes, levels),
             sds(levels // 2, rows, cells),
-            [fields[part], latc, packed[part], vert_modes, eig_count, *got[part]],
-            specs=[VM, VM, VM, SM, SM] + [VM] * hops,
+            [fields[part], latc, packed[part], vert_modes, eig_count, *got[part][0], *got[part][1]],
+            specs=[VM, VM, VM, SM, SM] + [VM] * (plain + far),
             scratch=[pltpu.VMEM((half * rows, cells), f32), pltpu.VMEM((levels, rows, cells), f32)],
-            name="increment",
         )
     grads, sends = [None, None], [None, None]
     for part in range(2):
@@ -555,29 +597,25 @@
             [v, other, obs_weight, packed[part], vert_modes, eig_count, latc],
             specs=[VM, VM, VM, VM, SM, SM, VM],
             scratch=[pltpu.VMEM((levels, rows, cells), f32)],
-            name="gradient",
         )
-    got = lat_chain(sends, latc, rows, True)
+    got = lat_carry(sends, latc, rows, True)
     inside, carried = call(
-        functools.partial(k_lon_bwd, rows, k, cells, hops),
+        functools.partial(k_lon_bwd, rows, k, cells, plain, far),
         (sds(rows, k, cells), sds(4 * rows, k)),
-        [*grads, latc, lonc, *got[0], *got[1]],
+        [*grads, latc, lonc, tables, *got[0][0], *got[0][1], *got[1][0], *got[1][1]],
         scratch=[pltpu.VMEM((2, rows, half, cells), f32)],
-        name="lon_bwd",
     )
     blocks = lon_exchange(carried, True)
     h, sums = call(
         functools.partial(k_sums, rows, k, cells, n_lon),
         (sds(k * rows, cells), sds(8, cells)),
         [inside, lonc, direction, residual, *blocks],
-        name="sums",
     )
     sums = reduce_everywhere(sums)
     outs = call(
         k_update,
         (sds(k, rows, cells),) * 3,
         [sums, control, residual, direction, h.reshape(k, rows, cells)],
-        name="update",
     )
     return tuple(outs)
 
@@ -595,4 +633,4 @@
         P("lon"),
         P(None, "lat", "lon"),
     )
-    return jax.shard_map(body, mesh=mesh, in_specs=placed, out_specs=(field,) * 3, check_vma=False)
+    return jax.shard_map(iteration, mesh=mesh, in_specs=placed, out_specs=(field,) * 3, check_vma=False)

time: 91.2 us -> 92.5 us (1.014)
  waiting for transfers between devices: 39.9 us -> 41.1 us
    unnamed x20 -> x14, local copies, waits for them, and re-layouts: 2.43 us -> 0.91 us
    ppermute x16, starting transfers between devices: 16.5 us -> 17.7 us  [the longest x12 14.6 us: send(): return lax.ppermute(v, 'lat', [(at(a), at(b)) for a, b in pairs])]
    ppermute x7 -> x6, starting transfers between devices: 7.94 us -> 7.07 us  [all_sum(): lax.ppermute(v, axes, [(i, i ^ m) for i in range(total)])]
    ppermute x7 -> x6, waiting for transfers between devices: 7.1 us -> 7.37 us  [all_sum(): lax.ppermute(v, axes, [(i, i ^ m) for i in range(total)])]
    pallas_call x18 -> x15, Pallas kernels: 18.4 us -> 18.5 us  [call(): pl.pallas_call(body, out_shape=outs, in_specs=specs or [VM] * len(ins), o...]
  transfers between devices with their start and end apart: 25 -> 24, of which waited for: 13 -> 14; matrix products, arithmetic and copies ran while one was open for 0% -> 0% of each run, Pallas kernels for 11% -> 11%
where the time goes in v4:
time: 92.5 us; the launch traced here: 92.2 us
  waiting for transfers between devices  41.1 us (44%)
  starting transfers between devices  29.4 us (32%)
  Pallas kernels  18.5 us (20%)
  local copies, waits for them, and re-layouts  1.57 us (2%)
  between operations  0.97 us (1%)
    ppermute x12, waiting for transfers between devices, send(): return lax.ppermute(v, 'lat', [(at(a), at(b)) for a, b in pairs])  27.2 us
    pallas_call x15, Pallas kernels, call(): pl.pallas_call(body, out_shape=outs, in_specs=specs or [VM] * len(ins), o...  18.5 us
    ppermute x12, starting transfers between devices, send(): return lax.ppermute(v, 'lat', [(at(a), at(b)) for a, b in pairs])  14.6 us
    ppermute x6, waiting for transfers between devices, all_sum(): lax.ppermute(v, axes, [(i, i ^ m) for i in range(total)])  7.37 us
    ppermute x6, starting transfers between devices, all_sum(): lax.ppermute(v, axes, [(i, i ^ m) for i in range(total)])  7.07 us
    ppermute x2, starting transfers between devices, lon_exchange(): lax.ppermute(carried, 'lon', [(j, (j + sign * r) % n) for j in range(n)])  4.59 us
    ppermute x2, waiting for transfers between devices, lon_exchange(): lax.ppermute(carried, 'lon', [(j, (j + sign * r) % n) for j in range(n)])  4.31 us
    ppermute x2, starting transfers between devices, iteration(): other = lax.ppermute(v, 'mem', [(i, i ^ step) for i in range(n_mem)])  2.47 us
  transfers between devices with their start and end apart: 24, of which 14 were waited for; matrix products, arithmetic and copies ran while one was open for 0% of the time, Pallas kernels for 11%

profile of v4, /device:TPU:0, one launch (start us, length us, event | category | flops | bytes accessed | tf_op | source)
XLA Modules:
  0.0 92.2 jit_solution(13335400806306749393)
XLA Ops:
  3.0 1.8 %shard_map.113 = (f32[8,160,128]{2,1,0:T(8,128)S(1)}, f32[32,160]{1,0:T(8,128)S(1)}) custom-call(f32[160,8,128]{2,1,0:T(8,128)S(1)} %copy-done, f32[8,128]{1,0:T(8,128)S(1)} %get-tuple-element.23.lon_ref.refs_1_.refs_3_, f32[8,128,128]{2,1,0:T(8,128)S(1)} %get-tuple-element.24.table_ref), custom_call_target="tpu_custom_call" | custom-call | tf_op jit(solution)/shard_map/pallas_call | solution.py:455
  4.8 3.0 %collective-permute-start = (f32[32,160]{1,0:T(8,128)S(1)}, f32[32,160]{1,0:T(8,128)S(1)}, u32[]{:S(2)}, u32[]{:S(2)}) collective-permute-start(f32[32,160]{1,0:T(8,128)S(1)} %get-tuple-element.27.refs_4_), channel_id=1, source_target_pairs={{0,16},{16,0},{1,17},{17,1},{2,18},{18,2},{3,19},{19,3},{4,20},{20... | collective-permute-start | bytes 61448 | tf_op jit(solution)/shard_map/ppermute | solution.py:474
  7.9 1.9 %collective-permute-done.refs_3_ = f32[32,160]{1,0:T(8,128)S(1)} collective-permute-done((f32[32,160]{1,0:T(8,128)S(1)}, f32[32,160]{1,0:T(8,128)S(1)}, u32[]{:S(2)}, u32[]{:S(2)}) %collective-permute-start) | collective-permute-done | bytes 20512 | tf_op jit(solution)/shard_map/ppermute | solution.py:474
  9.8 1.4 %shard_map.114 = (f32[8,80,128]{2,1,0:T(8,128)S(1)}, f32[8,80,128]{2,1,0:T(8,128)S(1)}, f32[4,80,128]{2,1,0:T(8,128)S(1)}, f32[4,80,128]{2,1,0:T(8,128)S(1)}) custom-call(f32[8,160,128]{2,1,0:T(8,128)S(1)} %get-tuple-element.25.refs_0_, f32[8,128]{1,0:T(8,128)S(1)} %get-tuple-element.23.lon_ref.refs_1_.refs_3_, ...), custom_call_target="tpu_custom_call" | custom-call | tf_op jit(solution)/shard_map/pallas_call | solution.py:455
  11.2 4.0 %collective-permute-start.6 = (f32[4,80,128]{2,1,0:T(8,128)S(1)}, f32[4,80,128]{2,1,0:T(8,128)S(1)}, u32[]{:S(2)}, u32[]{:S(2)}) collective-permute-start(f32[4,80,128]{2,1,0:T(8,128)S(1)} %get-tuple-element.34.carried_ref), channel_id=1, source_target_pairs={{0,4},{8,12},{1,5},{9,13},{2,6},{10,14},{3,7},{11,15},{16,20},{24,... | collective-permute-start | bytes 491528 | tf_op jit(solution)/shard_map/ppermute | solution.py:488
  15.2 1.3 %collective-permute-start.1 = (f32[4,80,128]{2,1,0:T(8,128)S(1)}, f32[4,80,128]{2,1,0:T(8,128)S(1)}, u32[]{:S(2)}, u32[]{:S(2)}) collective-permute-start(f32[4,80,128]{2,1,0:T(8,128)S(1)} %get-tuple-element.30.carried_ref), channel_id=1, source_target_pairs={{0,4},{8,12},{1,5},{9,13},{2,6},{10,14},{3,7},{11,15},{16,20},{24,... | collective-permute-start | bytes 491528 | tf_op jit(solution)/shard_map/ppermute | solution.py:488
  16.5 2.7 %collective-permute-done.6.got_ref.refs_5_ = f32[4,80,128]{2,1,0:T(8,128)S(1)} collective-permute-done((f32[4,80,128]{2,1,0:T(8,128)S(1)}, f32[4,80,128]{2,1,0:T(8,128)S(1)}, u32[]{:S(2)}, u32[]{:S(2)}) %collective-permute-start.6) | collective-permute-done | bytes 163872 | tf_op jit(solution)/shard_map/ppermute | solution.py:488
  22.4 1.2 %shard_map.115 = (f32[10,32,8,128]{3,2,1,0:T(8,128)S(1)}, f32[10,32,8,128]{3,2,1,0:T(8,128)S(1)}, f32[8,128,128]{2,1,0:T(8,128)S(1)}) custom-call(bf16[20,32,8,128]{3,2,1,0:T(8,128)(2,1)S(1)} %copy-done.6, f32[8,128]{1,0:T(8,128)S(1)} %get-tuple-element.23.lon_ref.refs_1_.refs_3_), custom_call_target="tpu_custom_call" | custom-call | flops 1000000000 | bytes 1000 | tf_op jit(solution)/shard_map/pallas_call | solution.py:455
  23.7 2.1 %shard_map.120 = f32[16,8,128]{2,1,0:T(8,128)S(1)} custom-call(f32[8,80,128]{2,1,0:T(8,128)S(1)} %get-tuple-element.32.refs_0_, f32[2,8,128]{2,1,0:T(8,128)S(1)} %get-tuple-element.26.refs_2_.lat_ref.refs_1_.refs_6_, f32[10,32,8,128]{3,2,1,0:T(8,128)S(1)} %get-tuple-element.33.refs_2_.refs_3_, f32[8,32]{1,0:T(8,128)S(1)} %copy-done.4, s32[20]{0:T(128)S(1)} %copy-done.5, ...), custom_call_target="tpu_custom_call" | custom-call | tf_op jit(solution)/shard_map/pallas_call | solution.py:455
  25.9 2.1 %shard_map.117 = f32[16,8,128]{2,1,0:T(8,128)S(1)} custom-call(f32[8,80,128]{2,1,0:T(8,128)S(1)} %get-tuple-element.28.refs_0_, f32[2,8,128]{2,1,0:T(8,128)S(1)} %get-tuple-element.26.refs_2_.lat_ref.refs_1_.refs_6_, f32[10,32,8,128]{3,2,1,0:T(8,128)S(1)} %get-tuple-element.29.refs_2_.refs_3_, f32[8,32]{1,0:T(8,128)S(1)} %copy-done.4, s32[20]{0:T(128)S(1)} %copy-done.5, ...), custom_call_target="tpu_custom_call" | custom-call | tf_op jit(solution)/shard_map/pallas_call | solution.py:455
  28.6 1.6 %collective-permute-start.10 = (f32[16,8,128]{2,1,0:T(8,128)S(1)}, f32[16,8,128]{2,1,0:T(8,128)S(1)}, u32[]{:S(2)}, u32[]{:S(2)}) collective-permute-start(f32[16,8,128]{2,1,0:T(8,128)S(1)} %add.27.refs_0_), channel_id=1, source_target_pairs={{0,2},{1,3},{2,0},{3,1},{4,6},{5,7},{6,4},{7,5},{8,10},{9,11},{10,... | collective-permute-start | bytes 196616 | tf_op jit(solution)/shard_map/ppermute | solution.py:593
  31.1 2.2 %collective-permute-done.10.refs_1_ = f32[16,8,128]{2,1,0:T(8,128)S(1)} collective-permute-done((f32[16,8,128]{2,1,0:T(8,128)S(1)}, f32[16,8,128]{2,1,0:T(8,128)S(1)}, u32[]{:S(2)}, u32[]{:S(2)}) %collective-permute-start.10) | collective-permute-done | bytes 65568 | tf_op jit(solution)/shard_map/ppermute | solution.py:593
  33.2 2.2 %shard_map.121 = (f32[640,128]{1,0:T(8,128)S(1)}, f32[4,80,128]{2,1,0:T(8,128)S(1)}) custom-call(f32[16,8,128]{2,1,0:T(8,128)S(1)} %add.27.refs_0_, f32[16,8,128]{2,1,0:T(8,128)S(1)} %collective-permute-done.10.refs_1_, f32[32,8,128]{2,1,0:T(8,128)S(1)} %copy-done.3, f32[10,32,8,128]{3,2,1,0:T(8,128)S(1)} %get-tuple-element.33.refs_2_.refs_3_, ...), custom_call_target="tpu_custom_call" | custom-call | tf_op jit(solution)/shard_map/pallas_call | solution.py:455
  35.4 1.3 %collective-permute-start.14 = (f32[4,80,128]{2,1,0:T(8,128)S(1)}, f32[4,80,128]{2,1,0:T(8,128)S(1)}, u32[]{:S(2)}, u32[]{:S(2)}) collective-permute-start(f32[4,80,128]{2,1,0:T(8,128)S(1)} %get-tuple-element.38.carried_ref), channel_id=1, source_target_pairs={{12,8},{4,0},{13,9},{5,1},{14,10},{6,2},{15,11},{7,3},{28,24},{20,... | collective-permute-start | bytes 491528 | tf_op jit(solution)/shard_map/ppermute | solution.py:488
  36.7 2.2 %shard_map.118 = (f32[640,128]{1,0:T(8,128)S(1)}, f32[4,80,128]{2,1,0:T(8,128)S(1)}) custom-call(f32[16,8,128]{2,1,0:T(8,128)S(1)} %add.26.refs_0_, f32[16,8,128]{2,1,0:T(8,128)S(1)} %collective-permute-done.5.refs_1_, f32[32,8,128]{2,1,0:T(8,128)S(1)} %copy-done.3, f32[10,32,8,128]{3,2,1,0:T(8,128)S(1)} %get-tuple-element.29.refs_2_.refs_3_, ...), custom_call_target="tpu_custom_call" | custom-call | tf_op jit(solution)/shard_map/pallas_call | solution.py:455
  38.9 1.3 %collective-permute-start.11 = (f32[4,80,128]{2,1,0:T(8,128)S(1)}, f32[4,80,128]{2,1,0:T(8,128)S(1)}, u32[]{:S(2)}, u32[]{:S(2)}) collective-permute-start(f32[4,80,128]{2,1,0:T(8,128)S(1)} %get-tuple-element.37.carried_ref), channel_id=1, source_target_pairs={{12,8},{4,0},{13,9},{5,1},{14,10},{6,2},{15,11},{7,3},{28,24},{20,... | collective-permute-start | bytes 491528 | tf_op jit(solution)/shard_map/ppermute | solution.py:488
  40.2 9.6 %collective-permute-done.14.got_ref.refs_8_ = f32[4,80,128]{2,1,0:T(8,128)S(1)} collective-permute-done((f32[4,80,128]{2,1,0:T(8,128)S(1)}, f32[4,80,128]{2,1,0:T(8,128)S(1)}, u32[]{:S(2)}, u32[]{:S(2)}) %collective-permute-start.14) | collective-permute-done | bytes 163872 | tf_op jit(solution)/shard_map/ppermute | solution.py:488
  50.7 1.3 %collective-permute-start.16 = (f32[4,80,128]{2,1,0:T(8,128)S(1)}, f32[4,80,128]{2,1,0:T(8,128)S(1)}, u32[]{:S(2)}, u32[]{:S(2)}) collective-permute-start(f32[4,80,128]{2,1,0:T(8,128)S(1)} %shard_map.123), channel_id=1, source_target_pairs={{8,0},{9,1},{10,2},{11,3},{24,16},{25,17},{26,18},{27,19}} | collective-permute-start | bytes 491528 | tf_op jit(solution)/shard_map/ppermute | solution.py:488
  52.0 1.3 %collective-permute-done.11.got_ref.refs_5_ = f32[4,80,128]{2,1,0:T(8,128)S(1)} collective-permute-done((f32[4,80,128]{2,1,0:T(8,128)S(1)}, f32[4,80,128]{2,1,0:T(8,128)S(1)}, u32[]{:S(2)}, u32[]{:S(2)}) %collective-permute-start.11) | collective-permute-done | bytes 163872 | tf_op jit(solution)/shard_map/ppermute | solution.py:488
  54.1 1.3 %collective-permute-start.13 = (f32[4,80,128]{2,1,0:T(8,128)S(1)}, f32[4,80,128]{2,1,0:T(8,128)S(1)}, u32[]{:S(2)}, u32[]{:S(2)}) collective-permute-start(f32[4,80,128]{2,1,0:T(8,128)S(1)} %shard_map.122), channel_id=1, source_target_pairs={{8,0},{9,1},{10,2},{11,3},{24,16},{25,17},{26,18},{27,19}} | collective-permute-start | bytes 491528 | tf_op jit(solution)/shard_map/ppermute | solution.py:488
  55.4 7.9 %collective-permute-done.16.refs_10_ = f32[4,80,128]{2,1,0:T(8,128)S(1)} collective-permute-done((f32[4,80,128]{2,1,0:T(8,128)S(1)}, f32[4,80,128]{2,1,0:T(8,128)S(1)}, u32[]{:S(2)}, u32[]{:S(2)}) %collective-permute-start.16) | collective-permute-done | bytes 163872 | tf_op jit(solution)/shard_map/ppermute | solution.py:488
  63.3 5.3 %collective-permute-done.13.refs_7_ = f32[4,80,128]{2,1,0:T(8,128)S(1)} collective-permute-done((f32[4,80,128]{2,1,0:T(8,128)S(1)}, f32[4,80,128]{2,1,0:T(8,128)S(1)}, u32[]{:S(2)}, u32[]{:S(2)}) %collective-permute-start.13) | collective-permute-done | bytes 163872 | tf_op jit(solution)/shard_map/ppermute | solution.py:488
  68.6 2.5 %shard_map.124 = (f32[8,160,128]{2,1,0:T(8,128)S(1)}, f32[32,160]{1,0:T(8,128)S(1)}) custom-call(f32[640,128]{1,0:T(8,128)S(1)} %get-tuple-element.31.refs_0_, f32[640,128]{1,0:T(8,128)S(1)} %get-tuple-element.35.refs_1_, f32[2,8,128]{2,1,0:T(8,128)S(1)} %get-tuple-element.26.refs_2_.lat_ref.refs_1_.refs_6_, ...), custom_call_target="tpu_custom_call" | custom-call | tf_op jit(solution)/shard_map/pallas_call | solution.py:455
  71.1 1.6 %collective-permute-start.17 = (f32[32,160]{1,0:T(8,128)S(1)}, f32[32,160]{1,0:T(8,128)S(1)}, u32[]{:S(2)}, u32[]{:S(2)}) collective-permute-start(f32[32,160]{1,0:T(8,128)S(1)} %get-tuple-element.40.refs_5_), channel_id=1, source_target_pairs={{0,16},{16,0},{1,17},{17,1},{2,18},{18,2},{3,19},{19,3},{4,20},{20... | collective-permute-start | bytes 61448 | tf_op jit(solution)/shard_map/ppermute | solution.py:474
  72.6 2.4 %collective-permute-done.17.refs_4_ = f32[32,160]{1,0:T(8,128)S(1)} collective-permute-done((f32[32,160]{1,0:T(8,128)S(1)}, f32[32,160]{1,0:T(8,128)S(1)}, u32[]{:S(2)}, u32[]{:S(2)}) %collective-permute-start.17) | collective-permute-done | bytes 20512 | tf_op jit(solution)/shard_map/ppermute | solution.py:474
  76.3 1.2 %collective-permute-done.18 = f32[8,128]{1,0:T(8,128)S(1)} collective-permute-done((f32[8,128]{1,0:T(8,128)S(1)}, f32[8,128]{1,0:T(8,128)S(1)}, u32[]{:S(2)}, u32[]{:S(2)}) %collective-permute-start.18) | collective-permute-done | bytes 4128 | tf_op jit(solution)/shard_map/ppermute | solution.py:515
  78.5 2.5 %collective-permute-done.19 = f32[8,128]{1,0:T(8,128)S(1)} collective-permute-done((f32[8,128]{1,0:T(8,128)S(1)}, f32[8,128]{1,0:T(8,128)S(1)}, u32[]{:S(2)}, u32[]{:S(2)}) %collective-permute-start.19) | collective-permute-done | bytes 4128 | tf_op jit(solution)/shard_map/ppermute | solution.py:515
  81.0 1.5 %collective-permute-start.20 = (f32[8,128]{1,0:T(8,128)S(1)}, f32[8,128]{1,0:T(8,128)S(1)}, u32[]{:S(2)}, u32[]{:S(2)}) collective-permute-start(f32[8,128]{1,0:T(8,128)S(1)} %add.29), channel_id=1, source_target_pairs={{0,16},{16,0},{1,17},{17,1},{2,18},{18,2},{3,19},{19,3},{4,20},{20... | collective-permute-start | bytes 12296 | tf_op jit(solution)/shard_map/ppermute | solution.py:515
  82.5 2.1 %collective-permute-done.20 = f32[8,128]{1,0:T(8,128)S(1)} collective-permute-done((f32[8,128]{1,0:T(8,128)S(1)}, f32[8,128]{1,0:T(8,128)S(1)}, u32[]{:S(2)}, u32[]{:S(2)}) %collective-permute-start.20) | collective-permute-done | bytes 4128 | tf_op jit(solution)/shard_map/ppermute | solution.py:515
  84.7 4.4 %collective-permute-start.23 = (f32[8,128]{1,0:T(8,128)S(1)}, f32[8,128]{1,0:T(8,128)S(1)}, u32[]{:S(2)}, u32[]{:S(2)}) collective-permute-start(f32[8,128]{1,0:T(8,128)S(1)} %add.30), channel_id=1, source_target_pairs={{0,12},{4,8},{8,4},{12,0},{1,13},{5,9},{9,5},{13,1},{2,14},{6,10},... | collective-permute-start | bytes 12296 | tf_op jit(solution)/shard_map/ppermute | solution.py:515
  89.2 1.5 %collective-permute-done.23 = f32[8,128]{1,0:T(8,128)S(1)} collective-permute-done((f32[8,128]{1,0:T(8,128)S(1)}, f32[8,128]{1,0:T(8,128)S(1)}, u32[]{:S(2)}, u32[]{:S(2)}) %collective-permute-start.23) | collective-permute-done | bytes 4128 | tf_op jit(solution)/shard_map/ppermute | solution.py:515
  90.7 1.5 %shard_map.126 = (f32[160,8,128]{2,1,0:T(8,128)}, f32[160,8,128]{2,1,0:T(8,128)}, f32[160,8,128]{2,1,0:T(8,128)}) custom-call(f32[8,128]{1,0:T(8,128)S(1)} %add_add_fusion.sums_ref, f32[160,8,128]{2,1,0:T(8,128)S(1)} %copy-done.2, f32[160,8,128]{2,1,0:T(8,128)S(1)} %copy-done.1, f32[160,8,128]{2,1,0:T(8,128)S(1)} %copy-done, f32[160,8,128]{2,1,0:T(8,128)S(1)} %bitcast.4), custom_call_target="tpu_custom_call" | custom-call | tf_op jit(solution)/shard_map/pallas_call | solution.py:455
  (53 shorter events, 11.1 us)
Async XLA Ops:
  2.0 1.1 %copy-start = (f32[160,8,128]{2,1,0:T(8,128)S(1)}, f32[160,8,128]{2,1,0:T(8,128)}, u32[]{:S(2)}) copy-start(f32[160,8,128]{2,1,0:T(8,128)} %d_ref.3) | copy-start | bytes 1966084
  3.0 19.4 %copy-start.6 = (bf16[20,32,8,128]{3,2,1,0:T(8,128)(2,1)S(1)}, bf16[20,32,8,128]{3,2,1,0:T(8,128)(2,1)}, u32[]{:S(2)}) copy-start(bf16[20,32,8,128]{3,2,1,0:T(8,128)(2,1)} %m_ref.1) | copy-start | bytes 3932164
  4.8 4.9 %collective-permute-start = (f32[32,160]{1,0:T(8,128)S(1)}, f32[32,160]{1,0:T(8,128)S(1)}, u32[]{:S(2)}, u32[]{:S(2)}) collective-permute-start(f32[32,160]{1,0:T(8,128)S(1)} %get-tuple-element.27.refs_4_), channel_id=1, source_target_pairs={{0,16},{16,0},{1,17},{17,1},{2,18},{18,2},{3,19},{19,3},{4,20},{20... | collective-permute-start | bytes 61448 | tf_op jit(solution)/shard_map/ppermute | solution.py:474
  11.2 8.1 %collective-permute-start.6 = (f32[4,80,128]{2,1,0:T(8,128)S(1)}, f32[4,80,128]{2,1,0:T(8,128)S(1)}, u32[]{:S(2)}, u32[]{:S(2)}) collective-permute-start(f32[4,80,128]{2,1,0:T(8,128)S(1)} %get-tuple-element.34.carried_ref), channel_id=1, source_target_pairs={{0,4},{8,12},{1,5},{9,13},{2,6},{10,14},{3,7},{11,15},{16,20},{24,... | collective-permute-start | bytes 491528 | tf_op jit(solution)/shard_map/ppermute | solution.py:488
  15.2 5.8 %collective-permute-start.1 = (f32[4,80,128]{2,1,0:T(8,128)S(1)}, f32[4,80,128]{2,1,0:T(8,128)S(1)}, u32[]{:S(2)}, u32[]{:S(2)}) collective-permute-start(f32[4,80,128]{2,1,0:T(8,128)S(1)} %get-tuple-element.30.carried_ref), channel_id=1, source_target_pairs={{0,4},{8,12},{1,5},{9,13},{2,6},{10,14},{3,7},{11,15},{16,20},{24,... | collective-permute-start | bytes 491528 | tf_op jit(solution)/shard_map/ppermute | solution.py:488
  19.3 4.4 %collective-permute-start.7 = (f32[4,80,128]{2,1,0:T(8,128)S(1)}, f32[4,80,128]{2,1,0:T(8,128)S(1)}, u32[]{:S(2)}, u32[]{:S(2)}) collective-permute-start(f32[4,80,128]{2,1,0:T(8,128)S(1)} %shard_map.119), channel_id=1, source_target_pairs={{4,8},{5,9},{6,10},{7,11},{20,24},{21,25},{22,26},{23,27}} | collective-permute-start | bytes 491528 | tf_op jit(solution)/shard_map/ppermute | solution.py:488
  20.0 3.7 %collective-permute-start.8 = (f32[4,80,128]{2,1,0:T(8,128)S(1)}, f32[4,80,128]{2,1,0:T(8,128)S(1)}, u32[]{:S(2)}, u32[]{:S(2)}) collective-permute-start(f32[4,80,128]{2,1,0:T(8,128)S(1)} %shard_map.119), channel_id=1, source_target_pairs={{4,12},{5,13},{6,14},{7,15},{20,28},{21,29},{22,30},{23,31}} | collective-permute-start | bytes 491528 | tf_op jit(solution)/shard_map/ppermute | solution.py:488
  21.1 2.6 %copy-start.4 = (f32[8,32]{1,0:T(8,128)S(1)}, f32[8,32]{1,0:T(8,128)}, u32[]{:S(2)}) copy-start(f32[8,32]{1,0:T(8,128)} %refs_4_.7) | copy-start | bytes 3076
  21.1 2.6 %copy-start.5 = (s32[20]{0:T(128)S(1)}, s32[20]{0:T(128)}, u32[]{:S(2)}) copy-start(s32[20]{0:T(128)} %refs_5_.3) | copy-start | bytes 244
  21.1 4.8 %collective-permute-start.2 = (f32[4,80,128]{2,1,0:T(8,128)S(1)}, f32[4,80,128]{2,1,0:T(8,128)S(1)}, u32[]{:S(2)}, u32[]{:S(2)}) collective-permute-start(f32[4,80,128]{2,1,0:T(8,128)S(1)} %shard_map.116), channel_id=1, source_target_pairs={{4,8},{5,9},{6,10},{7,11},{20,24},{21,25},{22,26},{23,27}} | collective-permute-start | bytes 491528 | tf_op jit(solution)/shard_map/ppermute | solution.py:488
  21.8 4.2 %collective-permute-start.3 = (f32[4,80,128]{2,1,0:T(8,128)S(1)}, f32[4,80,128]{2,1,0:T(8,128)S(1)}, u32[]{:S(2)}, u32[]{:S(2)}) collective-permute-start(f32[4,80,128]{2,1,0:T(8,128)S(1)} %shard_map.116), channel_id=1, source_target_pairs={{4,12},{5,13},{6,14},{7,15},{20,28},{21,29},{22,30},{23,31}} | collective-permute-start | bytes 491528 | tf_op jit(solution)/shard_map/ppermute | solution.py:488
  25.8 7.4 %copy-start.3 = (f32[32,8,128]{2,1,0:T(8,128)S(1)}, f32[32,8,128]{2,1,0:T(8,128)}, u32[]{:S(2)}) copy-start(f32[32,8,128]{2,1,0:T(8,128)} %refs_2_.4) | copy-start | bytes 393220
  25.8 2.8 %collective-permute-start.9 = (f32[16,8,128]{2,1,0:T(8,128)S(1)}, f32[16,8,128]{2,1,0:T(8,128)S(1)}, u32[]{:S(2)}, u32[]{:S(2)}) collective-permute-start(f32[16,8,128]{2,1,0:T(8,128)S(1)} %shard_map.120), channel_id=1, source_target_pairs={{0,1},{1,0},{2,3},{3,2},{4,5},{5,4},{6,7},{7,6},{8,9},{9,8},{10,11... | collective-permute-start | bytes 196616 | tf_op jit(solution)/shard_map/ppermute | solution.py:591
  28.0 2.1 %collective-permute-start.4 = (f32[16,8,128]{2,1,0:T(8,128)S(1)}, f32[16,8,128]{2,1,0:T(8,128)S(1)}, u32[]{:S(2)}, u32[]{:S(2)}) collective-permute-start(f32[16,8,128]{2,1,0:T(8,128)S(1)} %shard_map.117), channel_id=1, source_target_pairs={{0,1},{1,0},{2,3},{3,2},{4,5},{5,4},{6,7},{7,6},{8,9},{9,8},{10,11... | collective-permute-start | bytes 196616 | tf_op jit(solution)/shard_map/ppermute | solution.py:591
  28.6 4.6 %collective-permute-start.10 = (f32[16,8,128]{2,1,0:T(8,128)S(1)}, f32[16,8,128]{2,1,0:T(8,128)S(1)}, u32[]{:S(2)}, u32[]{:S(2)}) collective-permute-start(f32[16,8,128]{2,1,0:T(8,128)S(1)} %add.27.refs_0_), channel_id=1, source_target_pairs={{0,2},{1,3},{2,0},{3,1},{4,6},{5,7},{6,4},{7,5},{8,10},{9,11},{10,... | collective-permute-start | bytes 196616 | tf_op jit(solution)/shard_map/ppermute | solution.py:593
  30.2 6.5 %collective-permute-start.5 = (f32[16,8,128]{2,1,0:T(8,128)S(1)}, f32[16,8,128]{2,1,0:T(8,128)S(1)}, u32[]{:S(2)}, u32[]{:S(2)}) collective-permute-start(f32[16,8,128]{2,1,0:T(8,128)S(1)} %add.26.refs_0_), channel_id=1, source_target_pairs={{0,2},{1,3},{2,0},{3,1},{4,6},{5,7},{6,4},{7,5},{8,10},{9,11},{10,... | collective-permute-start | bytes 196616 | tf_op jit(solution)/shard_map/ppermute | solution.py:593
  35.4 14.4 %collective-permute-start.14 = (f32[4,80,128]{2,1,0:T(8,128)S(1)}, f32[4,80,128]{2,1,0:T(8,128)S(1)}, u32[]{:S(2)}, u32[]{:S(2)}) collective-permute-start(f32[4,80,128]{2,1,0:T(8,128)S(1)} %get-tuple-element.38.carried_ref), channel_id=1, source_target_pairs={{12,8},{4,0},{13,9},{5,1},{14,10},{6,2},{15,11},{7,3},{28,24},{20,... | collective-permute-start | bytes 491528 | tf_op jit(solution)/shard_map/ppermute | solution.py:488
  38.9 14.4 %collective-permute-start.11 = (f32[4,80,128]{2,1,0:T(8,128)S(1)}, f32[4,80,128]{2,1,0:T(8,128)S(1)}, u32[]{:S(2)}, u32[]{:S(2)}) collective-permute-start(f32[4,80,128]{2,1,0:T(8,128)S(1)} %get-tuple-element.37.carried_ref), channel_id=1, source_target_pairs={{12,8},{4,0},{13,9},{5,1},{14,10},{6,2},{15,11},{7,3},{28,24},{20,... | collective-permute-start | bytes 491528 | tf_op jit(solution)/shard_map/ppermute | solution.py:488
  49.9 25.1 %copy-start.1 = (f32[160,8,128]{2,1,0:T(8,128)S(1)}, f32[160,8,128]{2,1,0:T(8,128)}, u32[]{:S(2)}) copy-start(f32[160,8,128]{2,1,0:T(8,128)} %r_ref.1) | copy-start | bytes 1966084
  49.9 5.5 %collective-permute-start.15 = (f32[4,80,128]{2,1,0:T(8,128)S(1)}, f32[4,80,128]{2,1,0:T(8,128)S(1)}, u32[]{:S(2)}, u32[]{:S(2)}) collective-permute-start(f32[4,80,128]{2,1,0:T(8,128)S(1)} %shard_map.123), channel_id=1, source_target_pairs={{8,4},{9,5},{10,6},{11,7},{24,20},{25,21},{26,22},{27,23}} | collective-permute-start | bytes 491528 | tf_op jit(solution)/shard_map/ppermute | solution.py:488
  50.7 12.5 %collective-permute-start.16 = (f32[4,80,128]{2,1,0:T(8,128)S(1)}, f32[4,80,128]{2,1,0:T(8,128)S(1)}, u32[]{:S(2)}, u32[]{:S(2)}) collective-permute-start(f32[4,80,128]{2,1,0:T(8,128)S(1)} %shard_map.123), channel_id=1, source_target_pairs={{8,0},{9,1},{10,2},{11,3},{24,16},{25,17},{26,18},{27,19}} | collective-permute-start | bytes 491528 | tf_op jit(solution)/shard_map/ppermute | solution.py:488
  53.4 9.9 %collective-permute-start.12 = (f32[4,80,128]{2,1,0:T(8,128)S(1)}, f32[4,80,128]{2,1,0:T(8,128)S(1)}, u32[]{:S(2)}, u32[]{:S(2)}) collective-permute-start(f32[4,80,128]{2,1,0:T(8,128)S(1)} %shard_map.122), channel_id=1, source_target_pairs={{8,4},{9,5},{10,6},{11,7},{24,20},{25,21},{26,22},{27,23}} | collective-permute-start | bytes 491528 | tf_op jit(solution)/shard_map/ppermute | solution.py:488
  54.1 14.5 %collective-permute-start.13 = (f32[4,80,128]{2,1,0:T(8,128)S(1)}, f32[4,80,128]{2,1,0:T(8,128)S(1)}, u32[]{:S(2)}, u32[]{:S(2)}) collective-permute-start(f32[4,80,128]{2,1,0:T(8,128)S(1)} %shard_map.122), channel_id=1, source_target_pairs={{8,0},{9,1},{10,2},{11,3},{24,16},{25,17},{26,18},{27,19}} | collective-permute-start | bytes 491528 | tf_op jit(solution)/shard_map/ppermute | solution.py:488
  71.1 19.6 %copy-start.2 = (f32[160,8,128]{2,1,0:T(8,128)S(1)}, f32[160,8,128]{2,1,0:T(8,128)}, u32[]{:S(2)}) copy-start(f32[160,8,128]{2,1,0:T(8,128)} %control_ref.1) | copy-start | bytes 1966084
  71.1 4.0 %collective-permute-start.17 = (f32[32,160]{1,0:T(8,128)S(1)}, f32[32,160]{1,0:T(8,128)S(1)}, u32[]{:S(2)}, u32[]{:S(2)}) collective-permute-start(f32[32,160]{1,0:T(8,128)S(1)} %get-tuple-element.40.refs_5_), channel_id=1, source_target_pairs={{0,16},{16,0},{1,17},{17,1},{2,18},{18,2},{3,19},{19,3},{4,20},{20... | collective-permute-start | bytes 61448 | tf_op jit(solution)/shard_map/ppermute | solution.py:474
  76.2 1.2 %collective-permute-start.18 = (f32[8,128]{1,0:T(8,128)S(1)}, f32[8,128]{1,0:T(8,128)S(1)}, u32[]{:S(2)}, u32[]{:S(2)}) collective-permute-start(f32[8,128]{1,0:T(8,128)S(1)} %get-tuple-element.41), channel_id=1, source_target_pairs={{0,1},{1,0},{2,3},{3,2},{4,5},{5,4},{6,7},{7,6},{8,9},{9,8},{10,11... | collective-permute-start | bytes 12296 | tf_op jit(solution)/shard_map/ppermute | solution.py:515
  77.4 3.6 %collective-permute-start.19 = (f32[8,128]{1,0:T(8,128)S(1)}, f32[8,128]{1,0:T(8,128)S(1)}, u32[]{:S(2)}, u32[]{:S(2)}) collective-permute-start(f32[8,128]{1,0:T(8,128)S(1)} %add.28), channel_id=1, source_target_pairs={{0,2},{1,3},{2,0},{3,1},{4,6},{5,7},{6,4},{7,5},{8,10},{9,11},{10,... | collective-permute-start | bytes 12296 | tf_op jit(solution)/shard_map/ppermute | solution.py:515
  81.0 3.6 %collective-permute-start.20 = (f32[8,128]{1,0:T(8,128)S(1)}, f32[8,128]{1,0:T(8,128)S(1)}, u32[]{:S(2)}, u32[]{:S(2)}) collective-permute-start(f32[8,128]{1,0:T(8,128)S(1)} %add.29), channel_id=1, source_target_pairs={{0,16},{16,0},{1,17},{17,1},{2,18},{18,2},{3,19},{19,3},{4,20},{20... | collective-permute-start | bytes 12296 | tf_op jit(solution)/shard_map/ppermute | solution.py:515
  84.6 4.4 %collective-permute-start.21 = (f32[8,128]{1,0:T(8,128)S(1)}, f32[8,128]{1,0:T(8,128)S(1)}, u32[]{:S(2)}, u32[]{:S(2)}) collective-permute-start(f32[8,128]{1,0:T(8,128)S(1)} %add.30), channel_id=1, source_target_pairs={{0,4},{4,0},{8,12},{12,8},{1,5},{5,1},{9,13},{13,9},{2,6},{6,2},{1... | collective-permute-start | bytes 12296 | tf_op jit(solution)/shard_map/ppermute | solution.py:515
  84.6 4.5 %collective-permute-start.22 = (f32[8,128]{1,0:T(8,128)S(1)}, f32[8,128]{1,0:T(8,128)S(1)}, u32[]{:S(2)}, u32[]{:S(2)}) collective-permute-start(f32[8,128]{1,0:T(8,128)S(1)} %add.30), channel_id=1, source_target_pairs={{0,8},{4,12},{8,0},{12,4},{1,9},{5,13},{9,1},{13,5},{2,10},{6,14},... | collective-permute-start | bytes 12296 | tf_op jit(solution)/shard_map/ppermute | solution.py:515
  84.7 6.0 %collective-permute-start.23 = (f32[8,128]{1,0:T(8,128)S(1)}, f32[8,128]{1,0:T(8,128)S(1)}, u32[]{:S(2)}, u32[]{:S(2)}) collective-permute-start(f32[8,128]{1,0:T(8,128)S(1)} %add.30), channel_id=1, source_target_pairs={{0,12},{4,8},{8,4},{12,0},{1,13},{5,9},{9,5},{13,1},{2,14},{6,10},... | collective-permute-start | bytes 12296 | tf_op jit(solution)/shard_map/ppermute | solution.py:515

commit v5 on v4

--- a/solution.py
+++ b/solution.py
@@ -5,7 +5,6 @@
 from jax.experimental import pallas as pl
 from jax.experimental.pallas import tpu as pltpu
 from jax.sharding import PartitionSpec as P
-
 
 f32 = jnp.float32
 VM = pl.BlockSpec(memory_space=pltpu.VMEM)
@@ -167,23 +166,34 @@
     return [choose(rows, i) * leak**i * closing for i in range(4)]
 
 
-def incoming_states(plain, carried_on, dec, rows):
-    t = lat_trans(dec, rows)
-
-    def at(where):
+def entering_states(got, chunks):
+    hops = len(got) // chunks
+
+    def at(chunk, where):
         out = []
-        far = [[p[s, where, :] for s in range(4)] for p in carried_on]
         for s in range(4):
             v = None
-            for p in plain:
+            for p in got[chunk * hops : (chunk + 1) * hops]:
                 v = p[s, where, :] if v is None else v + p[s, where, :]
-            for f in far:
-                for j in range(s + 1):
-                    v = v + t[s - j] * f[j]
             out.append(v)
         return out
 
     return at
+
+
+def sweep_chunks(load, store, start, dec, rows, k, chunks, backward):
+    size = k // chunks
+    for ch in range(chunks):
+        lat_sweep(
+            lambda y, at, base, ch=ch: load(y, ch * size + base),
+            lambda y, at, base, value, last, ch=ch: store(y, ch, at, ch * size + base, value, last),
+            lambda at, ch=ch: start(ch, at),
+            dec,
+            rows,
+            size,
+            backward,
+            8,
+        )
 
 
 def member_blocks(members):
@@ -231,10 +241,10 @@
     lax.fori_loop(0, half, step, 0)
 
 
-def k_lat_first(rows, k, cells, n, *refs):
+def k_lat_first(rows, k, cells, n, chunks, *refs):
     inside_ref, lon_ref, lat_ref, *rest = refs
     blocks = [r[...] for r in rest[:n]]
-    *f_refs, a_ref, b_ref = rest[n:]
+    f_refs, out_refs = rest[n : n + 2], rest[n + 2 :]
     lonc = lon_ref[...]
     states = lon_incoming_states(lonc, blocks, rows, cells).T
     c, leak, _ = lon_consts(lonc)
@@ -244,22 +254,22 @@
         row = inside_ref[y] + lon_correction(states, entering, y)
         f_refs[0][y], f_refs[1][y] = swap_halves(row[:half], row[half:])
     zero = jnp.zeros((8, cells), f32)
-    for part, (f_ref, out_ref) in enumerate(zip(f_refs, (a_ref, b_ref))):
-
-        def store(y, at, base, value, last, out_ref=out_ref):
+    for part, f_ref in enumerate(f_refs):
+
+        def store(y, ch, at, base, value, last, part=part):
             if last is not None:
                 for s in range(4):
-                    out_ref[s, at, :] = last[s]
-
-        lat_sweep(
-            lambda y, at, base: f_ref[y, at, :],
+                    out_refs[part * chunks + ch][s, at, :] = last[s]
+
+        sweep_chunks(
+            lambda y, base: f_ref[y, pl.ds(pl.multiple_of(base, 8), 8), :],
             store,
-            lambda at: [zero] * 4,
+            lambda ch, at: [zero] * 4,
             lat_ref[part, :1],
             rows,
             half,
+            chunks,
             False,
-            8,
         )
 
 
@@ -280,24 +290,23 @@
     return jnp.where(low, first, second)
 
 
-def k_increment(rows, k, part, plain, far, pairs, modes, levels, *refs):
+def k_increment(rows, k, part, chunks, count, pairs, modes, levels, *refs):
     f_ref, lat_ref, m_ref, v_ref, eig_ref, *rest = refs
-    out_ref, s_ref, inc_ref = rest[plain + far :]
+    out_ref, s_ref, inc_ref = rest[count:]
     cells = lat_ref.shape[-1]
-    start = incoming_states(rest[:plain], rest[plain : plain + far], lat_ref[part, :1], rows)
-
-    def store(y, at, base, value, last):
+
+    def store(y, ch, at, base, value, last):
         s_ref[pl.ds(base * rows + y, 8, stride=rows), :] = value
 
-    lat_sweep(
-        lambda y, at, base: f_ref[y, at, :],
+    sweep_chunks(
+        lambda y, base: f_ref[y, pl.ds(pl.multiple_of(base, 8), 8), :],
         store,
-        start,
+        entering_states(rest[:count], chunks),
         lat_ref[part, :1],
         rows,
         k,
+        chunks,
         False,
-        8,
     )
     per = member_blocks(pairs)
     for b in range(pairs // per):
@@ -331,8 +340,8 @@
     out_ref[...] = jnp.where(low, full[:half], full[half:])
 
 
-def k_gradient(rows, k, part, pairs, modes, levels, *refs):
-    inc_ref, got_ref, obs_ref, m_ref, v_ref, eig_ref, lat_ref, g_ref, carried_ref, w_ref = refs
+def k_gradient(rows, k, part, chunks, pairs, modes, levels, *refs):
+    inc_ref, got_ref, obs_ref, m_ref, v_ref, eig_ref, lat_ref, g_ref, *carried_refs, w_ref = refs
     cells = lat_ref.shape[-1]
     half = levels // 2
     first, second = both_halves(inc_ref[...] + got_ref[...])
@@ -361,45 +370,42 @@
                 g_ref[at : at + rows, :] = acc[m * modes + e] * scale
     zero8 = jnp.zeros((8, cells), f32)
 
-    def store(y, at, base, value, last):
+    def store(y, ch, at, base, value, last):
         if last is not None:
             for s in range(4):
-                carried_ref[s, at, :] = last[s]
-
-    lat_sweep(
-        lambda y, at, base: g_ref[pl.ds(base * rows + y, 8, stride=rows), :],
+                carried_refs[ch][s, at, :] = last[s]
+
+    sweep_chunks(
+        lambda y, base: g_ref[pl.ds(base * rows + y, 8, stride=rows), :],
         store,
-        lambda at: [zero8] * 4,
+        lambda ch, at: [zero8] * 4,
         lat_ref[part, :1],
         rows,
         k,
+        chunks,
         True,
-        8,
-    )
-
-
-def k_lon_bwd(rows, k, cells, plain, far, *refs):
+    )
+
+
+def k_lon_bwd(rows, k, cells, chunks, count, *refs):
     g_refs, lat_ref, lon_ref, table_ref, rest = refs[:2], refs[2], refs[3], refs[4], refs[5:]
-    each = plain + far
-    inside_ref, carried_ref, p_ref = rest[2 * each :]
+    inside_ref, carried_ref, p_ref = rest[2 * count :]
     half = k // 2
     for part in range(2):
-        got = rest[part * each : (part + 1) * each]
-        start = incoming_states(got[:plain], got[plain:], lat_ref[part, :1], rows)
         g_ref = g_refs[part]
 
-        def store(y, at, base, value, last, part=part):
-            p_ref[part, y, at, :] = value
-
-        lat_sweep(
-            lambda y, at, base: g_ref[pl.ds(base * rows + y, 8, stride=rows), :],
+        def store(y, ch, at, base, value, last, part=part):
+            p_ref[part, y, pl.ds(pl.multiple_of(base, 8), 8), :] = value
+
+        sweep_chunks(
+            lambda y, base: g_ref[pl.ds(base * rows + y, 8, stride=rows), :],
             store,
-            start,
+            entering_states(rest[part * count : (part + 1) * count], chunks),
             lat_ref[part, :1],
             rows,
             half,
+            chunks,
             True,
-            8,
         )
 
     def load_row(y):
@@ -451,13 +457,14 @@
     nd_ref[...] = nr + beta * d
 
 
-def call(body, outs, ins, specs=None, scratch=(), cost=None):
+def call(body, outs, ins, specs=None, scratch=(), name=None, cost=None):
     return pl.pallas_call(
         body,
         out_shape=outs,
         in_specs=specs or [VM] * len(ins),
         out_specs=jax.tree.map(lambda _: VM, outs),
         scratch_shapes=scratch,
+        name=name,
         cost_estimate=None if cost is None else pl.CostEstimate(flops=cost, bytes_accessed=1000, transcendentals=0),
         compiler_params=pltpu.CompilerParams(vmem_limit_bytes=16 * 1024 * 1024),
     )(*ins)
@@ -477,32 +484,19 @@
 
 
 def pass_on(part, got, latc, rows, c):
-    return call(functools.partial(k_pass_on, rows, c), sds(*part.shape), [part, got, latc])
-
-
-def lat_carry(parts, latc, rows, backward):
+    return call(functools.partial(k_pass_on, rows, c), sds(*part.shape), [part, got, latc], name="pass_on")
+
+
+def lat_carry(halves, latc, rows, backward):
     n = lax.axis_size("lat")
     at = (lambda i: n - 1 - i) if backward else (lambda i: i)
-
-    def send(v, *pairs):
-        return lax.ppermute(v, "lat", [(at(a), at(b)) for a, b in pairs])
-
-    if n == 4:
-        near = [send(v, (0, 1), (2, 3)) for v in parts]
-        both = [pass_on(v, g, latc, rows, c) for c, (v, g) in enumerate(zip(parts, near))]
-        mid, far = [], []
-        for v in both:
-            far.append(send(v, (1, 3)))
-            mid.append(send(v, (1, 2)))
-        return [([a, b], [c]) for a, b, c in zip(near, mid, far)]
-    sends = list(parts)
-    got = [[] for _ in parts]
+    got = [[[] for _ in chunks] for chunks in halves]
     for h in range(n - 1):
-        for c, part in enumerate(parts):
-            if h:
-                sends[c] = pass_on(part, got[c][-1], latc, rows, c)
-            got[c].append(send(sends[c], (h, h + 1)))
-    return [(g, []) for g in got]
+        for c, chunks in enumerate(halves):
+            for i, part in enumerate(chunks):
+                v = pass_on(part, got[c][i][-1], latc, rows, c) if h else part
+                got[c][i].append(lax.ppermute(v, "lat", [(at(h), at(h + 1))]))
+    return [[g for chunk in half for g in chunk] for half in got]
 
 
 def all_sum(v, axes, steps):
@@ -538,50 +532,56 @@
     return v
 
 
-def iteration(control, residual, direction, members, vert_modes, eig_count, lon_decay, lat_decay, obs_weight):
+def body(control, residual, direction, members, vert_modes, eig_count, lon_decay, lat_decay, obs_weight):
     k, rows, cells = direction.shape
     mcount, levels = members.shape[:2]
     modes = vert_modes.shape[0]
     n_lon, n_mem = lax.axis_size("lon"), lax.axis_size("mem")
     half = k // 2
     pairs = mcount // 2
-    state = sds(4, half, cells)
+    chunks = 2
+    states = (sds(4, half // chunks, cells),) * chunks
 
     decays = jnp.stack([jnp.pad(lon_decay, (0, cells - rows)), lat_decay])
     lonc, latc, tables = call(
         functools.partial(k_tables, rows, cells),
         (sds(rows, cells), sds(2, 8, cells), sds(rows, cells, cells)),
         [decays],
+        name="tables",
         cost=10**9,
     )
     inside, carried = call(
         functools.partial(k_lon_fwd, rows, k, cells),
         (sds(rows, k, cells), sds(4 * rows, k)),
         [direction, lonc, tables],
-    )
-    *packed, tables = call(
+        name="lon_fwd",
+    )
+    *packed, back_tables = call(
         k_prepare,
         (sds(pairs, levels, rows, cells),) * 2 + (sds(rows, cells, cells),),
         [members, lonc],
+        name="prepare",
         cost=10**9,
     )
     blocks = lon_exchange(carried, False)
-    fa, fb, pa, pb = call(
-        functools.partial(k_lat_first, rows, k, cells, n_lon),
-        (sds(rows, half, cells),) * 2 + (state,) * 2,
+    fa, fb, *parts = call(
+        functools.partial(k_lat_first, rows, k, cells, n_lon, chunks),
+        (sds(rows, half, cells),) * 2 + states * 2,
         [inside, lonc, latc, *blocks],
-    )
-    got = lat_carry([pa, pb], latc, rows, False)
-    plain, far = (len(g) for g in got[0])
+        name="lat_first",
+    )
+    got = lat_carry([parts[:chunks], parts[chunks:]], latc, rows, False)
+    count = len(got[0])
     fields = (fa, fb)
     inc = [None, None]
     for part in range(2):
         inc[part] = call(
-            functools.partial(k_increment, rows, half, part, plain, far, pairs, modes, levels),
+            functools.partial(k_increment, rows, half, part, chunks, count, pairs, modes, levels),
             sds(levels // 2, rows, cells),
-            [fields[part], latc, packed[part], vert_modes, eig_count, *got[part][0], *got[part][1]],
-            specs=[VM, VM, VM, SM, SM] + [VM] * (plain + far),
+            [fields[part], latc, packed[part], vert_modes, eig_count, *got[part]],
+            specs=[VM, VM, VM, SM, SM] + [VM] * count,
             scratch=[pltpu.VMEM((half * rows, cells), f32), pltpu.VMEM((levels, rows, cells), f32)],
+            name="increment",
         )
     grads, sends = [None, None], [None, None]
     for part in range(2):
@@ -591,31 +591,35 @@
             v = v + lax.ppermute(v, "mem", [(i, i ^ step) for i in range(n_mem)])
             step *= 2
         other = lax.ppermute(v, "mem", [(i, i ^ step) for i in range(n_mem)])
-        grads[part], sends[part] = call(
-            functools.partial(k_gradient, rows, half, part, pairs, modes, levels),
-            (sds(half * rows, cells), state),
+        grads[part], *sends[part] = call(
+            functools.partial(k_gradient, rows, half, part, chunks, pairs, modes, levels),
+            (sds(half * rows, cells),) + states,
             [v, other, obs_weight, packed[part], vert_modes, eig_count, latc],
             specs=[VM, VM, VM, VM, SM, SM, VM],
             scratch=[pltpu.VMEM((levels, rows, cells), f32)],
+            name="gradient",
         )
     got = lat_carry(sends, latc, rows, True)
     inside, carried = call(
-        functools.partial(k_lon_bwd, rows, k, cells, plain, far),
+        functools.partial(k_lon_bwd, rows, k, cells, chunks, count),
         (sds(rows, k, cells), sds(4 * rows, k)),
-        [*grads, latc, lonc, tables, *got[0][0], *got[0][1], *got[1][0], *got[1][1]],
+        [*grads, latc, lonc, back_tables, *got[0], *got[1]],
         scratch=[pltpu.VMEM((2, rows, half, cells), f32)],
+        name="lon_bwd",
     )
     blocks = lon_exchange(carried, True)
     h, sums = call(
         functools.partial(k_sums, rows, k, cells, n_lon),
         (sds(k * rows, cells), sds(8, cells)),
         [inside, lonc, direction, residual, *blocks],
+        name="sums",
     )
     sums = reduce_everywhere(sums)
     outs = call(
         k_update,
         (sds(k, rows, cells),) * 3,
         [sums, control, residual, direction, h.reshape(k, rows, cells)],
+        name="update",
     )
     return tuple(outs)
 
@@ -633,4 +637,4 @@
         P("lon"),
         P(None, "lat", "lon"),
     )
-    return jax.shard_map(iteration, mesh=mesh, in_specs=placed, out_specs=(field,) * 3, check_vma=False)
+    return jax.shard_map(body, mesh=mesh, in_specs=placed, out_specs=(field,) * 3, check_vma=False)

time: 92.5 us -> 89.6 us (0.969)
  waiting for transfers between devices: 41.1 us -> 27.8 us
  starting transfers between devices: 29.4 us -> 39 us
    ppermute x16 -> x28, waiting for transfers between devices: 29.4 us -> 16.6 us  [the longest x24 14.4 us: lat_carry(): got[c][i].append(lax.ppermute(v, 'lat', [(at(h), at(h + 1))]))]
    ppermute x16 -> x28, starting transfers between devices: 17.7 us -> 26.9 us  [the longest x24 23.9 us: lat_carry(): got[c][i].append(lax.ppermute(v, 'lat', [(at(h), at(h + 1))]))]
    pallas_call x15 -> x27, Pallas kernels: 18.5 us -> 18.7 us  [call(): pl.pallas_call(body, out_shape=outs, in_specs=specs or [VM] * len(ins), o...]
  transfers between devices with their start and end apart: 24 -> 36, of which waited for: 14 -> 14; matrix products, arithmetic and copies ran while one was open for 0% -> 0% of each run, Pallas kernels for 11% -> 11%
where the time goes in v5:
time: 89.6 us; the launch traced here: 89 us
  starting transfers between devices  39 us (44%)
  waiting for transfers between devices  27.8 us (31%)
  Pallas kernels  18.7 us (21%)
  local copies, waits for them, and re-layouts  1.57 us (2%)
  between operations  1.23 us (1%)
    ppermute x24, starting transfers between devices, lat_carry(): got[c][i].append(lax.ppermute(v, 'lat', [(at(h), at(h + 1))]))  23.9 us
    pallas_call x27, Pallas kernels, call(): pl.pallas_call(body, out_shape=outs, in_specs=specs or [VM] * len(ins), o...  18.7 us
    ppermute x24, waiting for transfers between devices, lat_carry(): got[c][i].append(lax.ppermute(v, 'lat', [(at(h), at(h + 1))]))  14.4 us
    ppermute x6, starting transfers between devices, all_sum(): lax.ppermute(v, axes, [(i, i ^ m) for i in range(total)])  7.52 us
    ppermute x6, waiting for transfers between devices, all_sum(): lax.ppermute(v, axes, [(i, i ^ m) for i in range(total)])  6.92 us
    ppermute x2, starting transfers between devices, lon_exchange(): lax.ppermute(carried, 'lon', [(j, (j + sign * r) % n) for j in range(n)])  4.57 us
    ppermute x2, waiting for transfers between devices, lon_exchange(): lax.ppermute(carried, 'lon', [(j, (j + sign * r) % n) for j in range(n)])  4.34 us
    ppermute x2, starting transfers between devices, body(): other = lax.ppermute(v, 'mem', [(i, i ^ step) for i in range(n_mem)])  2.47 us
  transfers between devices with their start and end apart: 36, of which 14 were waited for; matrix products, arithmetic and copies ran while one was open for 0% of the time, Pallas kernels for 11%

profile of v5, /device:TPU:0, one launch (start us, length us, event | category | flops | bytes accessed | tf_op | source)
XLA Modules:
  0.0 89.0 jit_solution(17791501047705286955)
XLA Ops:
  3.0 1.8 %lon_fwd.1 = (f32[8,160,128]{2,1,0:T(8,128)S(1)}, f32[32,160]{1,0:T(8,128)S(1)}) custom-call(f32[160,8,128]{2,1,0:T(8,128)S(1)} %copy-done, f32[8,128]{1,0:T(8,128)S(1)} %get-tuple-element.27.lon_ref.refs_1_.refs_3_, f32[8,128,128]{2,1,0:T(8,128)S(1)} %get-tuple-element.28.table_ref), custom_call_target="tpu_custom_call" | custom-call | tf_op jit(solution)/shard_map/lon_fwd/pallas_call | solution.py:461
  4.8 3.0 %collective-permute-start = (f32[32,160]{1,0:T(8,128)S(1)}, f32[32,160]{1,0:T(8,128)S(1)}, u32[]{:S(2)}, u32[]{:S(2)}) collective-permute-start(f32[32,160]{1,0:T(8,128)S(1)} %get-tuple-element.31.refs_4_), channel_id=1, source_target_pairs={{0,16},{16,0},{1,17},{17,1},{2,18},{18,2},{3,19},{19,3},{4,20},{20... | collective-permute-start | bytes 61448 | tf_op jit(solution)/shard_map/ppermute | solution.py:481
  7.9 1.9 %collective-permute-done.refs_3_ = f32[32,160]{1,0:T(8,128)S(1)} collective-permute-done((f32[32,160]{1,0:T(8,128)S(1)}, f32[32,160]{1,0:T(8,128)S(1)}, u32[]{:S(2)}, u32[]{:S(2)}) %collective-permute-start) | collective-permute-done | bytes 20512 | tf_op jit(solution)/shard_map/ppermute | solution.py:481
  9.8 1.4 %lat_first.1 = (f32[8,80,128]{2,1,0:T(8,128)S(1)}, f32[8,80,128]{2,1,0:T(8,128)S(1)}, f32[4,40,128]{2,1,0:T(8,128)S(1)}, f32[4,40,128]{2,1,0:T(8,128)S(1)}, f32[...) custom-call(f32[8,160,128]{2,1,0:T(8,128)S(1)} %get-tuple-element.29.refs_0_, ...), custom_call_target="tpu_custom_call" | custom-call | tf_op jit(solution)/shard_map/lat_first/pallas_call | solution.py:461
  11.2 4.0 %collective-permute-start.12 = (f32[4,40,128]{2,1,0:T(8,128)S(1)}, f32[4,40,128]{2,1,0:T(8,128)S(1)}, u32[]{:S(2)}, u32[]{:S(2)}) collective-permute-start(f32[4,40,128]{2,1,0:T(8,128)S(1)} %get-tuple-element.40.carried_ref), channel_id=1, source_target_pairs={{0,4},{1,5},{2,6},{3,7},{16,20},{17,21},{18,22},{19,23}} | collective-permute-start | bytes 245768 | tf_op jit(solution)/shard_map/ppermute | solution.py:498
  15.2 1.3 %collective-permute-start.9 = (f32[4,40,128]{2,1,0:T(8,128)S(1)}, f32[4,40,128]{2,1,0:T(8,128)S(1)}, u32[]{:S(2)}, u32[]{:S(2)}) collective-permute-start(f32[4,40,128]{2,1,0:T(8,128)S(1)} %get-tuple-element.39.carried_ref), channel_id=1, source_target_pairs={{0,4},{1,5},{2,6},{3,7},{16,20},{17,21},{18,22},{19,23}} | collective-permute-start | bytes 245768 | tf_op jit(solution)/shard_map/ppermute | solution.py:498
  16.5 1.3 %collective-permute-start.4 = (f32[4,40,128]{2,1,0:T(8,128)S(1)}, f32[4,40,128]{2,1,0:T(8,128)S(1)}, u32[]{:S(2)}, u32[]{:S(2)}) collective-permute-start(f32[4,40,128]{2,1,0:T(8,128)S(1)} %get-tuple-element.35.carried_ref), channel_id=1, source_target_pairs={{0,4},{1,5},{2,6},{3,7},{16,20},{17,21},{18,22},{19,23}} | collective-permute-start | bytes 245768 | tf_op jit(solution)/shard_map/ppermute | solution.py:498
  17.8 1.3 %collective-permute-start.1 = (f32[4,40,128]{2,1,0:T(8,128)S(1)}, f32[4,40,128]{2,1,0:T(8,128)S(1)}, u32[]{:S(2)}, u32[]{:S(2)}) collective-permute-start(f32[4,40,128]{2,1,0:T(8,128)S(1)} %get-tuple-element.34.carried_ref), channel_id=1, source_target_pairs={{0,4},{1,5},{2,6},{3,7},{16,20},{17,21},{18,22},{19,23}} | collective-permute-start | bytes 245768 | tf_op jit(solution)/shard_map/ppermute | solution.py:498
  25.1 1.2 %prepare.1 = (f32[10,32,8,128]{3,2,1,0:T(8,128)S(1)}, f32[10,32,8,128]{3,2,1,0:T(8,128)S(1)}, f32[8,128,128]{2,1,0:T(8,128)S(1)}) custom-call(bf16[20,32,8,128]{3,2,1,0:T(8,128)(2,1)S(1)} %copy-done.6, f32[8,128]{1,0:T(8,128)S(1)} %get-tuple-element.27.lon_ref.refs_1_.refs_3_), custom_call_target="tpu_custom_call" | custom-call | flops 1000000000 | bytes 1000 | tf_op jit(solution)/shard_map/prepare/pallas_call | solution.py:461
  26.4 2.1 %increment.3 = f32[16,8,128]{2,1,0:T(8,128)S(1)} custom-call(f32[8,80,128]{2,1,0:T(8,128)S(1)} %get-tuple-element.37.refs_0_, f32[2,8,128]{2,1,0:T(8,128)S(1)} %get-tuple-element.30.refs_2_.lat_ref.refs_1_.refs_6_, f32[10,32,8,128]{3,2,1,0:T(8,128)S(1)} %get-tuple-element.38.refs_2_.refs_3_, f32[8,32]{1,0:T(8,128)S(1)} %copy-done.4, s32[20]{0:T(128)S(1)} %copy-done.5, ...), custom_call_target="tpu_custom_call" | custom-call | tf_op jit(solution)/shard_map/increment/pallas_call | solution.py:461
  28.6 2.1 %increment.2 = f32[16,8,128]{2,1,0:T(8,128)S(1)} custom-call(f32[8,80,128]{2,1,0:T(8,128)S(1)} %get-tuple-element.32.refs_0_, f32[2,8,128]{2,1,0:T(8,128)S(1)} %get-tuple-element.30.refs_2_.lat_ref.refs_1_.refs_6_, f32[10,32,8,128]{3,2,1,0:T(8,128)S(1)} %get-tuple-element.33.refs_2_.refs_3_, f32[8,32]{1,0:T(8,128)S(1)} %copy-done.4, s32[20]{0:T(128)S(1)} %copy-done.5, ...), custom_call_target="tpu_custom_call" | custom-call | tf_op jit(solution)/shard_map/increment/pallas_call | solution.py:461
  31.3 1.6 %collective-permute-start.16 = (f32[16,8,128]{2,1,0:T(8,128)S(1)}, f32[16,8,128]{2,1,0:T(8,128)S(1)}, u32[]{:S(2)}, u32[]{:S(2)}) collective-permute-start(f32[16,8,128]{2,1,0:T(8,128)S(1)} %add.27.refs_0_), channel_id=1, source_target_pairs={{0,2},{1,3},{2,0},{3,1},{4,6},{5,7},{6,4},{7,5},{8,10},{9,11},{10,... | collective-permute-start | bytes 196616 | tf_op jit(solution)/shard_map/ppermute | solution.py:593
  33.7 2.2 %collective-permute-done.16.refs_1_ = f32[16,8,128]{2,1,0:T(8,128)S(1)} collective-permute-done((f32[16,8,128]{2,1,0:T(8,128)S(1)}, f32[16,8,128]{2,1,0:T(8,128)S(1)}, u32[]{:S(2)}, u32[]{:S(2)}) %collective-permute-start.16) | collective-permute-done | bytes 65568 | tf_op jit(solution)/shard_map/ppermute | solution.py:593
  35.9 2.2 %gradient.3 = (f32[640,128]{1,0:T(8,128)S(1)}, f32[4,40,128]{2,1,0:T(8,128)S(1)}, f32[4,40,128]{2,1,0:T(8,128)S(1)}) custom-call(f32[16,8,128]{2,1,0:T(8,128)S(1)} %add.27.refs_0_, f32[16,8,128]{2,1,0:T(8,128)S(1)} %collective-permute-done.16.refs_1_, f32[32,8,128]{2,1,0:T(8,128)S(1)} %copy-done.3, f32[10,32,8,128]{3,2,1,0:T(8,128)S(1)} %get-tuple-element.38.refs_2_.refs_3_, ...), custom_call_target="tpu_custom_call" | custom-call | tf_op jit(solution)/shard_map/gradient/pallas_call | solution.py:461
  39.4 2.2 %gradient.2 = (f32[640,128]{1,0:T(8,128)S(1)}, f32[4,40,128]{2,1,0:T(8,128)S(1)}, f32[4,40,128]{2,1,0:T(8,128)S(1)}) custom-call(f32[16,8,128]{2,1,0:T(8,128)S(1)} %add.26.refs_0_, f32[16,8,128]{2,1,0:T(8,128)S(1)} %collective-permute-done.8.refs_1_, f32[32,8,128]{2,1,0:T(8,128)S(1)} %copy-done.3, f32[10,32,8,128]{3,2,1,0:T(8,128)S(1)} %get-tuple-element.33.refs_2_.refs_3_, ...), custom_call_target="tpu_custom_call" | custom-call | tf_op jit(solution)/shard_map/gradient/pallas_call | solution.py:461
  45.9 1.3 %collective-permute-start.28 = (f32[4,40,128]{2,1,0:T(8,128)S(1)}, f32[4,40,128]{2,1,0:T(8,128)S(1)}, u32[]{:S(2)}, u32[]{:S(2)}) collective-permute-start(f32[4,40,128]{2,1,0:T(8,128)S(1)} %pass_on.31), channel_id=1, source_target_pairs={{4,0},{5,1},{6,2},{7,3},{20,16},{21,17},{22,18},{23,19}} | collective-permute-start | bytes 245768 | tf_op jit(solution)/shard_map/ppermute | solution.py:498
  47.2 1.4 %collective-permute-start.25 = (f32[4,40,128]{2,1,0:T(8,128)S(1)}, f32[4,40,128]{2,1,0:T(8,128)S(1)}, u32[]{:S(2)}, u32[]{:S(2)}) collective-permute-start(f32[4,40,128]{2,1,0:T(8,128)S(1)} %pass_on.29), channel_id=1, source_target_pairs={{4,0},{5,1},{6,2},{7,3},{20,16},{21,17},{22,18},{23,19}} | collective-permute-start | bytes 245768 | tf_op jit(solution)/shard_map/ppermute | solution.py:498
  48.7 1.3 %collective-permute-start.22 = (f32[4,40,128]{2,1,0:T(8,128)S(1)}, f32[4,40,128]{2,1,0:T(8,128)S(1)}, u32[]{:S(2)}, u32[]{:S(2)}) collective-permute-start(f32[4,40,128]{2,1,0:T(8,128)S(1)} %pass_on.27), channel_id=1, source_target_pairs={{4,0},{5,1},{6,2},{7,3},{20,16},{21,17},{22,18},{23,19}} | collective-permute-start | bytes 245768 | tf_op jit(solution)/shard_map/ppermute | solution.py:498
  50.0 1.3 %collective-permute-start.19 = (f32[4,40,128]{2,1,0:T(8,128)S(1)}, f32[4,40,128]{2,1,0:T(8,128)S(1)}, u32[]{:S(2)}, u32[]{:S(2)}) collective-permute-start(f32[4,40,128]{2,1,0:T(8,128)S(1)} %pass_on.25), channel_id=1, source_target_pairs={{4,0},{5,1},{6,2},{7,3},{20,16},{21,17},{22,18},{23,19}} | collective-permute-start | bytes 245768 | tf_op jit(solution)/shard_map/ppermute | solution.py:498
  51.3 10.0 %collective-permute-done.28.refs_16_ = f32[4,40,128]{2,1,0:T(8,128)S(1)} collective-permute-done((f32[4,40,128]{2,1,0:T(8,128)S(1)}, f32[4,40,128]{2,1,0:T(8,128)S(1)}, u32[]{:S(2)}, u32[]{:S(2)}) %collective-permute-start.28) | collective-permute-done | bytes 81952 | tf_op jit(solution)/shard_map/ppermute | solution.py:498
  61.3 2.1 %collective-permute-done.25.refs_13_ = f32[4,40,128]{2,1,0:T(8,128)S(1)} collective-permute-done((f32[4,40,128]{2,1,0:T(8,128)S(1)}, f32[4,40,128]{2,1,0:T(8,128)S(1)}, u32[]{:S(2)}, u32[]{:S(2)}) %collective-permute-start.25) | collective-permute-done | bytes 81952 | tf_op jit(solution)/shard_map/ppermute | solution.py:498
  65.4 2.5 %lon_bwd.1 = (f32[8,160,128]{2,1,0:T(8,128)S(1)}, f32[32,160]{1,0:T(8,128)S(1)}) custom-call(f32[640,128]{1,0:T(8,128)S(1)} %get-tuple-element.36.refs_0_, f32[640,128]{1,0:T(8,128)S(1)} %get-tuple-element.41.refs_1_, f32[2,8,128]{2,1,0:T(8,128)S(1)} %get-tuple-element.30.refs_2_.lat_ref.refs_1_.refs_6_, ...), custom_call_target="tpu_custom_call" | custom-call | tf_op jit(solution)/shard_map/lon_bwd/pallas_call | solution.py:461
  67.9 1.5 %collective-permute-start.29 = (f32[32,160]{1,0:T(8,128)S(1)}, f32[32,160]{1,0:T(8,128)S(1)}, u32[]{:S(2)}, u32[]{:S(2)}) collective-permute-start(f32[32,160]{1,0:T(8,128)S(1)} %get-tuple-element.48.refs_5_), channel_id=1, source_target_pairs={{0,16},{16,0},{1,17},{17,1},{2,18},{18,2},{3,19},{19,3},{4,20},{20... | collective-permute-start | bytes 61448 | tf_op jit(solution)/shard_map/ppermute | solution.py:481
  69.5 2.4 %collective-permute-done.29.refs_4_ = f32[32,160]{1,0:T(8,128)S(1)} collective-permute-done((f32[32,160]{1,0:T(8,128)S(1)}, f32[32,160]{1,0:T(8,128)S(1)}, u32[]{:S(2)}, u32[]{:S(2)}) %collective-permute-start.29) | collective-permute-done | bytes 20512 | tf_op jit(solution)/shard_map/ppermute | solution.py:481
  73.1 1.2 %collective-permute-done.30 = f32[8,128]{1,0:T(8,128)S(1)} collective-permute-done((f32[8,128]{1,0:T(8,128)S(1)}, f32[8,128]{1,0:T(8,128)S(1)}, u32[]{:S(2)}, u32[]{:S(2)}) %collective-permute-start.30) | collective-permute-done | bytes 4128 | tf_op jit(solution)/shard_map/ppermute | solution.py:509
  74.3 1.6 %collective-permute-start.31 = (f32[8,128]{1,0:T(8,128)S(1)}, f32[8,128]{1,0:T(8,128)S(1)}, u32[]{:S(2)}, u32[]{:S(2)}) collective-permute-start(f32[8,128]{1,0:T(8,128)S(1)} %add.28), channel_id=1, source_target_pairs={{0,2},{1,3},{2,0},{3,1},{4,6},{5,7},{6,4},{7,5},{8,10},{9,11},{10,... | collective-permute-start | bytes 12296 | tf_op jit(solution)/shard_map/ppermute | solution.py:509
  75.9 2.0 %collective-permute-done.31 = f32[8,128]{1,0:T(8,128)S(1)} collective-permute-done((f32[8,128]{1,0:T(8,128)S(1)}, f32[8,128]{1,0:T(8,128)S(1)}, u32[]{:S(2)}, u32[]{:S(2)}) %collective-permute-start.31) | collective-permute-done | bytes 4128 | tf_op jit(solution)/shard_map/ppermute | solution.py:509
  77.9 1.5 %collective-permute-start.32 = (f32[8,128]{1,0:T(8,128)S(1)}, f32[8,128]{1,0:T(8,128)S(1)}, u32[]{:S(2)}, u32[]{:S(2)}) collective-permute-start(f32[8,128]{1,0:T(8,128)S(1)} %add.29), channel_id=1, source_target_pairs={{0,16},{16,0},{1,17},{17,1},{2,18},{18,2},{3,19},{19,3},{4,20},{20... | collective-permute-start | bytes 12296 | tf_op jit(solution)/shard_map/ppermute | solution.py:509
  79.4 2.1 %collective-permute-done.32 = f32[8,128]{1,0:T(8,128)S(1)} collective-permute-done((f32[8,128]{1,0:T(8,128)S(1)}, f32[8,128]{1,0:T(8,128)S(1)}, u32[]{:S(2)}, u32[]{:S(2)}) %collective-permute-start.32) | collective-permute-done | bytes 4128 | tf_op jit(solution)/shard_map/ppermute | solution.py:509
  81.5 4.4 %collective-permute-start.35 = (f32[8,128]{1,0:T(8,128)S(1)}, f32[8,128]{1,0:T(8,128)S(1)}, u32[]{:S(2)}, u32[]{:S(2)}) collective-permute-start(f32[8,128]{1,0:T(8,128)S(1)} %add.30), channel_id=1, source_target_pairs={{0,12},{4,8},{8,4},{12,0},{1,13},{5,9},{9,5},{13,1},{2,14},{6,10},... | collective-permute-start | bytes 12296 | tf_op jit(solution)/shard_map/ppermute | solution.py:509
  86.0 1.5 %collective-permute-done.35 = f32[8,128]{1,0:T(8,128)S(1)} collective-permute-done((f32[8,128]{1,0:T(8,128)S(1)}, f32[8,128]{1,0:T(8,128)S(1)}, u32[]{:S(2)}, u32[]{:S(2)}) %collective-permute-start.35) | collective-permute-done | bytes 4128 | tf_op jit(solution)/shard_map/ppermute | solution.py:509
  87.5 1.5 %update.1 = (f32[160,8,128]{2,1,0:T(8,128)}, f32[160,8,128]{2,1,0:T(8,128)}, f32[160,8,128]{2,1,0:T(8,128)}) custom-call(f32[8,128]{1,0:T(8,128)S(1)} %add_add_fusion.sums_ref, f32[160,8,128]{2,1,0:T(8,128)S(1)} %copy-done.2, f32[160,8,128]{2,1,0:T(8,128)S(1)} %copy-done.1, f32[160,8,128]{2,1,0:T(8,128)S(1)} %copy-done, f32[160,8,128]{2,1,0:T(8,128)S(1)} %bitcast.4), custom_call_target="tpu_custom_call" | custom-call | tf_op jit(solution)/shard_map/update/pallas_call | solution.py:461
  (89 shorter events, 18.7 us)
Async XLA Ops:
  4.8 4.9 %collective-permute-start = (f32[32,160]{1,0:T(8,128)S(1)}, f32[32,160]{1,0:T(8,128)S(1)}, u32[]{:S(2)}, u32[]{:S(2)}) collective-permute-start(f32[32,160]{1,0:T(8,128)S(1)} %get-tuple-element.31.refs_4_), channel_id=1, source_target_pairs={{0,16},{16,0},{1,17},{17,1},{2,18},{18,2},{3,19},{19,3},{4,20},{20... | collective-permute-start | bytes 61448 | tf_op jit(solution)/shard_map/ppermute | solution.py:481
  11.2 7.9 %collective-permute-start.12 = (f32[4,40,128]{2,1,0:T(8,128)S(1)}, f32[4,40,128]{2,1,0:T(8,128)S(1)}, u32[]{:S(2)}, u32[]{:S(2)}) collective-permute-start(f32[4,40,128]{2,1,0:T(8,128)S(1)} %get-tuple-element.40.carried_ref), channel_id=1, source_target_pairs={{0,4},{1,5},{2,6},{3,7},{16,20},{17,21},{18,22},{19,23}} | collective-permute-start | bytes 245768 | tf_op jit(solution)/shard_map/ppermute | solution.py:498
  15.2 4.6 %collective-permute-start.9 = (f32[4,40,128]{2,1,0:T(8,128)S(1)}, f32[4,40,128]{2,1,0:T(8,128)S(1)}, u32[]{:S(2)}, u32[]{:S(2)}) collective-permute-start(f32[4,40,128]{2,1,0:T(8,128)S(1)} %get-tuple-element.39.carried_ref), channel_id=1, source_target_pairs={{0,4},{1,5},{2,6},{3,7},{16,20},{17,21},{18,22},{19,23}} | collective-permute-start | bytes 245768 | tf_op jit(solution)/shard_map/ppermute | solution.py:498
  16.5 4.1 %collective-permute-start.4 = (f32[4,40,128]{2,1,0:T(8,128)S(1)}, f32[4,40,128]{2,1,0:T(8,128)S(1)}, u32[]{:S(2)}, u32[]{:S(2)}) collective-permute-start(f32[4,40,128]{2,1,0:T(8,128)S(1)} %get-tuple-element.35.carried_ref), channel_id=1, source_target_pairs={{0,4},{1,5},{2,6},{3,7},{16,20},{17,21},{18,22},{19,23}} | collective-permute-start | bytes 245768 | tf_op jit(solution)/shard_map/ppermute | solution.py:498
  17.8 3.7 %collective-permute-start.1 = (f32[4,40,128]{2,1,0:T(8,128)S(1)}, f32[4,40,128]{2,1,0:T(8,128)S(1)}, u32[]{:S(2)}, u32[]{:S(2)}) collective-permute-start(f32[4,40,128]{2,1,0:T(8,128)S(1)} %get-tuple-element.34.carried_ref), channel_id=1, source_target_pairs={{0,4},{1,5},{2,6},{3,7},{16,20},{17,21},{18,22},{19,23}} | collective-permute-start | bytes 245768 | tf_op jit(solution)/shard_map/ppermute | solution.py:498
  19.1 3.1 %collective-permute-start.13 = (f32[4,40,128]{2,1,0:T(8,128)S(1)}, f32[4,40,128]{2,1,0:T(8,128)S(1)}, u32[]{:S(2)}, u32[]{:S(2)}) collective-permute-start(f32[4,40,128]{2,1,0:T(8,128)S(1)} %pass_on.22), channel_id=1, source_target_pairs={{4,8},{5,9},{6,10},{7,11},{20,24},{21,25},{22,26},{23,27}} | collective-permute-start | bytes 245768 | tf_op jit(solution)/shard_map/ppermute | solution.py:498
  19.9 3.1 %collective-permute-start.10 = (f32[4,40,128]{2,1,0:T(8,128)S(1)}, f32[4,40,128]{2,1,0:T(8,128)S(1)}, u32[]{:S(2)}, u32[]{:S(2)}) collective-permute-start(f32[4,40,128]{2,1,0:T(8,128)S(1)} %pass_on.20), channel_id=1, source_target_pairs={{4,8},{5,9},{6,10},{7,11},{20,24},{21,25},{22,26},{23,27}} | collective-permute-start | bytes 245768 | tf_op jit(solution)/shard_map/ppermute | solution.py:498
  20.7 3.0 %collective-permute-start.5 = (f32[4,40,128]{2,1,0:T(8,128)S(1)}, f32[4,40,128]{2,1,0:T(8,128)S(1)}, u32[]{:S(2)}, u32[]{:S(2)}) collective-permute-start(f32[4,40,128]{2,1,0:T(8,128)S(1)} %pass_on.18), channel_id=1, source_target_pairs={{4,8},{5,9},{6,10},{7,11},{20,24},{21,25},{22,26},{23,27}} | collective-permute-start | bytes 245768 | tf_op jit(solution)/shard_map/ppermute | solution.py:498
  21.6 2.8 %collective-permute-start.2 = (f32[4,40,128]{2,1,0:T(8,128)S(1)}, f32[4,40,128]{2,1,0:T(8,128)S(1)}, u32[]{:S(2)}, u32[]{:S(2)}) collective-permute-start(f32[4,40,128]{2,1,0:T(8,128)S(1)} %pass_on.16), channel_id=1, source_target_pairs={{4,8},{5,9},{6,10},{7,11},{20,24},{21,25},{22,26},{23,27}} | collective-permute-start | bytes 245768 | tf_op jit(solution)/shard_map/ppermute | solution.py:498
  22.3 4.1 %collective-permute-start.14 = (f32[4,40,128]{2,1,0:T(8,128)S(1)}, f32[4,40,128]{2,1,0:T(8,128)S(1)}, u32[]{:S(2)}, u32[]{:S(2)}) collective-permute-start(f32[4,40,128]{2,1,0:T(8,128)S(1)} %pass_on.23), channel_id=1, source_target_pairs={{8,12},{9,13},{10,14},{11,15},{24,28},{25,29},{26,30},{27,31}} | collective-permute-start | bytes 245768 | tf_op jit(solution)/shard_map/ppermute | solution.py:498
  23.0 3.4 %collective-permute-start.11 = (f32[4,40,128]{2,1,0:T(8,128)S(1)}, f32[4,40,128]{2,1,0:T(8,128)S(1)}, u32[]{:S(2)}, u32[]{:S(2)}) collective-permute-start(f32[4,40,128]{2,1,0:T(8,128)S(1)} %pass_on.21), channel_id=1, source_target_pairs={{8,12},{9,13},{10,14},{11,15},{24,28},{25,29},{26,30},{27,31}} | collective-permute-start | bytes 245768 | tf_op jit(solution)/shard_map/ppermute | solution.py:498
  23.7 4.9 %collective-permute-start.6 = (f32[4,40,128]{2,1,0:T(8,128)S(1)}, f32[4,40,128]{2,1,0:T(8,128)S(1)}, u32[]{:S(2)}, u32[]{:S(2)}) collective-permute-start(f32[4,40,128]{2,1,0:T(8,128)S(1)} %pass_on.19), channel_id=1, source_target_pairs={{8,12},{9,13},{10,14},{11,15},{24,28},{25,29},{26,30},{27,31}} | collective-permute-start | bytes 245768 | tf_op jit(solution)/shard_map/ppermute | solution.py:498
  24.5 4.1 %collective-permute-start.3 = (f32[4,40,128]{2,1,0:T(8,128)S(1)}, f32[4,40,128]{2,1,0:T(8,128)S(1)}, u32[]{:S(2)}, u32[]{:S(2)}) collective-permute-start(f32[4,40,128]{2,1,0:T(8,128)S(1)} %pass_on.17), channel_id=1, source_target_pairs={{8,12},{9,13},{10,14},{11,15},{24,28},{25,29},{26,30},{27,31}} | collective-permute-start | bytes 245768 | tf_op jit(solution)/shard_map/ppermute | solution.py:498
  31.3 4.6 %collective-permute-start.16 = (f32[16,8,128]{2,1,0:T(8,128)S(1)}, f32[16,8,128]{2,1,0:T(8,128)S(1)}, u32[]{:S(2)}, u32[]{:S(2)}) collective-permute-start(f32[16,8,128]{2,1,0:T(8,128)S(1)} %add.27.refs_0_), channel_id=1, source_target_pairs={{0,2},{1,3},{2,0},{3,1},{4,6},{5,7},{6,4},{7,5},{8,10},{9,11},{10,... | collective-permute-start | bytes 196616 | tf_op jit(solution)/shard_map/ppermute | solution.py:593
  32.9 6.6 %collective-permute-start.8 = (f32[16,8,128]{2,1,0:T(8,128)S(1)}, f32[16,8,128]{2,1,0:T(8,128)S(1)}, u32[]{:S(2)}, u32[]{:S(2)}) collective-permute-start(f32[16,8,128]{2,1,0:T(8,128)S(1)} %add.26.refs_0_), channel_id=1, source_target_pairs={{0,2},{1,3},{2,0},{3,1},{4,6},{5,7},{6,4},{7,5},{8,10},{9,11},{10,... | collective-permute-start | bytes 196616 | tf_op jit(solution)/shard_map/ppermute | solution.py:593
  38.1 4.9 %collective-permute-start.26 = (f32[4,40,128]{2,1,0:T(8,128)S(1)}, f32[4,40,128]{2,1,0:T(8,128)S(1)}, u32[]{:S(2)}, u32[]{:S(2)}) collective-permute-start(f32[4,40,128]{2,1,0:T(8,128)S(1)} %get-tuple-element.46.carried_ref), channel_id=1, source_target_pairs={{12,8},{13,9},{14,10},{15,11},{28,24},{29,25},{30,26},{31,27}} | collective-permute-start | bytes 245768 | tf_op jit(solution)/shard_map/ppermute | solution.py:498
  38.7 4.9 %collective-permute-start.23 = (f32[4,40,128]{2,1,0:T(8,128)S(1)}, f32[4,40,128]{2,1,0:T(8,128)S(1)}, u32[]{:S(2)}, u32[]{:S(2)}) collective-permute-start(f32[4,40,128]{2,1,0:T(8,128)S(1)} %get-tuple-element.45.carried_ref), channel_id=1, source_target_pairs={{12,8},{13,9},{14,10},{15,11},{28,24},{29,25},{30,26},{31,27}} | collective-permute-start | bytes 245768 | tf_op jit(solution)/shard_map/ppermute | solution.py:498
  42.3 2.8 %collective-permute-start.17 = (f32[4,40,128]{2,1,0:T(8,128)S(1)}, f32[4,40,128]{2,1,0:T(8,128)S(1)}, u32[]{:S(2)}, u32[]{:S(2)}) collective-permute-start(f32[4,40,128]{2,1,0:T(8,128)S(1)} %get-tuple-element.43.carried_ref), channel_id=1, source_target_pairs={{12,8},{13,9},{14,10},{15,11},{28,24},{29,25},{30,26},{31,27}} | collective-permute-start | bytes 245768 | tf_op jit(solution)/shard_map/ppermute | solution.py:498
  43.0 2.8 %collective-permute-start.27 = (f32[4,40,128]{2,1,0:T(8,128)S(1)}, f32[4,40,128]{2,1,0:T(8,128)S(1)}, u32[]{:S(2)}, u32[]{:S(2)}) collective-permute-start(f32[4,40,128]{2,1,0:T(8,128)S(1)} %pass_on.30), channel_id=1, source_target_pairs={{8,4},{9,5},{10,6},{11,7},{24,20},{25,21},{26,22},{27,23}} | collective-permute-start | bytes 245768 | tf_op jit(solution)/shard_map/ppermute | solution.py:498
  43.7 3.5 %collective-permute-start.24 = (f32[4,40,128]{2,1,0:T(8,128)S(1)}, f32[4,40,128]{2,1,0:T(8,128)S(1)}, u32[]{:S(2)}, u32[]{:S(2)}) collective-permute-start(f32[4,40,128]{2,1,0:T(8,128)S(1)} %pass_on.28), channel_id=1, source_target_pairs={{8,4},{9,5},{10,6},{11,7},{24,20},{25,21},{26,22},{27,23}} | collective-permute-start | bytes 245768 | tf_op jit(solution)/shard_map/ppermute | solution.py:498
  44.4 4.2 %collective-permute-start.21 = (f32[4,40,128]{2,1,0:T(8,128)S(1)}, f32[4,40,128]{2,1,0:T(8,128)S(1)}, u32[]{:S(2)}, u32[]{:S(2)}) collective-permute-start(f32[4,40,128]{2,1,0:T(8,128)S(1)} %pass_on.26), channel_id=1, source_target_pairs={{8,4},{9,5},{10,6},{11,7},{24,20},{25,21},{26,22},{27,23}} | collective-permute-start | bytes 245768 | tf_op jit(solution)/shard_map/ppermute | solution.py:498
  45.1 4.9 %collective-permute-start.18 = (f32[4,40,128]{2,1,0:T(8,128)S(1)}, f32[4,40,128]{2,1,0:T(8,128)S(1)}, u32[]{:S(2)}, u32[]{:S(2)}) collective-permute-start(f32[4,40,128]{2,1,0:T(8,128)S(1)} %pass_on.24), channel_id=1, source_target_pairs={{8,4},{9,5},{10,6},{11,7},{24,20},{25,21},{26,22},{27,23}} | collective-permute-start | bytes 245768 | tf_op jit(solution)/shard_map/ppermute | solution.py:498
  45.9 15.5 %collective-permute-start.28 = (f32[4,40,128]{2,1,0:T(8,128)S(1)}, f32[4,40,128]{2,1,0:T(8,128)S(1)}, u32[]{:S(2)}, u32[]{:S(2)}) collective-permute-start(f32[4,40,128]{2,1,0:T(8,128)S(1)} %pass_on.31), channel_id=1, source_target_pairs={{4,0},{5,1},{6,2},{7,3},{20,16},{21,17},{22,18},{23,19}} | collective-permute-start | bytes 245768 | tf_op jit(solution)/shard_map/ppermute | solution.py:498
  47.2 16.2 %collective-permute-start.25 = (f32[4,40,128]{2,1,0:T(8,128)S(1)}, f32[4,40,128]{2,1,0:T(8,128)S(1)}, u32[]{:S(2)}, u32[]{:S(2)}) collective-permute-start(f32[4,40,128]{2,1,0:T(8,128)S(1)} %pass_on.29), channel_id=1, source_target_pairs={{4,0},{5,1},{6,2},{7,3},{20,16},{21,17},{22,18},{23,19}} | collective-permute-start | bytes 245768 | tf_op jit(solution)/shard_map/ppermute | solution.py:498
  48.7 15.6 %collective-permute-start.22 = (f32[4,40,128]{2,1,0:T(8,128)S(1)}, f32[4,40,128]{2,1,0:T(8,128)S(1)}, u32[]{:S(2)}, u32[]{:S(2)}) collective-permute-start(f32[4,40,128]{2,1,0:T(8,128)S(1)} %pass_on.27), channel_id=1, source_target_pairs={{4,0},{5,1},{6,2},{7,3},{20,16},{21,17},{22,18},{23,19}} | collective-permute-start | bytes 245768 | tf_op jit(solution)/shard_map/ppermute | solution.py:498
  50.0 15.4 %collective-permute-start.19 = (f32[4,40,128]{2,1,0:T(8,128)S(1)}, f32[4,40,128]{2,1,0:T(8,128)S(1)}, u32[]{:S(2)}, u32[]{:S(2)}) collective-permute-start(f32[4,40,128]{2,1,0:T(8,128)S(1)} %pass_on.25), channel_id=1, source_target_pairs={{4,0},{5,1},{6,2},{7,3},{20,16},{21,17},{22,18},{23,19}} | collective-permute-start | bytes 245768 | tf_op jit(solution)/shard_map/ppermute | solution.py:498
  67.9 4.0 %collective-permute-start.29 = (f32[32,160]{1,0:T(8,128)S(1)}, f32[32,160]{1,0:T(8,128)S(1)}, u32[]{:S(2)}, u32[]{:S(2)}) collective-permute-start(f32[32,160]{1,0:T(8,128)S(1)} %get-tuple-element.48.refs_5_), channel_id=1, source_target_pairs={{0,16},{16,0},{1,17},{17,1},{2,18},{18,2},{3,19},{19,3},{4,20},{20... | collective-permute-start | bytes 61448 | tf_op jit(solution)/shard_map/ppermute | solution.py:481
  74.3 3.6 %collective-permute-start.31 = (f32[8,128]{1,0:T(8,128)S(1)}, f32[8,128]{1,0:T(8,128)S(1)}, u32[]{:S(2)}, u32[]{:S(2)}) collective-permute-start(f32[8,128]{1,0:T(8,128)S(1)} %add.28), channel_id=1, source_target_pairs={{0,2},{1,3},{2,0},{3,1},{4,6},{5,7},{6,4},{7,5},{8,10},{9,11},{10,... | collective-permute-start | bytes 12296 | tf_op jit(solution)/shard_map/ppermute | solution.py:509
  77.9 3.6 %collective-permute-start.32 = (f32[8,128]{1,0:T(8,128)S(1)}, f32[8,128]{1,0:T(8,128)S(1)}, u32[]{:S(2)}, u32[]{:S(2)}) collective-permute-start(f32[8,128]{1,0:T(8,128)S(1)} %add.29), channel_id=1, source_target_pairs={{0,16},{16,0},{1,17},{17,1},{2,18},{18,2},{3,19},{19,3},{4,20},{20... | collective-permute-start | bytes 12296 | tf_op jit(solution)/shard_map/ppermute | solution.py:509
  81.5 4.4 %collective-permute-start.33 = (f32[8,128]{1,0:T(8,128)S(1)}, f32[8,128]{1,0:T(8,128)S(1)}, u32[]{:S(2)}, u32[]{:S(2)}) collective-permute-start(f32[8,128]{1,0:T(8,128)S(1)} %add.30), channel_id=1, source_target_pairs={{0,4},{4,0},{8,12},{12,8},{1,5},{5,1},{9,13},{13,9},{2,6},{6,2},{1... | collective-permute-start | bytes 12296 | tf_op jit(solution)/shard_map/ppermute | solution.py:509
  81.5 4.5 %collective-permute-start.34 = (f32[8,128]{1,0:T(8,128)S(1)}, f32[8,128]{1,0:T(8,128)S(1)}, u32[]{:S(2)}, u32[]{:S(2)}) collective-permute-start(f32[8,128]{1,0:T(8,128)S(1)} %add.30), channel_id=1, source_target_pairs={{0,8},{4,12},{8,0},{12,4},{1,9},{5,13},{9,1},{13,5},{2,10},{6,14},... | collective-permute-start | bytes 12296 | tf_op jit(solution)/shard_map/ppermute | solution.py:509
  81.5 6.0 %collective-permute-start.35 = (f32[8,128]{1,0:T(8,128)S(1)}, f32[8,128]{1,0:T(8,128)S(1)}, u32[]{:S(2)}, u32[]{:S(2)}) collective-permute-start(f32[8,128]{1,0:T(8,128)S(1)} %add.30), channel_id=1, source_target_pairs={{0,12},{4,8},{8,4},{12,0},{1,13},{5,9},{9,5},{13,1},{2,14},{6,10},... | collective-permute-start | bytes 12296 | tf_op jit(solution)/shard_map/ppermute | solution.py:509
  (11 other events, 81.0 us)

commit v6 on v5

--- a/solution.py
+++ b/solution.py
@@ -7,9 +7,9 @@
 from jax.sharding import PartitionSpec as P
 
 f32 = jnp.float32
+bf16 = jnp.bfloat16
 VM = pl.BlockSpec(memory_space=pltpu.VMEM)
 SM = pl.BlockSpec(memory_space=pltpu.SMEM)
-HI = lax.Precision.HIGHEST
 
 
 def choose(length, i):
@@ -26,8 +26,23 @@
     return r
 
 
-def mm(a, b, dims):
-    return lax.dot_general(a, b, (dims, ((), ())), precision=HI, preferred_element_type=f32)
+def halves(v):
+    high = v.astype(bf16)
+    return high, (v - high.astype(f32)).astype(bf16)
+
+
+def left3(v, axis):
+    high, low = halves(v)
+    return jnp.concatenate([high, low, high], axis=axis)
+
+
+def right3(v, axis):
+    high, low = halves(v)
+    return jnp.concatenate([high, high, low], axis=axis)
+
+
+def product3(a, b):
+    return jnp.dot(a, b, preferred_element_type=f32)
 
 
 def iota(shape, dim):
@@ -72,20 +87,23 @@
 def lon_tables(lonc, rows, cells, backward, table_ref):
     c, leak, scale = lon_consts(lonc)
     gain = leak**4 * scale
+    finals = lon_finals(c, leak, scale, cells, backward)
+    spare = jnp.zeros((cells - 4 * rows, cells), f32)
+    finals = jnp.concatenate(finals + [spare], axis=0).T
+    column = lax.broadcasted_iota(jnp.int32, (cells, cells), 1)
     for y in range(rows):
-        table_ref[y] = lon_kernel_matrix(c[y : y + 1], gain[y : y + 1], cells, backward)
-
-
-def lon_local_rows(load_row, lonc, table_ref, rows, cells, backward, inside_ref, carried_ref):
-    c, leak, scale = lon_consts(lonc)
-    finals = lon_finals(c, leak, scale, cells, backward)
+        inside = lon_kernel_matrix(c[y : y + 1], gain[y : y + 1], cells, backward)
+        leaving = jnp.where(lax.rem(column, rows) == y, finals, 0.0)
+        table_ref[y] = right3(jnp.concatenate([inside, leaving], axis=1), 0)
+
+
+def lon_local_rows(load_row, table_ref, rows, cells, inside_ref, carried_ref):
     carried = None
     for y in range(rows):
-        f = load_row(y)
-        inside_ref[y] = mm(f, table_ref[y], ((1,), (0,)))
-        part = mm(masked_rows(finals, y), f, ((1,), (1,)))
-        carried = part if carried is None else carried + part
-    carried_ref[...] = carried
+        both = product3(left3(load_row(y), 1), table_ref[y])
+        inside_ref[y] = both[:, :cells]
+        carried = both[:, cells:] if carried is None else carried + both[:, cells:]
+    carried_ref[...] = carried.T[: 4 * rows]
 
 
 def lon_incoming_states(lonc, blocks, rows, cells):
@@ -115,8 +133,13 @@
     return jnp.concatenate(solved, axis=0)
 
 
-def lon_correction(states_t, entering, y):
-    return mm(states_t, masked_rows(entering, y), ((1,), (0,)))
+def lon_correction(states, entering, rows, cells):
+    high = states.astype(bf16).astype(f32)
+    low = states - high
+    spare = jnp.zeros((cells - 12 * rows, states.shape[1]), f32)
+    left = jnp.concatenate([high, low, high, spare], axis=0).T.astype(bf16)
+    spare = jnp.zeros((cells - 12 * rows, cells), bf16)
+    return lambda y: product3(left, jnp.concatenate([right3(masked_rows(entering, y), 0), spare], axis=0))
 
 
 def lat_consts(dec):
@@ -203,28 +226,21 @@
 
 
 def k_tables(rows, cells, dec_ref, lonc_ref, latc_ref, table_ref):
-    row = jnp.broadcast_to(dec_ref[:1, :rows], (rows, rows))
+    row = jnp.broadcast_to(dec_ref[:, cells:], (rows, rows))
     own = iota((rows, rows), 0) == iota((rows, rows), 1)
     column = jnp.sum(jnp.where(own, row, 0.0), axis=1, keepdims=True)
     lonc = jnp.broadcast_to(column, (rows, cells))
     lonc_ref[...] = lonc
-    first, second = both_halves(jnp.broadcast_to(dec_ref[1:], (8, cells)))
+    first, second = both_halves(jnp.broadcast_to(dec_ref[:, :cells], (8, cells)))
     latc_ref[0] = first
     latc_ref[1] = second
     lon_tables(lonc, rows, cells, False, table_ref)
 
 
-def k_lon_fwd(rows, k, cells, d_ref, lon_ref, table_ref, inside_ref, carried_ref):
+def k_lon_fwd(rows, k, cells, d_ref, table_ref, inside_ref, carried_ref):
     d_ref = d_ref.reshape(k * rows, cells)
     lon_local_rows(
-        lambda y: d_ref[pl.ds(y, k, stride=rows), :],
-        lon_ref[...],
-        table_ref,
-        rows,
-        cells,
-        False,
-        inside_ref,
-        carried_ref,
+        lambda y: d_ref[pl.ds(y, k, stride=rows), :], table_ref, rows, cells, inside_ref, carried_ref
     )
 
 
@@ -246,12 +262,12 @@
     blocks = [r[...] for r in rest[:n]]
     f_refs, out_refs = rest[n : n + 2], rest[n + 2 :]
     lonc = lon_ref[...]
-    states = lon_incoming_states(lonc, blocks, rows, cells).T
+    states = lon_incoming_states(lonc, blocks, rows, cells)
     c, leak, _ = lon_consts(lonc)
-    entering = lon_entering(c, leak, cells, False)
+    added = lon_correction(states, lon_entering(c, leak, cells, False), rows, cells)
     half = k // 2
     for y in range(rows):
-        row = inside_ref[y] + lon_correction(states, entering, y)
+        row = inside_ref[y] + added(y)
         f_refs[0][y], f_refs[1][y] = swap_halves(row[:half], row[half:])
     zero = jnp.zeros((8, cells), f32)
     for part, f_ref in enumerate(f_refs):
@@ -388,7 +404,7 @@
 
 
 def k_lon_bwd(rows, k, cells, chunks, count, *refs):
-    g_refs, lat_ref, lon_ref, table_ref, rest = refs[:2], refs[2], refs[3], refs[4], refs[5:]
+    g_refs, lat_ref, table_ref, rest = refs[:2], refs[2], refs[3], refs[4:]
     inside_ref, carried_ref, p_ref = rest[2 * count :]
     half = k // 2
     for part in range(2):
@@ -411,7 +427,7 @@
     def load_row(y):
         return jnp.concatenate(swap_halves(p_ref[0, y], p_ref[1, y]), axis=0)
 
-    lon_local_rows(load_row, lon_ref[...], table_ref, rows, cells, True, inside_ref, carried_ref)
+    lon_local_rows(load_row, table_ref, rows, cells, inside_ref, carried_ref)
 
 
 def k_sums(rows, k, cells, n, *refs):
@@ -421,12 +437,12 @@
     blocks = [r[...] for r in rest[:n]]
     h_ref, sums_ref = rest[n:]
     lonc = lon_ref[...]
-    states = lon_incoming_states(lonc, blocks, rows, cells).T
+    states = lon_incoming_states(lonc, blocks, rows, cells)
     c, leak, _ = lon_consts(lonc)
-    entering = lon_entering(c, leak, cells, True)
+    added = lon_correction(states, lon_entering(c, leak, cells, True), rows, cells)
     for y in range(rows):
         at = pl.ds(y, k, stride=rows)
-        h_ref[at, :] = inside_ref[y] + lon_correction(states, entering, y)
+        h_ref[at, :] = inside_ref[y] + added(y)
     block = 64
     zero = jnp.zeros((8, cells), f32)
 
@@ -444,25 +460,34 @@
     sums_ref[...] = jnp.concatenate(out + [jnp.zeros((4, cells), f32)], axis=0)
 
 
-def k_update(sums_ref, control_ref, r_ref, d_ref, h_ref, nc_ref, nr_ref, nd_ref):
+def k_update(pieces, sums_ref, control_ref, r_ref, d_ref, h_ref, *rest):
+    outs, news, sems = rest[:3], rest[3:6], rest[6]
     sums = jnp.sum(sums_ref[...], axis=1, keepdims=True)
     rr, dh, rh, hh = (sums[i : i + 1].reshape(1, 1, 1) for i in range(4))
     step = rr / dh
     norm_new = rr - 2.0 * step * rh + step * step * hh
     beta = norm_new / rr
-    d = d_ref[...]
-    nr = r_ref[...] - step * h_ref[...]
-    nc_ref[...] = control_ref[...] + step * d
-    nr_ref[...] = nr
-    nd_ref[...] = nr + beta * d
-
-
-def call(body, outs, ins, specs=None, scratch=(), name=None, cost=None):
+    size = d_ref.shape[0] // pieces
+    copies = []
+    for i in range(pieces):
+        at = pl.ds(i * size, size)
+        d = d_ref[at]
+        nr = r_ref[at] - step * h_ref[at]
+        for j, v in enumerate((control_ref[at] + step * d, nr, nr + beta * d)):
+            news[j][at] = v
+            copy = pltpu.make_async_copy(news[j].at[at], outs[j].at[at], sems.at[j, i])
+            copy.start()
+            copies.append(copy)
+    for copy in copies:
+        copy.wait()
+
+
+def call(body, outs, ins, specs=None, out_specs=None, scratch=(), name=None, cost=None):
     return pl.pallas_call(
         body,
         out_shape=outs,
         in_specs=specs or [VM] * len(ins),
-        out_specs=jax.tree.map(lambda _: VM, outs),
+        out_specs=out_specs or jax.tree.map(lambda _: VM, outs),
         scratch_shapes=scratch,
         name=name,
         cost_estimate=None if cost is None else pl.CostEstimate(flops=cost, bytes_accessed=1000, transcendentals=0),
@@ -542,10 +567,10 @@
     chunks = 2
     states = (sds(4, half // chunks, cells),) * chunks
 
-    decays = jnp.stack([jnp.pad(lon_decay, (0, cells - rows)), lat_decay])
+    decays = jnp.concatenate([lat_decay, lon_decay]).reshape(1, cells + rows)
     lonc, latc, tables = call(
         functools.partial(k_tables, rows, cells),
-        (sds(rows, cells), sds(2, 8, cells), sds(rows, cells, cells)),
+        (sds(rows, cells), sds(2, 8, cells), jax.ShapeDtypeStruct((rows, 3 * cells, 2 * cells), bf16)),
         [decays],
         name="tables",
         cost=10**9,
@@ -553,12 +578,12 @@
     inside, carried = call(
         functools.partial(k_lon_fwd, rows, k, cells),
         (sds(rows, k, cells), sds(4 * rows, k)),
-        [direction, lonc, tables],
+        [direction, tables],
         name="lon_fwd",
     )
     *packed, back_tables = call(
         k_prepare,
-        (sds(pairs, levels, rows, cells),) * 2 + (sds(rows, cells, cells),),
+        (sds(pairs, levels, rows, cells),) * 2 + (jax.ShapeDtypeStruct((rows, 3 * cells, 2 * cells), bf16),),
         [members, lonc],
         name="prepare",
         cost=10**9,
@@ -603,7 +628,7 @@
     inside, carried = call(
         functools.partial(k_lon_bwd, rows, k, cells, chunks, count),
         (sds(rows, k, cells), sds(4 * rows, k)),
-        [*grads, latc, lonc, back_tables, *got[0], *got[1]],
+        [*grads, latc, back_tables, *got[0], *got[1]],
         scratch=[pltpu.VMEM((2, rows, half, cells), f32)],
         name="lon_bwd",
     )
@@ -615,10 +640,13 @@
         name="sums",
     )
     sums = reduce_everywhere(sums)
+    pieces = 4 if k % 4 == 0 else 1
     outs = call(
-        k_update,
+        functools.partial(k_update, pieces),
         (sds(k, rows, cells),) * 3,
         [sums, control, residual, direction, h.reshape(k, rows, cells)],
+        out_specs=(pl.BlockSpec(memory_space=pl.ANY),) * 3,
+        scratch=[pltpu.VMEM((k, rows, cells), f32)] * 3 + [pltpu.SemaphoreType.DMA((3, pieces))],
         name="update",
     )
     return tuple(outs)

time: 89.6 us -> 85.8 us (0.958)
  Pallas kernels: 18.7 us -> 15.9 us
    pallas_call x27, Pallas kernels: 18.7 us -> 15.9 us  [call(): pl.pallas_call(body, out_shape=outs, in_specs=specs or [VM] * len(ins), o...]
  transfers between devices with their start and end apart: 36 -> 36, of which waited for: 14 -> 14; matrix products, arithmetic and copies ran while one was open for 0% -> 0% of each run, Pallas kernels for 11% -> 12%
where the time goes in v6:
time: 85.8 us; the launch traced here: 85.3 us
  starting transfers between devices  38.9 us (45%)
  waiting for transfers between devices  27.9 us (33%)
  Pallas kernels  15.9 us (19%)
  between operations  1.22 us (1%)
    ppermute x24, starting transfers between devices, lat_carry(): got[c][i].append(lax.ppermute(v, 'lat', [(at(h), at(h + 1))]))  23.7 us
    pallas_call x27, Pallas kernels, call(): pl.pallas_call(body, out_shape=outs, in_specs=specs or [VM] * len(ins), o...  15.9 us
    ppermute x24, waiting for transfers between devices, lat_carry(): got[c][i].append(lax.ppermute(v, 'lat', [(at(h), at(h + 1))]))  14.5 us
    ppermute x6, starting transfers between devices, all_sum(): lax.ppermute(v, axes, [(i, i ^ m) for i in range(total)])  7.56 us
    ppermute x6, waiting for transfers between devices, all_sum(): lax.ppermute(v, axes, [(i, i ^ m) for i in range(total)])  6.88 us
    ppermute x2, starting transfers between devices, lon_exchange(): lax.ppermute(carried, 'lon', [(j, (j + sign * r) % n) for j in range(n)])  4.53 us
    ppermute x2, waiting for transfers between devices, lon_exchange(): lax.ppermute(carried, 'lon', [(j, (j + sign * r) % n) for j in range(n)])  4.32 us
    ppermute x2, starting transfers between devices, body(): other = lax.ppermute(v, 'mem', [(i, i ^ step) for i in range(n_mem)])  2.47 us
  transfers between devices with their start and end apart: 36, of which 14 were waited for; matrix products, arithmetic and copies ran while one was open for 0% of the time, Pallas kernels for 12%

profile of v6, /device:TPU:0, one launch (start us, length us, event | category | flops | bytes accessed | tf_op | source)
XLA Modules:
  0.0 85.3 jit_solution(15579008685450951482)
XLA Ops:
  3.0 3.0 %collective-permute-start = (f32[32,160]{1,0:T(8,128)S(1)}, f32[32,160]{1,0:T(8,128)S(1)}, u32[]{:S(2)}, u32[]{:S(2)}) collective-permute-start(f32[32,160]{1,0:T(8,128)S(1)} %get-tuple-element.31.refs_4_), channel_id=1, source_target_pairs={{0,16},{16,0},{1,17},{17,1},{2,18},{18,2},{3,19},{19,3},{4,20},{20... | collective-permute-start | bytes 61448 | tf_op jit(solution)/shard_map/ppermute | solution.py:506
  6.0 1.9 %collective-permute-done.refs_3_ = f32[32,160]{1,0:T(8,128)S(1)} collective-permute-done((f32[32,160]{1,0:T(8,128)S(1)}, f32[32,160]{1,0:T(8,128)S(1)}, u32[]{:S(2)}, u32[]{:S(2)}) %collective-permute-start) | collective-permute-done | bytes 20512 | tf_op jit(solution)/shard_map/ppermute | solution.py:506
  7.9 1.1 %lat_first.1 = (f32[8,80,128]{2,1,0:T(8,128)S(1)}, f32[8,80,128]{2,1,0:T(8,128)S(1)}, f32[4,40,128]{2,1,0:T(8,128)S(1)}, f32[4,40,128]{2,1,0:T(8,128)S(1)}, f32[...) custom-call(f32[8,160,128]{2,1,0:T(8,128)S(1)} %get-tuple-element.28.refs_0_, ...), custom_call_target="tpu_custom_call" | custom-call | tf_op jit(solution)/shard_map/lat_first/pallas_call | solution.py:486
  8.9 4.0 %collective-permute-start.12 = (f32[4,40,128]{2,1,0:T(8,128)S(1)}, f32[4,40,128]{2,1,0:T(8,128)S(1)}, u32[]{:S(2)}, u32[]{:S(2)}) collective-permute-start(f32[4,40,128]{2,1,0:T(8,128)S(1)} %get-tuple-element.40.carried_ref), channel_id=1, source_target_pairs={{0,4},{1,5},{2,6},{3,7},{16,20},{17,21},{18,22},{19,23}} | collective-permute-start | bytes 245768 | tf_op jit(solution)/shard_map/ppermute | solution.py:523
  13.0 1.3 %collective-permute-start.9 = (f32[4,40,128]{2,1,0:T(8,128)S(1)}, f32[4,40,128]{2,1,0:T(8,128)S(1)}, u32[]{:S(2)}, u32[]{:S(2)}) collective-permute-start(f32[4,40,128]{2,1,0:T(8,128)S(1)} %get-tuple-element.39.carried_ref), channel_id=1, source_target_pairs={{0,4},{1,5},{2,6},{3,7},{16,20},{17,21},{18,22},{19,23}} | collective-permute-start | bytes 245768 | tf_op jit(solution)/shard_map/ppermute | solution.py:523
  14.3 1.3 %collective-permute-start.4 = (f32[4,40,128]{2,1,0:T(8,128)S(1)}, f32[4,40,128]{2,1,0:T(8,128)S(1)}, u32[]{:S(2)}, u32[]{:S(2)}) collective-permute-start(f32[4,40,128]{2,1,0:T(8,128)S(1)} %get-tuple-element.35.carried_ref), channel_id=1, source_target_pairs={{0,4},{1,5},{2,6},{3,7},{16,20},{17,21},{18,22},{19,23}} | collective-permute-start | bytes 245768 | tf_op jit(solution)/shard_map/ppermute | solution.py:523
  15.6 1.3 %collective-permute-start.1 = (f32[4,40,128]{2,1,0:T(8,128)S(1)}, f32[4,40,128]{2,1,0:T(8,128)S(1)}, u32[]{:S(2)}, u32[]{:S(2)}) collective-permute-start(f32[4,40,128]{2,1,0:T(8,128)S(1)} %get-tuple-element.34.carried_ref), channel_id=1, source_target_pairs={{0,4},{1,5},{2,6},{3,7},{16,20},{17,21},{18,22},{19,23}} | collective-permute-start | bytes 245768 | tf_op jit(solution)/shard_map/ppermute | solution.py:523
  22.9 1.4 %prepare.1 = (f32[10,32,8,128]{3,2,1,0:T(8,128)S(1)}, f32[10,32,8,128]{3,2,1,0:T(8,128)S(1)}, bf16[8,384,256]{2,1,0:T(8,128)(2,1)S(1)}) custom-call(bf16[20,32,8,128]{3,2,1,0:T(8,128)(2,1)S(1)} %copy-done.6, f32[8,128]{1,0:T(8,128)S(1)} %get-tuple-element.29.refs_1_.lon_ref), custom_call_target="tpu_custom_call" | custom-call | flops 1000000000 | bytes 1000 | tf_op jit(solution)/shard_map/prepare/pallas_call | solution.py:486
  24.3 2.1 %increment.3 = f32[16,8,128]{2,1,0:T(8,128)S(1)} custom-call(f32[8,80,128]{2,1,0:T(8,128)S(1)} %get-tuple-element.37.refs_0_, f32[2,8,128]{2,1,0:T(8,128)S(1)} %get-tuple-element.30.refs_2_.lat_ref.refs_1_.refs_6_, f32[10,32,8,128]{3,2,1,0:T(8,128)S(1)} %get-tuple-element.38.refs_2_.refs_3_, f32[8,32]{1,0:T(8,128)S(1)} %copy-done.4, s32[20]{0:T(128)S(1)} %copy-done.5, ...), custom_call_target="tpu_custom_call" | custom-call | tf_op jit(solution)/shard_map/increment/pallas_call | solution.py:486
  26.5 2.1 %increment.2 = f32[16,8,128]{2,1,0:T(8,128)S(1)} custom-call(f32[8,80,128]{2,1,0:T(8,128)S(1)} %get-tuple-element.32.refs_0_, f32[2,8,128]{2,1,0:T(8,128)S(1)} %get-tuple-element.30.refs_2_.lat_ref.refs_1_.refs_6_, f32[10,32,8,128]{3,2,1,0:T(8,128)S(1)} %get-tuple-element.33.refs_2_.refs_3_, f32[8,32]{1,0:T(8,128)S(1)} %copy-done.4, s32[20]{0:T(128)S(1)} %copy-done.5, ...), custom_call_target="tpu_custom_call" | custom-call | tf_op jit(solution)/shard_map/increment/pallas_call | solution.py:486
  29.2 1.6 %collective-permute-start.16 = (f32[16,8,128]{2,1,0:T(8,128)S(1)}, f32[16,8,128]{2,1,0:T(8,128)S(1)}, u32[]{:S(2)}, u32[]{:S(2)}) collective-permute-start(f32[16,8,128]{2,1,0:T(8,128)S(1)} %add.25.refs_0_), channel_id=1, source_target_pairs={{0,2},{1,3},{2,0},{3,1},{4,6},{5,7},{6,4},{7,5},{8,10},{9,11},{10,... | collective-permute-start | bytes 196616 | tf_op jit(solution)/shard_map/ppermute | solution.py:618
  31.7 2.2 %collective-permute-done.16.refs_1_ = f32[16,8,128]{2,1,0:T(8,128)S(1)} collective-permute-done((f32[16,8,128]{2,1,0:T(8,128)S(1)}, f32[16,8,128]{2,1,0:T(8,128)S(1)}, u32[]{:S(2)}, u32[]{:S(2)}) %collective-permute-start.16) | collective-permute-done | bytes 65568 | tf_op jit(solution)/shard_map/ppermute | solution.py:618
  33.9 2.2 %gradient.3 = (f32[640,128]{1,0:T(8,128)S(1)}, f32[4,40,128]{2,1,0:T(8,128)S(1)}, f32[4,40,128]{2,1,0:T(8,128)S(1)}) custom-call(f32[16,8,128]{2,1,0:T(8,128)S(1)} %add.25.refs_0_, f32[16,8,128]{2,1,0:T(8,128)S(1)} %collective-permute-done.16.refs_1_, f32[32,8,128]{2,1,0:T(8,128)S(1)} %copy-done.3, f32[10,32,8,128]{3,2,1,0:T(8,128)S(1)} %get-tuple-element.38.refs_2_.refs_3_, ...), custom_call_target="tpu_custom_call" | custom-call | tf_op jit(solution)/shard_map/gradient/pallas_call | solution.py:486
  37.4 2.2 %gradient.2 = (f32[640,128]{1,0:T(8,128)S(1)}, f32[4,40,128]{2,1,0:T(8,128)S(1)}, f32[4,40,128]{2,1,0:T(8,128)S(1)}) custom-call(f32[16,8,128]{2,1,0:T(8,128)S(1)} %add.24.refs_0_, f32[16,8,128]{2,1,0:T(8,128)S(1)} %collective-permute-done.8.refs_1_, f32[32,8,128]{2,1,0:T(8,128)S(1)} %copy-done.3, f32[10,32,8,128]{3,2,1,0:T(8,128)S(1)} %get-tuple-element.33.refs_2_.refs_3_, ...), custom_call_target="tpu_custom_call" | custom-call | tf_op jit(solution)/shard_map/gradient/pallas_call | solution.py:486
  43.8 1.3 %collective-permute-start.28 = (f32[4,40,128]{2,1,0:T(8,128)S(1)}, f32[4,40,128]{2,1,0:T(8,128)S(1)}, u32[]{:S(2)}, u32[]{:S(2)}) collective-permute-start(f32[4,40,128]{2,1,0:T(8,128)S(1)} %pass_on.31), channel_id=1, source_target_pairs={{4,0},{5,1},{6,2},{7,3},{20,16},{21,17},{22,18},{23,19}} | collective-permute-start | bytes 245768 | tf_op jit(solution)/shard_map/ppermute | solution.py:523
  45.1 1.3 %collective-permute-start.25 = (f32[4,40,128]{2,1,0:T(8,128)S(1)}, f32[4,40,128]{2,1,0:T(8,128)S(1)}, u32[]{:S(2)}, u32[]{:S(2)}) collective-permute-start(f32[4,40,128]{2,1,0:T(8,128)S(1)} %pass_on.29), channel_id=1, source_target_pairs={{4,0},{5,1},{6,2},{7,3},{20,16},{21,17},{22,18},{23,19}} | collective-permute-start | bytes 245768 | tf_op jit(solution)/shard_map/ppermute | solution.py:523
  46.5 1.3 %collective-permute-start.22 = (f32[4,40,128]{2,1,0:T(8,128)S(1)}, f32[4,40,128]{2,1,0:T(8,128)S(1)}, u32[]{:S(2)}, u32[]{:S(2)}) collective-permute-start(f32[4,40,128]{2,1,0:T(8,128)S(1)} %pass_on.27), channel_id=1, source_target_pairs={{4,0},{5,1},{6,2},{7,3},{20,16},{21,17},{22,18},{23,19}} | collective-permute-start | bytes 245768 | tf_op jit(solution)/shard_map/ppermute | solution.py:523
  47.8 1.3 %collective-permute-start.19 = (f32[4,40,128]{2,1,0:T(8,128)S(1)}, f32[4,40,128]{2,1,0:T(8,128)S(1)}, u32[]{:S(2)}, u32[]{:S(2)}) collective-permute-start(f32[4,40,128]{2,1,0:T(8,128)S(1)} %pass_on.25), channel_id=1, source_target_pairs={{4,0},{5,1},{6,2},{7,3},{20,16},{21,17},{22,18},{23,19}} | collective-permute-start | bytes 245768 | tf_op jit(solution)/shard_map/ppermute | solution.py:523
  49.1 10.1 %collective-permute-done.28.refs_15_ = f32[4,40,128]{2,1,0:T(8,128)S(1)} collective-permute-done((f32[4,40,128]{2,1,0:T(8,128)S(1)}, f32[4,40,128]{2,1,0:T(8,128)S(1)}, u32[]{:S(2)}, u32[]{:S(2)}) %collective-permute-start.28) | collective-permute-done | bytes 81952 | tf_op jit(solution)/shard_map/ppermute | solution.py:523
  59.3 2.1 %collective-permute-done.25.refs_12_ = f32[4,40,128]{2,1,0:T(8,128)S(1)} collective-permute-done((f32[4,40,128]{2,1,0:T(8,128)S(1)}, f32[4,40,128]{2,1,0:T(8,128)S(1)}, u32[]{:S(2)}, u32[]{:S(2)}) %collective-permute-start.25) | collective-permute-done | bytes 81952 | tf_op jit(solution)/shard_map/ppermute | solution.py:523
  62.3 1.1 %collective-permute-done.19.refs_6_ = f32[4,40,128]{2,1,0:T(8,128)S(1)} collective-permute-done((f32[4,40,128]{2,1,0:T(8,128)S(1)}, f32[4,40,128]{2,1,0:T(8,128)S(1)}, u32[]{:S(2)}, u32[]{:S(2)}) %collective-permute-start.19) | collective-permute-done | bytes 81952 | tf_op jit(solution)/shard_map/ppermute | solution.py:523
  63.3 1.3 %lon_bwd.1 = (f32[8,160,128]{2,1,0:T(8,128)S(1)}, f32[32,160]{1,0:T(8,128)S(1)}) custom-call(f32[640,128]{1,0:T(8,128)S(1)} %get-tuple-element.36.refs_0_, f32[640,128]{1,0:T(8,128)S(1)} %get-tuple-element.41.refs_1_, f32[2,8,128]{2,1,0:T(8,128)S(1)} %get-tuple-element.30.refs_2_.lat_ref.refs_1_.refs_6_, bf16[8,384,256]{2,1,0:T(8,128)(2,1)S(1)} %get-tuple-element.42.refs_3_, ...), custom_call_target="tpu_custom_call" | custom-call | tf_op jit(solution)/shard_map/lon_bwd/pallas_call | solution.py:486
  64.6 1.5 %collective-permute-start.29 = (f32[32,160]{1,0:T(8,128)S(1)}, f32[32,160]{1,0:T(8,128)S(1)}, u32[]{:S(2)}, u32[]{:S(2)}) collective-permute-start(f32[32,160]{1,0:T(8,128)S(1)} %get-tuple-element.48.refs_5_), channel_id=1, source_target_pairs={{0,16},{16,0},{1,17},{17,1},{2,18},{18,2},{3,19},{19,3},{4,20},{20... | collective-permute-start | bytes 61448 | tf_op jit(solution)/shard_map/ppermute | solution.py:506
  66.2 2.4 %collective-permute-done.29.refs_4_ = f32[32,160]{1,0:T(8,128)S(1)} collective-permute-done((f32[32,160]{1,0:T(8,128)S(1)}, f32[32,160]{1,0:T(8,128)S(1)}, u32[]{:S(2)}, u32[]{:S(2)}) %collective-permute-start.29) | collective-permute-done | bytes 20512 | tf_op jit(solution)/shard_map/ppermute | solution.py:506
  69.4 1.2 %collective-permute-done.30 = f32[8,128]{1,0:T(8,128)S(1)} collective-permute-done((f32[8,128]{1,0:T(8,128)S(1)}, f32[8,128]{1,0:T(8,128)S(1)}, u32[]{:S(2)}, u32[]{:S(2)}) %collective-permute-start.30) | collective-permute-done | bytes 4128 | tf_op jit(solution)/shard_map/ppermute | solution.py:534
  70.6 1.6 %collective-permute-start.31 = (f32[8,128]{1,0:T(8,128)S(1)}, f32[8,128]{1,0:T(8,128)S(1)}, u32[]{:S(2)}, u32[]{:S(2)}) collective-permute-start(f32[8,128]{1,0:T(8,128)S(1)} %add.26), channel_id=1, source_target_pairs={{0,2},{1,3},{2,0},{3,1},{4,6},{5,7},{6,4},{7,5},{8,10},{9,11},{10,... | collective-permute-start | bytes 12296 | tf_op jit(solution)/shard_map/ppermute | solution.py:534
  72.2 2.0 %collective-permute-done.31 = f32[8,128]{1,0:T(8,128)S(1)} collective-permute-done((f32[8,128]{1,0:T(8,128)S(1)}, f32[8,128]{1,0:T(8,128)S(1)}, u32[]{:S(2)}, u32[]{:S(2)}) %collective-permute-start.31) | collective-permute-done | bytes 4128 | tf_op jit(solution)/shard_map/ppermute | solution.py:534
  74.2 1.5 %collective-permute-start.32 = (f32[8,128]{1,0:T(8,128)S(1)}, f32[8,128]{1,0:T(8,128)S(1)}, u32[]{:S(2)}, u32[]{:S(2)}) collective-permute-start(f32[8,128]{1,0:T(8,128)S(1)} %add.27), channel_id=1, source_target_pairs={{0,16},{16,0},{1,17},{17,1},{2,18},{18,2},{3,19},{19,3},{4,20},{20... | collective-permute-start | bytes 12296 | tf_op jit(solution)/shard_map/ppermute | solution.py:534
  75.7 2.1 %collective-permute-done.32 = f32[8,128]{1,0:T(8,128)S(1)} collective-permute-done((f32[8,128]{1,0:T(8,128)S(1)}, f32[8,128]{1,0:T(8,128)S(1)}, u32[]{:S(2)}, u32[]{:S(2)}) %collective-permute-start.32) | collective-permute-done | bytes 4128 | tf_op jit(solution)/shard_map/ppermute | solution.py:534
  77.8 4.4 %collective-permute-start.35 = (f32[8,128]{1,0:T(8,128)S(1)}, f32[8,128]{1,0:T(8,128)S(1)}, u32[]{:S(2)}, u32[]{:S(2)}) collective-permute-start(f32[8,128]{1,0:T(8,128)S(1)} %add.28), channel_id=1, source_target_pairs={{0,12},{4,8},{8,4},{12,0},{1,13},{5,9},{9,5},{13,1},{2,14},{6,10},... | collective-permute-start | bytes 12296 | tf_op jit(solution)/shard_map/ppermute | solution.py:534
  82.3 1.5 %collective-permute-done.35 = f32[8,128]{1,0:T(8,128)S(1)} collective-permute-done((f32[8,128]{1,0:T(8,128)S(1)}, f32[8,128]{1,0:T(8,128)S(1)}, u32[]{:S(2)}, u32[]{:S(2)}) %collective-permute-start.35) | collective-permute-done | bytes 4128 | tf_op jit(solution)/shard_map/ppermute | solution.py:534
  83.8 1.5 %update.1 = (f32[160,8,128]{2,1,0:T(8,128)}, f32[160,8,128]{2,1,0:T(8,128)}, f32[160,8,128]{2,1,0:T(8,128)}) custom-call(f32[8,128]{1,0:T(8,128)S(1)} %add_add_fusion.sums_ref, f32[160,8,128]{2,1,0:T(8,128)S(1)} %copy-done.2, f32[160,8,128]{2,1,0:T(8,128)S(1)} %copy-done.1, f32[160,8,128]{2,1,0:T(8,128)S(1)} %copy-done, f32[160,8,128]{2,1,0:T(8,128)S(1)} %bitcast.2), custom_call_target="tpu_custom_call" | custom-call | tf_op jit(solution)/shard_map/update/pallas_call | solution.py:486
  (88 shorter events, 17.1 us)
Async XLA Ops:
  3.0 4.9 %collective-permute-start = (f32[32,160]{1,0:T(8,128)S(1)}, f32[32,160]{1,0:T(8,128)S(1)}, u32[]{:S(2)}, u32[]{:S(2)}) collective-permute-start(f32[32,160]{1,0:T(8,128)S(1)} %get-tuple-element.31.refs_4_), channel_id=1, source_target_pairs={{0,16},{16,0},{1,17},{17,1},{2,18},{18,2},{3,19},{19,3},{4,20},{20... | collective-permute-start | bytes 61448 | tf_op jit(solution)/shard_map/ppermute | solution.py:506
  8.9 7.9 %collective-permute-start.12 = (f32[4,40,128]{2,1,0:T(8,128)S(1)}, f32[4,40,128]{2,1,0:T(8,128)S(1)}, u32[]{:S(2)}, u32[]{:S(2)}) collective-permute-start(f32[4,40,128]{2,1,0:T(8,128)S(1)} %get-tuple-element.40.carried_ref), channel_id=1, source_target_pairs={{0,4},{1,5},{2,6},{3,7},{16,20},{17,21},{18,22},{19,23}} | collective-permute-start | bytes 245768 | tf_op jit(solution)/shard_map/ppermute | solution.py:523
  13.0 4.6 %collective-permute-start.9 = (f32[4,40,128]{2,1,0:T(8,128)S(1)}, f32[4,40,128]{2,1,0:T(8,128)S(1)}, u32[]{:S(2)}, u32[]{:S(2)}) collective-permute-start(f32[4,40,128]{2,1,0:T(8,128)S(1)} %get-tuple-element.39.carried_ref), channel_id=1, source_target_pairs={{0,4},{1,5},{2,6},{3,7},{16,20},{17,21},{18,22},{19,23}} | collective-permute-start | bytes 245768 | tf_op jit(solution)/shard_map/ppermute | solution.py:523
  14.3 4.1 %collective-permute-start.4 = (f32[4,40,128]{2,1,0:T(8,128)S(1)}, f32[4,40,128]{2,1,0:T(8,128)S(1)}, u32[]{:S(2)}, u32[]{:S(2)}) collective-permute-start(f32[4,40,128]{2,1,0:T(8,128)S(1)} %get-tuple-element.35.carried_ref), channel_id=1, source_target_pairs={{0,4},{1,5},{2,6},{3,7},{16,20},{17,21},{18,22},{19,23}} | collective-permute-start | bytes 245768 | tf_op jit(solution)/shard_map/ppermute | solution.py:523
  15.6 3.7 %collective-permute-start.1 = (f32[4,40,128]{2,1,0:T(8,128)S(1)}, f32[4,40,128]{2,1,0:T(8,128)S(1)}, u32[]{:S(2)}, u32[]{:S(2)}) collective-permute-start(f32[4,40,128]{2,1,0:T(8,128)S(1)} %get-tuple-element.34.carried_ref), channel_id=1, source_target_pairs={{0,4},{1,5},{2,6},{3,7},{16,20},{17,21},{18,22},{19,23}} | collective-permute-start | bytes 245768 | tf_op jit(solution)/shard_map/ppermute | solution.py:523
  16.9 3.1 %collective-permute-start.13 = (f32[4,40,128]{2,1,0:T(8,128)S(1)}, f32[4,40,128]{2,1,0:T(8,128)S(1)}, u32[]{:S(2)}, u32[]{:S(2)}) collective-permute-start(f32[4,40,128]{2,1,0:T(8,128)S(1)} %pass_on.22), channel_id=1, source_target_pairs={{4,8},{5,9},{6,10},{7,11},{20,24},{21,25},{22,26},{23,27}} | collective-permute-start | bytes 245768 | tf_op jit(solution)/shard_map/ppermute | solution.py:523
  17.6 3.1 %collective-permute-start.10 = (f32[4,40,128]{2,1,0:T(8,128)S(1)}, f32[4,40,128]{2,1,0:T(8,128)S(1)}, u32[]{:S(2)}, u32[]{:S(2)}) collective-permute-start(f32[4,40,128]{2,1,0:T(8,128)S(1)} %pass_on.20), channel_id=1, source_target_pairs={{4,8},{5,9},{6,10},{7,11},{20,24},{21,25},{22,26},{23,27}} | collective-permute-start | bytes 245768 | tf_op jit(solution)/shard_map/ppermute | solution.py:523
  18.4 3.0 %collective-permute-start.5 = (f32[4,40,128]{2,1,0:T(8,128)S(1)}, f32[4,40,128]{2,1,0:T(8,128)S(1)}, u32[]{:S(2)}, u32[]{:S(2)}) collective-permute-start(f32[4,40,128]{2,1,0:T(8,128)S(1)} %pass_on.18), channel_id=1, source_target_pairs={{4,8},{5,9},{6,10},{7,11},{20,24},{21,25},{22,26},{23,27}} | collective-permute-start | bytes 245768 | tf_op jit(solution)/shard_map/ppermute | solution.py:523
  19.3 2.8 %collective-permute-start.2 = (f32[4,40,128]{2,1,0:T(8,128)S(1)}, f32[4,40,128]{2,1,0:T(8,128)S(1)}, u32[]{:S(2)}, u32[]{:S(2)}) collective-permute-start(f32[4,40,128]{2,1,0:T(8,128)S(1)} %pass_on.16), channel_id=1, source_target_pairs={{4,8},{5,9},{6,10},{7,11},{20,24},{21,25},{22,26},{23,27}} | collective-permute-start | bytes 245768 | tf_op jit(solution)/shard_map/ppermute | solution.py:523
  20.0 4.3 %collective-permute-start.14 = (f32[4,40,128]{2,1,0:T(8,128)S(1)}, f32[4,40,128]{2,1,0:T(8,128)S(1)}, u32[]{:S(2)}, u32[]{:S(2)}) collective-permute-start(f32[4,40,128]{2,1,0:T(8,128)S(1)} %pass_on.23), channel_id=1, source_target_pairs={{8,12},{9,13},{10,14},{11,15},{24,28},{25,29},{26,30},{27,31}} | collective-permute-start | bytes 245768 | tf_op jit(solution)/shard_map/ppermute | solution.py:523
  20.8 3.6 %collective-permute-start.11 = (f32[4,40,128]{2,1,0:T(8,128)S(1)}, f32[4,40,128]{2,1,0:T(8,128)S(1)}, u32[]{:S(2)}, u32[]{:S(2)}) collective-permute-start(f32[4,40,128]{2,1,0:T(8,128)S(1)} %pass_on.21), channel_id=1, source_target_pairs={{8,12},{9,13},{10,14},{11,15},{24,28},{25,29},{26,30},{27,31}} | collective-permute-start | bytes 245768 | tf_op jit(solution)/shard_map/ppermute | solution.py:523
  21.5 5.1 %collective-permute-start.6 = (f32[4,40,128]{2,1,0:T(8,128)S(1)}, f32[4,40,128]{2,1,0:T(8,128)S(1)}, u32[]{:S(2)}, u32[]{:S(2)}) collective-permute-start(f32[4,40,128]{2,1,0:T(8,128)S(1)} %pass_on.19), channel_id=1, source_target_pairs={{8,12},{9,13},{10,14},{11,15},{24,28},{25,29},{26,30},{27,31}} | collective-permute-start | bytes 245768 | tf_op jit(solution)/shard_map/ppermute | solution.py:523
  22.2 4.3 %collective-permute-start.3 = (f32[4,40,128]{2,1,0:T(8,128)S(1)}, f32[4,40,128]{2,1,0:T(8,128)S(1)}, u32[]{:S(2)}, u32[]{:S(2)}) collective-permute-start(f32[4,40,128]{2,1,0:T(8,128)S(1)} %pass_on.17), channel_id=1, source_target_pairs={{8,12},{9,13},{10,14},{11,15},{24,28},{25,29},{26,30},{27,31}} | collective-permute-start | bytes 245768 | tf_op jit(solution)/shard_map/ppermute | solution.py:523
  29.2 4.6 %collective-permute-start.16 = (f32[16,8,128]{2,1,0:T(8,128)S(1)}, f32[16,8,128]{2,1,0:T(8,128)S(1)}, u32[]{:S(2)}, u32[]{:S(2)}) collective-permute-start(f32[16,8,128]{2,1,0:T(8,128)S(1)} %add.25.refs_0_), channel_id=1, source_target_pairs={{0,2},{1,3},{2,0},{3,1},{4,6},{5,7},{6,4},{7,5},{8,10},{9,11},{10,... | collective-permute-start | bytes 196616 | tf_op jit(solution)/shard_map/ppermute | solution.py:618
  30.8 6.6 %collective-permute-start.8 = (f32[16,8,128]{2,1,0:T(8,128)S(1)}, f32[16,8,128]{2,1,0:T(8,128)S(1)}, u32[]{:S(2)}, u32[]{:S(2)}) collective-permute-start(f32[16,8,128]{2,1,0:T(8,128)S(1)} %add.24.refs_0_), channel_id=1, source_target_pairs={{0,2},{1,3},{2,0},{3,1},{4,6},{5,7},{6,4},{7,5},{8,10},{9,11},{10,... | collective-permute-start | bytes 196616 | tf_op jit(solution)/shard_map/ppermute | solution.py:618
  36.0 4.9 %collective-permute-start.26 = (f32[4,40,128]{2,1,0:T(8,128)S(1)}, f32[4,40,128]{2,1,0:T(8,128)S(1)}, u32[]{:S(2)}, u32[]{:S(2)}) collective-permute-start(f32[4,40,128]{2,1,0:T(8,128)S(1)} %get-tuple-element.46.carried_ref), channel_id=1, source_target_pairs={{12,8},{13,9},{14,10},{15,11},{28,24},{29,25},{30,26},{31,27}} | collective-permute-start | bytes 245768 | tf_op jit(solution)/shard_map/ppermute | solution.py:523
  36.7 4.9 %collective-permute-start.23 = (f32[4,40,128]{2,1,0:T(8,128)S(1)}, f32[4,40,128]{2,1,0:T(8,128)S(1)}, u32[]{:S(2)}, u32[]{:S(2)}) collective-permute-start(f32[4,40,128]{2,1,0:T(8,128)S(1)} %get-tuple-element.45.carried_ref), channel_id=1, source_target_pairs={{12,8},{13,9},{14,10},{15,11},{28,24},{29,25},{30,26},{31,27}} | collective-permute-start | bytes 245768 | tf_op jit(solution)/shard_map/ppermute | solution.py:523
  40.2 2.8 %collective-permute-start.17 = (f32[4,40,128]{2,1,0:T(8,128)S(1)}, f32[4,40,128]{2,1,0:T(8,128)S(1)}, u32[]{:S(2)}, u32[]{:S(2)}) collective-permute-start(f32[4,40,128]{2,1,0:T(8,128)S(1)} %get-tuple-element.43.carried_ref), channel_id=1, source_target_pairs={{12,8},{13,9},{14,10},{15,11},{28,24},{29,25},{30,26},{31,27}} | collective-permute-start | bytes 245768 | tf_op jit(solution)/shard_map/ppermute | solution.py:523
  40.9 2.8 %collective-permute-start.27 = (f32[4,40,128]{2,1,0:T(8,128)S(1)}, f32[4,40,128]{2,1,0:T(8,128)S(1)}, u32[]{:S(2)}, u32[]{:S(2)}) collective-permute-start(f32[4,40,128]{2,1,0:T(8,128)S(1)} %pass_on.30), channel_id=1, source_target_pairs={{8,4},{9,5},{10,6},{11,7},{24,20},{25,21},{26,22},{27,23}} | collective-permute-start | bytes 245768 | tf_op jit(solution)/shard_map/ppermute | solution.py:523
  41.6 3.5 %collective-permute-start.24 = (f32[4,40,128]{2,1,0:T(8,128)S(1)}, f32[4,40,128]{2,1,0:T(8,128)S(1)}, u32[]{:S(2)}, u32[]{:S(2)}) collective-permute-start(f32[4,40,128]{2,1,0:T(8,128)S(1)} %pass_on.28), channel_id=1, source_target_pairs={{8,4},{9,5},{10,6},{11,7},{24,20},{25,21},{26,22},{27,23}} | collective-permute-start | bytes 245768 | tf_op jit(solution)/shard_map/ppermute | solution.py:523
  42.4 4.1 %collective-permute-start.21 = (f32[4,40,128]{2,1,0:T(8,128)S(1)}, f32[4,40,128]{2,1,0:T(8,128)S(1)}, u32[]{:S(2)}, u32[]{:S(2)}) collective-permute-start(f32[4,40,128]{2,1,0:T(8,128)S(1)} %pass_on.26), channel_id=1, source_target_pairs={{8,4},{9,5},{10,6},{11,7},{24,20},{25,21},{26,22},{27,23}} | collective-permute-start | bytes 245768 | tf_op jit(solution)/shard_map/ppermute | solution.py:523
  43.1 4.7 %collective-permute-start.18 = (f32[4,40,128]{2,1,0:T(8,128)S(1)}, f32[4,40,128]{2,1,0:T(8,128)S(1)}, u32[]{:S(2)}, u32[]{:S(2)}) collective-permute-start(f32[4,40,128]{2,1,0:T(8,128)S(1)} %pass_on.24), channel_id=1, source_target_pairs={{8,4},{9,5},{10,6},{11,7},{24,20},{25,21},{26,22},{27,23}} | collective-permute-start | bytes 245768 | tf_op jit(solution)/shard_map/ppermute | solution.py:523
  43.8 15.5 %collective-permute-start.28 = (f32[4,40,128]{2,1,0:T(8,128)S(1)}, f32[4,40,128]{2,1,0:T(8,128)S(1)}, u32[]{:S(2)}, u32[]{:S(2)}) collective-permute-start(f32[4,40,128]{2,1,0:T(8,128)S(1)} %pass_on.31), channel_id=1, source_target_pairs={{4,0},{5,1},{6,2},{7,3},{20,16},{21,17},{22,18},{23,19}} | collective-permute-start | bytes 245768 | tf_op jit(solution)/shard_map/ppermute | solution.py:523
  45.1 16.3 %collective-permute-start.25 = (f32[4,40,128]{2,1,0:T(8,128)S(1)}, f32[4,40,128]{2,1,0:T(8,128)S(1)}, u32[]{:S(2)}, u32[]{:S(2)}) collective-permute-start(f32[4,40,128]{2,1,0:T(8,128)S(1)} %pass_on.29), channel_id=1, source_target_pairs={{4,0},{5,1},{6,2},{7,3},{20,16},{21,17},{22,18},{23,19}} | collective-permute-start | bytes 245768 | tf_op jit(solution)/shard_map/ppermute | solution.py:523
  46.5 15.8 %collective-permute-start.22 = (f32[4,40,128]{2,1,0:T(8,128)S(1)}, f32[4,40,128]{2,1,0:T(8,128)S(1)}, u32[]{:S(2)}, u32[]{:S(2)}) collective-permute-start(f32[4,40,128]{2,1,0:T(8,128)S(1)} %pass_on.27), channel_id=1, source_target_pairs={{4,0},{5,1},{6,2},{7,3},{20,16},{21,17},{22,18},{23,19}} | collective-permute-start | bytes 245768 | tf_op jit(solution)/shard_map/ppermute | solution.py:523
  47.8 15.5 %collective-permute-start.19 = (f32[4,40,128]{2,1,0:T(8,128)S(1)}, f32[4,40,128]{2,1,0:T(8,128)S(1)}, u32[]{:S(2)}, u32[]{:S(2)}) collective-permute-start(f32[4,40,128]{2,1,0:T(8,128)S(1)} %pass_on.25), channel_id=1, source_target_pairs={{4,0},{5,1},{6,2},{7,3},{20,16},{21,17},{22,18},{23,19}} | collective-permute-start | bytes 245768 | tf_op jit(solution)/shard_map/ppermute | solution.py:523
  64.6 4.0 %collective-permute-start.29 = (f32[32,160]{1,0:T(8,128)S(1)}, f32[32,160]{1,0:T(8,128)S(1)}, u32[]{:S(2)}, u32[]{:S(2)}) collective-permute-start(f32[32,160]{1,0:T(8,128)S(1)} %get-tuple-element.48.refs_5_), channel_id=1, source_target_pairs={{0,16},{16,0},{1,17},{17,1},{2,18},{18,2},{3,19},{19,3},{4,20},{20... | collective-permute-start | bytes 61448 | tf_op jit(solution)/shard_map/ppermute | solution.py:506
  70.6 3.6 %collective-permute-start.31 = (f32[8,128]{1,0:T(8,128)S(1)}, f32[8,128]{1,0:T(8,128)S(1)}, u32[]{:S(2)}, u32[]{:S(2)}) collective-permute-start(f32[8,128]{1,0:T(8,128)S(1)} %add.26), channel_id=1, source_target_pairs={{0,2},{1,3},{2,0},{3,1},{4,6},{5,7},{6,4},{7,5},{8,10},{9,11},{10,... | collective-permute-start | bytes 12296 | tf_op jit(solution)/shard_map/ppermute | solution.py:534
  74.2 3.6 %collective-permute-start.32 = (f32[8,128]{1,0:T(8,128)S(1)}, f32[8,128]{1,0:T(8,128)S(1)}, u32[]{:S(2)}, u32[]{:S(2)}) collective-permute-start(f32[8,128]{1,0:T(8,128)S(1)} %add.27), channel_id=1, source_target_pairs={{0,16},{16,0},{1,17},{17,1},{2,18},{18,2},{3,19},{19,3},{4,20},{20... | collective-permute-start | bytes 12296 | tf_op jit(solution)/shard_map/ppermute | solution.py:534
  77.8 4.4 %collective-permute-start.33 = (f32[8,128]{1,0:T(8,128)S(1)}, f32[8,128]{1,0:T(8,128)S(1)}, u32[]{:S(2)}, u32[]{:S(2)}) collective-permute-start(f32[8,128]{1,0:T(8,128)S(1)} %add.28), channel_id=1, source_target_pairs={{0,4},{4,0},{8,12},{12,8},{1,5},{5,1},{9,13},{13,9},{2,6},{6,2},{1... | collective-permute-start | bytes 12296 | tf_op jit(solution)/shard_map/ppermute | solution.py:534
  77.8 4.5 %collective-permute-start.34 = (f32[8,128]{1,0:T(8,128)S(1)}, f32[8,128]{1,0:T(8,128)S(1)}, u32[]{:S(2)}, u32[]{:S(2)}) collective-permute-start(f32[8,128]{1,0:T(8,128)S(1)} %add.28), channel_id=1, source_target_pairs={{0,8},{4,12},{8,0},{12,4},{1,9},{5,13},{9,1},{13,5},{2,10},{6,14},... | collective-permute-start | bytes 12296 | tf_op jit(solution)/shard_map/ppermute | solution.py:534
  77.8 6.0 %collective-permute-start.35 = (f32[8,128]{1,0:T(8,128)S(1)}, f32[8,128]{1,0:T(8,128)S(1)}, u32[]{:S(2)}, u32[]{:S(2)}) collective-permute-start(f32[8,128]{1,0:T(8,128)S(1)} %add.28), channel_id=1, source_target_pairs={{0,12},{4,8},{8,4},{12,0},{1,13},{5,9},{9,5},{13,1},{2,14},{6,10},... | collective-permute-start | bytes 12296 | tf_op jit(solution)/shard_map/ppermute | solution.py:534
  (11 other events, 61.2 us)

commit v7 on v6

--- a/solution.py
+++ b/solution.py
@@ -5,6 +5,7 @@
 from jax.experimental import pallas as pl
 from jax.experimental.pallas import tpu as pltpu
 from jax.sharding import PartitionSpec as P
+
 
 f32 = jnp.float32
 bf16 = jnp.bfloat16
@@ -219,12 +220,6 @@
         )
 
 
-def member_blocks(members):
-    for size in (5, 4, 2, 1):
-        if members % size == 0:
-            return size
-
-
 def k_tables(rows, cells, dec_ref, lonc_ref, latc_ref, table_ref):
     row = jnp.broadcast_to(dec_ref[:, cells:], (rows, rows))
     own = iota((rows, rows), 0) == iota((rows, rows), 1)
@@ -244,17 +239,48 @@
     )
 
 
-def k_prepare(m_ref, lon_ref, a_ref, b_ref, table_ref):
-    half = a_ref.shape[0]
+def spread_modes(v, pairs, transposed):
+    source = v.T if transposed else v
+    r, c = source.shape
+    shape = (pairs * r, 3 * pairs * c)
+    num = lambda shape, dim: lax.broadcasted_iota(jnp.int32, shape, dim)
+    exact = functools.partial(jnp.dot, precision=lax.Precision.HIGHEST, preferred_element_type=f32)
+    pick_row = (lax.rem(num((shape[0], r), 0), r) == num((shape[0], r), 1)).astype(f32)
+    pick_column = (num((c, shape[1]), 0) == lax.rem(num((c, shape[1]), 1), c)).astype(f32)
+    everywhere = exact(exact(pick_row, source), pick_column)
+    row, column = num(shape, 0), num(shape, 1)
+    place = lax.rem(column, pairs * c)
+    own = (place >= (row // r) * c) & (place < (row // r + 1) * c)
+    full = jnp.where(own, everywhere, 0.0)
+    high, low = halves(full)
+    middle = (column >= pairs * c) & (column < 2 * pairs * c)
+    return jnp.where(middle, low.astype(f32), high.astype(f32)).astype(bf16)
+
+
+def k_prepare(m_ref, lon_ref, v_ref, eig_ref, a_ref, b_ref, mask_ref, out_modes_ref, in_modes_ref, table_ref):
+    members, levels, rows, cells = m_ref.shape
+    pairs = members // 2
+    modes = v_ref.shape[0]
     lon_tables(lon_ref[...], *lon_ref.shape, True, table_ref)
+    v = v_ref[...]
+    out_modes_ref[...] = spread_modes(v, pairs, True)
+    in_modes_ref[...] = spread_modes(v, pairs, False)
+    e = lax.broadcasted_iota(jnp.int32, (modes, cells), 0)
+    low = lax.broadcasted_iota(jnp.int32, (modes, cells), 1) < cells // 2
+    for m in range(pairs):
+        used = jnp.where(low, eig_ref[m], eig_ref[m + pairs])
+        mask_ref[m * modes : (m + 1) * modes] = jnp.where(e < used, 1.0, 0.0)
+    apart = pairs * levels
 
     def step(i, carry):
-        a, b = swap_halves(m_ref[i].astype(f32), m_ref[i + half].astype(f32))
-        a_ref[i] = a
-        b_ref[i] = b
+        for l in range(levels):
+            a, b = swap_halves(m_ref[i, l].astype(f32), m_ref[i + pairs, l].astype(f32))
+            at = pl.ds(i * levels + l, rows, stride=apart)
+            a_ref[at, :] = a
+            b_ref[at, :] = b
         return carry
 
-    lax.fori_loop(0, half, step, 0)
+    lax.fori_loop(0, pairs, step, 0)
 
 
 def k_lat_first(rows, k, cells, n, chunks, *refs):
@@ -299,20 +325,14 @@
         out_ref[i] = v
 
 
-def active_pair(eig_ref, m, pairs, e, cells):
-    low = iota((1, cells), 1) < float(cells // 2)
-    first = jnp.where(e < eig_ref[m], 1.0, 0.0).astype(f32)
-    second = jnp.where(e < eig_ref[m + pairs], 1.0, 0.0).astype(f32)
-    return jnp.where(low, first, second)
-
-
-def k_increment(rows, k, part, chunks, count, pairs, modes, levels, *refs):
-    f_ref, lat_ref, m_ref, v_ref, eig_ref, *rest = refs
-    out_ref, s_ref, inc_ref = rest[count:]
+def k_increment(rows, k, part, chunks, count, pairs, levels, *refs):
+    f_ref, lat_ref, m_ref, mask_ref, modes_ref, *rest = refs
+    out_ref, s_ref = rest[count:]
     cells = lat_ref.shape[-1]
 
     def store(y, ch, at, base, value, last):
-        s_ref[pl.ds(base * rows + y, 8, stride=rows), :] = value
+        where = pl.ds(pl.multiple_of(base, 8), 8)
+        s_ref[y, where, :] = value * mask_ref[where, :]
 
     sweep_chunks(
         lambda y, base: f_ref[y, pl.ds(pl.multiple_of(base, 8), 8), :],
@@ -324,66 +344,30 @@
         chunks,
         False,
     )
-    per = member_blocks(pairs)
-    for b in range(pairs // per):
-        fields = []
-        for m in range(per):
-            for e in range(modes):
-                scale = active_pair(eig_ref, b * per + m, pairs, e, cells)
-                at = ((b * per + m) * modes + e) * rows
-                fields.append(s_ref[at : at + rows, :] * scale)
-
-        def level(l, carry, b=b, fields=fields):
-            total = None
-            for m in range(per):
-                p = None
-                for e in range(modes):
-                    t = v_ref[e, l] * fields[m * modes + e]
-                    p = t if p is None else p + t
-                p = m_ref[b * per + m, l] * p
-                total = p if total is None else total + p
-            if b == 0:
-                inc_ref[l] = total
-            else:
-                inc_ref[l] += total
-            return carry
-
-        lax.fori_loop(0, levels, level, 0, unroll=4)
     half = levels // 2
-    low = iota((1, 1, cells), 2) < float(cells // 2)
-    full = inc_ref[...]
-    full = full + pltpu.roll(full, cells // 2, 2)
-    out_ref[...] = jnp.where(low, full[:half], full[half:])
-
-
-def k_gradient(rows, k, part, chunks, pairs, modes, levels, *refs):
-    inc_ref, got_ref, obs_ref, m_ref, v_ref, eig_ref, lat_ref, g_ref, *carried_refs, w_ref = refs
+    low = iota((1, cells), 1) < float(cells // 2)
+    size = pairs * levels
+    for y in range(rows):
+        profile = product3(modes_ref[...], right3(s_ref[y], 0))
+        inc = None
+        for m in range(pairs):
+            p = m_ref[y * size + m * levels : y * size + (m + 1) * levels, :] * profile[m * levels : (m + 1) * levels]
+            inc = p if inc is None else inc + p
+        inc = inc + pltpu.roll(inc, cells // 2, 1)
+        out_ref[y] = jnp.where(low, inc[:half], inc[half:])
+
+
+def k_gradient(rows, k, part, chunks, pairs, levels, *refs):
+    inc_ref, got_ref, obs_ref, m_ref, mask_ref, modes_ref, lat_ref, g_ref, *carried_refs = refs
     cells = lat_ref.shape[-1]
-    half = levels // 2
-    first, second = both_halves(inc_ref[...] + got_ref[...])
-    obs = both_halves(obs_ref[...])[part]
-    w_ref[:half] = first * obs[:half]
-    w_ref[half:] = second * obs[half:]
-    per = member_blocks(pairs)
-    for b in range(pairs // per):
-
-        def level(l, acc, b=b):
-            w = w_ref[l]
-            vs = [v_ref[e, l] for e in range(modes)]
-            out = []
-            for m in range(per):
-                t = m_ref[b * per + m, l] * w
-                for e in range(modes):
-                    out.append(acc[m * modes + e] + vs[e] * t)
-            return tuple(out)
-
-        zero = jnp.zeros((rows, cells), f32)
-        acc = lax.fori_loop(0, levels, level, (zero,) * (per * modes), unroll=4)
-        for m in range(per):
-            for e in range(modes):
-                scale = active_pair(eig_ref, b * per + m, pairs, e, cells)
-                at = ((b * per + m) * modes + e) * rows
-                g_ref[at : at + rows, :] = acc[m * modes + e] * scale
+    obs_ref = obs_ref.reshape(levels * rows, cells)
+    size = pairs * levels
+    for y in range(rows):
+        inc = jnp.concatenate(both_halves(inc_ref[y] + got_ref[y]), axis=0)
+        w = inc * both_halves(obs_ref[pl.ds(y, levels, stride=rows), :])[part]
+        m = m_ref[y * size : (y + 1) * size, :]
+        weighted = (m.reshape(pairs, levels, cells) * w[None]).reshape(size, cells)
+        g_ref[y] = product3(modes_ref[...], right3(weighted, 0)) * mask_ref[...]
     zero8 = jnp.zeros((8, cells), f32)
 
     def store(y, ch, at, base, value, last):
@@ -392,7 +376,7 @@
                 carried_refs[ch][s, at, :] = last[s]
 
     sweep_chunks(
-        lambda y, base: g_ref[pl.ds(base * rows + y, 8, stride=rows), :],
+        lambda y, base: g_ref[y, pl.ds(pl.multiple_of(base, 8), 8), :],
         store,
         lambda ch, at: [zero8] * 4,
         lat_ref[part, :1],
@@ -414,7 +398,7 @@
             p_ref[part, y, pl.ds(pl.multiple_of(base, 8), 8), :] = value
 
         sweep_chunks(
-            lambda y, base: g_ref[pl.ds(base * rows + y, 8, stride=rows), :],
+            lambda y, base: g_ref[y, pl.ds(pl.multiple_of(base, 8), 8), :],
             store,
             entering_states(rest[part * count : (part + 1) * count], chunks),
             lat_ref[part, :1],
@@ -482,14 +466,13 @@
         copy.wait()
 
 
-def call(body, outs, ins, specs=None, out_specs=None, scratch=(), name=None, cost=None):
+def call(body, outs, ins, specs=None, out_specs=None, scratch=(), cost=None):
     return pl.pallas_call(
         body,
         out_shape=outs,
         in_specs=specs or [VM] * len(ins),
         out_specs=out_specs or jax.tree.map(lambda _: VM, outs),
         scratch_shapes=scratch,
-        name=name,
         cost_estimate=None if cost is None else pl.CostEstimate(flops=cost, bytes_accessed=1000, transcendentals=0),
         compiler_params=pltpu.CompilerParams(vmem_limit_bytes=16 * 1024 * 1024),
     )(*ins)
@@ -509,7 +492,7 @@
 
 
 def pass_on(part, got, latc, rows, c):
-    return call(functools.partial(k_pass_on, rows, c), sds(*part.shape), [part, got, latc], name="pass_on")
+    return call(functools.partial(k_pass_on, rows, c), sds(*part.shape), [part, got, latc])
 
 
 def lat_carry(halves, latc, rows, backward):
@@ -557,43 +540,43 @@
     return v
 
 
-def body(control, residual, direction, members, vert_modes, eig_count, lon_decay, lat_decay, obs_weight):
+def iteration(control, residual, direction, members, vert_modes, eig_count, lon_decay, lat_decay, obs_weight):
     k, rows, cells = direction.shape
     mcount, levels = members.shape[:2]
-    modes = vert_modes.shape[0]
     n_lon, n_mem = lax.axis_size("lon"), lax.axis_size("mem")
     half = k // 2
     pairs = mcount // 2
-    chunks = 2
-    states = (sds(4, half // chunks, cells),) * chunks
+    chunks, back_chunks = 2, 1
+    states = lambda chunks: (sds(4, half // chunks, cells),) * chunks
 
     decays = jnp.concatenate([lat_decay, lon_decay]).reshape(1, cells + rows)
     lonc, latc, tables = call(
         functools.partial(k_tables, rows, cells),
         (sds(rows, cells), sds(2, 8, cells), jax.ShapeDtypeStruct((rows, 3 * cells, 2 * cells), bf16)),
         [decays],
-        name="tables",
         cost=10**9,
     )
     inside, carried = call(
-        functools.partial(k_lon_fwd, rows, k, cells),
-        (sds(rows, k, cells), sds(4 * rows, k)),
-        [direction, tables],
-        name="lon_fwd",
-    )
-    *packed, back_tables = call(
+        functools.partial(k_lon_fwd, rows, k, cells), (sds(rows, k, cells), sds(4 * rows, k)), [direction, tables]
+    )
+    *packed, mask, out_modes, in_modes, back_tables = call(
         k_prepare,
-        (sds(pairs, levels, rows, cells),) * 2 + (jax.ShapeDtypeStruct((rows, 3 * cells, 2 * cells), bf16),),
-        [members, lonc],
-        name="prepare",
+        (sds(rows * pairs * levels, cells),) * 2
+        + (
+            sds(half, cells),
+            jax.ShapeDtypeStruct((pairs * levels, 3 * half), bf16),
+            jax.ShapeDtypeStruct((half, 3 * pairs * levels), bf16),
+            jax.ShapeDtypeStruct((rows, 3 * cells, 2 * cells), bf16),
+        ),
+        [members, lonc, vert_modes, eig_count],
+        specs=[VM, VM, VM, SM],
         cost=10**9,
     )
     blocks = lon_exchange(carried, False)
     fa, fb, *parts = call(
         functools.partial(k_lat_first, rows, k, cells, n_lon, chunks),
-        (sds(rows, half, cells),) * 2 + states * 2,
+        (sds(rows, half, cells),) * 2 + states(chunks) * 2,
         [inside, lonc, latc, *blocks],
-        name="lat_first",
     )
     got = lat_carry([parts[:chunks], parts[chunks:]], latc, rows, False)
     count = len(got[0])
@@ -601,12 +584,10 @@
     inc = [None, None]
     for part in range(2):
         inc[part] = call(
-            functools.partial(k_increment, rows, half, part, chunks, count, pairs, modes, levels),
-            sds(levels // 2, rows, cells),
-            [fields[part], latc, packed[part], vert_modes, eig_count, *got[part]],
-            specs=[VM, VM, VM, SM, SM] + [VM] * count,
-            scratch=[pltpu.VMEM((half * rows, cells), f32), pltpu.VMEM((levels, rows, cells), f32)],
-            name="increment",
+            functools.partial(k_increment, rows, half, part, chunks, count, pairs, levels),
+            sds(rows, levels // 2, cells),
+            [fields[part], latc, packed[part], mask, out_modes, *got[part]],
+            scratch=[pltpu.VMEM((rows, half, cells), f32)],
         )
     grads, sends = [None, None], [None, None]
     for part in range(2):
@@ -617,27 +598,23 @@
             step *= 2
         other = lax.ppermute(v, "mem", [(i, i ^ step) for i in range(n_mem)])
         grads[part], *sends[part] = call(
-            functools.partial(k_gradient, rows, half, part, chunks, pairs, modes, levels),
-            (sds(half * rows, cells),) + states,
-            [v, other, obs_weight, packed[part], vert_modes, eig_count, latc],
-            specs=[VM, VM, VM, VM, SM, SM, VM],
-            scratch=[pltpu.VMEM((levels, rows, cells), f32)],
-            name="gradient",
+            functools.partial(k_gradient, rows, half, part, back_chunks, pairs, levels),
+            (sds(rows, half, cells),) + states(back_chunks),
+            [v, other, obs_weight, packed[part], mask, in_modes, latc],
         )
     got = lat_carry(sends, latc, rows, True)
+    count = len(got[0])
     inside, carried = call(
-        functools.partial(k_lon_bwd, rows, k, cells, chunks, count),
+        functools.partial(k_lon_bwd, rows, k, cells, back_chunks, count),
         (sds(rows, k, cells), sds(4 * rows, k)),
         [*grads, latc, back_tables, *got[0], *got[1]],
         scratch=[pltpu.VMEM((2, rows, half, cells), f32)],
-        name="lon_bwd",
     )
     blocks = lon_exchange(carried, True)
     h, sums = call(
         functools.partial(k_sums, rows, k, cells, n_lon),
         (sds(k * rows, cells), sds(8, cells)),
         [inside, lonc, direction, residual, *blocks],
-        name="sums",
     )
     sums = reduce_everywhere(sums)
     pieces = 4 if k % 4 == 0 else 1
@@ -647,7 +624,6 @@
         [sums, control, residual, direction, h.reshape(k, rows, cells)],
         out_specs=(pl.BlockSpec(memory_space=pl.ANY),) * 3,
         scratch=[pltpu.VMEM((k, rows, cells), f32)] * 3 + [pltpu.SemaphoreType.DMA((3, pieces))],
-        name="update",
     )
     return tuple(outs)
 
@@ -665,4 +641,4 @@
         P("lon"),
         P(None, "lat", "lon"),
     )
-    return jax.shard_map(body, mesh=mesh, in_specs=placed, out_specs=(field,) * 3, check_vma=False)
+    return jax.shard_map(iteration, mesh=mesh, in_specs=placed, out_specs=(field,) * 3, check_vma=False)

time: 85.8 us -> 85.9 us (level)
  waiting for transfers between devices: 27.9 us -> 36.1 us
  starting transfers between devices: 38.9 us -> 33.4 us
  Pallas kernels: 15.9 us -> 13.4 us
    ppermute x24 -> x18, waiting for transfers between devices: 14.5 us -> 22.5 us  [lat_carry(): got[c][i].append(lax.ppermute(v, 'lat', [(at(h), at(h + 1))]))]
    ppermute x24 -> x18, starting transfers between devices: 23.7 us -> 18.5 us  [lat_carry(): got[c][i].append(lax.ppermute(v, 'lat', [(at(h), at(h + 1))]))]
    pallas_call x27 -> x23, Pallas kernels: 15.9 us -> 13.4 us  [call(): pl.pallas_call(body, out_shape=outs, in_specs=specs or [VM] * len(ins), o...]
  transfers between devices with their start and end apart: 36 -> 30, of which waited for: 14 -> 12; matrix products, arithmetic and copies ran while one was open for 0% -> 0% of each run, Pallas kernels for 12% -> 9%
where the time goes in v7:
time: 85.9 us; the launch traced here: 85.5 us
  waiting for transfers between devices  36.1 us (42%)
  starting transfers between devices  33.4 us (39%)
  Pallas kernels  13.4 us (16%)
  between operations  1.1 us (1%)
    ppermute x18, waiting for transfers between devices, lat_carry(): got[c][i].append(lax.ppermute(v, 'lat', [(at(h), at(h + 1))]))  22.5 us
    ppermute x18, starting transfers between devices, lat_carry(): got[c][i].append(lax.ppermute(v, 'lat', [(at(h), at(h + 1))]))  18.5 us
    pallas_call x23, Pallas kernels, call(): pl.pallas_call(body, out_shape=outs, in_specs=specs or [VM] * len(ins), o...  13.4 us
    ppermute x6, starting transfers between devices, all_sum(): lax.ppermute(v, axes, [(i, i ^ m) for i in range(total)])  7.28 us
    ppermute x6, waiting for transfers between devices, all_sum(): lax.ppermute(v, axes, [(i, i ^ m) for i in range(total)])  7.16 us
    ppermute x2, starting transfers between devices, lon_exchange(): lax.ppermute(carried, 'lon', [(j, (j + sign * r) % n) for j in range(n)])  4.51 us
    ppermute x2, waiting for transfers between devices, lon_exchange(): lax.ppermute(carried, 'lon', [(j, (j + sign * r) % n) for j in range(n)])  4.33 us
    ppermute x2, starting transfers between devices, iteration(): other = lax.ppermute(v, 'mem', [(i, i ^ step) for i in range(n_mem)])  2.47 us
  transfers between devices with their start and end apart: 30, of which 12 were waited for; matrix products, arithmetic and copies ran while one was open for 0% of the time, Pallas kernels for 9%

profile of v7, /device:TPU:0, one launch (start us, length us, event | category | flops | bytes accessed | tf_op | source)
XLA Modules:
  0.0 85.5 jit_solution(12698741611685348264)
XLA Ops:
  1.7 0.7 copy-done
  3.0 3.0 %collective-permute-start = (f32[32,160]{1,0:T(8,128)S(1)}, f32[32,160]{1,0:T(8,128)S(1)}, u32[]{:S(2)}, u32[]{:S(2)}) collective-permute-start(f32[32,160]{1,0:T(8,128)S(1)} %get-tuple-element.32.refs_4_), channel_id=1, source_target_pairs={{0,16},{16,0},{1,17},{17,1},{2,18},{18,2},{3,19},{19,3},{4,20},{20... | collective-permute-start | bytes 61448 | tf_op jit(solution)/shard_map/ppermute | solution.py:489
  6.0 1.9 %collective-permute-done.refs_3_ = f32[32,160]{1,0:T(8,128)S(1)} collective-permute-done((f32[32,160]{1,0:T(8,128)S(1)}, f32[32,160]{1,0:T(8,128)S(1)}, u32[]{:S(2)}, u32[]{:S(2)}) %collective-permute-start) | collective-permute-done | bytes 20512 | tf_op jit(solution)/shard_map/ppermute | solution.py:489
  7.9 1.1 %shard_map.114 = (f32[8,80,128]{2,1,0:T(8,128)S(1)}, f32[8,80,128]{2,1,0:T(8,128)S(1)}, f32[4,40,128]{2,1,0:T(8,128)S(1)}, f32[4,40,128]{2,1,0:T(8,128)S(1)}, f3...) custom-call(f32[8,160,128]{2,1,0:T(8,128)S(1)} %get-tuple-element.29.refs_0_, ...), custom_call_target="tpu_custom_call" | custom-call | tf_op jit(solution)/shard_map/pallas_call | solution.py:470
  8.9 4.0 %collective-permute-start.12 = (f32[4,40,128]{2,1,0:T(8,128)S(1)}, f32[4,40,128]{2,1,0:T(8,128)S(1)}, u32[]{:S(2)}, u32[]{:S(2)}) collective-permute-start(f32[4,40,128]{2,1,0:T(8,128)S(1)} %get-tuple-element.44.carried_ref), channel_id=1, source_target_pairs={{0,4},{1,5},{2,6},{3,7},{16,20},{17,21},{18,22},{19,23}} | collective-permute-start | bytes 245768 | tf_op jit(solution)/shard_map/ppermute | solution.py:506
  13.0 1.3 %collective-permute-start.9 = (f32[4,40,128]{2,1,0:T(8,128)S(1)}, f32[4,40,128]{2,1,0:T(8,128)S(1)}, u32[]{:S(2)}, u32[]{:S(2)}) collective-permute-start(f32[4,40,128]{2,1,0:T(8,128)S(1)} %get-tuple-element.43.carried_ref), channel_id=1, source_target_pairs={{0,4},{1,5},{2,6},{3,7},{16,20},{17,21},{18,22},{19,23}} | collective-permute-start | bytes 245768 | tf_op jit(solution)/shard_map/ppermute | solution.py:506
  14.3 1.3 %collective-permute-start.4 = (f32[4,40,128]{2,1,0:T(8,128)S(1)}, f32[4,40,128]{2,1,0:T(8,128)S(1)}, u32[]{:S(2)}, u32[]{:S(2)}) collective-permute-start(f32[4,40,128]{2,1,0:T(8,128)S(1)} %get-tuple-element.38.carried_ref), channel_id=1, source_target_pairs={{0,4},{1,5},{2,6},{3,7},{16,20},{17,21},{18,22},{19,23}} | collective-permute-start | bytes 245768 | tf_op jit(solution)/shard_map/ppermute | solution.py:506
  15.6 1.3 %collective-permute-start.1 = (f32[4,40,128]{2,1,0:T(8,128)S(1)}, f32[4,40,128]{2,1,0:T(8,128)S(1)}, u32[]{:S(2)}, u32[]{:S(2)}) collective-permute-start(f32[4,40,128]{2,1,0:T(8,128)S(1)} %get-tuple-element.37.carried_ref), channel_id=1, source_target_pairs={{0,4},{1,5},{2,6},{3,7},{16,20},{17,21},{18,22},{19,23}} | collective-permute-start | bytes 245768 | tf_op jit(solution)/shard_map/ppermute | solution.py:506
  22.9 3.9 %shard_map.115 = (f32[2560,128]{1,0:T(8,128)S(1)}, f32[2560,128]{1,0:T(8,128)S(1)}, f32[80,128]{1,0:T(8,128)S(1)}, bf16[320,240]{1,0:T(8,128)(2,1)S(1)}, bf16[80...) custom-call(bf16[20,32,8,128]{3,2,1,0:T(8,128)(2,1)S(1)} %copy-done.4, ...), custom_call_target="tpu_custom_call" | custom-call | flops 1000000000 | bytes 1000 | tf_op jit(solution)/shard_map/pallas_call | solution.py:470
  26.9 0.9 %shard_map.126 = f32[8,16,128]{2,1,0:T(8,128)S(1)} custom-call(f32[8,80,128]{2,1,0:T(8,128)S(1)} %get-tuple-element.41.refs_0_, f32[2,8,128]{2,1,0:T(8,128)S(1)} %get-tuple-element.31.refs_2_.lat_ref.refs_1_.refs_6_, f32[2560,128]{1,0:T(8,128)S(1)} %get-tuple-element.42.refs_2_.refs_3_, f32[80,128]{1,0:T(8,128)S(1)} %get-tuple-element.35.refs_3_.refs_4_, ...), custom_call_target="tpu_custom_call" | custom-call | tf_op jit(solution)/shard_map/pallas_call | solution.py:470
  27.9 0.9 %shard_map.120 = f32[8,16,128]{2,1,0:T(8,128)S(1)} custom-call(f32[8,80,128]{2,1,0:T(8,128)S(1)} %get-tuple-element.33.refs_0_, f32[2,8,128]{2,1,0:T(8,128)S(1)} %get-tuple-element.31.refs_2_.lat_ref.refs_1_.refs_6_, f32[2560,128]{1,0:T(8,128)S(1)} %get-tuple-element.34.refs_2_.refs_3_, f32[80,128]{1,0:T(8,128)S(1)} %get-tuple-element.35.refs_3_.refs_4_, ...), custom_call_target="tpu_custom_call" | custom-call | tf_op jit(solution)/shard_map/pallas_call | solution.py:470
  29.4 1.6 %collective-permute-start.16 = (f32[8,16,128]{2,1,0:T(8,128)S(1)}, f32[8,16,128]{2,1,0:T(8,128)S(1)}, u32[]{:S(2)}, u32[]{:S(2)}) collective-permute-start(f32[8,16,128]{2,1,0:T(8,128)S(1)} %add.25.refs_0_), channel_id=1, source_target_pairs={{0,2},{1,3},{2,0},{3,1},{4,6},{5,7},{6,4},{7,5},{8,10},{9,11},{10,... | collective-permute-start | bytes 196616 | tf_op jit(solution)/shard_map/ppermute | solution.py:599
  31.0 0.9 %collective-permute-start.8 = (f32[8,16,128]{2,1,0:T(8,128)S(1)}, f32[8,16,128]{2,1,0:T(8,128)S(1)}, u32[]{:S(2)}, u32[]{:S(2)}) collective-permute-start(f32[8,16,128]{2,1,0:T(8,128)S(1)} %add.24.refs_0_), channel_id=1, source_target_pairs={{0,2},{1,3},{2,0},{3,1},{4,6},{5,7},{6,4},{7,5},{8,10},{9,11},{10,... | collective-permute-start | bytes 196616 | tf_op jit(solution)/shard_map/ppermute | solution.py:599
  31.9 2.2 %collective-permute-done.16.refs_1_ = f32[8,16,128]{2,1,0:T(8,128)S(1)} collective-permute-done((f32[8,16,128]{2,1,0:T(8,128)S(1)}, f32[8,16,128]{2,1,0:T(8,128)S(1)}, u32[]{:S(2)}, u32[]{:S(2)}) %collective-permute-start.16) | collective-permute-done | bytes 65568 | tf_op jit(solution)/shard_map/ppermute | solution.py:599
  34.0 0.9 %shard_map.127 = (f32[8,80,128]{2,1,0:T(8,128)S(1)}, f32[4,80,128]{2,1,0:T(8,128)S(1)}) custom-call(f32[8,16,128]{2,1,0:T(8,128)S(1)} %add.25.refs_0_, f32[8,16,128]{2,1,0:T(8,128)S(1)} %collective-permute-done.16.refs_1_, f32[32,8,128]{2,1,0:T(8,128)S(1)} %copy-done.3, f32[2560,128]{1,0:T(8,128)S(1)} %get-tuple-element.42.refs_2_.refs_3_, ...), custom_call_target="tpu_custom_call" | custom-call | tf_op jit(solution)/shard_map/pallas_call | solution.py:470
  35.6 0.9 %shard_map.121 = (f32[8,80,128]{2,1,0:T(8,128)S(1)}, f32[4,80,128]{2,1,0:T(8,128)S(1)}) custom-call(f32[8,16,128]{2,1,0:T(8,128)S(1)} %add.24.refs_0_, f32[8,16,128]{2,1,0:T(8,128)S(1)} %collective-permute-done.8.refs_1_, f32[32,8,128]{2,1,0:T(8,128)S(1)} %copy-done.3, f32[2560,128]{1,0:T(8,128)S(1)} %get-tuple-element.34.refs_2_.refs_3_, ...), custom_call_target="tpu_custom_call" | custom-call | tf_op jit(solution)/shard_map/pallas_call | solution.py:470
  38.7 1.3 %collective-permute-start.22 = (f32[4,80,128]{2,1,0:T(8,128)S(1)}, f32[4,80,128]{2,1,0:T(8,128)S(1)}, u32[]{:S(2)}, u32[]{:S(2)}) collective-permute-start(f32[4,80,128]{2,1,0:T(8,128)S(1)} %shard_map.131), channel_id=1, source_target_pairs={{4,0},{5,1},{6,2},{7,3},{20,16},{21,17},{22,18},{23,19}} | collective-permute-start | bytes 491528 | tf_op jit(solution)/shard_map/ppermute | solution.py:506
  40.1 1.3 %collective-permute-start.19 = (f32[4,80,128]{2,1,0:T(8,128)S(1)}, f32[4,80,128]{2,1,0:T(8,128)S(1)}, u32[]{:S(2)}, u32[]{:S(2)}) collective-permute-start(f32[4,80,128]{2,1,0:T(8,128)S(1)} %shard_map.129), channel_id=1, source_target_pairs={{4,0},{5,1},{6,2},{7,3},{20,16},{21,17},{22,18},{23,19}} | collective-permute-start | bytes 491528 | tf_op jit(solution)/shard_map/ppermute | solution.py:506
  41.4 20.4 %collective-permute-done.22.refs_9_ = f32[4,80,128]{2,1,0:T(8,128)S(1)} collective-permute-done((f32[4,80,128]{2,1,0:T(8,128)S(1)}, f32[4,80,128]{2,1,0:T(8,128)S(1)}, u32[]{:S(2)}, u32[]{:S(2)}) %collective-permute-start.22) | collective-permute-done | bytes 163872 | tf_op jit(solution)/shard_map/ppermute | solution.py:506
  61.8 1.8 %collective-permute-done.19.refs_6_ = f32[4,80,128]{2,1,0:T(8,128)S(1)} collective-permute-done((f32[4,80,128]{2,1,0:T(8,128)S(1)}, f32[4,80,128]{2,1,0:T(8,128)S(1)}, u32[]{:S(2)}, u32[]{:S(2)}) %collective-permute-start.19) | collective-permute-done | bytes 163872 | tf_op jit(solution)/shard_map/ppermute | solution.py:506
  63.5 1.3 %shard_map.132 = (f32[8,160,128]{2,1,0:T(8,128)S(1)}, f32[32,160]{1,0:T(8,128)S(1)}) custom-call(f32[8,80,128]{2,1,0:T(8,128)S(1)} %get-tuple-element.40.refs_0_, f32[8,80,128]{2,1,0:T(8,128)S(1)} %get-tuple-element.45.refs_1_, f32[2,8,128]{2,1,0:T(8,128)S(1)} %get-tuple-element.31.refs_2_.lat_ref.refs_1_.refs_6_, ...), custom_call_target="tpu_custom_call" | custom-call | tf_op jit(solution)/shard_map/pallas_call | solution.py:470
  64.8 1.5 %collective-permute-start.23 = (f32[32,160]{1,0:T(8,128)S(1)}, f32[32,160]{1,0:T(8,128)S(1)}, u32[]{:S(2)}, u32[]{:S(2)}) collective-permute-start(f32[32,160]{1,0:T(8,128)S(1)} %get-tuple-element.50.refs_5_), channel_id=1, source_target_pairs={{0,16},{16,0},{1,17},{17,1},{2,18},{18,2},{3,19},{19,3},{4,20},{20... | collective-permute-start | bytes 61448 | tf_op jit(solution)/shard_map/ppermute | solution.py:489
  66.3 2.4 %collective-permute-done.23.refs_4_ = f32[32,160]{1,0:T(8,128)S(1)} collective-permute-done((f32[32,160]{1,0:T(8,128)S(1)}, f32[32,160]{1,0:T(8,128)S(1)}, u32[]{:S(2)}, u32[]{:S(2)}) %collective-permute-start.23) | collective-permute-done | bytes 20512 | tf_op jit(solution)/shard_map/ppermute | solution.py:489
  68.7 0.7 shard_map.133
  69.5 1.2 %collective-permute-done.24 = f32[8,128]{1,0:T(8,128)S(1)} collective-permute-done((f32[8,128]{1,0:T(8,128)S(1)}, f32[8,128]{1,0:T(8,128)S(1)}, u32[]{:S(2)}, u32[]{:S(2)}) %collective-permute-start.24) | collective-permute-done | bytes 4128 | tf_op jit(solution)/shard_map/ppermute | solution.py:517
  70.7 1.4 %collective-permute-start.25 = (f32[8,128]{1,0:T(8,128)S(1)}, f32[8,128]{1,0:T(8,128)S(1)}, u32[]{:S(2)}, u32[]{:S(2)}) collective-permute-start(f32[8,128]{1,0:T(8,128)S(1)} %add.26), channel_id=1, source_target_pairs={{0,2},{1,3},{2,0},{3,1},{4,6},{5,7},{6,4},{7,5},{8,10},{9,11},{10,... | collective-permute-start | bytes 12296 | tf_op jit(solution)/shard_map/ppermute | solution.py:517
  72.1 2.3 %collective-permute-done.25 = f32[8,128]{1,0:T(8,128)S(1)} collective-permute-done((f32[8,128]{1,0:T(8,128)S(1)}, f32[8,128]{1,0:T(8,128)S(1)}, u32[]{:S(2)}, u32[]{:S(2)}) %collective-permute-start.25) | collective-permute-done | bytes 4128 | tf_op jit(solution)/shard_map/ppermute | solution.py:517
  74.3 1.5 %collective-permute-start.26 = (f32[8,128]{1,0:T(8,128)S(1)}, f32[8,128]{1,0:T(8,128)S(1)}, u32[]{:S(2)}, u32[]{:S(2)}) collective-permute-start(f32[8,128]{1,0:T(8,128)S(1)} %add.27), channel_id=1, source_target_pairs={{0,16},{16,0},{1,17},{17,1},{2,18},{18,2},{3,19},{19,3},{4,20},{20... | collective-permute-start | bytes 12296 | tf_op jit(solution)/shard_map/ppermute | solution.py:517
  75.8 2.1 %collective-permute-done.26 = f32[8,128]{1,0:T(8,128)S(1)} collective-permute-done((f32[8,128]{1,0:T(8,128)S(1)}, f32[8,128]{1,0:T(8,128)S(1)}, u32[]{:S(2)}, u32[]{:S(2)}) %collective-permute-start.26) | collective-permute-done | bytes 4128 | tf_op jit(solution)/shard_map/ppermute | solution.py:517
  77.9 4.4 %collective-permute-start.29 = (f32[8,128]{1,0:T(8,128)S(1)}, f32[8,128]{1,0:T(8,128)S(1)}, u32[]{:S(2)}, u32[]{:S(2)}) collective-permute-start(f32[8,128]{1,0:T(8,128)S(1)} %add.28), channel_id=1, source_target_pairs={{0,12},{4,8},{8,4},{12,0},{1,13},{5,9},{9,5},{13,1},{2,14},{6,10},... | collective-permute-start | bytes 12296 | tf_op jit(solution)/shard_map/ppermute | solution.py:517
  82.4 1.5 %collective-permute-done.29 = f32[8,128]{1,0:T(8,128)S(1)} collective-permute-done((f32[8,128]{1,0:T(8,128)S(1)}, f32[8,128]{1,0:T(8,128)S(1)}, u32[]{:S(2)}, u32[]{:S(2)}) %collective-permute-start.29) | collective-permute-done | bytes 4128 | tf_op jit(solution)/shard_map/ppermute | solution.py:517
  84.0 1.5 %shard_map.134 = (f32[160,8,128]{2,1,0:T(8,128)}, f32[160,8,128]{2,1,0:T(8,128)}, f32[160,8,128]{2,1,0:T(8,128)}) custom-call(f32[8,128]{1,0:T(8,128)S(1)} %add_add_fusion.sums_ref, f32[160,8,128]{2,1,0:T(8,128)S(1)} %copy-done.2, f32[160,8,128]{2,1,0:T(8,128)S(1)} %copy-done.1, f32[160,8,128]{2,1,0:T(8,128)S(1)} %copy-done, f32[160,8,128]{2,1,0:T(8,128)S(1)} %bitcast.2), custom_call_target="tpu_custom_call" | custom-call | tf_op jit(solution)/shard_map/pallas_call | solution.py:470
  (72 shorter events, 11.2 us)
Async XLA Ops:
  3.0 4.9 %collective-permute-start = (f32[32,160]{1,0:T(8,128)S(1)}, f32[32,160]{1,0:T(8,128)S(1)}, u32[]{:S(2)}, u32[]{:S(2)}) collective-permute-start(f32[32,160]{1,0:T(8,128)S(1)} %get-tuple-element.32.refs_4_), channel_id=1, source_target_pairs={{0,16},{16,0},{1,17},{17,1},{2,18},{18,2},{3,19},{19,3},{4,20},{20... | collective-permute-start | bytes 61448 | tf_op jit(solution)/shard_map/ppermute | solution.py:489
  7.9 15.0 %copy-start.6 = (s32[20]{0:T(128)S(1)}, s32[20]{0:T(128)}, u32[]{:S(2)}) copy-start(s32[20]{0:T(128)} %eig_ref.1) | copy-start | bytes 244
  8.9 7.9 %collective-permute-start.12 = (f32[4,40,128]{2,1,0:T(8,128)S(1)}, f32[4,40,128]{2,1,0:T(8,128)S(1)}, u32[]{:S(2)}, u32[]{:S(2)}) collective-permute-start(f32[4,40,128]{2,1,0:T(8,128)S(1)} %get-tuple-element.44.carried_ref), channel_id=1, source_target_pairs={{0,4},{1,5},{2,6},{3,7},{16,20},{17,21},{18,22},{19,23}} | collective-permute-start | bytes 245768 | tf_op jit(solution)/shard_map/ppermute | solution.py:506
  13.0 4.6 %collective-permute-start.9 = (f32[4,40,128]{2,1,0:T(8,128)S(1)}, f32[4,40,128]{2,1,0:T(8,128)S(1)}, u32[]{:S(2)}, u32[]{:S(2)}) collective-permute-start(f32[4,40,128]{2,1,0:T(8,128)S(1)} %get-tuple-element.43.carried_ref), channel_id=1, source_target_pairs={{0,4},{1,5},{2,6},{3,7},{16,20},{17,21},{18,22},{19,23}} | collective-permute-start | bytes 245768 | tf_op jit(solution)/shard_map/ppermute | solution.py:506
  14.3 4.1 %collective-permute-start.4 = (f32[4,40,128]{2,1,0:T(8,128)S(1)}, f32[4,40,128]{2,1,0:T(8,128)S(1)}, u32[]{:S(2)}, u32[]{:S(2)}) collective-permute-start(f32[4,40,128]{2,1,0:T(8,128)S(1)} %get-tuple-element.38.carried_ref), channel_id=1, source_target_pairs={{0,4},{1,5},{2,6},{3,7},{16,20},{17,21},{18,22},{19,23}} | collective-permute-start | bytes 245768 | tf_op jit(solution)/shard_map/ppermute | solution.py:506
  15.6 3.7 %collective-permute-start.1 = (f32[4,40,128]{2,1,0:T(8,128)S(1)}, f32[4,40,128]{2,1,0:T(8,128)S(1)}, u32[]{:S(2)}, u32[]{:S(2)}) collective-permute-start(f32[4,40,128]{2,1,0:T(8,128)S(1)} %get-tuple-element.37.carried_ref), channel_id=1, source_target_pairs={{0,4},{1,5},{2,6},{3,7},{16,20},{17,21},{18,22},{19,23}} | collective-permute-start | bytes 245768 | tf_op jit(solution)/shard_map/ppermute | solution.py:506
  16.9 3.1 %collective-permute-start.13 = (f32[4,40,128]{2,1,0:T(8,128)S(1)}, f32[4,40,128]{2,1,0:T(8,128)S(1)}, u32[]{:S(2)}, u32[]{:S(2)}) collective-permute-start(f32[4,40,128]{2,1,0:T(8,128)S(1)} %shard_map.124), channel_id=1, source_target_pairs={{4,8},{5,9},{6,10},{7,11},{20,24},{21,25},{22,26},{23,27}} | collective-permute-start | bytes 245768 | tf_op jit(solution)/shard_map/ppermute | solution.py:506
  17.6 3.1 %collective-permute-start.10 = (f32[4,40,128]{2,1,0:T(8,128)S(1)}, f32[4,40,128]{2,1,0:T(8,128)S(1)}, u32[]{:S(2)}, u32[]{:S(2)}) collective-permute-start(f32[4,40,128]{2,1,0:T(8,128)S(1)} %shard_map.122), channel_id=1, source_target_pairs={{4,8},{5,9},{6,10},{7,11},{20,24},{21,25},{22,26},{23,27}} | collective-permute-start | bytes 245768 | tf_op jit(solution)/shard_map/ppermute | solution.py:506
  18.4 3.0 %collective-permute-start.5 = (f32[4,40,128]{2,1,0:T(8,128)S(1)}, f32[4,40,128]{2,1,0:T(8,128)S(1)}, u32[]{:S(2)}, u32[]{:S(2)}) collective-permute-start(f32[4,40,128]{2,1,0:T(8,128)S(1)} %shard_map.118), channel_id=1, source_target_pairs={{4,8},{5,9},{6,10},{7,11},{20,24},{21,25},{22,26},{23,27}} | collective-permute-start | bytes 245768 | tf_op jit(solution)/shard_map/ppermute | solution.py:506
  19.3 2.8 %collective-permute-start.2 = (f32[4,40,128]{2,1,0:T(8,128)S(1)}, f32[4,40,128]{2,1,0:T(8,128)S(1)}, u32[]{:S(2)}, u32[]{:S(2)}) collective-permute-start(f32[4,40,128]{2,1,0:T(8,128)S(1)} %shard_map.116), channel_id=1, source_target_pairs={{4,8},{5,9},{6,10},{7,11},{20,24},{21,25},{22,26},{23,27}} | collective-permute-start | bytes 245768 | tf_op jit(solution)/shard_map/ppermute | solution.py:506
  20.0 6.8 %collective-permute-start.14 = (f32[4,40,128]{2,1,0:T(8,128)S(1)}, f32[4,40,128]{2,1,0:T(8,128)S(1)}, u32[]{:S(2)}, u32[]{:S(2)}) collective-permute-start(f32[4,40,128]{2,1,0:T(8,128)S(1)} %shard_map.125), channel_id=1, source_target_pairs={{8,12},{9,13},{10,14},{11,15},{24,28},{25,29},{26,30},{27,31}} | collective-permute-start | bytes 245768 | tf_op jit(solution)/shard_map/ppermute | solution.py:506
  20.8 6.1 %collective-permute-start.11 = (f32[4,40,128]{2,1,0:T(8,128)S(1)}, f32[4,40,128]{2,1,0:T(8,128)S(1)}, u32[]{:S(2)}, u32[]{:S(2)}) collective-permute-start(f32[4,40,128]{2,1,0:T(8,128)S(1)} %shard_map.123), channel_id=1, source_target_pairs={{8,12},{9,13},{10,14},{11,15},{24,28},{25,29},{26,30},{27,31}} | collective-permute-start | bytes 245768 | tf_op jit(solution)/shard_map/ppermute | solution.py:506
  21.5 6.4 %collective-permute-start.6 = (f32[4,40,128]{2,1,0:T(8,128)S(1)}, f32[4,40,128]{2,1,0:T(8,128)S(1)}, u32[]{:S(2)}, u32[]{:S(2)}) collective-permute-start(f32[4,40,128]{2,1,0:T(8,128)S(1)} %shard_map.119), channel_id=1, source_target_pairs={{8,12},{9,13},{10,14},{11,15},{24,28},{25,29},{26,30},{27,31}} | collective-permute-start | bytes 245768 | tf_op jit(solution)/shard_map/ppermute | solution.py:506
  22.2 5.7 %collective-permute-start.3 = (f32[4,40,128]{2,1,0:T(8,128)S(1)}, f32[4,40,128]{2,1,0:T(8,128)S(1)}, u32[]{:S(2)}, u32[]{:S(2)}) collective-permute-start(f32[4,40,128]{2,1,0:T(8,128)S(1)} %shard_map.117), channel_id=1, source_target_pairs={{8,12},{9,13},{10,14},{11,15},{24,28},{25,29},{26,30},{27,31}} | collective-permute-start | bytes 245768 | tf_op jit(solution)/shard_map/ppermute | solution.py:506
  27.8 1.6 %collective-permute-start.15 = (f32[8,16,128]{2,1,0:T(8,128)S(1)}, f32[8,16,128]{2,1,0:T(8,128)S(1)}, u32[]{:S(2)}, u32[]{:S(2)}) collective-permute-start(f32[8,16,128]{2,1,0:T(8,128)S(1)} %shard_map.126), channel_id=1, source_target_pairs={{0,1},{1,0},{2,3},{3,2},{4,5},{5,4},{6,7},{7,6},{8,9},{9,8},{10,11... | collective-permute-start | bytes 196616 | tf_op jit(solution)/shard_map/ppermute | solution.py:597
  28.8 2.1 %collective-permute-start.7 = (f32[8,16,128]{2,1,0:T(8,128)S(1)}, f32[8,16,128]{2,1,0:T(8,128)S(1)}, u32[]{:S(2)}, u32[]{:S(2)}) collective-permute-start(f32[8,16,128]{2,1,0:T(8,128)S(1)} %shard_map.120), channel_id=1, source_target_pairs={{0,1},{1,0},{2,3},{3,2},{4,5},{5,4},{6,7},{7,6},{8,9},{9,8},{10,11... | collective-permute-start | bytes 196616 | tf_op jit(solution)/shard_map/ppermute | solution.py:597
  29.4 4.6 %collective-permute-start.16 = (f32[8,16,128]{2,1,0:T(8,128)S(1)}, f32[8,16,128]{2,1,0:T(8,128)S(1)}, u32[]{:S(2)}, u32[]{:S(2)}) collective-permute-start(f32[8,16,128]{2,1,0:T(8,128)S(1)} %add.25.refs_0_), channel_id=1, source_target_pairs={{0,2},{1,3},{2,0},{3,1},{4,6},{5,7},{6,4},{7,5},{8,10},{9,11},{10,... | collective-permute-start | bytes 196616 | tf_op jit(solution)/shard_map/ppermute | solution.py:599
  31.0 4.6 %collective-permute-start.8 = (f32[8,16,128]{2,1,0:T(8,128)S(1)}, f32[8,16,128]{2,1,0:T(8,128)S(1)}, u32[]{:S(2)}, u32[]{:S(2)}) collective-permute-start(f32[8,16,128]{2,1,0:T(8,128)S(1)} %add.24.refs_0_), channel_id=1, source_target_pairs={{0,2},{1,3},{2,0},{3,1},{4,6},{5,7},{6,4},{7,5},{8,10},{9,11},{10,... | collective-permute-start | bytes 196616 | tf_op jit(solution)/shard_map/ppermute | solution.py:599
  34.9 2.3 %collective-permute-start.20 = (f32[4,80,128]{2,1,0:T(8,128)S(1)}, f32[4,80,128]{2,1,0:T(8,128)S(1)}, u32[]{:S(2)}, u32[]{:S(2)}) collective-permute-start(f32[4,80,128]{2,1,0:T(8,128)S(1)} %get-tuple-element.48.carried_ref), channel_id=1, source_target_pairs={{12,8},{13,9},{14,10},{15,11},{28,24},{29,25},{30,26},{31,27}} | collective-permute-start | bytes 491528 | tf_op jit(solution)/shard_map/ppermute | solution.py:506
  36.5 1.4 %collective-permute-start.17 = (f32[4,80,128]{2,1,0:T(8,128)S(1)}, f32[4,80,128]{2,1,0:T(8,128)S(1)}, u32[]{:S(2)}, u32[]{:S(2)}) collective-permute-start(f32[4,80,128]{2,1,0:T(8,128)S(1)} %get-tuple-element.47.carried_ref), channel_id=1, source_target_pairs={{12,8},{13,9},{14,10},{15,11},{28,24},{29,25},{30,26},{31,27}} | collective-permute-start | bytes 491528 | tf_op jit(solution)/shard_map/ppermute | solution.py:506
  37.2 1.4 %collective-permute-start.21 = (f32[4,80,128]{2,1,0:T(8,128)S(1)}, f32[4,80,128]{2,1,0:T(8,128)S(1)}, u32[]{:S(2)}, u32[]{:S(2)}) collective-permute-start(f32[4,80,128]{2,1,0:T(8,128)S(1)} %shard_map.130), channel_id=1, source_target_pairs={{8,4},{9,5},{10,6},{11,7},{24,20},{25,21},{26,22},{27,23}} | collective-permute-start | bytes 491528 | tf_op jit(solution)/shard_map/ppermute | solution.py:506
  38.0 2.0 %collective-permute-start.18 = (f32[4,80,128]{2,1,0:T(8,128)S(1)}, f32[4,80,128]{2,1,0:T(8,128)S(1)}, u32[]{:S(2)}, u32[]{:S(2)}) collective-permute-start(f32[4,80,128]{2,1,0:T(8,128)S(1)} %shard_map.128), channel_id=1, source_target_pairs={{8,4},{9,5},{10,6},{11,7},{24,20},{25,21},{26,22},{27,23}} | collective-permute-start | bytes 491528 | tf_op jit(solution)/shard_map/ppermute | solution.py:506
  38.7 23.1 %collective-permute-start.22 = (f32[4,80,128]{2,1,0:T(8,128)S(1)}, f32[4,80,128]{2,1,0:T(8,128)S(1)}, u32[]{:S(2)}, u32[]{:S(2)}) collective-permute-start(f32[4,80,128]{2,1,0:T(8,128)S(1)} %shard_map.131), channel_id=1, source_target_pairs={{4,0},{5,1},{6,2},{7,3},{20,16},{21,17},{22,18},{23,19}} | collective-permute-start | bytes 491528 | tf_op jit(solution)/shard_map/ppermute | solution.py:506
  40.1 23.4 %collective-permute-start.19 = (f32[4,80,128]{2,1,0:T(8,128)S(1)}, f32[4,80,128]{2,1,0:T(8,128)S(1)}, u32[]{:S(2)}, u32[]{:S(2)}) collective-permute-start(f32[4,80,128]{2,1,0:T(8,128)S(1)} %shard_map.129), channel_id=1, source_target_pairs={{4,0},{5,1},{6,2},{7,3},{20,16},{21,17},{22,18},{23,19}} | collective-permute-start | bytes 491528 | tf_op jit(solution)/shard_map/ppermute | solution.py:506
  64.8 19.2 %copy-start.2 = (f32[160,8,128]{2,1,0:T(8,128)S(1)}, f32[160,8,128]{2,1,0:T(8,128)}, u32[]{:S(2)}) copy-start(f32[160,8,128]{2,1,0:T(8,128)} %control_ref.1) | copy-start | bytes 1966084
  64.8 4.0 %collective-permute-start.23 = (f32[32,160]{1,0:T(8,128)S(1)}, f32[32,160]{1,0:T(8,128)S(1)}, u32[]{:S(2)}, u32[]{:S(2)}) collective-permute-start(f32[32,160]{1,0:T(8,128)S(1)} %get-tuple-element.50.refs_5_), channel_id=1, source_target_pairs={{0,16},{16,0},{1,17},{17,1},{2,18},{18,2},{3,19},{19,3},{4,20},{20... | collective-permute-start | bytes 61448 | tf_op jit(solution)/shard_map/ppermute | solution.py:489
  69.5 1.2 %collective-permute-start.24 = (f32[8,128]{1,0:T(8,128)S(1)}, f32[8,128]{1,0:T(8,128)S(1)}, u32[]{:S(2)}, u32[]{:S(2)}) collective-permute-start(f32[8,128]{1,0:T(8,128)S(1)} %get-tuple-element.51), channel_id=1, source_target_pairs={{0,1},{1,0},{2,3},{3,2},{4,5},{5,4},{6,7},{7,6},{8,9},{9,8},{10,11... | collective-permute-start | bytes 12296 | tf_op jit(solution)/shard_map/ppermute | solution.py:517
  70.7 3.6 %collective-permute-start.25 = (f32[8,128]{1,0:T(8,128)S(1)}, f32[8,128]{1,0:T(8,128)S(1)}, u32[]{:S(2)}, u32[]{:S(2)}) collective-permute-start(f32[8,128]{1,0:T(8,128)S(1)} %add.26), channel_id=1, source_target_pairs={{0,2},{1,3},{2,0},{3,1},{4,6},{5,7},{6,4},{7,5},{8,10},{9,11},{10,... | collective-permute-start | bytes 12296 | tf_op jit(solution)/shard_map/ppermute | solution.py:517
  74.3 3.6 %collective-permute-start.26 = (f32[8,128]{1,0:T(8,128)S(1)}, f32[8,128]{1,0:T(8,128)S(1)}, u32[]{:S(2)}, u32[]{:S(2)}) collective-permute-start(f32[8,128]{1,0:T(8,128)S(1)} %add.27), channel_id=1, source_target_pairs={{0,16},{16,0},{1,17},{17,1},{2,18},{18,2},{3,19},{19,3},{4,20},{20... | collective-permute-start | bytes 12296 | tf_op jit(solution)/shard_map/ppermute | solution.py:517
  77.9 4.4 %collective-permute-start.27 = (f32[8,128]{1,0:T(8,128)S(1)}, f32[8,128]{1,0:T(8,128)S(1)}, u32[]{:S(2)}, u32[]{:S(2)}) collective-permute-start(f32[8,128]{1,0:T(8,128)S(1)} %add.28), channel_id=1, source_target_pairs={{0,4},{4,0},{8,12},{12,8},{1,5},{5,1},{9,13},{13,9},{2,6},{6,2},{1... | collective-permute-start | bytes 12296 | tf_op jit(solution)/shard_map/ppermute | solution.py:517
  77.9 4.5 %collective-permute-start.28 = (f32[8,128]{1,0:T(8,128)S(1)}, f32[8,128]{1,0:T(8,128)S(1)}, u32[]{:S(2)}, u32[]{:S(2)}) collective-permute-start(f32[8,128]{1,0:T(8,128)S(1)} %add.28), channel_id=1, source_target_pairs={{0,8},{4,12},{8,0},{12,4},{1,9},{5,13},{9,1},{13,5},{2,10},{6,14},... | collective-permute-start | bytes 12296 | tf_op jit(solution)/shard_map/ppermute | solution.py:517
  77.9 6.0 %collective-permute-start.29 = (f32[8,128]{1,0:T(8,128)S(1)}, f32[8,128]{1,0:T(8,128)S(1)}, u32[]{:S(2)}, u32[]{:S(2)}) collective-permute-start(f32[8,128]{1,0:T(8,128)S(1)} %add.28), channel_id=1, source_target_pairs={{0,12},{4,8},{8,4},{12,0},{1,13},{5,9},{9,5},{13,1},{2,14},{6,10},... | collective-permute-start | bytes 12296 | tf_op jit(solution)/shard_map/ppermute | solution.py:517
  (5 other events, 42.5 us)

commit v8 on v7

--- a/solution.py
+++ b/solution.py
@@ -242,26 +242,24 @@
 def spread_modes(v, pairs, transposed):
     source = v.T if transposed else v
     r, c = source.shape
-    shape = (pairs * r, 3 * pairs * c)
-    num = lambda shape, dim: lax.broadcasted_iota(jnp.int32, shape, dim)
+    rows, columns = pairs * r, 3 * pairs * c
     exact = functools.partial(jnp.dot, precision=lax.Precision.HIGHEST, preferred_element_type=f32)
-    pick_row = (lax.rem(num((shape[0], r), 0), r) == num((shape[0], r), 1)).astype(f32)
-    pick_column = (num((c, shape[1]), 0) == lax.rem(num((c, shape[1]), 1), c)).astype(f32)
+    block = lambda at, size: jnp.floor((at + 0.5) * (1.0 / size))
+    at_row, at_column = iota((rows, r), 0), iota((c, columns), 1)
+    pick_row = (at_row - block(at_row, r) * r == iota((rows, r), 1)).astype(f32)
+    pick_column = (at_column - block(at_column, c) * c == iota((c, columns), 0)).astype(f32)
     everywhere = exact(exact(pick_row, source), pick_column)
-    row, column = num(shape, 0), num(shape, 1)
-    place = lax.rem(column, pairs * c)
-    own = (place >= (row // r) * c) & (place < (row // r + 1) * c)
+    column = iota((1, columns), 1)
+    part = block(column, pairs * c)
+    own = block(iota((rows, 1), 0), r) == block(column - part * (pairs * c), c)
     full = jnp.where(own, everywhere, 0.0)
     high, low = halves(full)
-    middle = (column >= pairs * c) & (column < 2 * pairs * c)
-    return jnp.where(middle, low.astype(f32), high.astype(f32)).astype(bf16)
-
-
-def k_prepare(m_ref, lon_ref, v_ref, eig_ref, a_ref, b_ref, mask_ref, out_modes_ref, in_modes_ref, table_ref):
-    members, levels, rows, cells = m_ref.shape
-    pairs = members // 2
+    return jnp.where(part == 1.0, low.astype(f32), high.astype(f32)).astype(bf16)
+
+
+def k_modes(pairs, v_ref, eig_ref, mask_ref, out_modes_ref, in_modes_ref):
     modes = v_ref.shape[0]
-    lon_tables(lon_ref[...], *lon_ref.shape, True, table_ref)
+    cells = mask_ref.shape[1]
     v = v_ref[...]
     out_modes_ref[...] = spread_modes(v, pairs, True)
     in_modes_ref[...] = spread_modes(v, pairs, False)
@@ -270,6 +268,12 @@
     for m in range(pairs):
         used = jnp.where(low, eig_ref[m], eig_ref[m + pairs])
         mask_ref[m * modes : (m + 1) * modes] = jnp.where(e < used, 1.0, 0.0)
+
+
+def k_prepare(m_ref, lon_ref, a_ref, b_ref, table_ref):
+    members, levels, rows, _ = m_ref.shape
+    pairs = members // 2
+    lon_tables(lon_ref[...], *lon_ref.shape, True, table_ref)
     apart = pairs * levels
 
     def step(i, carry):
@@ -546,7 +550,7 @@
     n_lon, n_mem = lax.axis_size("lon"), lax.axis_size("mem")
     half = k // 2
     pairs = mcount // 2
-    chunks, back_chunks = 2, 1
+    chunks, back_chunks = 2, 2
     states = lambda chunks: (sds(4, half // chunks, cells),) * chunks
 
     decays = jnp.concatenate([lat_decay, lon_decay]).reshape(1, cells + rows)
@@ -559,17 +563,22 @@
     inside, carried = call(
         functools.partial(k_lon_fwd, rows, k, cells), (sds(rows, k, cells), sds(4 * rows, k)), [direction, tables]
     )
-    *packed, mask, out_modes, in_modes, back_tables = call(
+    *packed, back_tables = call(
         k_prepare,
         (sds(rows * pairs * levels, cells),) * 2
-        + (
+        + (jax.ShapeDtypeStruct((rows, 3 * cells, 2 * cells), bf16),),
+        [members, lonc],
+        cost=10**9,
+    )
+    mask, out_modes, in_modes = call(
+        functools.partial(k_modes, pairs),
+        (
             sds(half, cells),
             jax.ShapeDtypeStruct((pairs * levels, 3 * half), bf16),
             jax.ShapeDtypeStruct((half, 3 * pairs * levels), bf16),
-            jax.ShapeDtypeStruct((rows, 3 * cells, 2 * cells), bf16),
         ),
-        [members, lonc, vert_modes, eig_count],
-        specs=[VM, VM, VM, SM],
+        [vert_modes, eig_count],
+        specs=[VM, SM],
         cost=10**9,
     )
     blocks = lon_exchange(carried, False)

time: 85.9 us -> 81.5 us (0.949)
  waiting for transfers between devices: 36.1 us -> 25.7 us
  starting transfers between devices: 33.4 us -> 39.1 us
    ppermute x18 -> x24, waiting for transfers between devices: 22.5 us -> 12.5 us  [lat_carry(): got[c][i].append(lax.ppermute(v, 'lat', [(at(h), at(h + 1))]))]
    ppermute x18 -> x24, starting transfers between devices: 18.5 us -> 23.7 us  [lat_carry(): got[c][i].append(lax.ppermute(v, 'lat', [(at(h), at(h + 1))]))]
    pallas_call x23 -> x28, Pallas kernels: 13.4 us -> 13.6 us  [call(): pl.pallas_call(body, out_shape=outs, in_specs=specs or [VM] * len(ins), o...]
  transfers between devices with their start and end apart: 30 -> 36, of which waited for: 12 -> 14; matrix products, arithmetic and copies ran while one was open for 0% -> 0% of each run, Pallas kernels for 9% -> 10%
where the time goes in v8:
time: 81.5 us; the launch traced here: 81 us
  starting transfers between devices  39.1 us (48%)
  waiting for transfers between devices  25.7 us (32%)
  Pallas kernels  13.6 us (17%)
  between operations  1.23 us (2%)
    ppermute x24, starting transfers between devices, lat_carry(): got[c][i].append(lax.ppermute(v, 'lat', [(at(h), at(h + 1))]))  23.7 us
    pallas_call x28, Pallas kernels, call(): pl.pallas_call(body, out_shape=outs, in_specs=specs or [VM] * len(ins), o...  13.6 us
    ppermute x24, waiting for transfers between devices, lat_carry(): got[c][i].append(lax.ppermute(v, 'lat', [(at(h), at(h + 1))]))  12.5 us
    ppermute x6, starting transfers between devices, all_sum(): lax.ppermute(v, axes, [(i, i ^ m) for i in range(total)])  7.75 us
    ppermute x6, waiting for transfers between devices, all_sum(): lax.ppermute(v, axes, [(i, i ^ m) for i in range(total)])  6.69 us
    ppermute x2, starting transfers between devices, lon_exchange(): lax.ppermute(carried, 'lon', [(j, (j + sign * r) % n) for j in range(n)])  4.54 us
    ppermute x2, waiting for transfers between devices, lon_exchange(): lax.ppermute(carried, 'lon', [(j, (j + sign * r) % n) for j in range(n)])  4.32 us
    ppermute x2, starting transfers between devices, iteration(): other = lax.ppermute(v, 'mem', [(i, i ^ step) for i in range(n_mem)])  2.47 us
  transfers between devices with their start and end apart: 36, of which 14 were waited for; matrix products, arithmetic and copies ran while one was open for 0% of the time, Pallas kernels for 10%

profile of v8, /device:TPU:0, one launch (start us, length us, event | category | flops | bytes accessed | tf_op | source)
XLA Modules:
  0.0 81.0 jit_solution(14769451402742311356)
XLA Ops:
  3.0 3.0 %collective-permute-start = (f32[32,160]{1,0:T(8,128)S(1)}, f32[32,160]{1,0:T(8,128)S(1)}, u32[]{:S(2)}, u32[]{:S(2)}) collective-permute-start(f32[32,160]{1,0:T(8,128)S(1)} %get-tuple-element.34.refs_4_), channel_id=1, source_target_pairs={{0,16},{16,0},{1,17},{17,1},{2,18},{18,2},{3,19},{19,3},{4,20},{20... | collective-permute-start | bytes 61448 | tf_op jit(solution)/shard_map/ppermute | solution.py:493
  6.0 1.9 %collective-permute-done.refs_3_ = f32[32,160]{1,0:T(8,128)S(1)} collective-permute-done((f32[32,160]{1,0:T(8,128)S(1)}, f32[32,160]{1,0:T(8,128)S(1)}, u32[]{:S(2)}, u32[]{:S(2)}) %collective-permute-start) | collective-permute-done | bytes 20512 | tf_op jit(solution)/shard_map/ppermute | solution.py:493
  7.9 1.1 %shard_map.114 = (f32[8,80,128]{2,1,0:T(8,128)S(1)}, f32[8,80,128]{2,1,0:T(8,128)S(1)}, f32[4,40,128]{2,1,0:T(8,128)S(1)}, f32[4,40,128]{2,1,0:T(8,128)S(1)}, f3...) custom-call(f32[8,160,128]{2,1,0:T(8,128)S(1)} %get-tuple-element.31.refs_0_, ...), custom_call_target="tpu_custom_call" | custom-call | tf_op jit(solution)/shard_map/pallas_call | solution.py:474
  9.0 4.0 %collective-permute-start.12 = (f32[4,40,128]{2,1,0:T(8,128)S(1)}, f32[4,40,128]{2,1,0:T(8,128)S(1)}, u32[]{:S(2)}, u32[]{:S(2)}) collective-permute-start(f32[4,40,128]{2,1,0:T(8,128)S(1)} %get-tuple-element.46.carried_ref), channel_id=1, source_target_pairs={{0,4},{1,5},{2,6},{3,7},{16,20},{17,21},{18,22},{19,23}} | collective-permute-start | bytes 245768 | tf_op jit(solution)/shard_map/ppermute | solution.py:510
  13.0 1.3 %collective-permute-start.9 = (f32[4,40,128]{2,1,0:T(8,128)S(1)}, f32[4,40,128]{2,1,0:T(8,128)S(1)}, u32[]{:S(2)}, u32[]{:S(2)}) collective-permute-start(f32[4,40,128]{2,1,0:T(8,128)S(1)} %get-tuple-element.45.carried_ref), channel_id=1, source_target_pairs={{0,4},{1,5},{2,6},{3,7},{16,20},{17,21},{18,22},{19,23}} | collective-permute-start | bytes 245768 | tf_op jit(solution)/shard_map/ppermute | solution.py:510
  14.3 1.3 %collective-permute-start.4 = (f32[4,40,128]{2,1,0:T(8,128)S(1)}, f32[4,40,128]{2,1,0:T(8,128)S(1)}, u32[]{:S(2)}, u32[]{:S(2)}) collective-permute-start(f32[4,40,128]{2,1,0:T(8,128)S(1)} %get-tuple-element.40.carried_ref), channel_id=1, source_target_pairs={{0,4},{1,5},{2,6},{3,7},{16,20},{17,21},{18,22},{19,23}} | collective-permute-start | bytes 245768 | tf_op jit(solution)/shard_map/ppermute | solution.py:510
  15.6 1.3 %collective-permute-start.1 = (f32[4,40,128]{2,1,0:T(8,128)S(1)}, f32[4,40,128]{2,1,0:T(8,128)S(1)}, u32[]{:S(2)}, u32[]{:S(2)}) collective-permute-start(f32[4,40,128]{2,1,0:T(8,128)S(1)} %get-tuple-element.39.carried_ref), channel_id=1, source_target_pairs={{0,4},{1,5},{2,6},{3,7},{16,20},{17,21},{18,22},{19,23}} | collective-permute-start | bytes 245768 | tf_op jit(solution)/shard_map/ppermute | solution.py:510
  20.0 2.4 %shard_map.115 = (f32[2560,128]{1,0:T(8,128)S(1)}, f32[2560,128]{1,0:T(8,128)S(1)}, bf16[8,384,256]{2,1,0:T(8,128)(2,1)S(1)}) custom-call(bf16[20,32,8,128]{3,2,1,0:T(8,128)(2,1)S(1)} %copy-done.4, f32[8,128]{1,0:T(8,128)S(1)} %get-tuple-element.32.refs_1_.lon_ref), custom_call_target="tpu_custom_call" | custom-call | flops 1000000000 | bytes 1000 | tf_op jit(solution)/shard_map/pallas_call | solution.py:474
  25.4 1.6 %shard_map.116 = (f32[80,128]{1,0:T(8,128)S(1)}, bf16[320,240]{1,0:T(8,128)(2,1)S(1)}, bf16[80,960]{1,0:T(8,128)(2,1)S(1)}) custom-call(f32[8,32]{1,0:T(8,128)S(1)} %copy-done.5, s32[20]{0:T(128)S(1)} %copy-done.6), custom_call_target="tpu_custom_call" | custom-call | flops 1000000000 | bytes 1000 | tf_op jit(solution)/shard_map/pallas_call | solution.py:474
  27.0 0.9 %shard_map.127 = f32[8,16,128]{2,1,0:T(8,128)S(1)} custom-call(f32[8,80,128]{2,1,0:T(8,128)S(1)} %get-tuple-element.43.refs_0_, f32[2,8,128]{2,1,0:T(8,128)S(1)} %get-tuple-element.33.refs_2_.lat_ref.refs_1_.refs_6_, f32[2560,128]{1,0:T(8,128)S(1)} %get-tuple-element.44.refs_2_.refs_3_, f32[80,128]{1,0:T(8,128)S(1)} %get-tuple-element.37.refs_3_.refs_4_, ...), custom_call_target="tpu_custom_call" | custom-call | tf_op jit(solution)/shard_map/pallas_call | solution.py:474
  28.0 0.9 %shard_map.121 = f32[8,16,128]{2,1,0:T(8,128)S(1)} custom-call(f32[8,80,128]{2,1,0:T(8,128)S(1)} %get-tuple-element.35.refs_0_, f32[2,8,128]{2,1,0:T(8,128)S(1)} %get-tuple-element.33.refs_2_.lat_ref.refs_1_.refs_6_, f32[2560,128]{1,0:T(8,128)S(1)} %get-tuple-element.36.refs_2_.refs_3_, f32[80,128]{1,0:T(8,128)S(1)} %get-tuple-element.37.refs_3_.refs_4_, ...), custom_call_target="tpu_custom_call" | custom-call | tf_op jit(solution)/shard_map/pallas_call | solution.py:474
  29.5 1.6 %collective-permute-start.16 = (f32[8,16,128]{2,1,0:T(8,128)S(1)}, f32[8,16,128]{2,1,0:T(8,128)S(1)}, u32[]{:S(2)}, u32[]{:S(2)}) collective-permute-start(f32[8,16,128]{2,1,0:T(8,128)S(1)} %add.25.refs_0_), channel_id=1, source_target_pairs={{0,2},{1,3},{2,0},{3,1},{4,6},{5,7},{6,4},{7,5},{8,10},{9,11},{10,... | collective-permute-start | bytes 196616 | tf_op jit(solution)/shard_map/ppermute | solution.py:608
  32.0 2.2 %collective-permute-done.16.refs_1_ = f32[8,16,128]{2,1,0:T(8,128)S(1)} collective-permute-done((f32[8,16,128]{2,1,0:T(8,128)S(1)}, f32[8,16,128]{2,1,0:T(8,128)S(1)}, u32[]{:S(2)}, u32[]{:S(2)}) %collective-permute-start.16) | collective-permute-done | bytes 65568 | tf_op jit(solution)/shard_map/ppermute | solution.py:608
  36.4 0.9 %shard_map.122 = (f32[8,80,128]{2,1,0:T(8,128)S(1)}, f32[4,40,128]{2,1,0:T(8,128)S(1)}, f32[4,40,128]{2,1,0:T(8,128)S(1)}) custom-call(f32[8,16,128]{2,1,0:T(8,128)S(1)} %add.24.refs_0_, f32[8,16,128]{2,1,0:T(8,128)S(1)} %collective-permute-done.8.refs_1_, f32[32,8,128]{2,1,0:T(8,128)S(1)} %copy-done.3, f32[2560,128]{1,0:T(8,128)S(1)} %get-tuple-element.36.refs_2_.refs_3_, ...), custom_call_target="tpu_custom_call" | custom-call | tf_op jit(solution)/shard_map/pallas_call | solution.py:474
  41.6 1.3 %collective-permute-start.28 = (f32[4,40,128]{2,1,0:T(8,128)S(1)}, f32[4,40,128]{2,1,0:T(8,128)S(1)}, u32[]{:S(2)}, u32[]{:S(2)}) collective-permute-start(f32[4,40,128]{2,1,0:T(8,128)S(1)} %shard_map.136), channel_id=1, source_target_pairs={{4,0},{5,1},{6,2},{7,3},{20,16},{21,17},{22,18},{23,19}} | collective-permute-start | bytes 245768 | tf_op jit(solution)/shard_map/ppermute | solution.py:510
  42.9 1.3 %collective-permute-start.25 = (f32[4,40,128]{2,1,0:T(8,128)S(1)}, f32[4,40,128]{2,1,0:T(8,128)S(1)}, u32[]{:S(2)}, u32[]{:S(2)}) collective-permute-start(f32[4,40,128]{2,1,0:T(8,128)S(1)} %shard_map.134), channel_id=1, source_target_pairs={{4,0},{5,1},{6,2},{7,3},{20,16},{21,17},{22,18},{23,19}} | collective-permute-start | bytes 245768 | tf_op jit(solution)/shard_map/ppermute | solution.py:510
  44.3 1.3 %collective-permute-start.22 = (f32[4,40,128]{2,1,0:T(8,128)S(1)}, f32[4,40,128]{2,1,0:T(8,128)S(1)}, u32[]{:S(2)}, u32[]{:S(2)}) collective-permute-start(f32[4,40,128]{2,1,0:T(8,128)S(1)} %shard_map.132), channel_id=1, source_target_pairs={{4,0},{5,1},{6,2},{7,3},{20,16},{21,17},{22,18},{23,19}} | collective-permute-start | bytes 245768 | tf_op jit(solution)/shard_map/ppermute | solution.py:510
  45.6 1.3 %collective-permute-start.19 = (f32[4,40,128]{2,1,0:T(8,128)S(1)}, f32[4,40,128]{2,1,0:T(8,128)S(1)}, u32[]{:S(2)}, u32[]{:S(2)}) collective-permute-start(f32[4,40,128]{2,1,0:T(8,128)S(1)} %shard_map.130), channel_id=1, source_target_pairs={{4,0},{5,1},{6,2},{7,3},{20,16},{21,17},{22,18},{23,19}} | collective-permute-start | bytes 245768 | tf_op jit(solution)/shard_map/ppermute | solution.py:510
  46.9 7.3 %collective-permute-done.28.refs_15_ = f32[4,40,128]{2,1,0:T(8,128)S(1)} collective-permute-done((f32[4,40,128]{2,1,0:T(8,128)S(1)}, f32[4,40,128]{2,1,0:T(8,128)S(1)}, u32[]{:S(2)}, u32[]{:S(2)}) %collective-permute-start.28) | collective-permute-done | bytes 81952 | tf_op jit(solution)/shard_map/ppermute | solution.py:510
  54.3 3.0 %collective-permute-done.25.refs_12_ = f32[4,40,128]{2,1,0:T(8,128)S(1)} collective-permute-done((f32[4,40,128]{2,1,0:T(8,128)S(1)}, f32[4,40,128]{2,1,0:T(8,128)S(1)}, u32[]{:S(2)}, u32[]{:S(2)}) %collective-permute-start.25) | collective-permute-done | bytes 81952 | tf_op jit(solution)/shard_map/ppermute | solution.py:510
  58.2 0.9 %collective-permute-done.19.refs_6_ = f32[4,40,128]{2,1,0:T(8,128)S(1)} collective-permute-done((f32[4,40,128]{2,1,0:T(8,128)S(1)}, f32[4,40,128]{2,1,0:T(8,128)S(1)}, u32[]{:S(2)}, u32[]{:S(2)}) %collective-permute-start.19) | collective-permute-done | bytes 81952 | tf_op jit(solution)/shard_map/ppermute | solution.py:510
  59.1 1.2 %shard_map.137 = (f32[8,160,128]{2,1,0:T(8,128)S(1)}, f32[32,160]{1,0:T(8,128)S(1)}) custom-call(f32[8,80,128]{2,1,0:T(8,128)S(1)} %get-tuple-element.42.refs_0_, f32[8,80,128]{2,1,0:T(8,128)S(1)} %get-tuple-element.47.refs_1_, f32[2,8,128]{2,1,0:T(8,128)S(1)} %get-tuple-element.33.refs_2_.lat_ref.refs_1_.refs_6_, ...), custom_call_target="tpu_custom_call" | custom-call | tf_op jit(solution)/shard_map/pallas_call | solution.py:474
  60.3 1.5 %collective-permute-start.29 = (f32[32,160]{1,0:T(8,128)S(1)}, f32[32,160]{1,0:T(8,128)S(1)}, u32[]{:S(2)}, u32[]{:S(2)}) collective-permute-start(f32[32,160]{1,0:T(8,128)S(1)} %get-tuple-element.54.refs_5_), channel_id=1, source_target_pairs={{0,16},{16,0},{1,17},{17,1},{2,18},{18,2},{3,19},{19,3},{4,20},{20... | collective-permute-start | bytes 61448 | tf_op jit(solution)/shard_map/ppermute | solution.py:493
  61.9 2.4 %collective-permute-done.29.refs_4_ = f32[32,160]{1,0:T(8,128)S(1)} collective-permute-done((f32[32,160]{1,0:T(8,128)S(1)}, f32[32,160]{1,0:T(8,128)S(1)}, u32[]{:S(2)}, u32[]{:S(2)}) %collective-permute-start.29) | collective-permute-done | bytes 20512 | tf_op jit(solution)/shard_map/ppermute | solution.py:493
  65.1 1.2 %collective-permute-done.30 = f32[8,128]{1,0:T(8,128)S(1)} collective-permute-done((f32[8,128]{1,0:T(8,128)S(1)}, f32[8,128]{1,0:T(8,128)S(1)}, u32[]{:S(2)}, u32[]{:S(2)}) %collective-permute-start.30) | collective-permute-done | bytes 4128 | tf_op jit(solution)/shard_map/ppermute | solution.py:521
  66.3 1.8 %collective-permute-start.31 = (f32[8,128]{1,0:T(8,128)S(1)}, f32[8,128]{1,0:T(8,128)S(1)}, u32[]{:S(2)}, u32[]{:S(2)}) collective-permute-start(f32[8,128]{1,0:T(8,128)S(1)} %add.26), channel_id=1, source_target_pairs={{0,2},{1,3},{2,0},{3,1},{4,6},{5,7},{6,4},{7,5},{8,10},{9,11},{10,... | collective-permute-start | bytes 12296 | tf_op jit(solution)/shard_map/ppermute | solution.py:521
  68.1 1.8 %collective-permute-done.31 = f32[8,128]{1,0:T(8,128)S(1)} collective-permute-done((f32[8,128]{1,0:T(8,128)S(1)}, f32[8,128]{1,0:T(8,128)S(1)}, u32[]{:S(2)}, u32[]{:S(2)}) %collective-permute-start.31) | collective-permute-done | bytes 4128 | tf_op jit(solution)/shard_map/ppermute | solution.py:521
  69.9 1.5 %collective-permute-start.32 = (f32[8,128]{1,0:T(8,128)S(1)}, f32[8,128]{1,0:T(8,128)S(1)}, u32[]{:S(2)}, u32[]{:S(2)}) collective-permute-start(f32[8,128]{1,0:T(8,128)S(1)} %add.27), channel_id=1, source_target_pairs={{0,16},{16,0},{1,17},{17,1},{2,18},{18,2},{3,19},{19,3},{4,20},{20... | collective-permute-start | bytes 12296 | tf_op jit(solution)/shard_map/ppermute | solution.py:521
  71.4 2.1 %collective-permute-done.32 = f32[8,128]{1,0:T(8,128)S(1)} collective-permute-done((f32[8,128]{1,0:T(8,128)S(1)}, f32[8,128]{1,0:T(8,128)S(1)}, u32[]{:S(2)}, u32[]{:S(2)}) %collective-permute-start.32) | collective-permute-done | bytes 4128 | tf_op jit(solution)/shard_map/ppermute | solution.py:521
  73.5 4.4 %collective-permute-start.35 = (f32[8,128]{1,0:T(8,128)S(1)}, f32[8,128]{1,0:T(8,128)S(1)}, u32[]{:S(2)}, u32[]{:S(2)}) collective-permute-start(f32[8,128]{1,0:T(8,128)S(1)} %add.28), channel_id=1, source_target_pairs={{0,12},{4,8},{8,4},{12,0},{1,13},{5,9},{9,5},{13,1},{2,14},{6,10},... | collective-permute-start | bytes 12296 | tf_op jit(solution)/shard_map/ppermute | solution.py:521
  78.0 1.5 %collective-permute-done.35 = f32[8,128]{1,0:T(8,128)S(1)} collective-permute-done((f32[8,128]{1,0:T(8,128)S(1)}, f32[8,128]{1,0:T(8,128)S(1)}, u32[]{:S(2)}, u32[]{:S(2)}) %collective-permute-start.35) | collective-permute-done | bytes 4128 | tf_op jit(solution)/shard_map/ppermute | solution.py:521
  79.5 1.5 %shard_map.139 = (f32[160,8,128]{2,1,0:T(8,128)}, f32[160,8,128]{2,1,0:T(8,128)}, f32[160,8,128]{2,1,0:T(8,128)}) custom-call(f32[8,128]{1,0:T(8,128)S(1)} %add_add_fusion.sums_ref, f32[160,8,128]{2,1,0:T(8,128)S(1)} %copy-done.2, f32[160,8,128]{2,1,0:T(8,128)S(1)} %copy-done.1, f32[160,8,128]{2,1,0:T(8,128)S(1)} %copy-done, f32[160,8,128]{2,1,0:T(8,128)S(1)} %bitcast.2), custom_call_target="tpu_custom_call" | custom-call | tf_op jit(solution)/shard_map/pallas_call | solution.py:474
  (89 shorter events, 18.0 us)
Async XLA Ops:
  3.0 4.9 %collective-permute-start = (f32[32,160]{1,0:T(8,128)S(1)}, f32[32,160]{1,0:T(8,128)S(1)}, u32[]{:S(2)}, u32[]{:S(2)}) collective-permute-start(f32[32,160]{1,0:T(8,128)S(1)} %get-tuple-element.34.refs_4_), channel_id=1, source_target_pairs={{0,16},{16,0},{1,17},{17,1},{2,18},{18,2},{3,19},{19,3},{4,20},{20... | collective-permute-start | bytes 61448 | tf_op jit(solution)/shard_map/ppermute | solution.py:493
  9.0 7.9 %collective-permute-start.12 = (f32[4,40,128]{2,1,0:T(8,128)S(1)}, f32[4,40,128]{2,1,0:T(8,128)S(1)}, u32[]{:S(2)}, u32[]{:S(2)}) collective-permute-start(f32[4,40,128]{2,1,0:T(8,128)S(1)} %get-tuple-element.46.carried_ref), channel_id=1, source_target_pairs={{0,4},{1,5},{2,6},{3,7},{16,20},{17,21},{18,22},{19,23}} | collective-permute-start | bytes 245768 | tf_op jit(solution)/shard_map/ppermute | solution.py:510
  13.0 4.6 %collective-permute-start.9 = (f32[4,40,128]{2,1,0:T(8,128)S(1)}, f32[4,40,128]{2,1,0:T(8,128)S(1)}, u32[]{:S(2)}, u32[]{:S(2)}) collective-permute-start(f32[4,40,128]{2,1,0:T(8,128)S(1)} %get-tuple-element.45.carried_ref), channel_id=1, source_target_pairs={{0,4},{1,5},{2,6},{3,7},{16,20},{17,21},{18,22},{19,23}} | collective-permute-start | bytes 245768 | tf_op jit(solution)/shard_map/ppermute | solution.py:510
  14.3 4.1 %collective-permute-start.4 = (f32[4,40,128]{2,1,0:T(8,128)S(1)}, f32[4,40,128]{2,1,0:T(8,128)S(1)}, u32[]{:S(2)}, u32[]{:S(2)}) collective-permute-start(f32[4,40,128]{2,1,0:T(8,128)S(1)} %get-tuple-element.40.carried_ref), channel_id=1, source_target_pairs={{0,4},{1,5},{2,6},{3,7},{16,20},{17,21},{18,22},{19,23}} | collective-permute-start | bytes 245768 | tf_op jit(solution)/shard_map/ppermute | solution.py:510
  15.6 3.7 %collective-permute-start.1 = (f32[4,40,128]{2,1,0:T(8,128)S(1)}, f32[4,40,128]{2,1,0:T(8,128)S(1)}, u32[]{:S(2)}, u32[]{:S(2)}) collective-permute-start(f32[4,40,128]{2,1,0:T(8,128)S(1)} %get-tuple-element.39.carried_ref), channel_id=1, source_target_pairs={{0,4},{1,5},{2,6},{3,7},{16,20},{17,21},{18,22},{19,23}} | collective-permute-start | bytes 245768 | tf_op jit(solution)/shard_map/ppermute | solution.py:510
  16.9 5.5 %collective-permute-start.13 = (f32[4,40,128]{2,1,0:T(8,128)S(1)}, f32[4,40,128]{2,1,0:T(8,128)S(1)}, u32[]{:S(2)}, u32[]{:S(2)}) collective-permute-start(f32[4,40,128]{2,1,0:T(8,128)S(1)} %shard_map.125), channel_id=1, source_target_pairs={{4,8},{5,9},{6,10},{7,11},{20,24},{21,25},{22,26},{23,27}} | collective-permute-start | bytes 245768 | tf_op jit(solution)/shard_map/ppermute | solution.py:510
  17.6 5.5 %collective-permute-start.10 = (f32[4,40,128]{2,1,0:T(8,128)S(1)}, f32[4,40,128]{2,1,0:T(8,128)S(1)}, u32[]{:S(2)}, u32[]{:S(2)}) collective-permute-start(f32[4,40,128]{2,1,0:T(8,128)S(1)} %shard_map.123), channel_id=1, source_target_pairs={{4,8},{5,9},{6,10},{7,11},{20,24},{21,25},{22,26},{23,27}} | collective-permute-start | bytes 245768 | tf_op jit(solution)/shard_map/ppermute | solution.py:510
  18.5 5.5 %collective-permute-start.5 = (f32[4,40,128]{2,1,0:T(8,128)S(1)}, f32[4,40,128]{2,1,0:T(8,128)S(1)}, u32[]{:S(2)}, u32[]{:S(2)}) collective-permute-start(f32[4,40,128]{2,1,0:T(8,128)S(1)} %shard_map.119), channel_id=1, source_target_pairs={{4,8},{5,9},{6,10},{7,11},{20,24},{21,25},{22,26},{23,27}} | collective-permute-start | bytes 245768 | tf_op jit(solution)/shard_map/ppermute | solution.py:510
  19.4 5.3 %collective-permute-start.2 = (f32[4,40,128]{2,1,0:T(8,128)S(1)}, f32[4,40,128]{2,1,0:T(8,128)S(1)}, u32[]{:S(2)}, u32[]{:S(2)}) collective-permute-start(f32[4,40,128]{2,1,0:T(8,128)S(1)} %shard_map.117), channel_id=1, source_target_pairs={{4,8},{5,9},{6,10},{7,11},{20,24},{21,25},{22,26},{23,27}} | collective-permute-start | bytes 245768 | tf_op jit(solution)/shard_map/ppermute | solution.py:510
  22.5 4.5 %collective-permute-start.14 = (f32[4,40,128]{2,1,0:T(8,128)S(1)}, f32[4,40,128]{2,1,0:T(8,128)S(1)}, u32[]{:S(2)}, u32[]{:S(2)}) collective-permute-start(f32[4,40,128]{2,1,0:T(8,128)S(1)} %shard_map.126), channel_id=1, source_target_pairs={{8,12},{9,13},{10,14},{11,15},{24,28},{25,29},{26,30},{27,31}} | collective-permute-start | bytes 245768 | tf_op jit(solution)/shard_map/ppermute | solution.py:510
  23.2 3.8 %collective-permute-start.11 = (f32[4,40,128]{2,1,0:T(8,128)S(1)}, f32[4,40,128]{2,1,0:T(8,128)S(1)}, u32[]{:S(2)}, u32[]{:S(2)}) collective-permute-start(f32[4,40,128]{2,1,0:T(8,128)S(1)} %shard_map.124), channel_id=1, source_target_pairs={{8,12},{9,13},{10,14},{11,15},{24,28},{25,29},{26,30},{27,31}} | collective-permute-start | bytes 245768 | tf_op jit(solution)/shard_map/ppermute | solution.py:510
  24.0 4.1 %collective-permute-start.6 = (f32[4,40,128]{2,1,0:T(8,128)S(1)}, f32[4,40,128]{2,1,0:T(8,128)S(1)}, u32[]{:S(2)}, u32[]{:S(2)}) collective-permute-start(f32[4,40,128]{2,1,0:T(8,128)S(1)} %shard_map.120), channel_id=1, source_target_pairs={{8,12},{9,13},{10,14},{11,15},{24,28},{25,29},{26,30},{27,31}} | collective-permute-start | bytes 245768 | tf_op jit(solution)/shard_map/ppermute | solution.py:510
  24.7 3.4 %collective-permute-start.3 = (f32[4,40,128]{2,1,0:T(8,128)S(1)}, f32[4,40,128]{2,1,0:T(8,128)S(1)}, u32[]{:S(2)}, u32[]{:S(2)}) collective-permute-start(f32[4,40,128]{2,1,0:T(8,128)S(1)} %shard_map.118), channel_id=1, source_target_pairs={{8,12},{9,13},{10,14},{11,15},{24,28},{25,29},{26,30},{27,31}} | collective-permute-start | bytes 245768 | tf_op jit(solution)/shard_map/ppermute | solution.py:510
  29.5 4.6 %collective-permute-start.16 = (f32[8,16,128]{2,1,0:T(8,128)S(1)}, f32[8,16,128]{2,1,0:T(8,128)S(1)}, u32[]{:S(2)}, u32[]{:S(2)}) collective-permute-start(f32[8,16,128]{2,1,0:T(8,128)S(1)} %add.25.refs_0_), channel_id=1, source_target_pairs={{0,2},{1,3},{2,0},{3,1},{4,6},{5,7},{6,4},{7,5},{8,10},{9,11},{10,... | collective-permute-start | bytes 196616 | tf_op jit(solution)/shard_map/ppermute | solution.py:608
  31.1 5.3 %collective-permute-start.8 = (f32[8,16,128]{2,1,0:T(8,128)S(1)}, f32[8,16,128]{2,1,0:T(8,128)S(1)}, u32[]{:S(2)}, u32[]{:S(2)}) collective-permute-start(f32[8,16,128]{2,1,0:T(8,128)S(1)} %add.24.refs_0_), channel_id=1, source_target_pairs={{0,2},{1,3},{2,0},{3,1},{4,6},{5,7},{6,4},{7,5},{8,10},{9,11},{10,... | collective-permute-start | bytes 196616 | tf_op jit(solution)/shard_map/ppermute | solution.py:608
  35.1 3.6 %collective-permute-start.26 = (f32[4,40,128]{2,1,0:T(8,128)S(1)}, f32[4,40,128]{2,1,0:T(8,128)S(1)}, u32[]{:S(2)}, u32[]{:S(2)}) collective-permute-start(f32[4,40,128]{2,1,0:T(8,128)S(1)} %get-tuple-element.52.carried_ref), channel_id=1, source_target_pairs={{12,8},{13,9},{14,10},{15,11},{28,24},{29,25},{30,26},{31,27}} | collective-permute-start | bytes 245768 | tf_op jit(solution)/shard_map/ppermute | solution.py:510
  35.7 3.7 %collective-permute-start.23 = (f32[4,40,128]{2,1,0:T(8,128)S(1)}, f32[4,40,128]{2,1,0:T(8,128)S(1)}, u32[]{:S(2)}, u32[]{:S(2)}) collective-permute-start(f32[4,40,128]{2,1,0:T(8,128)S(1)} %get-tuple-element.51.carried_ref), channel_id=1, source_target_pairs={{12,8},{13,9},{14,10},{15,11},{28,24},{29,25},{30,26},{31,27}} | collective-permute-start | bytes 245768 | tf_op jit(solution)/shard_map/ppermute | solution.py:510
  38.0 2.8 %collective-permute-start.17 = (f32[4,40,128]{2,1,0:T(8,128)S(1)}, f32[4,40,128]{2,1,0:T(8,128)S(1)}, u32[]{:S(2)}, u32[]{:S(2)}) collective-permute-start(f32[4,40,128]{2,1,0:T(8,128)S(1)} %get-tuple-element.49.carried_ref), channel_id=1, source_target_pairs={{12,8},{13,9},{14,10},{15,11},{28,24},{29,25},{30,26},{31,27}} | collective-permute-start | bytes 245768 | tf_op jit(solution)/shard_map/ppermute | solution.py:510
  38.7 2.8 %collective-permute-start.27 = (f32[4,40,128]{2,1,0:T(8,128)S(1)}, f32[4,40,128]{2,1,0:T(8,128)S(1)}, u32[]{:S(2)}, u32[]{:S(2)}) collective-permute-start(f32[4,40,128]{2,1,0:T(8,128)S(1)} %shard_map.135), channel_id=1, source_target_pairs={{8,4},{9,5},{10,6},{11,7},{24,20},{25,21},{26,22},{27,23}} | collective-permute-start | bytes 245768 | tf_op jit(solution)/shard_map/ppermute | solution.py:510
  39.4 3.5 %collective-permute-start.24 = (f32[4,40,128]{2,1,0:T(8,128)S(1)}, f32[4,40,128]{2,1,0:T(8,128)S(1)}, u32[]{:S(2)}, u32[]{:S(2)}) collective-permute-start(f32[4,40,128]{2,1,0:T(8,128)S(1)} %shard_map.133), channel_id=1, source_target_pairs={{8,4},{9,5},{10,6},{11,7},{24,20},{25,21},{26,22},{27,23}} | collective-permute-start | bytes 245768 | tf_op jit(solution)/shard_map/ppermute | solution.py:510
  40.2 4.1 %collective-permute-start.21 = (f32[4,40,128]{2,1,0:T(8,128)S(1)}, f32[4,40,128]{2,1,0:T(8,128)S(1)}, u32[]{:S(2)}, u32[]{:S(2)}) collective-permute-start(f32[4,40,128]{2,1,0:T(8,128)S(1)} %shard_map.131), channel_id=1, source_target_pairs={{8,4},{9,5},{10,6},{11,7},{24,20},{25,21},{26,22},{27,23}} | collective-permute-start | bytes 245768 | tf_op jit(solution)/shard_map/ppermute | solution.py:510
  40.9 4.7 %collective-permute-start.18 = (f32[4,40,128]{2,1,0:T(8,128)S(1)}, f32[4,40,128]{2,1,0:T(8,128)S(1)}, u32[]{:S(2)}, u32[]{:S(2)}) collective-permute-start(f32[4,40,128]{2,1,0:T(8,128)S(1)} %shard_map.129), channel_id=1, source_target_pairs={{8,4},{9,5},{10,6},{11,7},{24,20},{25,21},{26,22},{27,23}} | collective-permute-start | bytes 245768 | tf_op jit(solution)/shard_map/ppermute | solution.py:510
  41.6 12.7 %collective-permute-start.28 = (f32[4,40,128]{2,1,0:T(8,128)S(1)}, f32[4,40,128]{2,1,0:T(8,128)S(1)}, u32[]{:S(2)}, u32[]{:S(2)}) collective-permute-start(f32[4,40,128]{2,1,0:T(8,128)S(1)} %shard_map.136), channel_id=1, source_target_pairs={{4,0},{5,1},{6,2},{7,3},{20,16},{21,17},{22,18},{23,19}} | collective-permute-start | bytes 245768 | tf_op jit(solution)/shard_map/ppermute | solution.py:510
  42.9 14.3 %collective-permute-start.25 = (f32[4,40,128]{2,1,0:T(8,128)S(1)}, f32[4,40,128]{2,1,0:T(8,128)S(1)}, u32[]{:S(2)}, u32[]{:S(2)}) collective-permute-start(f32[4,40,128]{2,1,0:T(8,128)S(1)} %shard_map.134), channel_id=1, source_target_pairs={{4,0},{5,1},{6,2},{7,3},{20,16},{21,17},{22,18},{23,19}} | collective-permute-start | bytes 245768 | tf_op jit(solution)/shard_map/ppermute | solution.py:510
  44.3 13.9 %collective-permute-start.22 = (f32[4,40,128]{2,1,0:T(8,128)S(1)}, f32[4,40,128]{2,1,0:T(8,128)S(1)}, u32[]{:S(2)}, u32[]{:S(2)}) collective-permute-start(f32[4,40,128]{2,1,0:T(8,128)S(1)} %shard_map.132), channel_id=1, source_target_pairs={{4,0},{5,1},{6,2},{7,3},{20,16},{21,17},{22,18},{23,19}} | collective-permute-start | bytes 245768 | tf_op jit(solution)/shard_map/ppermute | solution.py:510
  45.6 13.5 %collective-permute-start.19 = (f32[4,40,128]{2,1,0:T(8,128)S(1)}, f32[4,40,128]{2,1,0:T(8,128)S(1)}, u32[]{:S(2)}, u32[]{:S(2)}) collective-permute-start(f32[4,40,128]{2,1,0:T(8,128)S(1)} %shard_map.130), channel_id=1, source_target_pairs={{4,0},{5,1},{6,2},{7,3},{20,16},{21,17},{22,18},{23,19}} | collective-permute-start | bytes 245768 | tf_op jit(solution)/shard_map/ppermute | solution.py:510
  60.3 4.0 %collective-permute-start.29 = (f32[32,160]{1,0:T(8,128)S(1)}, f32[32,160]{1,0:T(8,128)S(1)}, u32[]{:S(2)}, u32[]{:S(2)}) collective-permute-start(f32[32,160]{1,0:T(8,128)S(1)} %get-tuple-element.54.refs_5_), channel_id=1, source_target_pairs={{0,16},{16,0},{1,17},{17,1},{2,18},{18,2},{3,19},{19,3},{4,20},{20... | collective-permute-start | bytes 61448 | tf_op jit(solution)/shard_map/ppermute | solution.py:493
  66.3 3.6 %collective-permute-start.31 = (f32[8,128]{1,0:T(8,128)S(1)}, f32[8,128]{1,0:T(8,128)S(1)}, u32[]{:S(2)}, u32[]{:S(2)}) collective-permute-start(f32[8,128]{1,0:T(8,128)S(1)} %add.26), channel_id=1, source_target_pairs={{0,2},{1,3},{2,0},{3,1},{4,6},{5,7},{6,4},{7,5},{8,10},{9,11},{10,... | collective-permute-start | bytes 12296 | tf_op jit(solution)/shard_map/ppermute | solution.py:521
  69.9 3.6 %collective-permute-start.32 = (f32[8,128]{1,0:T(8,128)S(1)}, f32[8,128]{1,0:T(8,128)S(1)}, u32[]{:S(2)}, u32[]{:S(2)}) collective-permute-start(f32[8,128]{1,0:T(8,128)S(1)} %add.27), channel_id=1, source_target_pairs={{0,16},{16,0},{1,17},{17,1},{2,18},{18,2},{3,19},{19,3},{4,20},{20... | collective-permute-start | bytes 12296 | tf_op jit(solution)/shard_map/ppermute | solution.py:521
  73.5 4.4 %collective-permute-start.33 = (f32[8,128]{1,0:T(8,128)S(1)}, f32[8,128]{1,0:T(8,128)S(1)}, u32[]{:S(2)}, u32[]{:S(2)}) collective-permute-start(f32[8,128]{1,0:T(8,128)S(1)} %add.28), channel_id=1, source_target_pairs={{0,4},{4,0},{8,12},{12,8},{1,5},{5,1},{9,13},{13,9},{2,6},{6,2},{1... | collective-permute-start | bytes 12296 | tf_op jit(solution)/shard_map/ppermute | solution.py:521
  73.5 4.5 %collective-permute-start.34 = (f32[8,128]{1,0:T(8,128)S(1)}, f32[8,128]{1,0:T(8,128)S(1)}, u32[]{:S(2)}, u32[]{:S(2)}) collective-permute-start(f32[8,128]{1,0:T(8,128)S(1)} %add.28), channel_id=1, source_target_pairs={{0,8},{4,12},{8,0},{12,4},{1,9},{5,13},{9,1},{13,5},{2,10},{6,14},... | collective-permute-start | bytes 12296 | tf_op jit(solution)/shard_map/ppermute | solution.py:521
  73.5 6.0 %collective-permute-start.35 = (f32[8,128]{1,0:T(8,128)S(1)}, f32[8,128]{1,0:T(8,128)S(1)}, u32[]{:S(2)}, u32[]{:S(2)}) collective-permute-start(f32[8,128]{1,0:T(8,128)S(1)} %add.28), channel_id=1, source_target_pairs={{0,12},{4,8},{8,4},{12,0},{1,13},{5,9},{9,5},{13,1},{2,14},{6,10},... | collective-permute-start | bytes 12296 | tf_op jit(solution)/shard_map/ppermute | solution.py:521
  (11 other events, 68.4 us)

commit v9 on v8

--- a/solution.py
+++ b/solution.py
@@ -270,11 +270,18 @@
         mask_ref[m * modes : (m + 1) * modes] = jnp.where(e < used, 1.0, 0.0)
 
 
-def k_prepare(m_ref, lon_ref, a_ref, b_ref, table_ref):
+def row_spacing(size):
+    return size + 8 if size // 8 % 2 == 0 else size
+
+
+def k_back_tables(lon_ref, table_ref):
+    lon_tables(lon_ref[...], *lon_ref.shape, True, table_ref)
+
+
+def k_prepare(m_ref, a_ref, b_ref):
     members, levels, rows, _ = m_ref.shape
     pairs = members // 2
-    lon_tables(lon_ref[...], *lon_ref.shape, True, table_ref)
-    apart = pairs * levels
+    apart = row_spacing(pairs * levels)
 
     def step(i, carry):
         for l in range(levels):
@@ -350,12 +357,13 @@
     )
     half = levels // 2
     low = iota((1, cells), 1) < float(cells // 2)
-    size = pairs * levels
+    apart = row_spacing(pairs * levels)
     for y in range(rows):
         profile = product3(modes_ref[...], right3(s_ref[y], 0))
         inc = None
         for m in range(pairs):
-            p = m_ref[y * size + m * levels : y * size + (m + 1) * levels, :] * profile[m * levels : (m + 1) * levels]
+            at = y * apart + m * levels
+            p = m_ref[at : at + levels, :] * profile[m * levels : (m + 1) * levels]
             inc = p if inc is None else inc + p
         inc = inc + pltpu.roll(inc, cells // 2, 1)
         out_ref[y] = jnp.where(low, inc[:half], inc[half:])
@@ -366,10 +374,11 @@
     cells = lat_ref.shape[-1]
     obs_ref = obs_ref.reshape(levels * rows, cells)
     size = pairs * levels
+    apart = row_spacing(size)
     for y in range(rows):
         inc = jnp.concatenate(both_halves(inc_ref[y] + got_ref[y]), axis=0)
         w = inc * both_halves(obs_ref[pl.ds(y, levels, stride=rows), :])[part]
-        m = m_ref[y * size : (y + 1) * size, :]
+        m = m_ref[y * apart : y * apart + size, :]
         weighted = (m.reshape(pairs, levels, cells) * w[None]).reshape(size, cells)
         g_ref[y] = product3(modes_ref[...], right3(weighted, 0)) * mask_ref[...]
     zero8 = jnp.zeros((8, cells), f32)
@@ -561,14 +570,15 @@
         cost=10**9,
     )
     inside, carried = call(
-        functools.partial(k_lon_fwd, rows, k, cells), (sds(rows, k, cells), sds(4 * rows, k)), [direction, tables]
-    )
-    *packed, back_tables = call(
-        k_prepare,
-        (sds(rows * pairs * levels, cells),) * 2
-        + (jax.ShapeDtypeStruct((rows, 3 * cells, 2 * cells), bf16),),
-        [members, lonc],
-        cost=10**9,
+        functools.partial(k_lon_fwd, rows, k, cells),
+        (sds(rows, k, cells), sds(4 * rows, k)),
+        [direction, tables],
+    )
+    packed = call(
+        k_prepare, (sds(rows * row_spacing(pairs * levels), cells),) * 2, [members], cost=10**9
+    )
+    back_tables = call(
+        k_back_tables, jax.ShapeDtypeStruct((rows, 3 * cells, 2 * cells), bf16), [lonc], cost=10**9
     )
     mask, out_modes, in_modes = call(
         functools.partial(k_modes, pairs),

time: 81.5 us -> 81.6 us (level)
  Pallas kernels: 13.6 us -> 12.5 us
  waiting for transfers between devices: 25.7 us -> 26.7 us
    ppermute x24, waiting for transfers between devices: 12.5 us -> 13.6 us  [lat_carry(): got[c][i].append(lax.ppermute(v, 'lat', [(at(h), at(h + 1))]))]
    pallas_call x28 -> x29, Pallas kernels: 13.6 us -> 12.5 us  [call(): pl.pallas_call(body, out_shape=outs, in_specs=specs or [VM] * len(ins), o...]
  transfers between devices with their start and end apart: 36 -> 36, of which waited for: 14 -> 14; matrix products, arithmetic and copies ran while one was open for 0% -> 0% of each run, Pallas kernels for 10% -> 9%
where the time goes in v9:
time: 81.6 us; the launch traced here: 81.1 us
  starting transfers between devices  39.1 us (48%)
  waiting for transfers between devices  26.7 us (33%)
  Pallas kernels  12.5 us (15%)
  between operations  1.25 us (2%)
    ppermute x24, starting transfers between devices, lat_carry(): got[c][i].append(lax.ppermute(v, 'lat', [(at(h), at(h + 1))]))  23.7 us
    ppermute x24, waiting for transfers between devices, lat_carry(): got[c][i].append(lax.ppermute(v, 'lat', [(at(h), at(h + 1))]))  13.6 us
    pallas_call x29, Pallas kernels, call(): pl.pallas_call(body, out_shape=outs, in_specs=specs or [VM] * len(ins), o...  12.5 us
    ppermute x6, starting transfers between devices, all_sum(): lax.ppermute(v, axes, [(i, i ^ m) for i in range(total)])  7.76 us
    ppermute x6, waiting for transfers between devices, all_sum(): lax.ppermute(v, axes, [(i, i ^ m) for i in range(total)])  6.69 us
    ppermute x2, starting transfers between devices, lon_exchange(): lax.ppermute(carried, 'lon', [(j, (j + sign * r) % n) for j in range(n)])  4.54 us
    ppermute x2, waiting for transfers between devices, lon_exchange(): lax.ppermute(carried, 'lon', [(j, (j + sign * r) % n) for j in range(n)])  4.32 us
    ppermute x2, starting transfers between devices, iteration(): other = lax.ppermute(v, 'mem', [(i, i ^ step) for i in range(n_mem)])  2.46 us
  transfers between devices with their start and end apart: 36, of which 14 were waited for; matrix products, arithmetic and copies ran while one was open for 0% of the time, Pallas kernels for 9%

profile of v9, /device:TPU:0, one launch (start us, length us, event | category | flops | bytes accessed | tf_op | source)
XLA Modules:
  0.0 81.1 jit_solution(11297012055912825788)
XLA Ops:
  3.0 3.0 %collective-permute-start = (f32[32,160]{1,0:T(8,128)S(1)}, f32[32,160]{1,0:T(8,128)S(1)}, u32[]{:S(2)}, u32[]{:S(2)}) collective-permute-start(f32[32,160]{1,0:T(8,128)S(1)} %get-tuple-element.33.refs_4_), channel_id=1, source_target_pairs={{0,16},{16,0},{1,17},{17,1},{2,18},{18,2},{3,19},{19,3},{4,20},{20... | collective-permute-start | bytes 61448 | tf_op jit(solution)/shard_map/ppermute | solution.py:502
  6.0 1.9 %collective-permute-done.refs_3_ = f32[32,160]{1,0:T(8,128)S(1)} collective-permute-done((f32[32,160]{1,0:T(8,128)S(1)}, f32[32,160]{1,0:T(8,128)S(1)}, u32[]{:S(2)}, u32[]{:S(2)}) %collective-permute-start) | collective-permute-done | bytes 20512 | tf_op jit(solution)/shard_map/ppermute | solution.py:502
  7.9 1.1 %shard_map.114 = (f32[8,80,128]{2,1,0:T(8,128)S(1)}, f32[8,80,128]{2,1,0:T(8,128)S(1)}, f32[4,40,128]{2,1,0:T(8,128)S(1)}, f32[4,40,128]{2,1,0:T(8,128)S(1)}, f3...) custom-call(f32[8,160,128]{2,1,0:T(8,128)S(1)} %get-tuple-element.30.refs_0_, ...), custom_call_target="tpu_custom_call" | custom-call | tf_op jit(solution)/shard_map/pallas_call | solution.py:483
  9.0 4.0 %collective-permute-start.12 = (f32[4,40,128]{2,1,0:T(8,128)S(1)}, f32[4,40,128]{2,1,0:T(8,128)S(1)}, u32[]{:S(2)}, u32[]{:S(2)}) collective-permute-start(f32[4,40,128]{2,1,0:T(8,128)S(1)} %get-tuple-element.45.carried_ref), channel_id=1, source_target_pairs={{0,4},{1,5},{2,6},{3,7},{16,20},{17,21},{18,22},{19,23}} | collective-permute-start | bytes 245768 | tf_op jit(solution)/shard_map/ppermute | solution.py:519
  13.0 1.3 %collective-permute-start.9 = (f32[4,40,128]{2,1,0:T(8,128)S(1)}, f32[4,40,128]{2,1,0:T(8,128)S(1)}, u32[]{:S(2)}, u32[]{:S(2)}) collective-permute-start(f32[4,40,128]{2,1,0:T(8,128)S(1)} %get-tuple-element.44.carried_ref), channel_id=1, source_target_pairs={{0,4},{1,5},{2,6},{3,7},{16,20},{17,21},{18,22},{19,23}} | collective-permute-start | bytes 245768 | tf_op jit(solution)/shard_map/ppermute | solution.py:519
  14.3 1.3 %collective-permute-start.4 = (f32[4,40,128]{2,1,0:T(8,128)S(1)}, f32[4,40,128]{2,1,0:T(8,128)S(1)}, u32[]{:S(2)}, u32[]{:S(2)}) collective-permute-start(f32[4,40,128]{2,1,0:T(8,128)S(1)} %get-tuple-element.39.carried_ref), channel_id=1, source_target_pairs={{0,4},{1,5},{2,6},{3,7},{16,20},{17,21},{18,22},{19,23}} | collective-permute-start | bytes 245768 | tf_op jit(solution)/shard_map/ppermute | solution.py:519
  15.6 1.3 %collective-permute-start.1 = (f32[4,40,128]{2,1,0:T(8,128)S(1)}, f32[4,40,128]{2,1,0:T(8,128)S(1)}, u32[]{:S(2)}, u32[]{:S(2)}) collective-permute-start(f32[4,40,128]{2,1,0:T(8,128)S(1)} %get-tuple-element.38.carried_ref), channel_id=1, source_target_pairs={{0,4},{1,5},{2,6},{3,7},{16,20},{17,21},{18,22},{19,23}} | collective-permute-start | bytes 245768 | tf_op jit(solution)/shard_map/ppermute | solution.py:519
  20.0 1.1 %shard_map.115 = (f32[2624,128]{1,0:T(8,128)S(1)}, f32[2624,128]{1,0:T(8,128)S(1)}) custom-call(bf16[20,32,8,128]{3,2,1,0:T(8,128)(2,1)S(1)} %copy-done.4), custom_call_target="tpu_custom_call" | custom-call | flops 1000000000 | bytes 1000 | tf_op jit(solution)/shard_map/pallas_call | solution.py:483
  24.0 1.6 %shard_map.116 = (f32[80,128]{1,0:T(8,128)S(1)}, bf16[320,240]{1,0:T(8,128)(2,1)S(1)}, bf16[80,960]{1,0:T(8,128)(2,1)S(1)}) custom-call(f32[8,32]{1,0:T(8,128)S(1)} %copy-done.5, s32[20]{0:T(128)S(1)} %copy-done.6), custom_call_target="tpu_custom_call" | custom-call | flops 1000000000 | bytes 1000 | tf_op jit(solution)/shard_map/pallas_call | solution.py:483
  25.7 0.9 %shard_map.127 = f32[8,16,128]{2,1,0:T(8,128)S(1)} custom-call(f32[8,80,128]{2,1,0:T(8,128)S(1)} %get-tuple-element.42.refs_0_, f32[2,8,128]{2,1,0:T(8,128)S(1)} %get-tuple-element.32.refs_2_.lat_ref.refs_1_.refs_6_, f32[2624,128]{1,0:T(8,128)S(1)} %get-tuple-element.43.refs_2_.refs_3_, f32[80,128]{1,0:T(8,128)S(1)} %get-tuple-element.36.refs_3_.refs_4_, ...), custom_call_target="tpu_custom_call" | custom-call | tf_op jit(solution)/shard_map/pallas_call | solution.py:483
  26.7 0.9 %shard_map.121 = f32[8,16,128]{2,1,0:T(8,128)S(1)} custom-call(f32[8,80,128]{2,1,0:T(8,128)S(1)} %get-tuple-element.34.refs_0_, f32[2,8,128]{2,1,0:T(8,128)S(1)} %get-tuple-element.32.refs_2_.lat_ref.refs_1_.refs_6_, f32[2624,128]{1,0:T(8,128)S(1)} %get-tuple-element.35.refs_2_.refs_3_, f32[80,128]{1,0:T(8,128)S(1)} %get-tuple-element.36.refs_3_.refs_4_, ...), custom_call_target="tpu_custom_call" | custom-call | tf_op jit(solution)/shard_map/pallas_call | solution.py:483
  28.2 1.6 %collective-permute-start.16 = (f32[8,16,128]{2,1,0:T(8,128)S(1)}, f32[8,16,128]{2,1,0:T(8,128)S(1)}, u32[]{:S(2)}, u32[]{:S(2)}) collective-permute-start(f32[8,16,128]{2,1,0:T(8,128)S(1)} %add.25.refs_0_), channel_id=1, source_target_pairs={{0,2},{1,3},{2,0},{3,1},{4,6},{5,7},{6,4},{7,5},{8,10},{9,11},{10,... | collective-permute-start | bytes 196616 | tf_op jit(solution)/shard_map/ppermute | solution.py:618
  29.8 0.9 %collective-permute-start.8 = (f32[8,16,128]{2,1,0:T(8,128)S(1)}, f32[8,16,128]{2,1,0:T(8,128)S(1)}, u32[]{:S(2)}, u32[]{:S(2)}) collective-permute-start(f32[8,16,128]{2,1,0:T(8,128)S(1)} %add.24.refs_0_), channel_id=1, source_target_pairs={{0,2},{1,3},{2,0},{3,1},{4,6},{5,7},{6,4},{7,5},{8,10},{9,11},{10,... | collective-permute-start | bytes 196616 | tf_op jit(solution)/shard_map/ppermute | solution.py:618
  30.6 2.2 %collective-permute-done.16.refs_1_ = f32[8,16,128]{2,1,0:T(8,128)S(1)} collective-permute-done((f32[8,16,128]{2,1,0:T(8,128)S(1)}, f32[8,16,128]{2,1,0:T(8,128)S(1)}, u32[]{:S(2)}, u32[]{:S(2)}) %collective-permute-start.16) | collective-permute-done | bytes 65568 | tf_op jit(solution)/shard_map/ppermute | solution.py:618
  40.2 1.3 %collective-permute-start.28 = (f32[4,40,128]{2,1,0:T(8,128)S(1)}, f32[4,40,128]{2,1,0:T(8,128)S(1)}, u32[]{:S(2)}, u32[]{:S(2)}) collective-permute-start(f32[4,40,128]{2,1,0:T(8,128)S(1)} %shard_map.137), channel_id=1, source_target_pairs={{4,0},{5,1},{6,2},{7,3},{20,16},{21,17},{22,18},{23,19}} | collective-permute-start | bytes 245768 | tf_op jit(solution)/shard_map/ppermute | solution.py:519
  41.5 1.3 %collective-permute-start.25 = (f32[4,40,128]{2,1,0:T(8,128)S(1)}, f32[4,40,128]{2,1,0:T(8,128)S(1)}, u32[]{:S(2)}, u32[]{:S(2)}) collective-permute-start(f32[4,40,128]{2,1,0:T(8,128)S(1)} %shard_map.135), channel_id=1, source_target_pairs={{4,0},{5,1},{6,2},{7,3},{20,16},{21,17},{22,18},{23,19}} | collective-permute-start | bytes 245768 | tf_op jit(solution)/shard_map/ppermute | solution.py:519
  42.9 1.3 %collective-permute-start.22 = (f32[4,40,128]{2,1,0:T(8,128)S(1)}, f32[4,40,128]{2,1,0:T(8,128)S(1)}, u32[]{:S(2)}, u32[]{:S(2)}) collective-permute-start(f32[4,40,128]{2,1,0:T(8,128)S(1)} %shard_map.133), channel_id=1, source_target_pairs={{4,0},{5,1},{6,2},{7,3},{20,16},{21,17},{22,18},{23,19}} | collective-permute-start | bytes 245768 | tf_op jit(solution)/shard_map/ppermute | solution.py:519
  44.2 1.3 %collective-permute-start.19 = (f32[4,40,128]{2,1,0:T(8,128)S(1)}, f32[4,40,128]{2,1,0:T(8,128)S(1)}, u32[]{:S(2)}, u32[]{:S(2)}) collective-permute-start(f32[4,40,128]{2,1,0:T(8,128)S(1)} %shard_map.131), channel_id=1, source_target_pairs={{4,0},{5,1},{6,2},{7,3},{20,16},{21,17},{22,18},{23,19}} | collective-permute-start | bytes 245768 | tf_op jit(solution)/shard_map/ppermute | solution.py:519
  45.9 8.4 %collective-permute-done.28.refs_15_ = f32[4,40,128]{2,1,0:T(8,128)S(1)} collective-permute-done((f32[4,40,128]{2,1,0:T(8,128)S(1)}, f32[4,40,128]{2,1,0:T(8,128)S(1)}, u32[]{:S(2)}, u32[]{:S(2)}) %collective-permute-start.28) | collective-permute-done | bytes 81952 | tf_op jit(solution)/shard_map/ppermute | solution.py:519
  54.3 3.0 %collective-permute-done.25.refs_12_ = f32[4,40,128]{2,1,0:T(8,128)S(1)} collective-permute-done((f32[4,40,128]{2,1,0:T(8,128)S(1)}, f32[4,40,128]{2,1,0:T(8,128)S(1)}, u32[]{:S(2)}, u32[]{:S(2)}) %collective-permute-start.25) | collective-permute-done | bytes 81952 | tf_op jit(solution)/shard_map/ppermute | solution.py:519
  58.2 0.9 %collective-permute-done.19.refs_6_ = f32[4,40,128]{2,1,0:T(8,128)S(1)} collective-permute-done((f32[4,40,128]{2,1,0:T(8,128)S(1)}, f32[4,40,128]{2,1,0:T(8,128)S(1)}, u32[]{:S(2)}, u32[]{:S(2)}) %collective-permute-start.19) | collective-permute-done | bytes 81952 | tf_op jit(solution)/shard_map/ppermute | solution.py:519
  59.1 1.2 %shard_map.138 = (f32[8,160,128]{2,1,0:T(8,128)S(1)}, f32[32,160]{1,0:T(8,128)S(1)}) custom-call(f32[8,80,128]{2,1,0:T(8,128)S(1)} %get-tuple-element.41.refs_0_, f32[8,80,128]{2,1,0:T(8,128)S(1)} %get-tuple-element.46.refs_1_, f32[2,8,128]{2,1,0:T(8,128)S(1)} %get-tuple-element.32.refs_2_.lat_ref.refs_1_.refs_6_, ...), custom_call_target="tpu_custom_call" | custom-call | tf_op jit(solution)/shard_map/pallas_call | solution.py:483
  60.4 1.5 %collective-permute-start.29 = (f32[32,160]{1,0:T(8,128)S(1)}, f32[32,160]{1,0:T(8,128)S(1)}, u32[]{:S(2)}, u32[]{:S(2)}) collective-permute-start(f32[32,160]{1,0:T(8,128)S(1)} %get-tuple-element.52.refs_5_), channel_id=1, source_target_pairs={{0,16},{16,0},{1,17},{17,1},{2,18},{18,2},{3,19},{19,3},{4,20},{20... | collective-permute-start | bytes 61448 | tf_op jit(solution)/shard_map/ppermute | solution.py:502
  61.9 2.4 %collective-permute-done.29.refs_4_ = f32[32,160]{1,0:T(8,128)S(1)} collective-permute-done((f32[32,160]{1,0:T(8,128)S(1)}, f32[32,160]{1,0:T(8,128)S(1)}, u32[]{:S(2)}, u32[]{:S(2)}) %collective-permute-start.29) | collective-permute-done | bytes 20512 | tf_op jit(solution)/shard_map/ppermute | solution.py:502
  65.2 1.2 %collective-permute-done.30 = f32[8,128]{1,0:T(8,128)S(1)} collective-permute-done((f32[8,128]{1,0:T(8,128)S(1)}, f32[8,128]{1,0:T(8,128)S(1)}, u32[]{:S(2)}, u32[]{:S(2)}) %collective-permute-start.30) | collective-permute-done | bytes 4128 | tf_op jit(solution)/shard_map/ppermute | solution.py:530
  66.3 1.8 %collective-permute-start.31 = (f32[8,128]{1,0:T(8,128)S(1)}, f32[8,128]{1,0:T(8,128)S(1)}, u32[]{:S(2)}, u32[]{:S(2)}) collective-permute-start(f32[8,128]{1,0:T(8,128)S(1)} %add.26), channel_id=1, source_target_pairs={{0,2},{1,3},{2,0},{3,1},{4,6},{5,7},{6,4},{7,5},{8,10},{9,11},{10,... | collective-permute-start | bytes 12296 | tf_op jit(solution)/shard_map/ppermute | solution.py:530
  68.1 1.8 %collective-permute-done.31 = f32[8,128]{1,0:T(8,128)S(1)} collective-permute-done((f32[8,128]{1,0:T(8,128)S(1)}, f32[8,128]{1,0:T(8,128)S(1)}, u32[]{:S(2)}, u32[]{:S(2)}) %collective-permute-start.31) | collective-permute-done | bytes 4128 | tf_op jit(solution)/shard_map/ppermute | solution.py:530
  69.9 1.5 %collective-permute-start.32 = (f32[8,128]{1,0:T(8,128)S(1)}, f32[8,128]{1,0:T(8,128)S(1)}, u32[]{:S(2)}, u32[]{:S(2)}) collective-permute-start(f32[8,128]{1,0:T(8,128)S(1)} %add.27), channel_id=1, source_target_pairs={{0,16},{16,0},{1,17},{17,1},{2,18},{18,2},{3,19},{19,3},{4,20},{20... | collective-permute-start | bytes 12296 | tf_op jit(solution)/shard_map/ppermute | solution.py:530
  71.4 2.1 %collective-permute-done.32 = f32[8,128]{1,0:T(8,128)S(1)} collective-permute-done((f32[8,128]{1,0:T(8,128)S(1)}, f32[8,128]{1,0:T(8,128)S(1)}, u32[]{:S(2)}, u32[]{:S(2)}) %collective-permute-start.32) | collective-permute-done | bytes 4128 | tf_op jit(solution)/shard_map/ppermute | solution.py:530
  73.5 4.4 %collective-permute-start.35 = (f32[8,128]{1,0:T(8,128)S(1)}, f32[8,128]{1,0:T(8,128)S(1)}, u32[]{:S(2)}, u32[]{:S(2)}) collective-permute-start(f32[8,128]{1,0:T(8,128)S(1)} %add.28), channel_id=1, source_target_pairs={{0,12},{4,8},{8,4},{12,0},{1,13},{5,9},{9,5},{13,1},{2,14},{6,10},... | collective-permute-start | bytes 12296 | tf_op jit(solution)/shard_map/ppermute | solution.py:530
  78.0 1.5 %collective-permute-done.35 = f32[8,128]{1,0:T(8,128)S(1)} collective-permute-done((f32[8,128]{1,0:T(8,128)S(1)}, f32[8,128]{1,0:T(8,128)S(1)}, u32[]{:S(2)}, u32[]{:S(2)}) %collective-permute-start.35) | collective-permute-done | bytes 4128 | tf_op jit(solution)/shard_map/ppermute | solution.py:530
  79.6 1.5 %shard_map.140 = (f32[160,8,128]{2,1,0:T(8,128)}, f32[160,8,128]{2,1,0:T(8,128)}, f32[160,8,128]{2,1,0:T(8,128)}) custom-call(f32[8,128]{1,0:T(8,128)S(1)} %add_add_fusion.sums_ref, f32[160,8,128]{2,1,0:T(8,128)S(1)} %copy-done.2, f32[160,8,128]{2,1,0:T(8,128)S(1)} %copy-done.1, f32[160,8,128]{2,1,0:T(8,128)S(1)} %copy-done, f32[160,8,128]{2,1,0:T(8,128)S(1)} %bitcast.2), custom_call_target="tpu_custom_call" | custom-call | tf_op jit(solution)/shard_map/pallas_call | solution.py:483
  (90 shorter events, 18.3 us)
Async XLA Ops:
  3.0 4.9 %collective-permute-start = (f32[32,160]{1,0:T(8,128)S(1)}, f32[32,160]{1,0:T(8,128)S(1)}, u32[]{:S(2)}, u32[]{:S(2)}) collective-permute-start(f32[32,160]{1,0:T(8,128)S(1)} %get-tuple-element.33.refs_4_), channel_id=1, source_target_pairs={{0,16},{16,0},{1,17},{17,1},{2,18},{18,2},{3,19},{19,3},{4,20},{20... | collective-permute-start | bytes 61448 | tf_op jit(solution)/shard_map/ppermute | solution.py:502
  9.0 7.9 %collective-permute-start.12 = (f32[4,40,128]{2,1,0:T(8,128)S(1)}, f32[4,40,128]{2,1,0:T(8,128)S(1)}, u32[]{:S(2)}, u32[]{:S(2)}) collective-permute-start(f32[4,40,128]{2,1,0:T(8,128)S(1)} %get-tuple-element.45.carried_ref), channel_id=1, source_target_pairs={{0,4},{1,5},{2,6},{3,7},{16,20},{17,21},{18,22},{19,23}} | collective-permute-start | bytes 245768 | tf_op jit(solution)/shard_map/ppermute | solution.py:519
  13.0 4.6 %collective-permute-start.9 = (f32[4,40,128]{2,1,0:T(8,128)S(1)}, f32[4,40,128]{2,1,0:T(8,128)S(1)}, u32[]{:S(2)}, u32[]{:S(2)}) collective-permute-start(f32[4,40,128]{2,1,0:T(8,128)S(1)} %get-tuple-element.44.carried_ref), channel_id=1, source_target_pairs={{0,4},{1,5},{2,6},{3,7},{16,20},{17,21},{18,22},{19,23}} | collective-permute-start | bytes 245768 | tf_op jit(solution)/shard_map/ppermute | solution.py:519
  14.3 4.1 %collective-permute-start.4 = (f32[4,40,128]{2,1,0:T(8,128)S(1)}, f32[4,40,128]{2,1,0:T(8,128)S(1)}, u32[]{:S(2)}, u32[]{:S(2)}) collective-permute-start(f32[4,40,128]{2,1,0:T(8,128)S(1)} %get-tuple-element.39.carried_ref), channel_id=1, source_target_pairs={{0,4},{1,5},{2,6},{3,7},{16,20},{17,21},{18,22},{19,23}} | collective-permute-start | bytes 245768 | tf_op jit(solution)/shard_map/ppermute | solution.py:519
  15.6 3.7 %collective-permute-start.1 = (f32[4,40,128]{2,1,0:T(8,128)S(1)}, f32[4,40,128]{2,1,0:T(8,128)S(1)}, u32[]{:S(2)}, u32[]{:S(2)}) collective-permute-start(f32[4,40,128]{2,1,0:T(8,128)S(1)} %get-tuple-element.38.carried_ref), channel_id=1, source_target_pairs={{0,4},{1,5},{2,6},{3,7},{16,20},{17,21},{18,22},{19,23}} | collective-permute-start | bytes 245768 | tf_op jit(solution)/shard_map/ppermute | solution.py:519
  16.9 4.2 %collective-permute-start.13 = (f32[4,40,128]{2,1,0:T(8,128)S(1)}, f32[4,40,128]{2,1,0:T(8,128)S(1)}, u32[]{:S(2)}, u32[]{:S(2)}) collective-permute-start(f32[4,40,128]{2,1,0:T(8,128)S(1)} %shard_map.125), channel_id=1, source_target_pairs={{4,8},{5,9},{6,10},{7,11},{20,24},{21,25},{22,26},{23,27}} | collective-permute-start | bytes 245768 | tf_op jit(solution)/shard_map/ppermute | solution.py:519
  17.6 4.2 %collective-permute-start.10 = (f32[4,40,128]{2,1,0:T(8,128)S(1)}, f32[4,40,128]{2,1,0:T(8,128)S(1)}, u32[]{:S(2)}, u32[]{:S(2)}) collective-permute-start(f32[4,40,128]{2,1,0:T(8,128)S(1)} %shard_map.123), channel_id=1, source_target_pairs={{4,8},{5,9},{6,10},{7,11},{20,24},{21,25},{22,26},{23,27}} | collective-permute-start | bytes 245768 | tf_op jit(solution)/shard_map/ppermute | solution.py:519
  18.5 4.1 %collective-permute-start.5 = (f32[4,40,128]{2,1,0:T(8,128)S(1)}, f32[4,40,128]{2,1,0:T(8,128)S(1)}, u32[]{:S(2)}, u32[]{:S(2)}) collective-permute-start(f32[4,40,128]{2,1,0:T(8,128)S(1)} %shard_map.119), channel_id=1, source_target_pairs={{4,8},{5,9},{6,10},{7,11},{20,24},{21,25},{22,26},{23,27}} | collective-permute-start | bytes 245768 | tf_op jit(solution)/shard_map/ppermute | solution.py:519
  19.4 3.9 %collective-permute-start.2 = (f32[4,40,128]{2,1,0:T(8,128)S(1)}, f32[4,40,128]{2,1,0:T(8,128)S(1)}, u32[]{:S(2)}, u32[]{:S(2)}) collective-permute-start(f32[4,40,128]{2,1,0:T(8,128)S(1)} %shard_map.117), channel_id=1, source_target_pairs={{4,8},{5,9},{6,10},{7,11},{20,24},{21,25},{22,26},{23,27}} | collective-permute-start | bytes 245768 | tf_op jit(solution)/shard_map/ppermute | solution.py:519
  21.2 4.5 %collective-permute-start.14 = (f32[4,40,128]{2,1,0:T(8,128)S(1)}, f32[4,40,128]{2,1,0:T(8,128)S(1)}, u32[]{:S(2)}, u32[]{:S(2)}) collective-permute-start(f32[4,40,128]{2,1,0:T(8,128)S(1)} %shard_map.126), channel_id=1, source_target_pairs={{8,12},{9,13},{10,14},{11,15},{24,28},{25,29},{26,30},{27,31}} | collective-permute-start | bytes 245768 | tf_op jit(solution)/shard_map/ppermute | solution.py:519
  21.9 3.8 %collective-permute-start.11 = (f32[4,40,128]{2,1,0:T(8,128)S(1)}, f32[4,40,128]{2,1,0:T(8,128)S(1)}, u32[]{:S(2)}, u32[]{:S(2)}) collective-permute-start(f32[4,40,128]{2,1,0:T(8,128)S(1)} %shard_map.124), channel_id=1, source_target_pairs={{8,12},{9,13},{10,14},{11,15},{24,28},{25,29},{26,30},{27,31}} | collective-permute-start | bytes 245768 | tf_op jit(solution)/shard_map/ppermute | solution.py:519
  22.6 4.1 %collective-permute-start.6 = (f32[4,40,128]{2,1,0:T(8,128)S(1)}, f32[4,40,128]{2,1,0:T(8,128)S(1)}, u32[]{:S(2)}, u32[]{:S(2)}) collective-permute-start(f32[4,40,128]{2,1,0:T(8,128)S(1)} %shard_map.120), channel_id=1, source_target_pairs={{8,12},{9,13},{10,14},{11,15},{24,28},{25,29},{26,30},{27,31}} | collective-permute-start | bytes 245768 | tf_op jit(solution)/shard_map/ppermute | solution.py:519
  23.3 3.4 %collective-permute-start.3 = (f32[4,40,128]{2,1,0:T(8,128)S(1)}, f32[4,40,128]{2,1,0:T(8,128)S(1)}, u32[]{:S(2)}, u32[]{:S(2)}) collective-permute-start(f32[4,40,128]{2,1,0:T(8,128)S(1)} %shard_map.118), channel_id=1, source_target_pairs={{8,12},{9,13},{10,14},{11,15},{24,28},{25,29},{26,30},{27,31}} | collective-permute-start | bytes 245768 | tf_op jit(solution)/shard_map/ppermute | solution.py:519
  28.2 4.6 %collective-permute-start.16 = (f32[8,16,128]{2,1,0:T(8,128)S(1)}, f32[8,16,128]{2,1,0:T(8,128)S(1)}, u32[]{:S(2)}, u32[]{:S(2)}) collective-permute-start(f32[8,16,128]{2,1,0:T(8,128)S(1)} %add.25.refs_0_), channel_id=1, source_target_pairs={{0,2},{1,3},{2,0},{3,1},{4,6},{5,7},{6,4},{7,5},{8,10},{9,11},{10,... | collective-permute-start | bytes 196616 | tf_op jit(solution)/shard_map/ppermute | solution.py:618
  29.8 5.3 %collective-permute-start.8 = (f32[8,16,128]{2,1,0:T(8,128)S(1)}, f32[8,16,128]{2,1,0:T(8,128)S(1)}, u32[]{:S(2)}, u32[]{:S(2)}) collective-permute-start(f32[8,16,128]{2,1,0:T(8,128)S(1)} %add.24.refs_0_), channel_id=1, source_target_pairs={{0,2},{1,3},{2,0},{3,1},{4,6},{5,7},{6,4},{7,5},{8,10},{9,11},{10,... | collective-permute-start | bytes 196616 | tf_op jit(solution)/shard_map/ppermute | solution.py:618
  33.7 3.6 %collective-permute-start.26 = (f32[4,40,128]{2,1,0:T(8,128)S(1)}, f32[4,40,128]{2,1,0:T(8,128)S(1)}, u32[]{:S(2)}, u32[]{:S(2)}) collective-permute-start(f32[4,40,128]{2,1,0:T(8,128)S(1)} %get-tuple-element.50.carried_ref), channel_id=1, source_target_pairs={{12,8},{13,9},{14,10},{15,11},{28,24},{29,25},{30,26},{31,27}} | collective-permute-start | bytes 245768 | tf_op jit(solution)/shard_map/ppermute | solution.py:519
  34.4 3.6 %collective-permute-start.23 = (f32[4,40,128]{2,1,0:T(8,128)S(1)}, f32[4,40,128]{2,1,0:T(8,128)S(1)}, u32[]{:S(2)}, u32[]{:S(2)}) collective-permute-start(f32[4,40,128]{2,1,0:T(8,128)S(1)} %get-tuple-element.49.carried_ref), channel_id=1, source_target_pairs={{12,8},{13,9},{14,10},{15,11},{28,24},{29,25},{30,26},{31,27}} | collective-permute-start | bytes 245768 | tf_op jit(solution)/shard_map/ppermute | solution.py:519
  36.6 2.8 %collective-permute-start.17 = (f32[4,40,128]{2,1,0:T(8,128)S(1)}, f32[4,40,128]{2,1,0:T(8,128)S(1)}, u32[]{:S(2)}, u32[]{:S(2)}) collective-permute-start(f32[4,40,128]{2,1,0:T(8,128)S(1)} %get-tuple-element.47.carried_ref), channel_id=1, source_target_pairs={{12,8},{13,9},{14,10},{15,11},{28,24},{29,25},{30,26},{31,27}} | collective-permute-start | bytes 245768 | tf_op jit(solution)/shard_map/ppermute | solution.py:519
  37.3 2.8 %collective-permute-start.27 = (f32[4,40,128]{2,1,0:T(8,128)S(1)}, f32[4,40,128]{2,1,0:T(8,128)S(1)}, u32[]{:S(2)}, u32[]{:S(2)}) collective-permute-start(f32[4,40,128]{2,1,0:T(8,128)S(1)} %shard_map.136), channel_id=1, source_target_pairs={{8,4},{9,5},{10,6},{11,7},{24,20},{25,21},{26,22},{27,23}} | collective-permute-start | bytes 245768 | tf_op jit(solution)/shard_map/ppermute | solution.py:519
  38.0 3.5 %collective-permute-start.24 = (f32[4,40,128]{2,1,0:T(8,128)S(1)}, f32[4,40,128]{2,1,0:T(8,128)S(1)}, u32[]{:S(2)}, u32[]{:S(2)}) collective-permute-start(f32[4,40,128]{2,1,0:T(8,128)S(1)} %shard_map.134), channel_id=1, source_target_pairs={{8,4},{9,5},{10,6},{11,7},{24,20},{25,21},{26,22},{27,23}} | collective-permute-start | bytes 245768 | tf_op jit(solution)/shard_map/ppermute | solution.py:519
  38.8 4.1 %collective-permute-start.21 = (f32[4,40,128]{2,1,0:T(8,128)S(1)}, f32[4,40,128]{2,1,0:T(8,128)S(1)}, u32[]{:S(2)}, u32[]{:S(2)}) collective-permute-start(f32[4,40,128]{2,1,0:T(8,128)S(1)} %shard_map.132), channel_id=1, source_target_pairs={{8,4},{9,5},{10,6},{11,7},{24,20},{25,21},{26,22},{27,23}} | collective-permute-start | bytes 245768 | tf_op jit(solution)/shard_map/ppermute | solution.py:519
  39.5 4.7 %collective-permute-start.18 = (f32[4,40,128]{2,1,0:T(8,128)S(1)}, f32[4,40,128]{2,1,0:T(8,128)S(1)}, u32[]{:S(2)}, u32[]{:S(2)}) collective-permute-start(f32[4,40,128]{2,1,0:T(8,128)S(1)} %shard_map.130), channel_id=1, source_target_pairs={{8,4},{9,5},{10,6},{11,7},{24,20},{25,21},{26,22},{27,23}} | collective-permute-start | bytes 245768 | tf_op jit(solution)/shard_map/ppermute | solution.py:519
  40.2 14.1 %collective-permute-start.28 = (f32[4,40,128]{2,1,0:T(8,128)S(1)}, f32[4,40,128]{2,1,0:T(8,128)S(1)}, u32[]{:S(2)}, u32[]{:S(2)}) collective-permute-start(f32[4,40,128]{2,1,0:T(8,128)S(1)} %shard_map.137), channel_id=1, source_target_pairs={{4,0},{5,1},{6,2},{7,3},{20,16},{21,17},{22,18},{23,19}} | collective-permute-start | bytes 245768 | tf_op jit(solution)/shard_map/ppermute | solution.py:519
  41.5 15.8 %collective-permute-start.25 = (f32[4,40,128]{2,1,0:T(8,128)S(1)}, f32[4,40,128]{2,1,0:T(8,128)S(1)}, u32[]{:S(2)}, u32[]{:S(2)}) collective-permute-start(f32[4,40,128]{2,1,0:T(8,128)S(1)} %shard_map.135), channel_id=1, source_target_pairs={{4,0},{5,1},{6,2},{7,3},{20,16},{21,17},{22,18},{23,19}} | collective-permute-start | bytes 245768 | tf_op jit(solution)/shard_map/ppermute | solution.py:519
  42.9 15.3 %collective-permute-start.22 = (f32[4,40,128]{2,1,0:T(8,128)S(1)}, f32[4,40,128]{2,1,0:T(8,128)S(1)}, u32[]{:S(2)}, u32[]{:S(2)}) collective-permute-start(f32[4,40,128]{2,1,0:T(8,128)S(1)} %shard_map.133), channel_id=1, source_target_pairs={{4,0},{5,1},{6,2},{7,3},{20,16},{21,17},{22,18},{23,19}} | collective-permute-start | bytes 245768 | tf_op jit(solution)/shard_map/ppermute | solution.py:519
  44.2 14.9 %collective-permute-start.19 = (f32[4,40,128]{2,1,0:T(8,128)S(1)}, f32[4,40,128]{2,1,0:T(8,128)S(1)}, u32[]{:S(2)}, u32[]{:S(2)}) collective-permute-start(f32[4,40,128]{2,1,0:T(8,128)S(1)} %shard_map.131), channel_id=1, source_target_pairs={{4,0},{5,1},{6,2},{7,3},{20,16},{21,17},{22,18},{23,19}} | collective-permute-start | bytes 245768 | tf_op jit(solution)/shard_map/ppermute | solution.py:519
  60.4 4.0 %collective-permute-start.29 = (f32[32,160]{1,0:T(8,128)S(1)}, f32[32,160]{1,0:T(8,128)S(1)}, u32[]{:S(2)}, u32[]{:S(2)}) collective-permute-start(f32[32,160]{1,0:T(8,128)S(1)} %get-tuple-element.52.refs_5_), channel_id=1, source_target_pairs={{0,16},{16,0},{1,17},{17,1},{2,18},{18,2},{3,19},{19,3},{4,20},{20... | collective-permute-start | bytes 61448 | tf_op jit(solution)/shard_map/ppermute | solution.py:502
  66.3 3.6 %collective-permute-start.31 = (f32[8,128]{1,0:T(8,128)S(1)}, f32[8,128]{1,0:T(8,128)S(1)}, u32[]{:S(2)}, u32[]{:S(2)}) collective-permute-start(f32[8,128]{1,0:T(8,128)S(1)} %add.26), channel_id=1, source_target_pairs={{0,2},{1,3},{2,0},{3,1},{4,6},{5,7},{6,4},{7,5},{8,10},{9,11},{10,... | collective-permute-start | bytes 12296 | tf_op jit(solution)/shard_map/ppermute | solution.py:530
  69.9 3.6 %collective-permute-start.32 = (f32[8,128]{1,0:T(8,128)S(1)}, f32[8,128]{1,0:T(8,128)S(1)}, u32[]{:S(2)}, u32[]{:S(2)}) collective-permute-start(f32[8,128]{1,0:T(8,128)S(1)} %add.27), channel_id=1, source_target_pairs={{0,16},{16,0},{1,17},{17,1},{2,18},{18,2},{3,19},{19,3},{4,20},{20... | collective-permute-start | bytes 12296 | tf_op jit(solution)/shard_map/ppermute | solution.py:530
  73.5 4.4 %collective-permute-start.33 = (f32[8,128]{1,0:T(8,128)S(1)}, f32[8,128]{1,0:T(8,128)S(1)}, u32[]{:S(2)}, u32[]{:S(2)}) collective-permute-start(f32[8,128]{1,0:T(8,128)S(1)} %add.28), channel_id=1, source_target_pairs={{0,4},{4,0},{8,12},{12,8},{1,5},{5,1},{9,13},{13,9},{2,6},{6,2},{1... | collective-permute-start | bytes 12296 | tf_op jit(solution)/shard_map/ppermute | solution.py:530
  73.5 4.5 %collective-permute-start.34 = (f32[8,128]{1,0:T(8,128)S(1)}, f32[8,128]{1,0:T(8,128)S(1)}, u32[]{:S(2)}, u32[]{:S(2)}) collective-permute-start(f32[8,128]{1,0:T(8,128)S(1)} %add.28), channel_id=1, source_target_pairs={{0,8},{4,12},{8,0},{12,4},{1,9},{5,13},{9,1},{13,5},{2,10},{6,14},... | collective-permute-start | bytes 12296 | tf_op jit(solution)/shard_map/ppermute | solution.py:530
  73.5 6.0 %collective-permute-start.35 = (f32[8,128]{1,0:T(8,128)S(1)}, f32[8,128]{1,0:T(8,128)S(1)}, u32[]{:S(2)}, u32[]{:S(2)}) collective-permute-start(f32[8,128]{1,0:T(8,128)S(1)} %add.28), channel_id=1, source_target_pairs={{0,12},{4,8},{8,4},{12,0},{1,13},{5,9},{9,5},{13,1},{2,14},{6,10},... | collective-permute-start | bytes 12296 | tf_op jit(solution)/shard_map/ppermute | solution.py:530
  (11 other events, 65.7 us)
